TPU v7x, 32 devices: a whole 2x2x4 slice. The times are simulated.
32 devices in a mesh: dp: 2 (over x), fsdp: 16 (over z, y, core).
Axes of the slice: x: 2, y: 2, z: 4, core: 2. Of those that a mesh axis runs over, the one named last changes fastest.
Arguments:
- tokens: bfloat16 [16384, 768], P(('dp', 'fsdp')), may hold values from -6 to 6
- cotangent: bfloat16 [16384, 768], P(('dp', 'fsdp')), may hold values from -6 to 6
- image_ids: int32 [16384], P(('dp', 'fsdp')), may hold values from 0 to 2, as said below
- in_weight: float32 [768, 5376], P('fsdp'), may hold values from -0.21875 to 0.21875
- out_weight: float32 [3840, 768], P('fsdp'), may hold values from -1.5 to 1.5
- vectors: float32 [4, 768], P(None, 'fsdp'), may hold values from -1.5 to 1.5
- in_moment: float32 [768, 5376], P('fsdp'), may hold values from -0.66 to 0.66
- out_moment: float32 [3840, 768], P('fsdp'), may hold values from -0.66 to 0.66
- vec_moment: float32 [4, 768], P(None, 'fsdp'), may hold values from -0.66 to 0.66
- in_second: float32 [768, 5376], P('fsdp'), may hold values from 0.01 to 0.1
- out_second: float32 [3840, 768], P('fsdp'), may hold values from 0.01 to 0.1
- vec_second: float32 [4, 768], P(None, 'fsdp'), may hold values from 0.01 to 0.1
Outputs:
- activations: bfloat16 [16384, 768], P(('dp', 'fsdp'))
- input_grad: float32 [16384, 768], P(('dp', 'fsdp'))
- in_grad: float32 [768, 5376], P('fsdp')
- out_grad: float32 [3840, 768], P('fsdp')
- vec_grad: float32 [4, 768], P(None, 'fsdp')
- grad_norm: float32 [], replicated
- in_update: float32 [768, 5376], P('fsdp')
- out_update: float32 [3840, 768], P('fsdp')
- vec_update: float32 [4, 768], P(None, 'fsdp')
- in_mean: float32 [768, 5376], P('fsdp')
- out_mean: float32 [3840, 768], P('fsdp')
- vec_mean: float32 [4, 768], P(None, 'fsdp')
- in_square: float32 [768, 5376], P('fsdp')
- out_square: float32 [3840, 768], P('fsdp')
- vec_square: float32 [4, 768], P(None, 'fsdp')
Inputs may be any that keep to these rules, and one draw needn't show every extreme that they name: `image_ids`: tokens of one image all lie within one device's 512 rows, and ids never decrease along a device's rows. One eighth of the devices each hold a single image of 512 tokens with id 0; every other device holds images of 196 tokens numbered 0, 1, 2, ... followed by one shorter image.
All inputs are finite; a program needn't handle non-finite values.
Results may differ from a plain program's by a relative error of at most 0.02.
Values may be sent and summed in bfloat16 or wider, within the bound.
No kernel may reach another device: no remote copies, remote signals or barrier semaphores. Data moves between devices by JAX's collectives and lax.ppermute only.
A program may use at most 128 MiB of HBM per device.

v0:
```python
import math

import jax
import jax.numpy as jnp
from jax import lax
from jax.sharding import PartitionSpec as P

D = 768
H = 12
HD = 64
ADAM_STEP = 10
PARAMS = 7080960


beta_one = 0.9
beta_two = 0.95
learning = 0.03
decay_rate = 0.1
epsilon = 1e-08
norm_eps = 1e-06
masked = -1e30


def row_norm(values):
    centre = values - jnp.mean(values, axis=-1, keepdims=True)
    spread = jnp.mean(centre * centre, axis=-1, keepdims=True)
    return centre * lax.rsqrt(spread + norm_eps)


def input_norm(rows, gain):
    return row_norm(rows) * gain


def head_norm(raw, gain, factor):
    heads = raw.reshape(raw.shape[0], H, HD)
    return row_norm(heads) * gain.reshape(H, HD) * factor


def activation(values):
    return jax.nn.gelu(values, approximate=True)


def attention_forward(query_lo, key_lo, value_lo, image_ids):
    count = query_lo.shape[0]
    block = min(512, count)
    blocks = count // block

    def one_block(pair):
        query_block, ids_block = pair
        scores = jnp.einsum("qhd,khd->hqk", query_block, key_lo, preferred_element_type=jnp.float32)
        same = (ids_block[:, None] == image_ids[None, :])[None]
        scores = jnp.where(same, scores, masked)
        largest = jnp.max(scores, axis=-1, keepdims=True)
        raised = jnp.exp(scores - largest)
        totals = jnp.sum(raised, axis=-1, keepdims=True)
        probs_lo = (raised / totals).astype(jnp.bfloat16)
        attended = jnp.einsum(
            "hqk,khd->qhd", probs_lo, value_lo, preferred_element_type=jnp.float32
        )
        return (attended, (largest + jnp.log(totals))[:, :, 0])

    attended, log_total = lax.map(
        one_block, (query_lo.reshape(blocks, block, H, HD), image_ids.reshape(blocks, block))
    )
    return (attended.reshape(count, H, HD), log_total)


def attention_backward(query_lo, key_lo, value_lo, image_ids, log_total, d_attended):
    count = query_lo.shape[0]
    block = min(512, count)
    blocks = count // block

    def one_block(carry, pieces):
        key_acc, value_acc = carry
        query_block, ids_block, total_block, grad_block = pieces
        scores = jnp.einsum("qhd,khd->hqk", query_block, key_lo, preferred_element_type=jnp.float32)
        same = (ids_block[:, None] == image_ids[None, :])[None]
        scores = jnp.where(same, scores, masked)
        probs = jnp.exp(scores - total_block[:, :, None])
        probs_lo = probs.astype(jnp.bfloat16)
        value_acc = value_acc + jnp.einsum(
            "hqk,qhd->khd", probs_lo, grad_block, preferred_element_type=jnp.float32
        )
        d_probs = jnp.einsum(
            "qhd,khd->hqk", grad_block, value_lo, preferred_element_type=jnp.float32
        )
        centre = jnp.sum(probs * d_probs, axis=-1, keepdims=True)
        d_scores = (probs * (d_probs - centre)).astype(jnp.bfloat16)
        d_query = jnp.einsum("hqk,khd->qhd", d_scores, key_lo, preferred_element_type=jnp.float32)
        key_acc = key_acc + jnp.einsum(
            "hqk,qhd->khd", d_scores, query_block, preferred_element_type=jnp.float32
        )
        return ((key_acc, value_acc), d_query)

    zeros = jnp.zeros((count, H, HD), jnp.float32)
    pieces = (
        query_lo.reshape(blocks, block, H, HD),
        image_ids.reshape(blocks, block),
        log_total,
        d_attended.reshape(blocks, block, H, HD),
    )
    (d_key, d_value), d_query = lax.scan(one_block, (zeros, zeros), pieces)
    return (d_query.reshape(count, H, HD), d_key, d_value)


def forward_pass(tokens, image_ids, full):
    full_in, full_out, full_vec = full
    gains = full_vec.astype(jnp.float32)
    rows = tokens.astype(jnp.float32)
    scaled_lo = input_norm(rows, gains[0]).astype(jnp.bfloat16)
    hidden = jnp.dot(scaled_lo, full_in, preferred_element_type=jnp.float32)
    query_raw = hidden[:, :D]
    key_raw = hidden[:, D : 2 * D]
    value_lo = hidden[:, 2 * D : 3 * D].astype(jnp.bfloat16).reshape(-1, H, HD)
    inner = hidden[:, 3 * D :]
    query_lo = head_norm(query_raw, gains[1], HD ** (-0.5)).astype(jnp.bfloat16)
    key_lo = head_norm(key_raw, gains[2], 1.0).astype(jnp.bfloat16)
    attended, log_total = attention_forward(query_lo, key_lo, value_lo, image_ids)
    mixed_lo = jnp.concatenate([attended.reshape(-1, D), activation(inner)], axis=1).astype(
        jnp.bfloat16
    )
    branch = jnp.dot(mixed_lo, full_out, preferred_element_type=jnp.float32) + gains[3]
    result = (rows + branch).astype(jnp.bfloat16)
    return (
        result,
        (scaled_lo, query_raw, key_raw, query_lo, key_lo, value_lo, inner, mixed_lo, log_total),
    )


def backward_pass(tokens, cotangent, image_ids, full, saved):
    full_in, full_out, full_vec = full
    gains = full_vec.astype(jnp.float32)
    scaled_lo, query_raw, key_raw, query_lo, key_lo, value_lo, inner, mixed_lo, log_total = saved
    contract_rows = (((0,), (0,)), ((), ()))
    contract_cols = (((1,), (1,)), ((), ()))
    out_grad = lax.dot_general(
        mixed_lo, cotangent, contract_rows, preferred_element_type=jnp.float32
    )
    d_mixed = lax.dot_general(
        cotangent, full_out, contract_cols, preferred_element_type=jnp.float32
    ).astype(jnp.bfloat16)
    d_attended = d_mixed[:, :D].reshape(-1, H, HD)
    d_query, d_key, d_value = attention_backward(
        query_lo, key_lo, value_lo, image_ids, log_total, d_attended
    )
    d_inner = jax.vjp(activation, inner)[1](d_mixed[:, D:].astype(jnp.float32))[0]
    query_back = jax.vjp(lambda raw, gain: head_norm(raw, gain, HD ** (-0.5)), query_raw, gains[1])[
        1
    ]
    key_back = jax.vjp(lambda raw, gain: head_norm(raw, gain, 1.0), key_raw, gains[2])[1]
    d_query_raw, d_query_gain = query_back(d_query)
    d_key_raw, d_key_gain = key_back(d_key)
    d_hidden = jnp.concatenate(
        [d_query_raw, d_key_raw, d_value.reshape(-1, D), d_inner], axis=1
    ).astype(jnp.bfloat16)
    in_grad = lax.dot_general(
        scaled_lo, d_hidden, contract_rows, preferred_element_type=jnp.float32
    )
    d_scaled = lax.dot_general(d_hidden, full_in, contract_cols, preferred_element_type=jnp.float32)
    rows = tokens.astype(jnp.float32)
    norm_back = jax.vjp(input_norm, rows, gains[0])[1]
    d_rows, d_norm_gain = norm_back(d_scaled)
    cot_rows = cotangent.astype(jnp.float32)
    input_grad = cot_rows + d_rows
    vec_grad = jnp.stack([d_norm_gain, d_query_gain, d_key_gain, jnp.sum(cot_rows, axis=0)], axis=0)
    return (input_grad, in_grad, out_grad, vec_grad)


def square_total(partial_sum):
    return lax.psum(partial_sum, "fsdp")


def adamw(master, first, second, grad, factor):
    clipped = grad * factor
    first_new = beta_one * first + (1.0 - beta_one) * clipped
    second_new = beta_two * second + (1.0 - beta_two) * clipped * clipped
    first_hat = first_new / (1.0 - beta_one**ADAM_STEP)
    second_hat = second_new / (1.0 - beta_two**ADAM_STEP)
    update = -learning * (first_hat / (jnp.sqrt(second_hat) + epsilon) + decay_rate * master)
    return (update, first_new, second_new)


def local(
    tokens,
    cotangent,
    image_ids,
    in_weight,
    out_weight,
    vectors,
    in_moment,
    out_moment,
    vec_moment,
    in_second,
    out_second,
    vec_second,
):
    low_in = in_weight.astype(jnp.bfloat16)
    low_out = out_weight.astype(jnp.bfloat16)
    low_vec = vectors.astype(jnp.bfloat16)
    full = (
        lax.all_gather(low_in, "fsdp", axis=0, tiled=True),
        lax.all_gather(low_out, "fsdp", axis=0, tiled=True),
        lax.all_gather(low_vec, "fsdp", axis=1, tiled=True),
    )
    result, saved = forward_pass(tokens, image_ids, full)
    full = (
        lax.all_gather(low_in, "fsdp", axis=0, tiled=True),
        lax.all_gather(low_out, "fsdp", axis=0, tiled=True),
        lax.all_gather(low_vec, "fsdp", axis=1, tiled=True),
    )
    unused, saved = forward_pass(tokens, image_ids, full)
    input_grad, in_local, out_local, vec_local = backward_pass(
        tokens, cotangent, image_ids, full, saved
    )
    in_part, out_part, vec_part = (
        lax.psum_scatter(
            in_local.astype(jnp.bfloat16), "fsdp", scatter_dimension=0, tiled=True
        ).astype(jnp.float32),
        lax.psum_scatter(
            out_local.astype(jnp.bfloat16), "fsdp", scatter_dimension=0, tiled=True
        ).astype(jnp.float32),
        lax.psum_scatter(
            vec_local.astype(jnp.bfloat16), "fsdp", scatter_dimension=1, tiled=True
        ).astype(jnp.float32),
    )
    in_grad, out_grad, vec_grad = lax.psum((in_part, out_part, vec_part), "dp")
    total = square_total(
        jnp.sum(in_grad * in_grad) + jnp.sum(out_grad * out_grad) + jnp.sum(vec_grad * vec_grad)
    )
    grad_norm = jnp.sqrt(total)
    factor = jnp.minimum(1.0, math.sqrt(PARAMS) / grad_norm)
    in_update, in_mean, in_square = adamw(in_weight, in_moment, in_second, in_grad, factor)
    out_update, out_mean, out_square = adamw(out_weight, out_moment, out_second, out_grad, factor)
    vec_update, vec_mean, vec_square = adamw(vectors, vec_moment, vec_second, vec_grad, factor)
    return (
        result,
        input_grad,
        in_grad,
        out_grad,
        vec_grad,
        grad_norm,
        in_update,
        out_update,
        vec_update,
        in_mean,
        out_mean,
        vec_mean,
        in_square,
        out_square,
        vec_square,
    )


def solution(mesh):
    in_specs = (
        P(("dp", "fsdp"), None),
        P(("dp", "fsdp"), None),
        P(("dp", "fsdp")),
        P("fsdp", None),
        P("fsdp", None),
        P(None, "fsdp"),
        P("fsdp", None),
        P("fsdp", None),
        P(None, "fsdp"),
        P("fsdp", None),
        P("fsdp", None),
        P(None, "fsdp"),
    )
    out_specs = (
        P(("dp", "fsdp"), None),
        P(("dp", "fsdp"), None),
        P("fsdp", None),
        P("fsdp", None),
        P(None, "fsdp"),
        P(),
        P("fsdp", None),
        P("fsdp", None),
        P(None, "fsdp"),
        P("fsdp", None),
        P("fsdp", None),
        P(None, "fsdp"),
        P("fsdp", None),
        P("fsdp", None),
        P(None, "fsdp"),
    )
    return jax.shard_map(local, mesh=mesh, in_specs=in_specs, out_specs=out_specs, check_vma=False)
```

profile of v0, /device:TPU:0, one launch (start us, length us, event | category | flops | bytes accessed | tf_op | source)
XLA Modules:
  0.0 581.6 jit_solution(2606356663764410176)
XLA Ops:
  7.2 2.0 convert_element_type.86
  11.0 23.1 %all-gather = bf16[16,48,4]{1,2,0:T(4,128)(2,1)S(1)} all-gather(bf16[1,48,4]{1,2,0:T(4,128)(2,1)S(1)} %convert_bitcast_fusion), channel_id=1, replica_groups=mesh['dp'=2,'fsdp'=16] {'fsdp'}, dimensions={0}, use_global_device_ids=true | all-gather | bytes 6528 | tf_op jit(solution)/shard_map/all_gather | solution.py:203
  35.8 37.3 %all-gather.6.cloned.1.call-done = bf16[3840,768]{1,0:T(8,128)(2,1)} async-done(((bf16[240,768]{1,0:T(8,128)(2,1)}), bf16[3840,768]{1,0:T(8,128)(2,1)}) %all-gather.6.cloned.1.call-update) | async-done | bytes 5898256 | tf_op jit(solution)/shard_map/all_gather | solution.py:202
  73.1 6.2 %convolution_convert_fusion.2 = bf16[512,3840]{1,0:T(8,128)(2,1)S(1)} fusion(bf16[512,768]{1,0:T(8,128)(2,1)S(1)} %copy-done.12, bf16[3840,768]{1,0:T(8,128)(2,1)} %all-gather.6.cloned.1.call-done), kind=kOutput, calls=%fused_computation.30 | convolution fusion | flops 3021864960 | bytes 10616832 | tf_op jit(solution)/shard_map/dot_general | solution.py:139
  82.4 66.3 %all-gather.4.cloned.1.call-done = bf16[768,5376]{1,0:T(8,128)(2,1)} async-done(((bf16[48,5376]{1,0:T(8,128)(2,1)}), bf16[768,5376]{1,0:T(8,128)(2,1)}) %all-gather.4.cloned.1.call-update) | async-done | bytes 8257552 | tf_op jit(solution)/shard_map/all_gather | solution.py:201
  148.7 7.2 %fusion.56 = f32[512,5376]{1,0:T(8,128)S(1)} fusion(bf16[768,5376]{1,0:T(8,128)(2,1)} %all-gather.4.cloned.1.call-done, bf16[512,768]{1,0:T(8,128)(2,1)S(1)} %copy-done.3, f32[768]{0:T(1024)S(1)} %get-tuple-element.91, f32[512]{0:T(512)S(1)} %fusion.47, f32[512]{0:T(512)S(1)} %broadcast_multiply_fusion.3), kind=kOutput, calls=%fused_computation.122 | convolution fusion | flops 4229824512 | bytes 20061184 | tf_op jit(solution)/shard_map/dot_general | solution.py:111
  156.0 6.7 %fusion.4 = (bf16[512,3072]{1,0:T(8,128)(2,1)}, bf16[512,3072]{1,0:T(8,128)(2,1)}) fusion(f32[512,5376]{1,0:T(8,128)S(1)} %fusion.56, bf16[512,3840]{1,0:T(8,128)(2,1)S(1)} %copy-done.9), kind=kLoop, calls=%fused_computation.16 | loop fusion | flops 36175872 | bytes 15728640 | tf_op jit(solution)/shard_map/convert.11
  170.2 2.5 select_reduce_fusion
  172.8 2.2 fusion
  175.0 5.8 fusion.36
  180.8 3.6 fusion.33
  184.3 7.2 %multiply_reduce_fusion = (f32[12,512]{1,0:T(8,128)}, f32[12,512,512]{1,2,0:T(8,128)}) fusion(f32[12,512,512]{1,2,0:T(8,128)S(1)} %get-tuple-element.120, f32[12,512]{1,0:T(8,128)S(1)} %log_add_fusion, pred[512,512]{0,1:T(8,128)(4,1)S(1)} %broadcast_compare_fusion, bf16[512,12,64]{0,2,1:T(8,128)(2,1)S(1)} %bitcast.76, bf16[512,12,64]{0,2,1:T(8,128)(2,1)S(1)} %bitcast.78), kind=kOutput, calls=%fused_computation.1 | convolution fusion | flops 415229952 | bytes 27049984 | tf_op jit(solution)/shard_map/while/body/eval_jaxpr/qhd,khd->hqk/dot_general | solution.py:84
  191.5 2.3 copy.72
  193.8 2.3 copy.79
  196.1 10.0 %multiply_convert_fusion = bf16[12,512,512]{1,2,0:T(8,128)(2,1)S(1)} fusion(f32[12,512,512]{1,2,0:T(8,128)} %get-tuple-element.122, f32[12,512,512]{1,2,0:T(8,128)} %copy-done, f32[12,512]{1,0:T(8,128)} %get-tuple-element.121, f32[12,512]{1,0:T(8,128)} %copy-done.24, pred[512,512]{0,1:T(8,128)(4,1)S(1)} %broadcast_compare_fusion), kind=kLoop, calls=%fused_computation | loop fusion | flops 15728640 | bytes 31768576 | tf_op jit(solution)/shard_map/while/body/eval_jaxpr/convert_element_type | solution.py:88
  206.1 2.1 multiply_reduce_fusion.1
  208.2 2.5 fusion.32
  213.1 2.9 add_convert_fusion
  216.0 2.4 copy.78
  221.7 2.4 copy.77
  224.2 9.0 %fusion.28 = (f32[512]{0:T(512)S(1)}, f32[512,768]{1,0:T(8,128)S(1)}) fusion(bf16[512,768]{1,0:T(8,128)(2,1)S(1)} %copy-done.4, f32[768]{0:T(1024)S(1)} %copy-done.29, f32[512]{0:T(512)S(1)} %copy-done.31, bf16[768,5376]{1,0:T(8,128)(2,1)} %all-gather.4.cloned.1.call-done, bf16[512,3072]{1,0:T(8,128)(2,1)} %get-tuple-element.115, ...), kind=kOutput, calls=%fused_computation.49 | convolution fusion | flops 4251844096 | bytes 16129024 | tf_op jit(solution)/shard_map/dot_general | solution.py:159
  235.2 7.9 %convolution_convert_fusion.1 = bf16[3840,768]{1,0:T(8,128)(2,1)} fusion(bf16[512,768]{1,0:T(8,128)(2,1)S(1)} %copy-done.13, bf16[512,3072]{1,0:T(8,128)(2,1)} %get-tuple-element.116, bf16[512,768]{1,0:T(8,128)(2,1)} %copy.72), kind=kOutput, calls=%fused_computation.13 | convolution fusion | flops 3030712320 | bytes 10616832 | tf_op jit(solution)/shard_map/dot_general | solution.py:136
  244.3 10.2 %convolution_convert_fusion = bf16[768,5376]{1,0:T(8,128)(2,1)} fusion(bf16[512,3072]{1,0:T(8,128)(2,1)} %get-tuple-element.115, bf16[512,768]{1,0:T(8,128)(2,1)S(1)} %copy-done.18, bf16[512,768]{1,0:T(8,128)(2,1)} %copy.78, bf16[512,768]{1,0:T(8,128)(2,1)} %copy.77, bf16[512,768]{1,0:T(8,128)(2,1)S(1)} %copy-done.4, f32[768]{0:T(1024)S(1)} %copy-done.29, ...), kind=kOutput, calls=%fused_computation.7 | convolution fusion | flops 4255973376 | bytes 14556160 | tf_op jit(solution)/shard_map/dot_general | solution.py:156
  255.6 7.7 %fusion.29 = bf16[512,768]{1,0:T(8,128)(2,1)} fusion(bf16[512,768]{1,0:T(8,128)(2,1)S(1)} %copy-done.4, bf16[3840,768]{1,0:T(8,128)(2,1)} %all-gather.6.cloned.1.call-done, bf16[512,3072]{1,0:T(8,128)(2,1)} %get-tuple-element.116, bf16[512,768]{1,0:T(8,128)(2,1)S(1)} %copy-done.16, f32[768]{0:T(1024)S(1)} %copy-done.42), kind=kOutput, calls=%fused_computation.50 | convolution fusion | flops 3029336064 | bytes 11406336 | tf_op jit(solution)/shard_map/dot_general | solution.py:122
  263.3 23.7 %reduce-scatter.10.cloned.1.call-done = bf16[48,4]{1,0:T(8,128)(2,1)} async-done(((bf16[768,4]{1,0:T(8,128)(2,1)}), bf16[48,4]{1,0:T(8,128)(2,1)}) %reduce-scatter.10.cloned.1.call-update) | async-done | bytes 400
  287.8 84.8 %reduce-scatter.8.cloned.1.call-done = bf16[240,768]{1,0:T(8,128)(2,1)} async-done(((bf16[3840,768]{1,0:T(8,128)(2,1)}), bf16[240,768]{1,0:T(8,128)(2,1)}) %reduce-scatter.8.cloned.1.call-update) | async-done | bytes 368656 | tf_op jit(solution)/shard_map/reduce_scatter | solution.py:219
  372.6 107.5 %reduce-scatter.6.cloned.1.call-done = bf16[48,5376]{1,0:T(8,128)(2,1)} async-done(((bf16[768,5376]{1,0:T(8,128)(2,1)}), bf16[48,5376]{1,0:T(8,128)(2,1)}) %reduce-scatter.6.cloned.1.call-update) | async-done | bytes 516112 | tf_op jit(solution)/shard_map/reduce_scatter | solution.py:216
  480.0 46.4 %all-reduce.2 = (f32[48,5376]{1,0:T(8,128)S(1)}, f32[240,768]{1,0:T(8,128)}, f32[4,48]{1,0:T(4,128)S(1)}) all-reduce(bf16[48,5376]{1,0:T(8,128)(2,1)} %reduce-scatter.6.cloned.1.call-done, bf16[240,768]{1,0:T(8,128)(2,1)} %reduce-scatter.8.cloned.1.call-done, bf16[4,48]{1,0:T(4,128)(2,1)S(1)} %copy.85), channel_id=1, replica_groups=mesh['dp'=2,'fsdp'=16] {'dp'}, use_global_device_ids=true, to_apply=%region_16.17 | all-reduce | flops 442560 | bytes 2655360 | tf_op jit(solution)/shard_map/psum | solution.py:226
  531.9 2.9 add_add_fusion.3
  534.7 31.6 %psum.31 = f32[]{:T(128)} all-reduce(f32[]{:T(128)S(6)} %add.160), channel_id=1, replica_groups=mesh['dp'=2,'fsdp'=16] {'fsdp'}, use_global_device_ids=true, to_apply=%region_28.29 | all-reduce | flops 1 | bytes 8 | tf_op jit(solution)/shard_map/psum | solution.py:170
  567.7 3.6 add_multiply_fusion.1
  571.4 2.2 add_multiply_fusion
  (150 shorter events, 28.9 us)
Async XLA Ops:
  7.2 3.1 copy-start.12
  7.2 65.9 %all-gather.6.cloned.1.call-start = ((), (), s32[]{:S(2)}) async-start(), calls=%async_computation.4 | async-start | bytes 6266880 | tf_op jit(solution)/shard_map/all_gather | solution.py:202
  9.3 25.7 %copy-start.3 = (bf16[512,768]{1,0:T(8,128)(2,1)S(1)}, bf16[512,768]{1,0:T(8,128)(2,1)}, u32[]{:S(2)}) copy-start(bf16[512,768]{1,0:T(8,128)(2,1)} %param.12) | copy-start | bytes 2359300
  9.3 139.4 %all-gather.4.cloned.1.call-start = ((), (), s32[]{:S(2)}) async-start(), calls=%async_computation.3 | async-start | bytes 8773632 | tf_op jit(solution)/shard_map/all_gather | solution.py:201
  10.2 25.4 %copy-start.38 = (s32[512]{0:T(512)S(1)}, s32[512]{0:T(512)}, u32[]{:S(2)}) copy-start(s32[512]{0:T(512)} %param.14) | copy-start | bytes 6148
  10.2 276.8 %reduce-scatter.10.cloned.1.call-start = ((), (), s32[]{:S(2)}) async-start(), calls=%async_computation.7 | async-start | bytes 208896
  34.8 113.9 %copy-start.28 = (f32[768]{0:T(1024)}, f32[768]{0:T(1024)S(1)}, u32[]{:S(2)}) copy-start(f32[768]{0:T(1024)S(1)} %get-tuple-element.91) | copy-start | bytes 9220
  35.0 44.3 %copy-start.25 = (f32[12,64]{1,0:T(8,128)}, f32[12,64]{1,0:T(8,128)S(1)}, u32[]{:S(2)}) copy-start(f32[12,64]{1,0:T(8,128)S(1)} %mul.423) | copy-start | bytes 9220
  35.2 113.5 %copy-start.30 = (f32[512]{0:T(512)}, f32[512]{0:T(512)S(1)}, u32[]{:S(2)}) copy-start(f32[512]{0:T(512)S(1)} %broadcast_multiply_fusion.3) | copy-start | bytes 6148
  35.5 43.8 %copy-start.32 = (f32[512]{0:T(512)}, f32[512]{0:T(512)S(1)}, u32[]{:S(2)}) copy-start(f32[512]{0:T(512)S(1)} %fusion.27) | copy-start | bytes 6148
  35.6 113.2 %copy-start.34 = (f32[512]{0:T(512)}, f32[512]{0:T(512)S(1)}, u32[]{:S(2)}) copy-start(f32[512]{0:T(512)S(1)} %fusion.47) | copy-start | bytes 6148
  148.7 7.3 %copy-start.9 = (bf16[512,3840]{1,0:T(8,128)(2,1)S(1)}, bf16[512,3840]{1,0:T(8,128)(2,1)}, u32[]{:S(2)}) copy-start(bf16[512,3840]{1,0:T(8,128)(2,1)} %copy-done.8) | copy-start | bytes 11796484
  172.7 11.6 %copy-start = (f32[12,512,512]{1,2,0:T(8,128)}, f32[12,512,512]{1,2,0:T(8,128)S(1)}, u32[]{:S(2)}) copy-start(f32[12,512,512]{1,2,0:T(8,128)S(1)} %get-tuple-element.120) | copy-start | bytes 37748740
  175.0 9.4 %copy-start.24 = (f32[12,512]{1,0:T(8,128)}, f32[12,512]{1,0:T(8,128)S(1)}, u32[]{:S(2)}) copy-start(f32[12,512]{1,0:T(8,128)S(1)} %log_add_fusion) | copy-start | bytes 73732
  175.0 5.8 copy-start.10
  180.8 3.6 copy-start.11
  196.1 10.0 %copy-start.27 = (f32[12,64]{1,0:T(8,128)S(1)}, f32[12,64]{1,0:T(8,128)}, u32[]{:S(2)}) copy-start(f32[12,64]{1,0:T(8,128)} %copy-done.25) | copy-start | bytes 9220
  208.2 3.2 copy-start.2
  208.2 3.2 copy-start.23
  220.3 3.9 copy-start.29
  224.2 9.0 %copy-start.33 = (f32[512]{0:T(512)S(1)}, f32[512]{0:T(512)}, u32[]{:S(2)}) copy-start(f32[512]{0:T(512)} %copy-done.32) | copy-start | bytes 6148
  224.2 9.0 %copy-start.35 = (f32[512]{0:T(512)S(1)}, f32[512]{0:T(512)}, u32[]{:S(2)}) copy-start(f32[512]{0:T(512)} %copy-done.34) | copy-start | bytes 6148
  234.9 137.7 %reduce-scatter.8.cloned.1.call-start = ((), (), s32[]{:S(2)}) async-start(), calls=%async_computation.6 | async-start | bytes 6266880 | tf_op jit(solution)/shard_map/reduce_scatter | solution.py:219
  243.2 236.9 %reduce-scatter.6.cloned.1.call-start = ((), (), s32[]{:S(2)}) async-start(), calls=%async_computation.5 | async-start | bytes 8773632 | tf_op jit(solution)/shard_map/reduce_scatter | solution.py:216
  526.4 40.7 %copy-start.39 = (f32[4,48]{1,0:T(4,128)}, f32[4,48]{1,0:T(4,128)S(1)}, u32[]{:S(2)}) copy-start(f32[4,48]{1,0:T(4,128)S(1)} %get-tuple-element.105) | copy-start | bytes 2308
  526.4 44.9 %copy-start.7 = (f32[48,5376]{1,0:T(8,128)}, f32[48,5376]{1,0:T(8,128)S(1)}, u32[]{:S(2)}) copy-start(f32[48,5376]{1,0:T(8,128)S(1)} %get-tuple-element.92) | copy-start | bytes 3096580
  531.8 35.3 %copy-start.41 = (f32[4,48]{1,0:T(4,128)S(1)}, f32[4,48]{1,0:T(4,128)}, u32[]{:S(2)}) copy-start(f32[4,48]{1,0:T(4,128)} %param.17) | copy-start | bytes 2308
  531.8 35.3 %copy-start.43 = (f32[4,48]{1,0:T(4,128)S(1)}, f32[4,48]{1,0:T(4,128)}, u32[]{:S(2)}) copy-start(f32[4,48]{1,0:T(4,128)} %param.20) | copy-start | bytes 2308
  531.8 35.3 %copy-start.44 = (f32[4,48]{1,0:T(4,128)S(1)}, f32[4,48]{1,0:T(4,128)}, u32[]{:S(2)}) copy-start(f32[4,48]{1,0:T(4,128)} %param.23) | copy-start | bytes 2308
  567.7 3.6 copy-start.6
  567.7 3.6 copy-start.14
  567.7 3.6 copy-start.15
  (18 other events, 29.8 us)
Sparse Core Ops, SparseCore 0:
  10.9 62.2 all-gather.5
  76.0 72.6 all-gather.3
  235.0 51.9 reduce-scatter.9
  290.8 81.7 reduce-scatter.7
  377.1 102.9 reduce-scatter.5
where the time goes:
time: 588 us; the launch traced here: 582 us
  waiting for transfers between devices  320 us (54%)
  blocking collectives  101 us (17%)
  matrix products  71.8 us (12%)
  other arithmetic  45.4 us (8%)
  local copies, waits for them, and re-layouts  24.6 us (4%)
  between operations  18.6 us (3%)
    reduce_scatter x1, waiting for transfers between devices, local(): lax.psum_scatter(in_local.astype(jnp.bfloat16), 'fsdp', scatter_dimension...  107 us
    reduce_scatter x1, waiting for transfers between devices, local(): lax.psum_scatter(out_local.astype(jnp.bfloat16), 'fsdp', scatter_dimensio...  84.8 us
    all_gather x1, waiting for transfers between devices, local(): lax.all_gather(low_in, 'fsdp', axis=0, tiled=True)  66.3 us
    psum x1, blocking collectives, local(): in_grad, out_grad, vec_grad = lax.psum((in_part, out_part, vec_part), 'dp')  46.4 us
    all_gather x1, waiting for transfers between devices, local(): lax.all_gather(low_out, 'fsdp', axis=0, tiled=True)  37.3 us
    psum x1, blocking collectives, square_total(): return lax.psum(partial_sum, 'fsdp')  31.6 us
    unnamed x6, waiting for transfers between devices  23.8 us
    all_gather x1, blocking collectives, local(): lax.all_gather(low_vec, 'fsdp', axis=1, tiled=True)  23.1 us
  transfers between devices with their start and end apart: 5, of which 5 were waited for; matrix products, arithmetic and copies ran while one was open for 6% of the time, Pallas kernels for 0%

commit v1 on v0

v1 whole, which is shorter than its diff:
```python
import math

import jax
import jax.numpy as jnp
from jax import lax
from jax.experimental import pallas as pl
from jax.experimental.pallas import tpu as pltpu
from jax.sharding import PartitionSpec as P

D = 768
H = 12
HD = 64
FF = 3072
ADAM_STEP = 10
PARAMS = 7080960

beta_one = 0.9
beta_two = 0.95
learning = 0.03
decay_rate = 0.1
epsilon = 1e-08
norm_eps = 1e-06

F32 = jnp.float32
BF16 = jnp.bfloat16
DH = D // 2
FH = FF // 2
PAIR = 128
PAIRS = DH // PAIR
QKV = 3 * PAIR
QW = PAIRS * QKV
VEC = 128
GELU_C = math.sqrt(2.0 / math.pi)
MIB = 1 << 20

NT = (((1,), (1,)), ((), ()))
TN = (((0,), (0,)), ((), ()))


def mm(a, b, dims=(((1,), (0,)), ((), ()))):
    return lax.dot_general(a, b, dims, preferred_element_type=F32)


class Plan:
    def __init__(self, n_fsdp, n_dp):
        chips = n_fsdp // 2
        self.n, self.n_dp, self.chips = n_fsdp, n_dp, chips
        self.zs = 4 if chips % 4 == 0 else chips
        self.ys = chips // self.zs
        index = lax.axis_index("fsdp")
        self.core = index % 2
        self.y = (index // 2) % self.ys
        self.z = index // (2 * self.ys)
        self.pos = jnp.stack([self.z, self.y, self.core]).astype(jnp.int32)
        self.order = [(t, s) for t in range(self.ys) for s in range(self.zs)]

    def index(self, z, y, core):
        return ((z % self.zs) * self.ys + y % self.ys) * 2 + core

    def all(self):
        return [
            (z, y, c) for z in range(self.zs) for y in range(self.ys) for c in range(2)
        ]

    def from_z(self, a, s):
        pairs = [(self.index(z + s, y, c), self.index(z, y, c)) for z, y, c in self.all()]
        return lax.ppermute(a, "fsdp", pairs)

    def from_y(self, a, t):
        pairs = [(self.index(z, y + t, c), self.index(z, y, c)) for z, y, c in self.all()]
        return lax.ppermute(a, "fsdp", pairs)

    def swap_core(self, a):
        pairs = [(self.index(z, y, c), self.index(z, y, 1 - c)) for z, y, c in self.all()]
        return lax.ppermute(a, "fsdp", pairs)

    def gather(self, piece):
        column = [piece] + [self.from_z(piece, s) for s in range(1, self.zs)]
        out = list(column)
        for t in range(1, self.ys):
            out += [self.from_y(a, t) for a in column]
        return out

    def scatter(self, pieces):
        column = []
        for s in range(self.zs):
            total = pieces[s].astype(F32)
            for t in range(1, self.ys):
                total = total + self.from_y(pieces[t * self.zs + s], -t).astype(F32)
            column.append(total)
        total = column[0]
        for s in range(1, self.zs):
            total = total + self.from_z(column[s].astype(BF16), -s).astype(F32)
        return total

    def over_dp(self, a):
        if self.n_dp == 2:
            other = lax.ppermute(a, "dp", [(0, 1), (1, 0)])
            return a.astype(F32) + other.astype(F32)
        return lax.psum(a.astype(F32), "dp")

    def total(self, a):
        m = 1
        while m < self.n:
            a = a + lax.ppermute(a, "fsdp", [(i, i ^ m) for i in range(self.n)])
            m *= 2
        return a

    def row(self, pos_ref, t, s, rows):
        z = lax.rem(pos_ref[0] + s, self.zs)
        y = lax.rem(pos_ref[1] + t, self.ys)
        return pl.multiple_of((z * self.ys + y) * rows, 16)


def smem():
    return pl.BlockSpec(memory_space=pltpu.SMEM)


def whole(shape):
    return pl.BlockSpec(shape, lambda *_: (0,) * len(shape))


def params(mib):
    return pltpu.CompilerParams(
        dimension_semantics=("arbitrary",), vmem_limit_bytes=mib * MIB
    )


def cost(flops, nbytes, exps=0):
    return pl.CostEstimate(flops=int(flops), bytes_accessed=int(nbytes), transcendentals=int(exps))


def place(plan, pos_ref, refs, rows, out_ref):
    for (t, s), ref in zip(plan.order, refs):
        out_ref[pl.ds(plan.row(pos_ref, t, s, rows), rows), :] = ref[...]


def mlp_forward(plan, x_own, xc_other, pieces):
    tok = x_own.shape[0]
    rows = pieces[0].shape[0]
    tile = 512
    n = len(pieces)

    def kernel(pos_ref, xo_ref, xp_ref, *rest):
        refs, (mix_ref, slope_ref, w_ref) = rest[:n], rest[n:]
        place(plan, pos_ref, refs, rows, w_ref)
        for half, x_ref in enumerate((xo_ref, xp_ref)):
            v = mm(x_ref[...], w_ref[...])
            v2 = v * v
            t = jnp.tanh(v * (GELU_C + (GELU_C * 0.044715) * v2))
            h = 0.5 + 0.5 * t
            g = v * h
            slope = h + 2.0 * g * (1.0 - h) * (GELU_C + (3.0 * GELU_C * 0.044715) * v2)
            mix_ref[half] = g.astype(BF16)
            slope_ref[half] = slope.astype(BF16)

    block = pl.BlockSpec((2, tok, tile), lambda j: (0, 0, j))
    return pl.pallas_call(
        kernel,
        grid=(FH // tile,),
        in_specs=[
            smem(),
            whole((tok, D)),
            pl.BlockSpec((tok, D), lambda j: (0, 0)),
        ]
        + [pl.BlockSpec((rows, tile), lambda j: (0, j))] * n,
        out_specs=[block, block],
        out_shape=[jax.ShapeDtypeStruct((2, tok, FH), BF16)] * 2,
        scratch_shapes=[pltpu.VMEM((D, tile), BF16)],
        compiler_params=params(40),
        cost_estimate=cost(4 * tok * D * FH, 12 * tok * FH, 2 * tok * FH),
        name="mlp_forward",
    )(plan.pos, x_own, xc_other, *pieces)


def head_means(a, block_ref):
    high = a.astype(BF16)
    low = (a - high.astype(F32)).astype(BF16)
    return mm(high, block_ref[...]) + mm(low, block_ref[...])


def attention_forward(plan, x_own, xc_other, pieces, id_row, id_col, block):
    tok = x_own.shape[0]
    rows = pieces[0].shape[0]
    n = len(pieces)

    def kernel(pos_ref, xo_ref, xp_ref, idr_ref, idc_ref, block_ref, *rest):
        refs, vec_refs = rest[:n], rest[n : 2 * n]
        (
            q_ref, k_ref, v_ref, nq_ref, nk_ref, rq_ref, rk_ref, att_ref, p_ref, gain_ref,
            w_ref, vs_ref,
        ) = rest[2 * n :]
        step = pl.program_id(0)

        @pl.when(step == 0)
        def _():
            place(plan, pos_ref, vec_refs, rows, vs_ref)
            gain_ref[...] = vs_ref[...].astype(F32).T[:8]

        place(plan, pos_ref, refs, rows, w_ref)
        column = pl.ds(pl.multiple_of(pos_ref[2] * DH + step * PAIR, PAIR), PAIR)
        q_gain = gain_ref[0:1, column] * (HD ** (-0.5))
        k_gain = gain_ref[1:2, column]
        lane = lax.broadcasted_iota(jnp.int32, (tok, PAIR), 1)
        first = lane < HD
        for half, x_ref in enumerate((xo_ref, xp_ref)):
            raw = mm(x_ref[...], w_ref[...])

            def normed(a, gain, n_ref, r_ref, out_ref):
                centre = a - head_means(a, block_ref)
                r = lax.rsqrt(head_means(centre * centre, block_ref) + norm_eps)
                normal = centre * r
                n_ref[half] = normal.astype(BF16)
                r_ref[half] = r.astype(BF16)
                low = (normal * gain).astype(BF16)
                out_ref[half] = low
                return low

            q = normed(raw[:, :PAIR], q_gain, nq_ref, rq_ref, q_ref)
            k = normed(raw[:, PAIR : 2 * PAIR], k_gain, nk_ref, rk_ref, k_ref)
            v = raw[:, 2 * PAIR :].astype(BF16)
            v_ref[half] = v
            same = idc_ref[half] == idr_ref[half]
            att = []
            zero = jnp.zeros_like(q)
            for head in range(2):
                qh = jnp.where(first, q, zero) if head == 0 else jnp.where(first, zero, q)
                e = jnp.where(same, jnp.exp(mm(qh, k, NT)), 0.0)
                p = (e * (1.0 / jnp.sum(e, axis=1, keepdims=True))).astype(BF16)
                p_ref[half, head] = p
                att.append(mm(p, v))
            att_ref[half] = jnp.where(first, att[0], att[1]).astype(BF16)

    pair = pl.BlockSpec((2, tok, PAIR), lambda j: (0, 0, j))
    small = jax.ShapeDtypeStruct((2, tok, DH), BF16)
    return pl.pallas_call(
        kernel,
        grid=(PAIRS,),
        in_specs=[
            smem(),
            whole((tok, D)),
            pl.BlockSpec((tok, D), lambda j: (0, 0)),
            whole((2, 1, tok)),
            whole((2, tok, 1)),
            whole((PAIR, PAIR)),
        ]
        + [pl.BlockSpec((rows, QKV), lambda j: (0, j))] * n
        + [pl.BlockSpec((rows, VEC), lambda j: (0, QW // VEC))] * n,
        out_specs=[pair] * 8
        + [pl.BlockSpec((2, 2, tok, tok), lambda j: (0, j, 0, 0)), whole((8, D))],
        out_shape=[small] * 8
        + [
            jax.ShapeDtypeStruct((2, 2 * PAIRS, tok, tok), BF16),
            jax.ShapeDtypeStruct((8, D), F32),
        ],
        scratch_shapes=[pltpu.VMEM((D, QKV), BF16), pltpu.VMEM((D, VEC), BF16)],
        compiler_params=params(48),
        cost_estimate=cost(4 * tok * D * QW, 20 * MIB, 12 * tok * tok),
        name="attention_forward",
    )(plan.pos, x_own, xc_other, id_row, id_col, block, *pieces, *pieces)


def output_step(plan, att, mixed, slope, cot_own, xc_other, w_own, w_other):
    tok = cot_own.shape[0]
    rows = w_own.shape[0] // plan.chips
    tile = DH
    steps = 1 + FH // tile

    def kernel(
        pos_ref, att_ref, mix_ref, slope_ref, co_ref, cp_ref, wo_ref, wp_ref,
        out_own_ref, out_other_ref, d_att_ref, d_in_ref, g_own_ref, g_other_ref,
        w_ref, acc_ref, cot_ref,
    ):
        step = pl.program_id(0)
        core = pos_ref[2]
        own = pl.ds(pl.multiple_of(core * DH, DH), DH)
        other = pl.ds(pl.multiple_of((1 - core) * DH, DH), DH)

        @pl.when(step == 0)
        def _():
            for i, (t, s) in enumerate(plan.order):
                at = pl.ds(plan.row(pos_ref, t, s, rows), rows)
                w_ref[at, own] = wo_ref[i * rows : (i + 1) * rows, :]
                w_ref[at, other] = wp_ref[i * rows : (i + 1) * rows, :]
            acc_ref[...] = jnp.zeros_like(acc_ref)
            cot_ref[:tok] = co_ref[...]
            cot_ref[tok:] = cp_ref[...]

        start = jnp.where(step == 0, core * DH, D + core * FH + (step - 1) * tile)
        w = w_ref[pl.ds(pl.multiple_of(start, tile), tile), :]
        m = jnp.where(step == 0, att_ref[...], mix_ref[...]).reshape(2 * tok, tile)
        cot = cot_ref[...]
        acc_ref[...] += mm(m, w)
        d = mm(cot, w, NT)

        @pl.when(step == 0)
        def _():
            d_att_ref[...] = d.astype(BF16).reshape(2, tok, tile)

        slopes = slope_ref[...].reshape(2 * tok, tile).astype(F32)
        d_in_ref[...] = (d * slopes).astype(BF16).reshape(2, tok, tile)
        g_own_ref[...] = mm(m, cot_ref[:, own], TN).astype(BF16)
        g_other_ref[...] = mm(m, cot_ref[:, other], TN).astype(BF16)

        @pl.when(step == steps - 1)
        def _():
            out_own_ref[...] = acc_ref[:tok]
            out_other_ref[...] = acc_ref[tok:].astype(BF16)

    hidden = pl.BlockSpec((2, tok, tile), lambda j: (0, 0, jnp.maximum(j - 1, 0)))
    grad = pl.BlockSpec((tile, DH), lambda j: (j, 0))
    return pl.pallas_call(
        kernel,
        grid=(steps,),
        in_specs=[
            smem(),
            whole((2, tok, tile)),
            hidden,
            hidden,
            whole((tok, D)),
            pl.BlockSpec((tok, D), lambda j: (0, 1)),
            whole(w_own.shape),
            whole(w_other.shape),
        ],
        out_specs=[whole((tok, D)), whole((tok, D)), whole((2, tok, tile)), hidden, grad, grad],
        out_shape=[
            jax.ShapeDtypeStruct((tok, D), F32),
            jax.ShapeDtypeStruct((tok, D), BF16),
            jax.ShapeDtypeStruct((2, tok, DH), BF16),
            jax.ShapeDtypeStruct((2, tok, FH), BF16),
            jax.ShapeDtypeStruct((steps * tile, DH), BF16),
            jax.ShapeDtypeStruct((steps * tile, DH), BF16),
        ],
        scratch_shapes=[
            pltpu.VMEM((D + FF, D), BF16),
            pltpu.VMEM((2 * tok, D), F32),
            pltpu.VMEM((2 * tok, D), BF16),
        ],
        compiler_params=params(56),
        cost_estimate=cost(6 * 2 * tok * steps * tile * D, 30 * MIB),
        name="output_step",
    )(plan.pos, att, mixed, slope, cot_own, xc_other, w_own, w_other)


def turned(plan, pos_ref, xt_ref, xs_ref, rows):
    for i, (t, s) in enumerate(plan.order):
        xs_ref[i * rows : (i + 1) * rows, :] = xt_ref[
            pl.ds(plan.row(pos_ref, t, s, rows), rows), :
        ]


def mlp_backward(plan, xt, d_inner, pieces):
    tok = d_inner.shape[1]
    rows = pieces[0].shape[0]
    n = len(pieces)
    tile = 512
    steps = FH // tile

    def kernel(pos_ref, xt_ref, d_ref, *rest):
        refs, grads = rest[:n], rest[n : 2 * n]
        e_own_ref, e_other_ref, w_ref, xs_ref, acc_ref = rest[2 * n :]
        step = pl.program_id(0)

        @pl.when(step == 0)
        def _():
            turned(plan, pos_ref, xt_ref, xs_ref, rows)
            acc_ref[...] = jnp.zeros_like(acc_ref)

        place(plan, pos_ref, refs, rows, w_ref)
        d = d_ref[...].reshape(2 * tok, tile)
        g = mm(xs_ref[...], d).astype(BF16)
        for i, ref in enumerate(grads):
            ref[...] = g[i * rows : (i + 1) * rows]
        acc_ref[...] += mm(d, w_ref[...], NT)

        @pl.when(step == steps - 1)
        def _():
            e_own_ref[...] = acc_ref[:tok]
            e_other_ref[...] = acc_ref[tok:]

    piece = pl.BlockSpec((rows, tile), lambda j: (0, j))
    out = pl.pallas_call(
        kernel,
        grid=(steps,),
        in_specs=[
            smem(),
            whole((D, 2 * tok)),
            pl.BlockSpec((2, tok, tile), lambda j: (0, 0, j)),
        ]
        + [piece] * n,
        out_specs=[piece] * n + [whole((tok, D))] * 2,
        out_shape=[jax.ShapeDtypeStruct((rows, FH), BF16)] * n
        + [jax.ShapeDtypeStruct((tok, D), F32)] * 2,
        scratch_shapes=[
            pltpu.VMEM((D, tile), BF16),
            pltpu.VMEM((D, 2 * tok), BF16),
            pltpu.VMEM((2 * tok, D), F32),
        ],
        compiler_params=params(48),
        cost_estimate=cost(8 * tok * D * FH, 20 * MIB),
        name="mlp_backward",
    )(plan.pos, xt, d_inner, *pieces)
    return out[:n], out[n], out[n + 1]


def attention_backward(plan, xt, saved, d_att, block, gains, pieces, e_own, e_other):
    q, k, v, nq, nk, rq, rk, probs = saved
    tok = d_att.shape[1]
    rows = pieces[0].shape[0]
    n = len(pieces)

    def kernel(pos_ref, xt_ref, q_ref, k_ref, v_ref, nq_ref, nk_ref, rq_ref, rk_ref, p_ref,
               da_ref, block_ref, gain_ref, ein_own_ref, ein_other_ref, *rest):
        refs, grads = rest[:n], rest[n : 2 * n]
        e_own_ref, e_other_ref, gg_ref, w_ref, xs_ref, d_ref = rest[2 * n :]
        step = pl.program_id(0)

        @pl.when(step == 0)
        def _():
            turned(plan, pos_ref, xt_ref, xs_ref, rows)
            e_own_ref[...] = ein_own_ref[...]
            e_other_ref[...] = ein_other_ref[...]

        place(plan, pos_ref, refs, rows, w_ref)
        column = pl.ds(pl.multiple_of(pos_ref[2] * DH + step * PAIR, PAIR), PAIR)
        q_gain = gain_ref[0:1, column]
        k_gain = gain_ref[1:2, column]
        first = lax.broadcasted_iota(jnp.int32, (tok, PAIR), 1) < HD
        sums = [jnp.zeros((1, PAIR), F32), jnp.zeros((1, PAIR), F32)]
        for half in range(2):
            qb, kb, vb, da = q_ref[half], k_ref[half], v_ref[half], da_ref[half]
            q_t, da_t = qb.T, da.T
            zero = jnp.zeros_like(da)
            dq, dk_t, dv_t = [], [], []
            for head in range(2):
                at = slice(head * HD, (head + 1) * HD)
                dah = jnp.where(first, da, zero) if head == 0 else jnp.where(first, zero, da)
                p_low = p_ref[half, head]
                p = p_low.astype(F32)
                t = p * mm(dah, vb, NT)
                ds = (t - p * jnp.sum(t, axis=1, keepdims=True)).astype(BF16)
                dv_t.append(mm(da_t[at], p_low))
                dk_t.append(mm(q_t[at], ds))
                dq.append(mm(ds, kb))
            d_query = jnp.where(first, dq[0], dq[1])
            d_key = jnp.concatenate(dk_t, axis=0).T
            d_value = jnp.concatenate(dv_t, axis=0).T

            def back(d, gain, n_ref, r_ref, which, factor):
                normal = n_ref[half].astype(F32)
                d = d * factor
                sums[which] = sums[which] + jnp.sum(d * normal, axis=0, keepdims=True)
                e = d * gain
                mean = head_means(e, block_ref)
                along = head_means(e * normal, block_ref)
                return (r_ref[half].astype(F32) * (e - mean - normal * along)).astype(BF16)

            at = slice(half * tok, (half + 1) * tok)
            d_ref[at, :PAIR] = back(d_query, q_gain, nq_ref, rq_ref, 0, HD ** (-0.5))
            d_ref[at, PAIR : 2 * PAIR] = back(d_key, k_gain, nk_ref, rk_ref, 1, 1.0)
            d_ref[at, 2 * PAIR :] = d_value.astype(BF16)
        gg_ref[...] = jnp.concatenate(sums + [jnp.zeros((6, PAIR), F32)], axis=0)
        g = mm(xs_ref[...], d_ref[...]).astype(BF16)
        for i, ref in enumerate(grads):
            ref[...] = g[i * rows : (i + 1) * rows]
        e_own_ref[...] += mm(d_ref[:tok], w_ref[...], NT)
        e_other_ref[...] += mm(d_ref[tok:], w_ref[...], NT)

    piece = pl.BlockSpec((rows, QKV), lambda j: (0, j))
    pair = pl.BlockSpec((2, tok, PAIR), lambda j: (0, 0, j))
    out = pl.pallas_call(
        kernel,
        grid=(PAIRS,),
        in_specs=[smem(), whole((D, 2 * tok))]
        + [pair] * 7
        + [
            pl.BlockSpec((2, 2, tok, tok), lambda j: (0, j, 0, 0)),
            pair,
            whole((PAIR, PAIR)),
            whole((8, D)),
            whole((tok, D)),
            whole((tok, D)),
        ]
        + [piece] * n,
        out_specs=[piece] * n
        + [whole((tok, D))] * 2
        + [pl.BlockSpec((8, PAIR), lambda j: (0, j))],
        out_shape=[jax.ShapeDtypeStruct((rows, QW), BF16)] * n
        + [jax.ShapeDtypeStruct((tok, D), F32)] * 2
        + [jax.ShapeDtypeStruct((8, DH), F32)],
        scratch_shapes=[
            pltpu.VMEM((D, QKV), BF16),
            pltpu.VMEM((D, 2 * tok), BF16),
            pltpu.VMEM((2 * tok, QKV), BF16),
        ],
        compiler_params=params(56),
        cost_estimate=cost(8 * tok * D * QW, 20 * MIB),
        name="attention_backward",
    )(plan.pos, xt, q, k, v, nq, nk, rq, rk, probs, d_att, block, gains, e_own, e_other, *pieces)
    return out[:n], out[n], out[n + 1], out[n + 2]


def row_stats(rows):
    centre = rows - jnp.mean(rows, axis=-1, keepdims=True)
    r = lax.rsqrt(jnp.mean(centre * centre, axis=-1, keepdims=True) + norm_eps)
    return centre * r, r


def adamw(master, first, second, grad, factor):
    clipped = grad * factor
    first_new = beta_one * first + (1.0 - beta_one) * clipped
    second_new = beta_two * second + (1.0 - beta_two) * clipped * clipped
    first_hat = first_new / (1.0 - beta_one**ADAM_STEP)
    second_hat = second_new / (1.0 - beta_two**ADAM_STEP)
    update = -learning * (first_hat / (jnp.sqrt(second_hat) + epsilon) + decay_rate * master)
    return (update, first_new, second_new)


def pick(a, index, axis):
    return lax.dynamic_index_in_dim(a, index, axis, keepdims=False)


def both(core, own, other, axis):
    return jnp.concatenate(
        [jnp.where(core == 0, own, other), jnp.where(core == 0, other, own)], axis=axis
    )


def local(
    tokens,
    cotangent,
    image_ids,
    in_weight,
    out_weight,
    vectors,
    in_moment,
    out_moment,
    vec_moment,
    in_second,
    out_second,
    vec_second,
):
    plan = Plan(lax.axis_size("fsdp"), lax.axis_size("dp"))
    core = plan.core
    tok = tokens.shape[0]
    rows = in_weight.shape[0]
    out_rows = out_weight.shape[0]

    low_in = in_weight.astype(BF16)
    low_out = out_weight.astype(BF16)
    low_vec = vectors.astype(BF16)
    gain = low_vec[0].astype(F32)[:, None]
    scaled_in = (low_in.astype(F32) * gain).astype(BF16)
    qkv_all = scaled_in[:, : 3 * D].reshape(rows, 3, 2, PAIRS, PAIR)
    mlp_all = scaled_in[:, 3 * D :].reshape(rows, 2, FH)
    vec_cols = jnp.pad(low_vec[1:].T, ((0, 0), (0, VEC - 3)))

    def qkv_of(c):
        part = pick(qkv_all, c, 2).transpose(0, 2, 1, 3).reshape(rows, QW)
        return jnp.concatenate([part, vec_cols], axis=1)

    def joined(own, other_wants):
        return both(core, own, plan.swap_core(other_wants), 0)

    mlp_piece = joined(pick(mlp_all, core, 1), pick(mlp_all, 1 - core, 1))
    qkv_piece = joined(qkv_of(core), qkv_of(1 - core))
    out_all = low_out.reshape(out_rows, 2, DH)
    out_piece = joined(pick(out_all, core, 1), pick(out_all, 1 - core, 1))

    normal, _ = row_stats(tokens.astype(F32))
    x_own = normal.astype(BF16)
    xc_other = plan.swap_core(jnp.concatenate([x_own, cotangent], axis=1))
    ids_other = plan.swap_core(image_ids)
    ids = jnp.stack([image_ids, ids_other])
    xt = jnp.concatenate([x_own, xc_other[:, :D]], axis=0).T
    lane = jnp.arange(PAIR) // HD
    block = jnp.where(lane[:, None] == lane[None, :], 1.0 / HD, 0.0).astype(BF16)

    mlp_pieces = plan.gather(mlp_piece)
    qkv_pieces = plan.gather(qkv_piece)
    out_pieces = plan.gather(out_piece)

    mixed, slope = mlp_forward(plan, x_own, xc_other, mlp_pieces)
    *saved, att, probs, gains = attention_forward(
        plan, x_own, xc_other, qkv_pieces, ids[:, None, :], ids[:, :, None], block
    )
    w_own = jnp.concatenate(out_pieces, axis=0)
    w_other = plan.swap_core(w_own)
    out_own, out_other, d_att, d_inner, g_own, g_other = output_step(
        plan, att, mixed, slope, cotangent, xc_other, w_own, w_other
    )
    out_recv = plan.swap_core(out_other)
    result = (
        tokens.astype(F32) + out_own + out_recv.astype(F32) + gains[2][None, :]
    ).astype(BF16)

    g_recv = plan.swap_core(g_other)
    full = jnp.concatenate(
        [both(core, g_own[:DH], g_recv[:DH], 0), both(core, g_own[DH:], g_recv[DH:], 0)], axis=0
    ).reshape(plan.zs, plan.ys, 2 * out_rows, DH)
    parts = [
        lax.dynamic_slice(
            full,
            ((plan.z + s) % plan.zs, (plan.y + t) % plan.ys, 0, 0),
            (1, 1, 2 * out_rows, DH),
        )[0, 0]
        for t, s in plan.order
    ]
    out_sum = plan.scatter(parts)

    mlp_grads, e_own, e_other = mlp_backward(plan, xt, d_inner, mlp_pieces)
    mlp_sum = plan.scatter(mlp_grads)
    qkv_grads, e_own, e_other, gain_grads = attention_backward(
        plan, xt, tuple(saved) + (probs,), d_att, block, gains, qkv_pieces, e_own, e_other
    )
    half = jnp.zeros((2, DH), F32)
    cot_sum = jnp.sum(cotangent.astype(F32), axis=0)
    head_rows = jnp.zeros((2, D), F32)
    head_rows = lax.dynamic_update_slice(head_rows, gain_grads[:2], (0, core * DH))
    vec_rows = jnp.concatenate([head_rows, cot_sum[None]], axis=0)
    vec_local = jnp.pad(vec_rows.T, ((0, 0), (0, VEC - 3))).astype(BF16)
    vec_local = vec_local.reshape(plan.zs, plan.ys, 2 * rows, VEC)
    vec_parts = [
        lax.dynamic_slice(
            vec_local,
            ((plan.z + s) % plan.zs, (plan.y + t) % plan.ys, 0, 0),
            (1, 1, 2 * rows, VEC),
        )[0, 0]
        for t, s in plan.order
    ]
    qkv_sum = plan.scatter(
        [jnp.concatenate([a, b], axis=1) for a, b in zip(qkv_grads, vec_parts)]
    )

    e_recv = plan.swap_core(e_other.astype(BF16))
    e = e_own + e_recv.astype(F32)
    normal, r = row_stats(tokens.astype(F32))
    mean = jnp.mean(e, axis=-1, keepdims=True)
    along = jnp.mean(e * normal, axis=-1, keepdims=True)
    input_grad = cotangent.astype(F32) + r * (e - mean - normal * along)

    def finish(total, count):
        total = total.astype(BF16)
        own = lax.dynamic_slice_in_dim(total, core * count, count, 0)
        other = plan.swap_core(lax.dynamic_slice_in_dim(total, (1 - core) * count, count, 0))
        return plan.over_dp(own), plan.over_dp(other)

    out_grad = both(core, *finish(out_sum, out_rows), 1)
    mlp_hat = both(core, *finish(mlp_sum, rows), 1)
    qkv_own, qkv_other = finish(qkv_sum, rows)
    qkv_hat = jnp.stack(
        [
            jnp.where(core == 0, qkv_own[:, :QW], qkv_other[:, :QW]),
            jnp.where(core == 0, qkv_other[:, :QW], qkv_own[:, :QW]),
        ],
        axis=1,
    )
    qkv_hat = (
        qkv_hat.reshape(rows, 2, PAIRS, 3, PAIR).transpose(0, 3, 1, 2, 4).reshape(rows, 3 * D)
    )
    hat = jnp.concatenate([qkv_hat, mlp_hat], axis=1)
    in_grad = hat * gain
    gain_grad = jnp.sum(hat * low_in.astype(F32), axis=1)
    vec_tail = (qkv_own[:, QW:] + qkv_other[:, QW:])[:, :3].T
    vec_grad = jnp.concatenate([gain_grad[None], vec_tail], axis=0)

    square = (
        jnp.sum(in_grad * in_grad) + jnp.sum(out_grad * out_grad) + jnp.sum(vec_grad * vec_grad)
    )
    total = plan.total(jnp.full((8, 128), square, F32))[0, 0]
    grad_norm = jnp.sqrt(total)
    factor = jnp.minimum(1.0, math.sqrt(PARAMS) / grad_norm)
    in_update, in_mean, in_square = adamw(in_weight, in_moment, in_second, in_grad, factor)
    out_update, out_mean, out_square = adamw(out_weight, out_moment, out_second, out_grad, factor)
    vec_update, vec_mean, vec_square = adamw(vectors, vec_moment, vec_second, vec_grad, factor)
    return (
        result,
        input_grad,
        in_grad,
        out_grad,
        vec_grad,
        grad_norm,
        in_update,
        out_update,
        vec_update,
        in_mean,
        out_mean,
        vec_mean,
        in_square,
        out_square,
        vec_square,
    )


def solution(mesh):
    in_specs = (
        P(("dp", "fsdp"), None),
        P(("dp", "fsdp"), None),
        P(("dp", "fsdp")),
        P("fsdp", None),
        P("fsdp", None),
        P(None, "fsdp"),
        P("fsdp", None),
        P("fsdp", None),
        P(None, "fsdp"),
        P("fsdp", None),
        P("fsdp", None),
        P(None, "fsdp"),
    )
    out_specs = (
        P(("dp", "fsdp"), None),
        P(("dp", "fsdp"), None),
        P("fsdp", None),
        P("fsdp", None),
        P(None, "fsdp"),
        P(),
        P("fsdp", None),
        P("fsdp", None),
        P(None, "fsdp"),
        P("fsdp", None),
        P("fsdp", None),
        P(None, "fsdp"),
        P("fsdp", None),
        P("fsdp", None),
        P(None, "fsdp"),
    )
    return jax.shard_map(local, mesh=mesh, in_specs=in_specs, out_specs=out_specs, check_vma=False)
```

time: 588 us -> 448 us (0.76)
  waiting for transfers between devices: 320 us -> 200 us
  blocking collectives: 101 us -> 0 us
  Pallas kernels: 0 us -> 81.8 us
  matrix products: 71.8 us -> 0 us
  starting transfers between devices: 0.46 us -> 72.1 us
  local copies, waits for them, and re-layouts: 24.6 us -> 41.4 us
  between operations: 18.6 us -> 6.06 us
    ppermute x0 -> x64, waiting for transfers between devices: none -> 200 us  [the longest x18 103 us: from_z(): return lax.ppermute(a, 'fsdp', pairs)]
    reduce_scatter x2 -> x0, waiting for transfers between devices: 192 us -> none  [the longest x1 107 us: local(): lax.psum_scatter(in_local.astype(jnp.bfloat16), 'fsdp', scatter_dimension...]
    all_gather x2 -> x0, waiting for transfers between devices: 104 us -> none  [the longest x1 66.3 us: local(): lax.all_gather(low_in, 'fsdp', axis=0, tiled=True)]
    pallas_call x0 -> x5, Pallas kernels: none -> 81.8 us  [the longest x1 26.4 us: output_step(): pl.pallas_call(kernel, grid=(steps,), in_specs=[smem(), whole((2, tok, ti...]
    psum x2 -> x0, blocking collectives: 78 us -> none  [the longest x1 46.4 us: local(): in_grad, out_grad, vec_grad = lax.psum((in_part, out_part, vec_part), 'dp')]
    ppermute x0 -> x64, starting transfers between devices: none -> 72.1 us  [the longest x18 31.2 us: from_z(): return lax.ppermute(a, 'fsdp', pairs)]
    dot_general x12 -> x0, matrix products: 71.8 us -> none  [the longest x1 10.2 us: backward_pass(): lax.dot_general(scaled_lo, d_hidden, contract_rows, preferred_element_typ...]
    unnamed x6 -> x0, waiting for transfers between devices: 23.8 us -> none
  transfers between devices with their start and end apart: 5 -> 64, of which waited for: 5 -> 28; matrix products, arithmetic and copies ran while one was open for 6% -> 13% of each run, Pallas kernels for 0% -> 5%
where the time goes in v1:
time: 448 us; the launch traced here: 442 us
  waiting for transfers between devices  200 us (45%)
  Pallas kernels  81.8 us (18%)
  starting transfers between devices  72.1 us (16%)
  local copies, waits for them, and re-layouts  41.4 us (9%)
  other arithmetic  40.2 us (9%)
  between operations  6.06 us (1%)
    ppermute x18, waiting for transfers between devices, from_z(): return lax.ppermute(a, 'fsdp', pairs)  103 us
    ppermute x24, waiting for transfers between devices, from_y(): return lax.ppermute(a, 'fsdp', pairs)  78.9 us
    ppermute x18, starting transfers between devices, from_z(): return lax.ppermute(a, 'fsdp', pairs)  31.2 us
    ppermute x24, starting transfers between devices, from_y(): return lax.ppermute(a, 'fsdp', pairs)  29.5 us
    pallas_call x1, Pallas kernels, output_step(): pl.pallas_call(kernel, grid=(steps,), in_specs=[smem(), whole((2, tok, ti...  26.4 us
    pallas_call x1, Pallas kernels, attention_backward(): pl.pallas_call(kernel, grid=(PAIRS,), in_specs=[smem(), whole((D, 2 * tok...  22.2 us
    pallas_call x1, Pallas kernels, attention_forward(): pl.pallas_call(kernel, grid=(PAIRS,), in_specs=[smem(), whole((tok, D)),...  16.2 us
    unnamed x126, local copies, waits for them, and re-layouts  14.4 us
  transfers between devices with their start and end apart: 64, of which 28 were waited for; matrix products, arithmetic and copies ran while one was open for 13% of the time, Pallas kernels for 5%

profile of v1, /device:TPU:0, one launch (start us, length us, event | category | flops | bytes accessed | tf_op | source)
XLA Modules:
  0.0 441.9 jit_solution(6762238887650138742)
XLA Ops:
  10.0 5.0 %collective-permute-start.19 = (bf16[480,384]{1,0:T(8,128)(2,1)S(1)}, bf16[480,384]{1,0:T(8,128)(2,1)S(1)}, u32[]{:S(2)}, u32[]{:S(2)}) collective-permute-start(bf16[480,384]{1,0:T(8,128)(2,1)S(1)} %pad_maximum_fusion.4), channel_id=1, source_target_pairs={{4,0},{5,1},{6,2},{7,3},{8,4},{9,5},{10,6},{11,7},{12,8},{13,9},{1... | collective-permute-start | bytes 1105928 | tf_op jit(solution)/shard_map/ppermute | solution.py:67
  18.2 5.9 %collective-permute-done.19 = bf16[480,384]{1,0:T(8,128)(2,1)S(1)} collective-permute-done((bf16[480,384]{1,0:T(8,128)(2,1)S(1)}, bf16[480,384]{1,0:T(8,128)(2,1)S(1)}, u32[]{:S(2)}, u32[]{:S(2)}) %collective-permute-start.19) | collective-permute-done | bytes 368672 | tf_op jit(solution)/shard_map/ppermute | solution.py:67
  26.3 20.4 %collective-permute-done.20 = bf16[480,384]{1,0:T(8,128)(2,1)S(1)} collective-permute-done((bf16[480,384]{1,0:T(8,128)(2,1)S(1)}, bf16[480,384]{1,0:T(8,128)(2,1)S(1)}, u32[]{:S(2)}, u32[]{:S(2)}) %collective-permute-start.20) | collective-permute-done | bytes 368672 | tf_op jit(solution)/shard_map/ppermute | solution.py:67
  52.4 5.8 %collective-permute-done.24 = bf16[480,384]{1,0:T(8,128)(2,1)S(1)} collective-permute-done((bf16[480,384]{1,0:T(8,128)(2,1)S(1)}, bf16[480,384]{1,0:T(8,128)(2,1)S(1)}, u32[]{:S(2)}, u32[]{:S(2)}) %collective-permute-start.24) | collective-permute-done | bytes 368672 | tf_op jit(solution)/shard_map/ppermute | solution.py:71
  59.0 5.4 %collective-permute-done.25 = bf16[480,384]{1,0:T(8,128)(2,1)S(1)} collective-permute-done((bf16[480,384]{1,0:T(8,128)(2,1)S(1)}, bf16[480,384]{1,0:T(8,128)(2,1)S(1)}, u32[]{:S(2)}, u32[]{:S(2)}) %collective-permute-start.25) | collective-permute-done | bytes 368672 | tf_op jit(solution)/shard_map/ppermute | solution.py:71
  66.8 4.0 collective-permute-done.10
  70.9 3.8 collective-permute-done.3.rest_1_.rest_9_
  77.4 12.1 %collective-permute-done.4.rest_2_.rest_10_ = bf16[96,1280]{1,0:T(8,128)(2,1)S(1)} collective-permute-done((bf16[96,1280]{1,0:T(8,128)(2,1)S(1)}, bf16[96,1280]{1,0:T(8,128)(2,1)S(1)}, u32[]{:S(2)}, u32[]{:S(2)}) %collective-permute-start.4) | collective-permute-done | bytes 245792 | tf_op jit(solution)/shard_map/ppermute | solution.py:67
  91.2 6.1 %collective-permute-done.6.rest_4_.rest_12_ = bf16[96,1280]{1,0:T(8,128)(2,1)S(1)} collective-permute-done((bf16[96,1280]{1,0:T(8,128)(2,1)S(1)}, bf16[96,1280]{1,0:T(8,128)(2,1)S(1)}, u32[]{:S(2)}, u32[]{:S(2)}) %collective-permute-start.6) | collective-permute-done | bytes 245792 | tf_op jit(solution)/shard_map/ppermute | solution.py:71
  97.3 12.9 %collective-permute-start.13 = (bf16[96,1536]{1,0:T(8,128)(2,1)S(1)}, bf16[96,1536]{1,0:T(8,128)(2,1)}, u32[]{:S(2)}, u32[]{:S(2)}) collective-permute-start(bf16[96,1536]{1,0:T(8,128)(2,1)S(1)} %pad_maximum_fusion.5.rest_0_), channel_id=1, source_target_pairs={{12,0},{13,1},{14,2},{15,3},{0,4},{1,5},{2,6},{3,7},{4,8},{5,9},{6... | collective-permute-start | bytes 884744 | tf_op jit(solution)/shard_map/ppermute | solution.py:67
  130.3 16.2 %attention_forward.1 = (bf16[2,512,384]{2,1,0:T(8,128)(2,1)S(1)}, bf16[2,512,384]{2,1,0:T(8,128)(2,1)S(1)}, bf16[2,512,384]{2,1,0:T(8,128)(2,1)S(1)}, bf16[2,512...) custom-call(s32[3]{0:T(128)S(1)} %pad_add_fusion.1.pos_ref, ...), custom_call_target="tpu_custom_call" | custom-call | flops 1811939328 | bytes 20971520 | tf_op jit(solution)/shard_map/attention_forward/pallas_call | solution.py:236
  153.1 7.0 %mlp_forward.1 = (bf16[2,512,1536]{2,1,0:T(8,128)(2,1)S(1)}, bf16[2,512,1536]{2,1,0:T(8,128)(2,1)S(1)}) custom-call(s32[3]{0:T(128)S(1)} %pad_add_fusion.1.pos_ref, bf16[512,768]{1,0:T(8,128)(2,1)S(1)} %copy-done.2, bf16[512,1536]{1,0:T(8,128)(2,1)S(1)} %copy-done, bf16[96,1536]{1,0:T(8,128)(2,1)S(1)} %pad_maximum_fusion.5.rest_0_, ...), custom_call_target="tpu_custom_call" | custom-call | flops 2415919104 | bytes 9437184 | tf_op jit(solution)/shard_map/mlp_forward/pallas_call | solution.py:158
  163.4 26.4 %output_step.1 = (f32[512,768]{1,0:T(8,128)}, bf16[512,768]{1,0:T(8,128)(2,1)}, bf16[2,512,384]{2,1,0:T(8,128)(2,1)}, bf16[2,512,1536]{2,1,0:T(8,128)(2,1)}, bf1...) custom-call(s32[3]{0:T(128)} %copy-done.16, bf16[2,512,384]{2,1,0:T(8,128)(2,1)} %get-tuple-element.54.att_ref, ...), custom_call_target="tpu_custom_call" | custom-call | flops 9059696640 | bytes 31457280 | tf_op jit(solution)/shard_map/output_step/pallas_call | solution.py:312
  189.8 10.1 %mlp_backward.1 = (bf16[96,1536]{1,0:T(8,128)(2,1)S(1)}, bf16[96,1536]{1,0:T(8,128)(2,1)S(1)}, bf16[96,1536]{1,0:T(8,128)(2,1)S(1)}, bf16[96,1536]{1,0:T(8,128)(...) custom-call(s32[3]{0:T(128)S(1)} %copy-done.17, ...), custom_call_target="tpu_custom_call" | custom-call | flops 4831838208 | bytes 20971520 | tf_op jit(solution)/shard_map/mlp_backward/pallas_call | solution.py:382
  199.9 22.2 %attention_backward.1 = (bf16[96,1152]{1,0:T(8,128)(2,1)}, bf16[96,1152]{1,0:T(8,128)(2,1)}, bf16[96,1152]{1,0:T(8,128)(2,1)}, bf16[96,1152]{1,0:T(8,128)(2,1)},...) custom-call(s32[3]{0:T(128)} %copy-done.16, ...), custom_call_target="tpu_custom_call" | custom-call | flops 3623878656 | bytes 20971520 | tf_op jit(solution)/shard_map/attention_backward/pallas_call | solution.py:471
  240.8 23.4 %collective-permute-done.34 = bf16[96,1280]{1,0:T(8,128)(2,1)S(1)} collective-permute-done((bf16[96,1280]{1,0:T(8,128)(2,1)S(1)}, bf16[96,1280]{1,0:T(8,128)(2,1)S(1)}, u32[]{:S(2)}, u32[]{:S(2)}) %collective-permute-start.34) | collective-permute-done | bytes 245792 | tf_op jit(solution)/shard_map/ppermute | solution.py:71
  265.8 4.9 %collective-permute-done.32 = bf16[96,1280]{1,0:T(8,128)(2,1)S(1)} collective-permute-done((bf16[96,1280]{1,0:T(8,128)(2,1)S(1)}, bf16[96,1280]{1,0:T(8,128)(2,1)S(1)}, u32[]{:S(2)}, u32[]{:S(2)}) %collective-permute-start.32) | collective-permute-done | bytes 245792 | tf_op jit(solution)/shard_map/ppermute | solution.py:71
  272.3 6.0 %collective-permute-done.30 = bf16[96,1280]{1,0:T(8,128)(2,1)S(1)} collective-permute-done((bf16[96,1280]{1,0:T(8,128)(2,1)S(1)}, bf16[96,1280]{1,0:T(8,128)(2,1)S(1)}, u32[]{:S(2)}, u32[]{:S(2)}) %collective-permute-start.30) | collective-permute-done | bytes 245792 | tf_op jit(solution)/shard_map/ppermute | solution.py:71
  281.1 5.1 %collective-permute-start.33 = (bf16[96,1280]{1,0:T(8,128)(2,1)S(1)}, bf16[96,1280]{1,0:T(8,128)(2,1)S(1)}, u32[]{:S(2)}, u32[]{:S(2)}) collective-permute-start(bf16[96,1280]{1,0:T(8,128)(2,1)S(1)} %add_convert_fusion.6), channel_id=1, source_target_pairs={{8,0},{9,1},{10,2},{11,3},{12,4},{13,5},{14,6},{15,7},{0,8},{1,9},... | collective-permute-start | bytes 737288 | tf_op jit(solution)/shard_map/ppermute | solution.py:67
  286.5 4.5 %collective-permute-done.35 = bf16[96,1280]{1,0:T(8,128)(2,1)S(1)} collective-permute-done((bf16[96,1280]{1,0:T(8,128)(2,1)S(1)}, bf16[96,1280]{1,0:T(8,128)(2,1)S(1)}, u32[]{:S(2)}, u32[]{:S(2)}) %collective-permute-start.35) | collective-permute-done | bytes 245792 | tf_op jit(solution)/shard_map/ppermute | solution.py:67
  291.0 17.8 %collective-permute-done.33 = bf16[96,1280]{1,0:T(8,128)(2,1)S(1)} collective-permute-done((bf16[96,1280]{1,0:T(8,128)(2,1)S(1)}, bf16[96,1280]{1,0:T(8,128)(2,1)S(1)}, u32[]{:S(2)}, u32[]{:S(2)}) %collective-permute-start.33) | collective-permute-done | bytes 245792 | tf_op jit(solution)/shard_map/ppermute | solution.py:67
  311.9 11.9 %collective-permute-done.43 = bf16[96,1536]{1,0:T(8,128)(2,1)S(1)} collective-permute-done((bf16[96,1536]{1,0:T(8,128)(2,1)S(1)}, bf16[96,1536]{1,0:T(8,128)(2,1)S(1)}, u32[]{:S(2)}, u32[]{:S(2)}) %collective-permute-start.43) | collective-permute-done | bytes 294944 | tf_op jit(solution)/shard_map/ppermute | solution.py:67
  327.3 8.4 %pad_maximum_fusion = bf16[3840,384]{1,0:T(8,128)(2,1)S(1)} fusion(bf16[1536,384]{1,0:T(8,128)(2,1)S(1)} %get-tuple-element.184, bf16[1536,384]{1,0:T(8,128)(2,1)S(1)} %get-tuple-element.183, bf16[384,384]{1,0:T(8,128)(2,1)S(1)} %get-tuple-element.182, bf16[384,384]{1,0:T(8,128)(2,1)S(1)} %get-tuple-element.181), kind=kLoop, calls=%fused_computation | loop fusion | flops 11796480 | bytes 5898240 | tf_op jit(solution)/shard_map/concatenate | solution.py:598
  340.7 7.3 %collective-permute-done.51 = bf16[480,384]{1,0:T(8,128)(2,1)S(1)} collective-permute-done((bf16[480,384]{1,0:T(8,128)(2,1)S(1)}, bf16[480,384]{1,0:T(8,128)(2,1)S(1)}, u32[]{:S(2)}, u32[]{:S(2)}) %collective-permute-start.51) | collective-permute-done | bytes 368672 | tf_op jit(solution)/shard_map/ppermute | solution.py:71
  348.0 7.9 %collective-permute-done.55 = bf16[480,384]{1,0:T(8,128)(2,1)S(1)} collective-permute-done((bf16[480,384]{1,0:T(8,128)(2,1)S(1)}, bf16[480,384]{1,0:T(8,128)(2,1)S(1)}, u32[]{:S(2)}, u32[]{:S(2)}) %collective-permute-start.55) | collective-permute-done | bytes 368672 | tf_op jit(solution)/shard_map/ppermute | solution.py:71
  355.9 7.9 %collective-permute-done.53 = bf16[480,384]{1,0:T(8,128)(2,1)S(1)} collective-permute-done((bf16[480,384]{1,0:T(8,128)(2,1)S(1)}, bf16[480,384]{1,0:T(8,128)(2,1)S(1)}, u32[]{:S(2)}, u32[]{:S(2)}) %collective-permute-start.53) | collective-permute-done | bytes 368672 | tf_op jit(solution)/shard_map/ppermute | solution.py:71
  373.0 4.3 collective-permute-done.56
  377.8 19.1 %collective-permute-done.54 = bf16[480,384]{1,0:T(8,128)(2,1)} collective-permute-done((bf16[480,384]{1,0:T(8,128)(2,1)}, bf16[480,384]{1,0:T(8,128)(2,1)}, u32[]{:S(2)}, u32[]{:S(2)}) %collective-permute-start.54) | collective-permute-done | bytes 368672 | tf_op jit(solution)/shard_map/ppermute | solution.py:67
  399.1 3.1 collective-permute-done.48
  420.4 3.6 collective-permute-done.62
  425.9 3.3 fusion.8
  433.9 4.1 add_multiply_fusion
  (337 shorter events, 129.8 us)
Async XLA Ops:
  4.7 111.5 %collective-permute-start = (bf16[512,1536]{0,1:T(8,128)(2,1)}, bf16[512,1536]{0,1:T(8,128)(2,1)}, u32[]{:S(2)}, u32[]{:S(2)}) collective-permute-start(bf16[512,1536]{0,1:T(8,128)(2,1)} %pad_maximum_fusion.1), channel_id=1, source_target_pairs={{0,1},{1,0},{2,3},{3,2},{4,5},{5,4},{6,7},{7,6},{8,9},{9,8},{10,11... | collective-permute-start | bytes 4718600 | tf_op jit(solution)/shard_map/ppermute | solution.py:75
  15.0 31.7 %collective-permute-start.20 = (bf16[480,384]{1,0:T(8,128)(2,1)S(1)}, bf16[480,384]{1,0:T(8,128)(2,1)S(1)}, u32[]{:S(2)}, u32[]{:S(2)}) collective-permute-start(bf16[480,384]{1,0:T(8,128)(2,1)S(1)} %pad_maximum_fusion.4), channel_id=1, source_target_pairs={{8,0},{9,1},{10,2},{11,3},{12,4},{13,5},{14,6},{15,7},{0,8},{1,9},... | collective-permute-start | bytes 1105928 | tf_op jit(solution)/shard_map/ppermute | solution.py:67
  15.3 33.7 %collective-permute-start.21 = (bf16[480,384]{1,0:T(8,128)(2,1)S(1)}, bf16[480,384]{1,0:T(8,128)(2,1)S(1)}, u32[]{:S(2)}, u32[]{:S(2)}) collective-permute-start(bf16[480,384]{1,0:T(8,128)(2,1)S(1)} %pad_maximum_fusion.4), channel_id=1, source_target_pairs={{12,0},{13,1},{14,2},{15,3},{0,4},{1,5},{2,6},{3,7},{4,8},{5,9},{6... | collective-permute-start | bytes 1105928 | tf_op jit(solution)/shard_map/ppermute | solution.py:67
  16.4 33.9 %collective-permute-start.22 = (bf16[480,384]{1,0:T(8,128)(2,1)S(1)}, bf16[480,384]{1,0:T(8,128)(2,1)S(1)}, u32[]{:S(2)}, u32[]{:S(2)}) collective-permute-start(bf16[480,384]{1,0:T(8,128)(2,1)S(1)} %pad_maximum_fusion.4), channel_id=1, source_target_pairs={{2,0},{3,1},{0,2},{1,3},{6,4},{7,5},{4,6},{5,7},{10,8},{11,9},{8,1... | collective-permute-start | bytes 1105928 | tf_op jit(solution)/shard_map/ppermute | solution.py:71
  24.0 27.1 %collective-permute-start.23 = (bf16[480,384]{1,0:T(8,128)(2,1)S(1)}, bf16[480,384]{1,0:T(8,128)(2,1)S(1)}, u32[]{:S(2)}, u32[]{:S(2)}) collective-permute-start(bf16[480,384]{1,0:T(8,128)(2,1)S(1)} %collective-permute-done.19), channel_id=1, source_target_pairs={{2,0},{3,1},{0,2},{1,3},{6,4},{7,5},{4,6},{5,7},{10,8},{11,9},{8,1... | collective-permute-start | bytes 1105928 | tf_op jit(solution)/shard_map/ppermute | solution.py:71
  50.3 20.5 %collective-permute-start.1 = (s32[512]{0:T(512)S(1)}, s32[512]{0:T(512)S(1)}, u32[]{:S(2)}, u32[]{:S(2)}) collective-permute-start(s32[512]{0:T(512)S(1)} %copy-done.53), channel_id=1, source_target_pairs={{0,1},{1,0},{2,3},{3,2},{4,5},{5,4},{6,7},{7,6},{8,9},{9,8},{10,11... | collective-permute-start | bytes 6152 | tf_op jit(solution)/shard_map/ppermute | solution.py:75
  65.2 98.2 %collective-permute-start.26 = (bf16[3840,384]{1,0:T(8,128)(2,1)}, bf16[3840,384]{1,0:T(8,128)(2,1)}, u32[]{:S(2)}, u32[]{:S(2)}) collective-permute-start(bf16[3840,384]{1,0:T(8,128)(2,1)} %constant_dynamic-update-slice_fusion.wo_ref), channel_id=1, source_target_pairs={{0,1},{1,0},{2,3},{3,2},{4,5},{5,4},{6,7},{7,6},{8,9},{9,8},{10,11... | collective-permute-start | bytes 8847368 | tf_op jit(solution)/shard_map/ppermute | solution.py:75
  74.8 35.4 %collective-permute-start.11 = (bf16[96,1536]{1,0:T(8,128)(2,1)S(1)}, bf16[96,1536]{1,0:T(8,128)(2,1)S(1)}, u32[]{:S(2)}, u32[]{:S(2)}) collective-permute-start(bf16[96,1536]{1,0:T(8,128)(2,1)S(1)} %pad_maximum_fusion.5.rest_0_), channel_id=1, source_target_pairs={{4,0},{5,1},{6,2},{7,3},{8,4},{9,5},{10,6},{11,7},{12,8},{13,9},{1... | collective-permute-start | bytes 884744 | tf_op jit(solution)/shard_map/ppermute | solution.py:67
  89.6 25.1 %collective-permute-start.12 = (bf16[96,1536]{1,0:T(8,128)(2,1)S(1)}, bf16[96,1536]{1,0:T(8,128)(2,1)S(1)}, u32[]{:S(2)}, u32[]{:S(2)}) collective-permute-start(bf16[96,1536]{1,0:T(8,128)(2,1)S(1)} %pad_maximum_fusion.5.rest_0_), channel_id=1, source_target_pairs={{8,0},{9,1},{10,2},{11,3},{12,4},{13,5},{14,6},{15,7},{0,8},{1,9},... | collective-permute-start | bytes 884744 | tf_op jit(solution)/shard_map/ppermute | solution.py:67
  97.3 26.3 %collective-permute-start.13 = (bf16[96,1536]{1,0:T(8,128)(2,1)S(1)}, bf16[96,1536]{1,0:T(8,128)(2,1)}, u32[]{:S(2)}, u32[]{:S(2)}) collective-permute-start(bf16[96,1536]{1,0:T(8,128)(2,1)S(1)} %pad_maximum_fusion.5.rest_0_), channel_id=1, source_target_pairs={{12,0},{13,1},{14,2},{15,3},{0,4},{1,5},{2,6},{3,7},{4,8},{5,9},{6... | collective-permute-start | bytes 884744 | tf_op jit(solution)/shard_map/ppermute | solution.py:67
  123.6 26.8 %collective-permute-start.14 = (bf16[96,1536]{1,0:T(8,128)(2,1)S(1)}, bf16[96,1536]{1,0:T(8,128)(2,1)S(1)}, u32[]{:S(2)}, u32[]{:S(2)}) collective-permute-start(bf16[96,1536]{1,0:T(8,128)(2,1)S(1)} %pad_maximum_fusion.5.rest_0_), channel_id=1, source_target_pairs={{2,0},{3,1},{0,2},{1,3},{6,4},{7,5},{4,6},{5,7},{10,8},{11,9},{8,1... | collective-permute-start | bytes 884744 | tf_op jit(solution)/shard_map/ppermute | solution.py:71
  125.2 25.3 %collective-permute-start.15 = (bf16[96,1536]{1,0:T(8,128)(2,1)S(1)}, bf16[96,1536]{1,0:T(8,128)(2,1)S(1)}, u32[]{:S(2)}, u32[]{:S(2)}) collective-permute-start(bf16[96,1536]{1,0:T(8,128)(2,1)S(1)} %collective-permute-done.11.rest_1_), channel_id=1, source_target_pairs={{2,0},{3,1},{0,2},{1,3},{6,4},{7,5},{4,6},{5,7},{10,8},{11,9},{8,1... | collective-permute-start | bytes 884744 | tf_op jit(solution)/shard_map/ppermute | solution.py:71
  125.7 24.8 %collective-permute-start.16 = (bf16[96,1536]{1,0:T(8,128)(2,1)S(1)}, bf16[96,1536]{1,0:T(8,128)(2,1)S(1)}, u32[]{:S(2)}, u32[]{:S(2)}) collective-permute-start(bf16[96,1536]{1,0:T(8,128)(2,1)S(1)} %collective-permute-done.12.rest_2_), channel_id=1, source_target_pairs={{2,0},{3,1},{0,2},{1,3},{6,4},{7,5},{4,6},{5,7},{10,8},{11,9},{8,1... | collective-permute-start | bytes 884744 | tf_op jit(solution)/shard_map/ppermute | solution.py:71
  128.8 24.3 %collective-permute-start.17 = (bf16[96,1536]{1,0:T(8,128)(2,1)}, bf16[96,1536]{1,0:T(8,128)(2,1)S(1)}, u32[]{:S(2)}, u32[]{:S(2)}) collective-permute-start(bf16[96,1536]{1,0:T(8,128)(2,1)} %collective-permute-done.13.rest_3_), channel_id=1, source_target_pairs={{2,0},{3,1},{0,2},{1,3},{6,4},{7,5},{4,6},{5,7},{10,8},{11,9},{8,1... | collective-permute-start | bytes 884744 | tf_op jit(solution)/shard_map/ppermute | solution.py:71
  231.9 47.9 %collective-permute-start.44 = (bf16[96,1536]{1,0:T(8,128)(2,1)S(1)}, bf16[96,1536]{1,0:T(8,128)(2,1)}, u32[]{:S(2)}, u32[]{:S(2)}) collective-permute-start(bf16[96,1536]{1,0:T(8,128)(2,1)S(1)} %get-tuple-element.90), channel_id=1, source_target_pairs={{2,0},{3,1},{0,2},{1,3},{6,4},{7,5},{4,6},{5,7},{10,8},{11,9},{8,1... | collective-permute-start | bytes 884744 | tf_op jit(solution)/shard_map/ppermute | solution.py:71
  233.4 47.6 %collective-permute-start.42 = (bf16[96,1536]{1,0:T(8,128)(2,1)S(1)}, bf16[96,1536]{1,0:T(8,128)(2,1)S(1)}, u32[]{:S(2)}, u32[]{:S(2)}) collective-permute-start(bf16[96,1536]{1,0:T(8,128)(2,1)S(1)} %get-tuple-element.88), channel_id=1, source_target_pairs={{2,0},{3,1},{0,2},{1,3},{6,4},{7,5},{4,6},{5,7},{10,8},{11,9},{8,1... | collective-permute-start | bytes 884744 | tf_op jit(solution)/shard_map/ppermute | solution.py:71
  234.0 52.3 %collective-permute-start.40 = (bf16[96,1536]{1,0:T(8,128)(2,1)S(1)}, bf16[96,1536]{1,0:T(8,128)(2,1)S(1)}, u32[]{:S(2)}, u32[]{:S(2)}) collective-permute-start(bf16[96,1536]{1,0:T(8,128)(2,1)S(1)} %get-tuple-element.86), channel_id=1, source_target_pairs={{2,0},{3,1},{0,2},{1,3},{6,4},{7,5},{4,6},{5,7},{10,8},{11,9},{8,1... | collective-permute-start | bytes 884744 | tf_op jit(solution)/shard_map/ppermute | solution.py:71
  235.5 74.9 %collective-permute-start.39 = (bf16[96,1536]{1,0:T(8,128)(2,1)S(1)}, bf16[96,1536]{1,0:T(8,128)(2,1)S(1)}, u32[]{:S(2)}, u32[]{:S(2)}) collective-permute-start(bf16[96,1536]{1,0:T(8,128)(2,1)S(1)} %get-tuple-element.84), channel_id=1, source_target_pairs={{2,0},{3,1},{0,2},{1,3},{6,4},{7,5},{4,6},{5,7},{10,8},{11,9},{8,1... | collective-permute-start | bytes 884744 | tf_op jit(solution)/shard_map/ppermute | solution.py:71
  238.2 26.0 %collective-permute-start.34 = (bf16[96,1280]{1,0:T(8,128)(2,1)S(1)}, bf16[96,1280]{1,0:T(8,128)(2,1)S(1)}, u32[]{:S(2)}, u32[]{:S(2)}) collective-permute-start(bf16[96,1280]{1,0:T(8,128)(2,1)S(1)} %pad_maximum_fusion.10), channel_id=1, source_target_pairs={{2,0},{3,1},{0,2},{1,3},{6,4},{7,5},{4,6},{5,7},{10,8},{11,9},{8,1... | collective-permute-start | bytes 737288 | tf_op jit(solution)/shard_map/ppermute | solution.py:71
  281.1 27.7 %collective-permute-start.33 = (bf16[96,1280]{1,0:T(8,128)(2,1)S(1)}, bf16[96,1280]{1,0:T(8,128)(2,1)S(1)}, u32[]{:S(2)}, u32[]{:S(2)}) collective-permute-start(bf16[96,1280]{1,0:T(8,128)(2,1)S(1)} %add_convert_fusion.6), channel_id=1, source_target_pairs={{8,0},{9,1},{10,2},{11,3},{12,4},{13,5},{14,6},{15,7},{0,8},{1,9},... | collective-permute-start | bytes 737288 | tf_op jit(solution)/shard_map/ppermute | solution.py:67
  286.3 22.6 %collective-permute-start.31 = (bf16[96,1280]{1,0:T(8,128)(2,1)S(1)}, bf16[96,1280]{1,0:T(8,128)(2,1)S(1)}, u32[]{:S(2)}, u32[]{:S(2)}) collective-permute-start(bf16[96,1280]{1,0:T(8,128)(2,1)S(1)} %add_convert_fusion.7), channel_id=1, source_target_pairs={{12,0},{13,1},{14,2},{15,3},{0,4},{1,5},{2,6},{3,7},{4,8},{5,9},{6... | collective-permute-start | bytes 737288 | tf_op jit(solution)/shard_map/ppermute | solution.py:67
  286.4 40.5 %collective-permute-start.49 = (bf16[1920,384]{1,0:T(8,128)(2,1)S(1)}, bf16[1920,384]{1,0:T(8,128)(2,1)S(1)}, u32[]{:S(2)}, u32[]{:S(2)}) collective-permute-start(bf16[1920,384]{1,0:T(8,128)(2,1)S(1)} %copy-done.56), channel_id=1, source_target_pairs={{0,1},{1,0},{2,3},{3,2},{4,5},{5,4},{6,7},{7,6},{8,9},{9,8},{10,11... | collective-permute-start | bytes 4423688 | tf_op jit(solution)/shard_map/ppermute | solution.py:75
  291.0 19.4 %collective-permute-start.45 = (bf16[96,1536]{1,0:T(8,128)(2,1)S(1)}, bf16[96,1536]{1,0:T(8,128)(2,1)S(1)}, u32[]{:S(2)}, u32[]{:S(2)}) collective-permute-start(bf16[96,1536]{1,0:T(8,128)(2,1)S(1)} %add_convert_fusion.1), channel_id=1, source_target_pairs={{4,0},{5,1},{6,2},{7,3},{8,4},{9,5},{10,6},{11,7},{12,8},{13,9},{1... | collective-permute-start | bytes 884744 | tf_op jit(solution)/shard_map/ppermute | solution.py:67
  324.8 47.6 %collective-permute-start.47 = (bf16[48,1536]{1,0:T(8,128)(2,1)}, bf16[48,1536]{1,0:T(8,128)(2,1)}, u32[]{:S(2)}, u32[]{:S(2)}) collective-permute-start(bf16[48,1536]{1,0:T(8,128)(2,1)} %get-tuple-element.200), channel_id=1, source_target_pairs={{0,1},{1,0},{2,3},{3,2},{4,5},{5,4},{6,7},{7,6},{8,9},{9,8},{10,11... | collective-permute-start | bytes 442376 | tf_op jit(solution)/shard_map/ppermute | solution.py:75
  337.0 18.8 %collective-permute-start.55 = (bf16[480,384]{1,0:T(8,128)(2,1)S(1)}, bf16[480,384]{1,0:T(8,128)(2,1)S(1)}, u32[]{:S(2)}, u32[]{:S(2)}) collective-permute-start(bf16[480,384]{1,0:T(8,128)(2,1)S(1)} %get-tuple-element.175), channel_id=1, source_target_pairs={{2,0},{3,1},{0,2},{1,3},{6,4},{7,5},{4,6},{5,7},{10,8},{11,9},{8,1... | collective-permute-start | bytes 1105928 | tf_op jit(solution)/shard_map/ppermute | solution.py:71
  338.6 25.2 %collective-permute-start.53 = (bf16[480,384]{1,0:T(8,128)(2,1)S(1)}, bf16[480,384]{1,0:T(8,128)(2,1)S(1)}, u32[]{:S(2)}, u32[]{:S(2)}) collective-permute-start(bf16[480,384]{1,0:T(8,128)(2,1)S(1)} %get-tuple-element.176), channel_id=1, source_target_pairs={{2,0},{3,1},{0,2},{1,3},{6,4},{7,5},{4,6},{5,7},{10,8},{11,9},{8,1... | collective-permute-start | bytes 1105928 | tf_op jit(solution)/shard_map/ppermute | solution.py:71
  339.1 33.4 %collective-permute-start.50 = (bf16[480,384]{1,0:T(8,128)(2,1)}, bf16[480,384]{1,0:T(8,128)(2,1)}, u32[]{:S(2)}, u32[]{:S(2)}) collective-permute-start(bf16[480,384]{1,0:T(8,128)(2,1)} %get-tuple-element.174), channel_id=1, source_target_pairs={{2,0},{3,1},{0,2},{1,3},{6,4},{7,5},{4,6},{5,7},{10,8},{11,9},{8,1... | collective-permute-start | bytes 1105928 | tf_op jit(solution)/shard_map/ppermute | solution.py:71
  364.9 32.0 %collective-permute-start.54 = (bf16[480,384]{1,0:T(8,128)(2,1)}, bf16[480,384]{1,0:T(8,128)(2,1)}, u32[]{:S(2)}, u32[]{:S(2)}) collective-permute-start(bf16[480,384]{1,0:T(8,128)(2,1)} %get-tuple-element.180), channel_id=1, source_target_pairs={{8,0},{9,1},{10,2},{11,3},{12,4},{13,5},{14,6},{15,7},{0,8},{1,9},... | collective-permute-start | bytes 1105928 | tf_op jit(solution)/shard_map/ppermute | solution.py:67
  367.8 29.6 %collective-permute-start.52 = (bf16[480,384]{1,0:T(8,128)(2,1)}, bf16[480,384]{1,0:T(8,128)(2,1)}, u32[]{:S(2)}, u32[]{:S(2)}) collective-permute-start(bf16[480,384]{1,0:T(8,128)(2,1)} %get-tuple-element.178), channel_id=1, source_target_pairs={{12,0},{13,1},{14,2},{15,3},{0,4},{1,5},{2,6},{3,7},{4,8},{5,9},{6... | collective-permute-start | bytes 1105928 | tf_op jit(solution)/shard_map/ppermute | solution.py:67
  372.4 42.5 %collective-permute-start.28 = (bf16[512,768]{0,1:T(8,128)(2,1)}, bf16[512,768]{0,1:T(8,128)(2,1)}, u32[]{:S(2)}, u32[]{:S(2)}) collective-permute-start(bf16[512,768]{0,1:T(8,128)(2,1)} %copy.162), channel_id=1, source_target_pairs={{0,1},{1,0},{2,3},{3,2},{4,5},{5,4},{6,7},{7,6},{8,9},{9,8},{10,11... | collective-permute-start | bytes 2359304 | tf_op jit(solution)/shard_map/ppermute | solution.py:75
  372.5 53.4 %collective-permute-start.27 = (bf16[512,768]{0,1:T(8,128)(2,1)}, bf16[512,768]{0,1:T(8,128)(2,1)}, u32[]{:S(2)}, u32[]{:S(2)}) collective-permute-start(bf16[512,768]{0,1:T(8,128)(2,1)} %copy.160), channel_id=1, source_target_pairs={{0,1},{1,0},{2,3},{3,2},{4,5},{5,4},{6,7},{7,6},{8,9},{9,8},{10,11... | collective-permute-start | bytes 2359304 | tf_op jit(solution)/shard_map/ppermute | solution.py:75
  377.3 21.8 %collective-permute-start.46 = (bf16[48,1536]{1,0:T(8,128)(2,1)}, bf16[48,1536]{1,0:T(8,128)(2,1)S(1)}, u32[]{:S(2)}, u32[]{:S(2)}) collective-permute-start(bf16[48,1536]{1,0:T(8,128)(2,1)} %get-tuple-element.201), channel_id=1, source_target_pairs={{0,16},{16,0},{1,17},{17,1},{2,18},{18,2},{3,19},{19,3},{4,20},{20... | collective-permute-start | bytes 442376 | tf_op jit(solution)/shard_map/ppermute | solution.py:98
  (89 other events, 1150.6 us)

commit v2 on v1

v2 whole, which is shorter than its diff:
```python
import math

import jax
import jax.numpy as jnp
from jax import lax
from jax.experimental import pallas as pl
from jax.experimental.pallas import tpu as pltpu
from jax.sharding import PartitionSpec as P

D = 768
H = 12
HD = 64
FF = 3072
ADAM_STEP = 10
PARAMS = 7080960

beta_one = 0.9
beta_two = 0.95
learning = 0.03
decay_rate = 0.1
epsilon = 1e-08
norm_eps = 1e-06

F32 = jnp.float32
BF16 = jnp.bfloat16
DH = D // 2
FH = FF // 2
PAIR = 128
PAIRS = DH // PAIR
QKV = 3 * PAIR
QW = PAIRS * QKV
VEC = 128
GELU_C = math.sqrt(2.0 / math.pi)
MIB = 1 << 20

NT = (((1,), (1,)), ((), ()))
TN = (((0,), (0,)), ((), ()))


def mm(a, b, dims=(((1,), (0,)), ((), ()))):
    return lax.dot_general(a, b, dims, preferred_element_type=F32)


def fence(*arrays):
    return lax.optimization_barrier(arrays)


class Plan:
    def __init__(self, n_fsdp, n_dp):
        chips = n_fsdp // 2
        self.n, self.n_dp, self.chips = n_fsdp, n_dp, chips
        self.zs = 4 if chips % 4 == 0 else chips
        self.ys = chips // self.zs
        index = lax.axis_index("fsdp")
        self.core = index % 2
        self.y = (index // 2) % self.ys
        self.z = index // (2 * self.ys)
        self.plane = lax.axis_index("dp") % 2
        self.pos = jnp.stack([self.z, self.y, self.core, self.plane]).astype(jnp.int32)
        self.order = [
            (c, t, s) for c in range(2) for t in range(self.ys) for s in range(self.zs)
        ]

    def index(self, z, y, core):
        return ((z % self.zs) * self.ys + y % self.ys) * 2 + core

    def all(self):
        return [
            (z, y, c) for z in range(self.zs) for y in range(self.ys) for c in range(2)
        ]

    def from_z(self, a, s):
        pairs = [(self.index(z + s, y, c), self.index(z, y, c)) for z, y, c in self.all()]
        return lax.ppermute(a, "fsdp", pairs)

    def from_y(self, a, t):
        pairs = [(self.index(z, y + t, c), self.index(z, y, c)) for z, y, c in self.all()]
        return lax.ppermute(a, "fsdp", pairs)

    def swap_core(self, a):
        pairs = [(self.index(z, y, c), self.index(z, y, 1 - c)) for z, y, c in self.all()]
        return lax.ppermute(a, "fsdp", pairs)

    def swap_plane(self, a):
        return lax.ppermute(a, "dp", [(i, i ^ 1) for i in range(self.n_dp)])

    def over_pairs(self, a):
        if self.n_dp == 2:
            return a
        groups = [list(range(p, self.n_dp, 2)) for p in range(2)]
        return lax.psum(a.astype(F32), "dp", axis_index_groups=groups)

    def total(self, a):
        m = 1
        while m < self.n:
            a = a + lax.ppermute(a, "fsdp", [(i, i ^ m) for i in range(self.n)])
            m *= 2
        return a

    def row(self, pos_ref, piece, rows):
        c, t, s = piece
        z = lax.rem(pos_ref[0] + s, self.zs)
        y = lax.rem(pos_ref[1] + t, self.ys)
        core = lax.rem(pos_ref[2] + c, 2)
        at = ((z * self.ys + y) * 2 + core) * rows
        return pl.multiple_of(at, math.gcd(rows, 16))


class Scatter:
    def __init__(self, plan, own, other):
        self.plan, self.own, self.other = plan, own, other
        self.rows = own.shape[0] // plan.chips

    def by_core(self):
        self.recv = self.plan.swap_core(self.other)

    def sums(self, begin, end, arrays):
        total = self.own[begin:end].astype(F32) + self.recv[begin:end].astype(F32)
        for a in arrays:
            total = total + a.astype(F32)
        return total

    def by_y(self):
        size = self.plan.zs * self.rows
        self.y_got = [
            self.plan.from_y(self.sums(t * size, (t + 1) * size, ()).astype(BF16), -t)
            for t in range(1, self.plan.ys)
        ]

    def part(self, s):
        at = slice(s * self.rows, (s + 1) * self.rows)
        return self.sums(at.start, at.stop, [a[at] for a in self.y_got])

    def by_z(self):
        parts = [self.part(s).astype(BF16) for s in range(1, self.plan.zs)]
        self.z_got = [self.plan.from_z(a, -s - 1) for s, a in enumerate(parts)]

    def total(self):
        total = self.part(0)
        for a in self.z_got:
            total = total + a.astype(F32)
        return total.astype(BF16)


def smem():
    return pl.BlockSpec(memory_space=pltpu.SMEM)


def whole(shape):
    return pl.BlockSpec(shape, lambda *_: (0,) * len(shape))


def params(mib=58):
    return pltpu.CompilerParams(
        dimension_semantics=("arbitrary",), vmem_limit_bytes=mib * MIB
    )


def cost(flops, nbytes, exps=0):
    return pl.CostEstimate(flops=int(flops), bytes_accessed=int(nbytes), transcendentals=int(exps))


def row_type(rows):
    return BF16 if rows % 16 == 0 else F32


def place(plan, pos_ref, refs, rows, out_ref):
    for piece, ref in zip(plan.order, refs):
        out_ref[pl.ds(plan.row(pos_ref, piece, rows), rows), :] = ref[...].astype(out_ref.dtype)


def turn(plan, pos_ref, from_ref, rows, put):
    for i, piece in enumerate(plan.order):
        put(i * rows, from_ref[pl.ds(plan.row(pos_ref, piece, rows), rows), :])


def pack_in(plan, in_weight, vec_t):
    rows = in_weight.shape[0]

    def kernel(pos_ref, w_ref, vec_ref, mlp_ref, qkv_ref):
        plane = pos_ref[3]
        gain = vec_ref[:, :1]

        def take(source, width):
            at = pl.ds(pl.multiple_of(source, PAIR), width)
            low = w_ref[:, at].astype(BF16).astype(F32)
            return (low * gain).astype(BF16)

        mlp_ref[...] = take(3 * D + plane * FH, FH)
        for pair in range(PAIRS):
            for which in range(3):
                to = pair * QKV + which * PAIR
                source = which * D + plane * DH + pair * PAIR
                qkv_ref[:, to : to + PAIR] = take(source, PAIR)
        qkv_ref[:, QW:] = vec_ref[...].astype(BF16)

    return pl.pallas_call(
        kernel,
        grid=(1,),
        in_specs=[smem(), whole(in_weight.shape), whole((rows, VEC))],
        out_specs=[whole((rows, FH)), whole((rows, QW + VEC))],
        out_shape=[
            jax.ShapeDtypeStruct((rows, FH), BF16),
            jax.ShapeDtypeStruct((rows, QW + VEC), BF16),
        ],
        compiler_params=params(16),
        cost_estimate=cost(2 * rows * 3 * D, 6 * rows * 7 * D),
        name="pack_in",
    )(plan.pos, in_weight, vec_t)


def pack_out(plan, blocks):
    n, rows, width = blocks.shape

    def kernel(pos_ref, in_ref, out_ref, full_ref):
        plane = pos_ref[3]
        for i in range(n):
            full_ref[:, i * width : (i + 1) * width] = in_ref[i].astype(F32)
        mlp = full_ref[:, pl.ds(pl.multiple_of(D + plane * FH, PAIR), FH)]
        out_ref[:, :FH] = mlp.astype(BF16)
        heads = full_ref[:, pl.ds(pl.multiple_of(plane * DH, PAIR), DH)]
        out_ref[:, FH:] = heads.astype(BF16)

    return pl.pallas_call(
        kernel,
        grid=(1,),
        in_specs=[smem(), whole(blocks.shape)],
        out_specs=whole((rows, FH + DH)),
        out_shape=jax.ShapeDtypeStruct((rows, FH + DH), BF16),
        scratch_shapes=[pltpu.VMEM((rows, D + FF), F32)],
        compiler_params=params(16),
        cost_estimate=cost(rows * (D + FF), 6 * rows * D),
        name="pack_out",
    )(plan.pos, blocks)


def unpack_out(plan, own, swap, own_heads, swap_heads):
    rows = own.shape[0]
    width = (D + FF) // plan.n

    def kernel(pos_ref, own_ref, swap_ref, own_h_ref, swap_h_ref, out_ref, full_ref):
        first = pos_ref[3] == 0
        pairs = ((own_h_ref, swap_h_ref, 0, DH), (own_ref, swap_ref, D, FH))
        for a_ref, b_ref, at, size in pairs:
            a, b = a_ref[...].astype(F32), b_ref[...].astype(F32)
            full_ref[:, at : at + size] = jnp.where(first, a, b)
            full_ref[:, at + size : at + 2 * size] = jnp.where(first, b, a)
        for i in range(plan.n):
            out_ref[i] = full_ref[:, i * width : (i + 1) * width].astype(BF16)

    return pl.pallas_call(
        kernel,
        grid=(1,),
        in_specs=[smem(), whole(own.shape), whole(own.shape)]
        + [pl.BlockSpec((rows, DH), lambda j: (0, FH // DH))] * 2,
        out_specs=whole((plan.n, rows, width)),
        out_shape=jax.ShapeDtypeStruct((plan.n, rows, width), BF16),
        scratch_shapes=[pltpu.VMEM((rows, D + FF), F32)],
        compiler_params=params(16),
        cost_estimate=cost(rows * (D + FF), 6 * rows * D),
        name="unpack_out",
    )(plan.pos, own, swap, own_heads, swap_heads)


def fold(a):
    total = a[:, :PAIR]
    for i in range(1, a.shape[1] // PAIR):
        total = total + a[:, i * PAIR : (i + 1) * PAIR]
    return total


def finish_out(blocks):
    n, rows, width = blocks.shape

    def kernel(in_ref, out_ref, sq_ref):
        grad = in_ref[...].reshape(n * rows, width).astype(F32).T
        out_ref[...] = grad
        sq_ref[...] = jnp.broadcast_to(
            jnp.sum(fold(grad * grad), axis=0, keepdims=True) * 0.125, (8, PAIR)
        )

    return pl.pallas_call(
        kernel,
        grid=(1,),
        in_specs=[whole(blocks.shape)],
        out_specs=[whole((width, D)), whole((8, PAIR))],
        out_shape=[
            jax.ShapeDtypeStruct((width, D), F32),
            jax.ShapeDtypeStruct((8, PAIR), F32),
        ],
        compiler_params=params(16),
        cost_estimate=cost(4 * width * D, 6 * width * D),
        name="finish_out",
    )(blocks)


def finish_mlp(plan, own, swap, in_weight, vec_t):
    rows = in_weight.shape[0]

    def kernel(pos_ref, own_ref, swap_ref, w_ref, vec_ref, grad_ref, sq_ref, dot_ref):
        step = pl.program_id(0)

        @pl.when(step == 0)
        def _():
            sq_ref[...] = jnp.zeros_like(sq_ref)
            dot_ref[...] = jnp.zeros_like(dot_ref)

        mine = step // 2 == pos_ref[3]
        hat = jnp.where(mine, own_ref[...].astype(F32), swap_ref[...].astype(F32))
        grad = hat * vec_ref[:, :1]
        grad_ref[...] = grad
        sq_ref[...] += fold(grad * grad)
        dot_ref[...] += fold(w_ref[...].astype(BF16).astype(F32) * hat)

    part = pl.BlockSpec((rows, D), lambda j: (0, j % 2))
    columns = pl.BlockSpec((rows, D), lambda j: (0, 3 + j))
    small = jax.ShapeDtypeStruct((rows, VEC), F32)
    return pl.pallas_call(
        kernel,
        grid=(FF // D,),
        in_specs=[smem(), part, part, columns, whole((rows, VEC))],
        out_specs=[columns, whole((rows, VEC)), whole((rows, VEC))],
        out_shape=[jax.ShapeDtypeStruct(in_weight.shape, F32), small, small],
        compiler_params=params(16),
        cost_estimate=cost(8 * rows * FF, 12 * rows * FF),
        name="finish_mlp",
    )(plan.pos, own, swap, in_weight, vec_t)


def finish_qkv(plan, own, swap, in_weight, vec_t, grad, sq, dot, sq_out):
    rows = in_weight.shape[0]

    def kernel(
        pos_ref, own_ref, swap_ref, w_ref, vec_ref, _, sq_in_ref, dot_in_ref, sqo_ref,
        grad_ref, vg_ref, total_ref, sq_ref, dot_ref,
    ):
        step = pl.program_id(0)

        @pl.when(step == 0)
        def _():
            sq_ref[...] = sq_in_ref[...]
            dot_ref[...] = dot_in_ref[...]

        first = pos_ref[3] == 0
        parts = []
        for pair in range(PAIRS):
            at = pl.ds(pl.multiple_of(pair * QKV + step * PAIR, PAIR), PAIR)
            parts.append((own_ref[:, at].astype(F32), swap_ref[:, at].astype(F32)))
        low = [jnp.where(first, a, b) for a, b in parts]
        high = [jnp.where(first, b, a) for a, b in parts]
        hat = jnp.concatenate(low + high, axis=1)
        grad = hat * vec_ref[:, :1]
        grad_ref[...] = grad
        sq_ref[...] += fold(grad * grad)
        dot_ref[...] += fold(w_ref[...].astype(BF16).astype(F32) * hat)

        @pl.when(step == 2)
        def _():
            tail = own_ref[:, QW:].astype(F32) + swap_ref[:, QW:].astype(F32)
            gain = jnp.sum(dot_ref[...], axis=1, keepdims=True)
            lane = lax.broadcasted_iota(jnp.int32, tail.shape, 1)
            vec = jnp.where(lane == 0, gain, tail)
            vg_ref[...] = vec
            total = jnp.sum(sq_ref[...] + vec * vec, axis=0, keepdims=True)
            total_ref[...] = jnp.broadcast_to(total * 0.125, (8, PAIR)) + sqo_ref[...]

    columns = pl.BlockSpec((rows, D), lambda j: (0, j))
    small = whole((rows, VEC))
    return pl.pallas_call(
        kernel,
        grid=(3,),
        in_specs=[
            smem(), whole(own.shape), whole(own.shape), columns, small,
            pl.BlockSpec(memory_space=pl.ANY), small, small, whole((8, PAIR)),
        ],
        out_specs=[columns, small, whole((8, PAIR))],
        out_shape=[
            jax.ShapeDtypeStruct(in_weight.shape, F32),
            jax.ShapeDtypeStruct((rows, VEC), F32),
            jax.ShapeDtypeStruct((8, PAIR), F32),
        ],
        scratch_shapes=[pltpu.VMEM((rows, VEC), F32)] * 2,
        input_output_aliases={5: 0},
        compiler_params=params(16),
        cost_estimate=cost(24 * rows * D, 36 * rows * D),
        name="finish_qkv",
    )(plan.pos, own, swap, in_weight, vec_t, grad, sq, dot, sq_out)


def normalize(tokens, cotangent):
    tok = tokens.shape[0]

    def kernel(t_ref, c_ref, out_ref):
        rows = t_ref[...].astype(F32)
        centre = rows - jnp.mean(rows, axis=-1, keepdims=True)
        r = lax.rsqrt(jnp.mean(centre * centre, axis=-1, keepdims=True) + norm_eps)
        out_ref[:, :D] = (centre * r).astype(BF16)
        out_ref[:, D:] = c_ref[...]

    block = pl.BlockSpec((tok // 4, D), lambda j: (j, 0))
    return pl.pallas_call(
        kernel,
        grid=(4,),
        in_specs=[block, block],
        out_specs=pl.BlockSpec((tok // 4, 2 * D), lambda j: (j, 0)),
        out_shape=jax.ShapeDtypeStruct((tok, 2 * D), BF16),
        compiler_params=params(16),
        cost_estimate=cost(10 * tok * D, 8 * tok * D),
        name="normalize",
    )(tokens, cotangent)


def transposes(plan, xc_own, xc_other, rows):
    tok = xc_own.shape[0]
    kind = row_type(rows)

    def kernel(pos_ref, own_ref, other_ref, out_ref, sum_ref, t_ref):
        for half, ref in enumerate((own_ref, other_ref)):
            t_ref[...] = ref[...].astype(F32).T.astype(kind)

            def put(at, a):
                out_ref[0, at : at + rows, half * tok : (half + 1) * tok] = a.astype(BF16)

            turn(plan, pos_ref, t_ref, rows, put)
        total = jnp.sum(own_ref[...].astype(F32), axis=0, keepdims=True)
        sum_ref[0] = jnp.broadcast_to(total, (8, D))

    return pl.pallas_call(
        kernel,
        grid=(2,),
        in_specs=[smem()] + [pl.BlockSpec((tok, D), lambda j: (0, j))] * 2,
        out_specs=[
            pl.BlockSpec((1, D, 2 * tok), lambda j: (j, 0, 0)),
            pl.BlockSpec((1, 8, D), lambda j: (j, 0, 0)),
        ],
        out_shape=[
            jax.ShapeDtypeStruct((2, D, 2 * tok), BF16),
            jax.ShapeDtypeStruct((2, 8, D), F32),
        ],
        scratch_shapes=[pltpu.VMEM((D, tok), kind)],
        compiler_params=params(24),
        cost_estimate=cost(10 * tok * D, 16 * tok * D),
        name="transposes",
    )(plan.pos, xc_own, xc_other)


def mlp_forward(plan, xc_own, xc_other, turned, pieces):
    tok = xc_own.shape[0]
    rows = pieces[0].shape[0]
    tile = 512
    n = len(pieces)

    half_d = D // 2

    def kernel(pos_ref, xo_ref, xp_ref, ct_ref, *rest):
        refs, (mix_ref, slope_ref, g_own_ref, g_other_ref, w_ref) = rest[:n], rest[n:]
        place(plan, pos_ref, refs, rows, w_ref)
        w = w_ref[...].astype(BF16)
        for half, x_ref in enumerate((xo_ref, xp_ref)):
            v = mm(x_ref[...], w)
            v2 = v * v
            t = jnp.tanh(v * (GELU_C + (GELU_C * 0.044715) * v2))
            h = 0.5 + 0.5 * t
            g = v * h
            slope = h + 2.0 * g * (1.0 - h) * (GELU_C + (3.0 * GELU_C * 0.044715) * v2)
            mix_ref[half] = g.astype(BF16)
            slope_ref[half] = slope.astype(BF16)
        g = mm(ct_ref[0], mix_ref[...].reshape(2 * tok, tile)).astype(BF16)
        g_own_ref[...] = g[:half_d]
        g_other_ref[...] = g[half_d:]

    block = pl.BlockSpec((2, tok, tile), lambda j: (0, 0, j))
    grad = pl.BlockSpec((half_d, tile), lambda j: (0, j))
    return pl.pallas_call(
        kernel,
        grid=(FH // tile,),
        in_specs=[smem()]
        + [pl.BlockSpec((tok, D), lambda j: (0, 0))] * 2
        + [pl.BlockSpec((1, D, 2 * tok), lambda j: (1, 0, 0))]
        + [pl.BlockSpec((rows, tile), lambda j: (0, j))] * n,
        out_specs=[block, block, grad, grad],
        out_shape=[jax.ShapeDtypeStruct((2, tok, FH), BF16)] * 2
        + [jax.ShapeDtypeStruct((half_d, FH), BF16)] * 2,
        scratch_shapes=[pltpu.VMEM((D, tile), row_type(rows))],
        compiler_params=params(),
        cost_estimate=cost(8 * tok * D * FH, 12 * tok * FH, 2 * tok * FH),
        name="mlp_forward",
    )(plan.pos, xc_own, xc_other, turned, *pieces)


def head_means(a, block_ref):
    high = a.astype(BF16)
    low = (a - high.astype(F32)).astype(BF16)
    return mm(high, block_ref[...]) + mm(low, block_ref[...])


def attention_forward(plan, xc_own, xc_other, pieces, id_row, id_col, block, turned):
    tok = xc_own.shape[0]
    rows = pieces[0].shape[0]
    n = len(pieces)

    half_d = D // 2

    def kernel(pos_ref, xo_ref, xp_ref, idr_ref, idc_ref, block_ref, ct_ref, *rest):
        refs, vec_refs = rest[:n], rest[n : 2 * n]
        (
            q_ref, k_ref, v_ref, nq_ref, nk_ref, rq_ref, rk_ref, att_ref, p_ref, gain_ref,
            g_own_ref, g_other_ref, w_ref, vs_ref,
        ) = rest[2 * n :]
        step = pl.program_id(0)

        @pl.when(step == 0)
        def _():
            place(plan, pos_ref, vec_refs, rows, vs_ref)
            gain_ref[...] = vs_ref[...].astype(F32).T[:8]

        place(plan, pos_ref, refs, rows, w_ref)
        w = w_ref[...].astype(BF16)
        column = pl.ds(pl.multiple_of(pos_ref[3] * DH + step * PAIR, PAIR), PAIR)
        q_gain = gain_ref[1:2, column] * (HD ** (-0.5))
        k_gain = gain_ref[2:3, column]
        lane = lax.broadcasted_iota(jnp.int32, (tok, PAIR), 1)
        first = lane < HD
        for half, x_ref in enumerate((xo_ref, xp_ref)):
            raw = mm(x_ref[...], w)

            def normed(a, gain, n_ref, r_ref, out_ref):
                centre = a - head_means(a, block_ref)
                r = lax.rsqrt(head_means(centre * centre, block_ref) + norm_eps)
                normal = centre * r
                n_ref[half] = normal.astype(BF16)
                r_ref[half] = r.astype(BF16)
                low = (normal * gain).astype(BF16)
                out_ref[half] = low
                return low

            q = normed(raw[:, :PAIR], q_gain, nq_ref, rq_ref, q_ref)
            k = normed(raw[:, PAIR : 2 * PAIR], k_gain, nk_ref, rk_ref, k_ref)
            v = raw[:, 2 * PAIR :].astype(BF16)
            v_ref[half] = v
            same = idc_ref[half] == idr_ref[half]
            att = []
            zero = jnp.zeros_like(q)
            for head in range(2):
                qh = jnp.where(first, q, zero) if head == 0 else jnp.where(first, zero, q)
                e = jnp.where(same, jnp.exp(mm(qh, k, NT)), 0.0)
                p = (e * (1.0 / jnp.sum(e, axis=1, keepdims=True))).astype(BF16)
                p_ref[half, head] = p
                att.append(mm(p, v))
            att_ref[half] = jnp.where(first, att[0], att[1]).astype(BF16)
        g = mm(ct_ref[0], att_ref[...].reshape(2 * tok, PAIR)).astype(BF16)
        g_own_ref[...] = g[:half_d]
        g_other_ref[...] = g[half_d:]

    pair = pl.BlockSpec((2, tok, PAIR), lambda j: (0, 0, j))
    small = jax.ShapeDtypeStruct((2, tok, DH), BF16)
    return pl.pallas_call(
        kernel,
        grid=(PAIRS,),
        in_specs=[smem()]
        + [pl.BlockSpec((tok, D), lambda j: (0, 0))] * 2
        + [whole((2, 1, tok)), whole((2, tok, 1)), whole((PAIR, PAIR))]
        + [pl.BlockSpec((1, D, 2 * tok), lambda j: (1, 0, 0))]
        + [pl.BlockSpec((rows, QKV), lambda j: (0, j))] * n
        + [pl.BlockSpec((rows, VEC), lambda j: (0, QW // VEC))] * n,
        out_specs=[pair] * 8
        + [pl.BlockSpec((2, 2, tok, tok), lambda j: (0, j, 0, 0)), whole((8, D))]
        + [pl.BlockSpec((half_d, PAIR), lambda j: (0, FH // PAIR + j))] * 2,
        out_shape=[small] * 8
        + [
            jax.ShapeDtypeStruct((2, 2 * PAIRS, tok, tok), BF16),
            jax.ShapeDtypeStruct((8, D), F32),
            jax.ShapeDtypeStruct((half_d, FH + DH), BF16),
            jax.ShapeDtypeStruct((half_d, FH + DH), BF16),
        ],
        scratch_shapes=[
            pltpu.VMEM((D, QKV), row_type(rows)),
            pltpu.VMEM((D, VEC), row_type(rows)),
        ],
        compiler_params=params(),
        cost_estimate=cost(4 * tok * D * QW, 20 * MIB, 12 * tok * tok),
        name="attention_forward",
    )(
        plan.pos, xc_own, xc_other, id_row, id_col, block, turned,
        *pieces, *pieces,
    )


def output_step(plan, att, mixed, slope, xc_own, xc_other, pieces):
    tok = xc_own.shape[0]
    rows = pieces[0].shape[0]
    n = len(pieces)
    tile = DH
    steps = 1 + FH // tile

    def kernel(pos_ref, att_ref, mix_ref, slope_ref, co_ref, cp_ref, *rest):
        refs = rest[:n]
        out_own_ref, out_other_ref, d_att_ref, d_in_ref, w_ref, acc_ref = rest[n:]
        step = pl.program_id(0)

        place(plan, pos_ref, refs, rows, w_ref)
        w = w_ref[...].astype(BF16)

        @pl.when(step == 0)
        def _():
            for half, ref in enumerate((co_ref, cp_ref)):
                d_att_ref[half] = mm(ref[...], w).astype(BF16)
                acc_ref[half] = mm(att_ref[half], w, NT)

        @pl.when(step > 0)
        def _():
            for half, ref in enumerate((co_ref, cp_ref)):
                d = mm(ref[...], w)
                d_in_ref[half] = (d * slope_ref[half].astype(F32)).astype(BF16)
                acc_ref[half] += mm(mix_ref[half], w, NT)

        @pl.when(step == steps - 1)
        def _():
            out_own_ref[...] = acc_ref[0]
            out_other_ref[...] = acc_ref[1].astype(BF16)

    hidden = pl.BlockSpec((2, tok, tile), lambda j: (0, 0, jnp.maximum(j - 1, 0)))
    return pl.pallas_call(
        kernel,
        grid=(steps,),
        in_specs=[smem(), whole((2, tok, tile)), hidden, hidden]
        + [pl.BlockSpec((tok, D), lambda j: (0, 1))] * 2
        + [pl.BlockSpec((rows, tile), lambda j: (0, jnp.where(j == 0, steps - 1, j - 1)))] * n,
        out_specs=[whole((tok, D)), whole((tok, D)), whole((2, tok, tile)), hidden],
        out_shape=[
            jax.ShapeDtypeStruct((tok, D), F32),
            jax.ShapeDtypeStruct((tok, D), BF16),
            jax.ShapeDtypeStruct((2, tok, DH), BF16),
            jax.ShapeDtypeStruct((2, tok, FH), BF16),
        ],
        scratch_shapes=[
            pltpu.VMEM((D, tile), row_type(rows)),
            pltpu.VMEM((2, tok, D), F32),
        ],
        compiler_params=params(),
        cost_estimate=cost(4 * 2 * tok * steps * tile * D, 20 * MIB),
        name="output_step",
    )(plan.pos, att, mixed, slope, xc_own, xc_other, *pieces)


def mlp_backward(plan, turned, d_inner, pieces, g_own, g_other):
    tok = d_inner.shape[1]
    rows = pieces[0].shape[0]
    n = len(pieces)
    half_d = D // 2
    tile = 512
    steps = FH // tile

    def kernel(pos_ref, xt_ref, d_ref, *rest):
        refs = rest[:n]
        g_own_ref, g_other_ref, e_own_ref, e_other_ref, w_ref, acc_ref = rest[n + 2 :]
        step = pl.program_id(0)

        @pl.when(step == 0)
        def _():
            acc_ref[...] = jnp.zeros_like(acc_ref)

        place(plan, pos_ref, refs, rows, w_ref)
        d = d_ref[...].reshape(2 * tok, tile)
        g = mm(xt_ref[0], d).astype(BF16)
        g_own_ref[...] = g[:half_d]
        g_other_ref[...] = g[half_d:]
        acc_ref[...] += mm(d, w_ref[...].astype(BF16), NT)

        @pl.when(step == steps - 1)
        def _():
            e_own_ref[...] = acc_ref[:tok]
            e_other_ref[...] = acc_ref[tok:]

    grad = pl.BlockSpec((half_d, tile), lambda j: (0, j))
    return pl.pallas_call(
        kernel,
        grid=(steps,),
        in_specs=[
            smem(),
            pl.BlockSpec((1, D, 2 * tok), lambda j: (0, 0, 0)),
            pl.BlockSpec((2, tok, tile), lambda j: (0, 0, j)),
        ]
        + [pl.BlockSpec((rows, tile), lambda j: (0, j))] * n
        + [pl.BlockSpec(memory_space=pl.ANY)] * 2,
        out_specs=[grad, grad] + [whole((tok, D))] * 2,
        input_output_aliases={3 + n: 0, 4 + n: 1},
        out_shape=[jax.ShapeDtypeStruct((half_d, FH + DH), BF16)] * 2
        + [jax.ShapeDtypeStruct((tok, D), F32)] * 2,
        scratch_shapes=[
            pltpu.VMEM((D, tile), row_type(rows)),
            pltpu.VMEM((2 * tok, D), F32),
        ],
        compiler_params=params(),
        cost_estimate=cost(8 * tok * D * FH, 20 * MIB),
        name="mlp_backward",
    )(plan.pos, turned, d_inner, *pieces, g_own, g_other)


def attention_backward(
    plan, turned, saved, d_att, block, gains, cot_sum, pieces, e_own, e_other, before, begin, end
):
    q, k, v, nq, nk, rq, rk, probs = saved
    tok = d_att.shape[1]
    rows = pieces[0].shape[0]
    n = len(pieces)
    half_d = D // 2
    kind = row_type(rows)
    n_before = len(before)

    def kernel(pos_ref, xt_ref, q_ref, k_ref, v_ref, nq_ref, nk_ref, rq_ref, rk_ref, p_ref,
               da_ref, block_ref, gain_ref, cot_ref, ein_own_ref, ein_other_ref, *rest):
        refs, rest = rest[:n], rest[n:]
        befores, rest = rest[:n_before], rest[n_before:]
        (
            g_own_ref, g_other_ref, e_own_ref, e_other_ref, vec_ref, w_ref, d_ref, turn_ref,
        ) = rest
        step = pl.program_id(0) + begin

        @pl.when(step == begin)
        def _():
            e_own_ref[...] = ein_own_ref[...]
            e_other_ref[...] = ein_other_ref[...]
            if befores:
                before_own_ref, before_other_ref, before_vec_ref = befores
                vec_ref[...] = before_vec_ref[...]
                g_own_ref[:, : begin * QKV] = before_own_ref[...]
                g_other_ref[:, : begin * QKV] = before_other_ref[...]
            else:
                vec_ref[...] = jnp.zeros_like(vec_ref)
                vec_ref[3:4, :] = cot_ref[0, :1]

        place(plan, pos_ref, refs, rows, w_ref)
        w = w_ref[...].astype(BF16)
        column = pl.ds(pl.multiple_of(pos_ref[3] * DH + step * PAIR, PAIR), PAIR)
        q_gain = gain_ref[1:2, column]
        k_gain = gain_ref[2:3, column]
        first = lax.broadcasted_iota(jnp.int32, (tok, PAIR), 1) < HD
        for half in range(2):
            qb, kb, vb, da = q_ref[half], k_ref[half], v_ref[half], da_ref[half]
            q_t, da_t = qb.T, da.T
            zero = jnp.zeros_like(da)
            dq, dk_t, dv_t = [], [], []
            for head in range(2):
                at = slice(head * HD, (head + 1) * HD)
                dah = jnp.where(first, da, zero) if head == 0 else jnp.where(first, zero, da)
                p_low = p_ref[half, head]
                p = p_low.astype(F32)
                t = p * mm(dah, vb, NT)
                ds = (t - p * jnp.sum(t, axis=1, keepdims=True)).astype(BF16)
                dv_t.append(mm(da_t[at], p_low))
                dk_t.append(mm(q_t[at], ds))
                dq.append(mm(ds, kb))
            d_query = jnp.where(first, dq[0], dq[1])
            d_key = jnp.concatenate(dk_t, axis=0).T
            d_value = jnp.concatenate(dv_t, axis=0).T

            def back(d, gain, n_ref, r_ref, which, factor):
                normal = n_ref[half].astype(F32)
                d = d * factor
                vec_ref[which : which + 1, column] += jnp.sum(d * normal, axis=0, keepdims=True)
                e = d * gain
                mean = head_means(e, block_ref)
                along = head_means(e * normal, block_ref)
                return (r_ref[half].astype(F32) * (e - mean - normal * along)).astype(BF16)

            at = slice(half * tok, (half + 1) * tok)
            d_ref[at, :PAIR] = back(d_query, q_gain, nq_ref, rq_ref, 1, HD ** (-0.5))
            d_ref[at, PAIR : 2 * PAIR] = back(d_key, k_gain, nk_ref, rk_ref, 2, 1.0)
            d_ref[at, 2 * PAIR :] = d_value.astype(BF16)
        g = mm(xt_ref[0], d_ref[...]).astype(BF16)
        at = pl.ds(pl.multiple_of(step * QKV, QKV), QKV)
        g_own_ref[:, at] = g[:half_d]
        g_other_ref[:, at] = g[half_d:]
        e_own_ref[...] += mm(d_ref[:tok], w, NT)
        e_other_ref[...] += mm(d_ref[tok:], w, NT)

        if end < PAIRS:
            return

        @pl.when(step == PAIRS - 1)
        def _():
            turn_ref[...] = vec_ref[...].T.astype(kind)

            def put(at, a):
                ref = g_own_ref if at < half_d else g_other_ref
                ref[at % half_d : at % half_d + rows, QW:] = a.astype(BF16)

            turn(plan, pos_ref, turn_ref, rows, put)

    width = QW + VEC if end == PAIRS else end * QKV
    pair = pl.BlockSpec((2, tok, PAIR), lambda j: (0, 0, begin + j))
    return pl.pallas_call(
        kernel,
        grid=(end - begin,),
        in_specs=[smem(), pl.BlockSpec((1, D, 2 * tok), lambda j: (0, 0, 0))]
        + [pair] * 7
        + [
            pl.BlockSpec((2, 2, tok, tok), lambda j: (0, begin + j, 0, 0)),
            pair,
            whole((PAIR, PAIR)),
            whole((8, D)),
            pl.BlockSpec((1, 8, D), lambda j: (1, 0, 0)),
            whole((tok, D)),
            whole((tok, D)),
        ]
        + [pl.BlockSpec((rows, QKV), lambda j: (0, begin + j))] * n
        + [whole(a.shape) for a in before],
        out_specs=[whole((half_d, width))] * 2 + [whole((tok, D))] * 2 + [whole((VEC, D))],
        out_shape=[jax.ShapeDtypeStruct((half_d, width), BF16)] * 2
        + [jax.ShapeDtypeStruct((tok, D), F32)] * 2
        + [jax.ShapeDtypeStruct((VEC, D), F32)],
        scratch_shapes=[
            pltpu.VMEM((D, QKV), kind),
            pltpu.VMEM((2 * tok, QKV), BF16),
            pltpu.VMEM((D, VEC), kind),
        ],
        compiler_params=params(),
        cost_estimate=cost(20 * tok * D * QKV * (end - begin), 8 * MIB * (end - begin)),
        name="attention_backward",
    )(
        plan.pos, turned, q, k, v, nq, nk, rq, rk, probs, d_att, block, gains, cot_sum,
        e_own, e_other, *pieces, *before,
    )


def token_gradient(tokens, cotangent, e_own, e_recv):
    tok = tokens.shape[0]

    def kernel(t_ref, c_ref, own_ref, recv_ref, out_ref):
        rows = t_ref[...].astype(F32)
        centre = rows - jnp.mean(rows, axis=-1, keepdims=True)
        r = lax.rsqrt(jnp.mean(centre * centre, axis=-1, keepdims=True) + norm_eps)
        normal = centre * r
        e = own_ref[...] + recv_ref[...].astype(F32)
        mean = jnp.mean(e, axis=-1, keepdims=True)
        along = jnp.mean(e * normal, axis=-1, keepdims=True)
        out_ref[...] = c_ref[...].astype(F32) + r * (e - mean - normal * along)

    block = pl.BlockSpec((tok // 4, D), lambda j: (j, 0))
    return pl.pallas_call(
        kernel,
        grid=(4,),
        in_specs=[block] * 4,
        out_specs=block,
        out_shape=jax.ShapeDtypeStruct((tok, D), F32),
        compiler_params=params(16),
        cost_estimate=cost(20 * tok * D, 14 * tok * D),
        name="token_gradient",
    )(tokens, cotangent, e_own, e_recv)


def adamw(master, first, second, grad, factor):
    clipped = grad * factor
    first_new = beta_one * first + (1.0 - beta_one) * clipped
    second_new = beta_two * second + (1.0 - beta_two) * clipped * clipped
    first_hat = first_new / (1.0 - beta_one**ADAM_STEP)
    second_hat = second_new / (1.0 - beta_two**ADAM_STEP)
    update = -learning * (first_hat / (jnp.sqrt(second_hat) + epsilon) + decay_rate * master)
    return (update, first_new, second_new)


def local(
    tokens,
    cotangent,
    image_ids,
    in_weight,
    out_weight,
    vectors,
    in_moment,
    out_moment,
    vec_moment,
    in_second,
    out_second,
    vec_second,
):
    plan = Plan(lax.axis_size("fsdp"), lax.axis_size("dp"))
    rows = in_weight.shape[0]
    out_rows = out_weight.shape[0]

    low_vec = vectors.astype(BF16).astype(F32)
    vec_t = jnp.pad(low_vec.T, ((0, 0), (0, VEC - 4)))
    mlp_piece, qkv_piece = pack_in(plan, in_weight, vec_t)
    xc_own = normalize(tokens, cotangent)

    def z_all(piece):
        return [plan.from_z(piece, s) for s in range(1, plan.zs)]

    def y_all(pieces):
        return [[plan.from_y(a, t) for a in pieces] for t in range(1, plan.ys)]

    def join(y_first, y_rest):
        return [a for first, rest in zip(y_first, y_rest) for a in first + rest]

    def core_all(pieces):
        return [plan.swap_core(a) for a in pieces]

    def held(groups):
        flat = iter(fence(*[a for group in groups for a in group]))
        return [[next(flat) for _ in group] for group in groups]

    mlp_z = z_all(mlp_piece)
    mlp_y0 = y_all([mlp_piece])
    xc_other = plan.swap_plane(xc_own)
    ids_other = plan.swap_plane(image_ids)
    out_now, mlp_z[0] = fence(out_weight, mlp_z[0])
    blocks = out_now.astype(BF16).T.reshape(plan.n, rows, out_rows)
    blocks = lax.all_to_all(blocks, "fsdp", 0, 0)
    (qkv_piece,), mlp_z = held([[qkv_piece], mlp_z])
    mlp_col = [mlp_piece] + mlp_z
    mlp_y1 = y_all(mlp_z)
    qkv_z = z_all(qkv_piece)
    qkv_y0 = y_all([qkv_piece])
    mlp_core = core_all(mlp_col)
    out_piece = pack_out(plan, blocks)
    mlp_y = join(mlp_y0, mlp_y1)
    mlp_y, qkv_z, mlp_core, (out_piece,) = held([mlp_y, qkv_z, mlp_core, [out_piece]])
    qkv_col = [qkv_piece] + qkv_z
    mlp_core = mlp_core + core_all(mlp_y)
    mlp_pieces = mlp_col + mlp_y + mlp_core
    qkv_y1 = y_all(qkv_z)
    out_z = z_all(out_piece)
    out_y0 = y_all([out_piece])
    qkv_core = core_all(qkv_col)
    turned, cot_sum = transposes(plan, xc_own, xc_other, rows)
    mixed, slope, g_own, g_other = mlp_forward(plan, xc_own, xc_other, turned, mlp_pieces)
    qkv_y = join(qkv_y0, qkv_y1)
    qkv_y, out_z, qkv_core, (mixed, slope, g_own, g_other) = held(
        [qkv_y, out_z, qkv_core, [mixed, slope, g_own, g_other]]
    )
    s_out = Scatter(plan, g_own, g_other)
    s_out.by_core()
    out_col = [out_piece] + out_z
    qkv_core = qkv_core + core_all(qkv_y)
    qkv_pieces = qkv_col + qkv_y + qkv_core
    out_y1 = y_all(out_z)
    out_core = core_all(out_col)
    ids = jnp.stack([image_ids, ids_other])
    lane = jnp.arange(PAIR) // HD
    block = jnp.where(lane[:, None] == lane[None, :], 1.0 / HD, 0.0).astype(BF16)
    *saved, att, probs, gains, m_own, m_other = attention_forward(
        plan, xc_own, xc_other, qkv_pieces, ids[:, None, :], ids[:, :, None], block, turned
    )
    saved = tuple(saved) + (probs,)
    out_y = join(out_y0, out_y1)
    out_y, out_core, (att, s_out.recv) = held([out_y, out_core, [att, s_out.recv]])
    s_out.by_y()
    out_core = out_core + core_all(out_y)
    out_pieces = out_col + out_y + out_core
    out_mine, out_theirs, d_att, d_inner = output_step(
        plan, att, mixed, slope, xc_own, xc_other, out_pieces
    )
    s_out.y_got, (out_theirs, d_att, d_inner) = held([s_out.y_got, [out_theirs, d_att, d_inner]])
    s_out.by_z()
    out_recv = plan.swap_plane(out_theirs)
    g_own, g_other, e_own, e_other = mlp_backward(
        plan, turned, d_inner, mlp_pieces, m_own, m_other
    )
    s_out.z_got, (g_own, g_other, e_own, e_other) = held(
        [s_out.z_got, [g_own, g_other, e_own, e_other]]
    )
    s_mlp = Scatter(plan, g_own, g_other)
    s_mlp.by_core()
    out_sum = s_out.total()
    s_mlp.recv, e_own = fence(s_mlp.recv, e_own)
    s_mlp.by_y()
    out_swap = plan.swap_plane(out_sum)
    g_own, g_other, e_own, e_other, _ = attention_backward(
        plan, turned, saved, d_att, block, gains, cot_sum, qkv_pieces, e_own, e_other, (),
        0, PAIRS,
    )
    s_mlp.y_got, (g_own, g_other, e_own, e_other, out_swap, out_recv) = held(
        [s_mlp.y_got, [g_own, g_other, e_own, e_other, out_swap, out_recv]]
    )
    s_qkv = Scatter(plan, g_own, g_other)
    s_qkv.by_core()
    s_mlp.by_z()
    e_recv = plan.swap_plane(e_other.astype(BF16))
    result = (
        tokens.astype(F32) + out_mine + out_recv.astype(F32) + gains[3][None, :]
    ).astype(BF16)
    s_qkv.recv, result = fence(s_qkv.recv, result)
    s_qkv.by_y()
    s_mlp.z_got, s_qkv.y_got, (e_recv,) = held([s_mlp.z_got, s_qkv.y_got, [e_recv]])
    s_qkv.by_z()
    mlp_sum = s_mlp.total()
    mlp_swap = plan.swap_plane(mlp_sum)
    mlp_sum, mlp_swap = plan.over_pairs(mlp_sum), plan.over_pairs(mlp_swap)
    blocks = unpack_out(
        plan, plan.over_pairs(out_sum), plan.over_pairs(out_swap), mlp_sum, mlp_swap
    )
    blocks = lax.all_to_all(blocks, "fsdp", 0, 0)
    input_grad = token_gradient(tokens, cotangent, e_own, e_recv)
    in_grad, sq, dot = finish_mlp(plan, mlp_sum, mlp_swap, in_weight, vec_t)
    s_qkv.z_got, (input_grad, in_grad) = held([s_qkv.z_got, [input_grad, in_grad]])
    qkv_sum = s_qkv.total()
    qkv_swap = plan.swap_plane(qkv_sum)
    out_grad, sq_out = finish_out(blocks)
    in_grad, vec_cols, square = finish_qkv(
        plan, plan.over_pairs(qkv_sum), plan.over_pairs(qkv_swap), in_weight, vec_t, in_grad,
        sq, dot, sq_out,
    )
    vec_grad = vec_cols[:, :4].T
    total = jnp.sum(plan.total(square))
    grad_norm = jnp.sqrt(total)
    factor = jnp.minimum(1.0, math.sqrt(PARAMS) / grad_norm)
    in_update, in_mean, in_square = adamw(in_weight, in_moment, in_second, in_grad, factor)
    out_update, out_mean, out_square = adamw(out_weight, out_moment, out_second, out_grad, factor)
    vec_update, vec_mean, vec_square = adamw(vectors, vec_moment, vec_second, vec_grad, factor)
    return (
        result,
        input_grad,
        in_grad,
        out_grad,
        vec_grad,
        grad_norm,
        in_update,
        out_update,
        vec_update,
        in_mean,
        out_mean,
        vec_mean,
        in_square,
        out_square,
        vec_square,
    )


def solution(mesh):
    in_specs = (
        P(("dp", "fsdp"), None),
        P(("dp", "fsdp"), None),
        P(("dp", "fsdp")),
        P("fsdp", None),
        P("fsdp", None),
        P(None, "fsdp"),
        P("fsdp", None),
        P("fsdp", None),
        P(None, "fsdp"),
        P("fsdp", None),
        P("fsdp", None),
        P(None, "fsdp"),
    )
    out_specs = (
        P(("dp", "fsdp"), None),
        P(("dp", "fsdp"), None),
        P("fsdp", None),
        P("fsdp", None),
        P(None, "fsdp"),
        P(),
        P("fsdp", None),
        P("fsdp", None),
        P(None, "fsdp"),
        P("fsdp", None),
        P("fsdp", None),
        P(None, "fsdp"),
        P("fsdp", None),
        P("fsdp", None),
        P(None, "fsdp"),
    )
    return jax.shard_map(local, mesh=mesh, in_specs=in_specs, out_specs=out_specs, check_vma=False)
```

time: 448 us -> 286 us (0.64); the launches traced: 442 us -> 285 us
  waiting for transfers between devices: 200 us -> 76.4 us
  local copies, waits for them, and re-layouts: 41.4 us -> 16.9 us
  other arithmetic: 40.2 us -> 16.1 us
  Pallas kernels: 81.8 us -> 91.6 us
  starting transfers between devices: 72.1 us -> 81.1 us
    ppermute x18, waiting for transfers between devices: 103 us -> 43.4 us  [from_z(): return lax.ppermute(a, 'fsdp', pairs)]
    ppermute x24 -> x15, waiting for transfers between devices: 78.9 us -> 20 us  [from_y(): return lax.ppermute(a, 'fsdp', pairs)]
    pallas_call x4 -> x13, Pallas kernels: 55.5 us -> 77 us  [the longest x1 23.2 us: attention_backward(): pl.pallas_call(kernel, grid=(end - begin,), in_specs=[smem(), pl.BlockSpe...]
    concatenate x11 -> x0, other arithmetic: 11.9 us -> none  [the longest x1 8.37 us: local(): jnp.concatenate([both(core, g_own[:DH], g_recv[:DH], 0), both(core, g_own...]
    pallas_call x1, Pallas kernels: 26.4 us -> 14.6 us  [output_step(): pl.pallas_call(kernel, grid=(steps,), in_specs=[smem(), whole((2, tok, ti...]
    ppermute x24 -> x15, starting transfers between devices: 29.5 us -> 18.6 us  [from_y(): return lax.ppermute(a, 'fsdp', pairs)]
    all_to_all x0 -> x2, starting transfers between devices: none -> 10.8 us  [local(): blocks = lax.all_to_all(blocks, 'fsdp', 0, 0)]
    pallas_call x4 -> x0, local copies, waits for them, and re-layouts: 9.84 us -> none  [the longest x2 5.66 us: attention_backward(): pl.pallas_call(kernel, grid=(PAIRS,), in_specs=[smem(), whole((D, 2 * tok...]
  transfers between devices with their start and end apart: 64 -> 73, of which waited for: 28 -> 24; matrix products, arithmetic and copies ran while one was open for 13% -> 5% of each run, Pallas kernels for 5% -> 31%
where the time goes in v2:
time: 286 us; the launch traced here: 285 us
  Pallas kernels  91.6 us (32%)
  starting transfers between devices  81.1 us (28%)
  waiting for transfers between devices  76.4 us (27%)
  local copies, waits for them, and re-layouts  16.9 us (6%)
  other arithmetic  16.1 us (6%)
  between operations  3.39 us (1%)
    ppermute x18, waiting for transfers between devices, from_z(): return lax.ppermute(a, 'fsdp', pairs)  43.4 us
    ppermute x18, starting transfers between devices, from_z(): return lax.ppermute(a, 'fsdp', pairs)  32.5 us
    pallas_call x1, Pallas kernels, attention_backward(): pl.pallas_call(kernel, grid=(end - begin,), in_specs=[smem(), pl.BlockSpe...  23.2 us
    ppermute x15, waiting for transfers between devices, from_y(): return lax.ppermute(a, 'fsdp', pairs)  20 us
    ppermute x15, starting transfers between devices, from_y(): return lax.ppermute(a, 'fsdp', pairs)  18.6 us
    pallas_call x1, Pallas kernels, attention_forward(): pl.pallas_call(kernel, grid=(PAIRS,), in_specs=[smem()] + [pl.BlockSpec((...  18.5 us
    pallas_call x1, Pallas kernels, output_step(): pl.pallas_call(kernel, grid=(steps,), in_specs=[smem(), whole((2, tok, ti...  14.6 us
    unnamed x140, local copies, waits for them, and re-layouts  12.7 us
  transfers between devices with their start and end apart: 73, of which 24 were waited for; matrix products, arithmetic and copies ran while one was open for 5% of the time, Pallas kernels for 31%

profile of v2, /device:TPU:0, one launch (start us, length us, event | category | flops | bytes accessed | tf_op | source)
XLA Modules:
  0.0 285.4 jit_solution(6675051097712317876)
XLA Ops:
  4.0 3.0 %collective-permute-start.25 = (bf16[512,1536]{1,0:T(8,128)(2,1)S(1)}, bf16[512,1536]{1,0:T(8,128)(2,1)}, u32[]{:S(2)}, u32[]{:S(2)}) collective-permute-start(bf16[512,1536]{1,0:T(8,128)(2,1)S(1)} %normalize.1.own_ref.xo_ref.co_ref), channel_id=1, source_target_pairs={{0,16},{16,0},{1,17},{17,1},{2,18},{18,2},{3,19},{19,3},{4,20},{20... | collective-permute-start | bytes 4718600 | tf_op jit(solution)/shard_map/ppermute | solution.py:85
  7.9 3.7 %collective-permute-start = (bf16[48,1536]{1,0:T(8,128)(2,1)S(1)}, bf16[48,1536]{1,0:T(8,128)(2,1)}, u32[]{:S(2)}, u32[]{:S(2)}) collective-permute-start(bf16[48,1536]{1,0:T(8,128)(2,1)S(1)} %get-tuple-element.131.rest_0_), channel_id=1, source_target_pairs={{4,0},{5,1},{6,2},{7,3},{8,4},{9,5},{10,6},{11,7},{12,8},{13,9},{1... | collective-permute-start | bytes 442376 | tf_op jit(solution)/shard_map/ppermute | solution.py:74
  11.6 2.8 collective-permute-done.rest_1_
  15.4 6.7 %all-to-all-start = ((bf16[16,48,240]{2,1,0:T(8,128)(2,1)}), bf16[16,48,240]{2,1,0:T(8,128)(2,1)S(1)}, u32[]{:S(2)}, u32[]{:S(2)}) async-start(bf16[16,48,240]{2,1,0:T(8,128)(2,1)} %bitcast.20), calls=%async_computation | async-start | bytes 786432 | tf_op jit(solution)/shard_map/all_to_all | solution.py:908
  22.1 2.8 collective-permute-start.1
  27.9 16.3 %collective-permute-done.1.rest_2_ = bf16[48,1536]{1,0:T(8,128)(2,1)} collective-permute-done((bf16[48,1536]{1,0:T(8,128)(2,1)S(1)}, bf16[48,1536]{1,0:T(8,128)(2,1)}, u32[]{:S(2)}, u32[]{:S(2)}) %collective-permute-start.1) | collective-permute-done | bytes 147488 | tf_op jit(solution)/shard_map/ppermute | solution.py:74
  44.1 3.8 %collective-permute-start.8 = (bf16[48,1280]{1,0:T(8,128)(2,1)S(1)}, bf16[48,1280]{1,0:T(8,128)(2,1)S(1)}, u32[]{:S(2)}, u32[]{:S(2)}) collective-permute-start(bf16[48,1280]{1,0:T(8,128)(2,1)S(1)} %get-tuple-element.133.rest_0_.rest_16_), channel_id=1, source_target_pairs={{4,0},{5,1},{6,2},{7,3},{8,4},{9,5},{10,6},{11,7},{12,8},{13,9},{1... | collective-permute-start | bytes 368648 | tf_op jit(solution)/shard_map/ppermute | solution.py:74
  48.6 3.6 %collective-permute-done.10.rest_3_.rest_19_ = bf16[48,1280]{1,0:T(8,128)(2,1)S(1)} collective-permute-done((bf16[48,1280]{1,0:T(8,128)(2,1)S(1)}, bf16[48,1280]{1,0:T(8,128)(2,1)S(1)}, u32[]{:S(2)}, u32[]{:S(2)}) %collective-permute-start.10) | collective-permute-done | bytes 122912 | tf_op jit(solution)/shard_map/ppermute | solution.py:74
  52.3 5.7 %collective-permute-done.9.rest_2_.rest_18_ = bf16[48,1280]{1,0:T(8,128)(2,1)S(1)} collective-permute-done((bf16[48,1280]{1,0:T(8,128)(2,1)S(1)}, bf16[48,1280]{1,0:T(8,128)(2,1)S(1)}, u32[]{:S(2)}, u32[]{:S(2)}) %collective-permute-start.9) | collective-permute-done | bytes 122912 | tf_op jit(solution)/shard_map/ppermute | solution.py:74
  67.9 3.0 %collective-permute-done.7.rest_7_ = bf16[48,1536]{1,0:T(8,128)(2,1)} collective-permute-done((bf16[48,1536]{1,0:T(8,128)(2,1)}, bf16[48,1536]{1,0:T(8,128)(2,1)}, u32[]{:S(2)}, u32[]{:S(2)}) %collective-permute-start.7) | collective-permute-done | bytes 147488 | tf_op jit(solution)/shard_map/ppermute | solution.py:78
  79.6 2.6 transposes.1
  83.9 2.9 %collective-permute-start.18 = (bf16[48,1920]{1,0:T(8,128)(2,1)S(1)}, bf16[48,1920]{1,0:T(8,128)(2,1)}, u32[]{:S(2)}, u32[]{:S(2)}) collective-permute-start(bf16[48,1920]{1,0:T(8,128)(2,1)S(1)} %pack_out.1.rest_0_), channel_id=1, source_target_pairs={{4,0},{5,1},{6,2},{7,3},{8,4},{9,5},{10,6},{11,7},{12,8},{13,9},{1... | collective-permute-start | bytes 552968 | tf_op jit(solution)/shard_map/ppermute | solution.py:74
  88.2 11.3 %mlp_forward.1 = (bf16[2,512,1536]{2,1,0:T(8,128)(2,1)}, bf16[2,512,1536]{2,1,0:T(8,128)(2,1)}, bf16[384,1536]{1,0:T(8,128)(2,1)}, bf16[384,1536]{1,0:T(8,128)(2,1)}) custom-call(s32[4]{0:T(128)} %copy-done.13, bf16[512,1536]{1,0:T(8,128)(2,1)} %copy-done.1, bf16[512,1536]{1,0:T(8,128)(2,1)} %collective-permute-done.25.other_ref.xp_ref.cp_ref, ...), custom_call_target="tpu_custom_call" | custom-call | flops 4831838208 | bytes 9437184 | tf_op jit(solution)/shard_map/mlp_forward/pallas_call | solution.py:474
  99.6 2.5 collective-permute-done.19.rest_2_
  104.3 3.0 %collective-permute-done.38 = s32[512]{0:T(512)S(1)} collective-permute-done((s32[512]{0:T(512)S(1)}, s32[512]{0:T(512)S(1)}, u32[]{:S(2)}, u32[]{:S(2)}) %collective-permute-start.38) | collective-permute-done | bytes 2080 | tf_op jit(solution)/shard_map/ppermute | solution.py:85
  113.1 4.4 %collective-permute-done.31.rest_5_ = bf16[48,1920]{1,0:T(8,128)(2,1)S(1)} collective-permute-done((bf16[48,1920]{1,0:T(8,128)(2,1)}, bf16[48,1920]{1,0:T(8,128)(2,1)S(1)}, u32[]{:S(2)}, u32[]{:S(2)}) %collective-permute-start.31) | collective-permute-done | bytes 184352 | tf_op jit(solution)/shard_map/ppermute | solution.py:78
  119.0 2.5 collective-permute-done.32.rest_6_
  123.1 18.5 %attention_forward.1 = (bf16[2,512,384]{2,1,0:T(8,128)(2,1)}, bf16[2,512,384]{2,1,0:T(8,128)(2,1)}, bf16[2,512,384]{2,1,0:T(8,128)(2,1)}, bf16[2,512,384]{2,1,0:...) custom-call(s32[4]{0:T(128)} %copy-done.13, ...), custom_call_target="tpu_custom_call" | custom-call | flops 1811939328 | bytes 20971520 | tf_op jit(solution)/shard_map/attention_forward/pallas_call | solution.py:557
  146.0 14.6 %output_step.1 = (f32[512,768]{1,0:T(8,128)}, bf16[512,768]{1,0:T(8,128)(2,1)}, bf16[2,512,384]{2,1,0:T(8,128)(2,1)}, bf16[2,512,1536]{2,1,0:T(8,128)(2,1)}) custom-call(s32[4]{0:T(128)} %copy-done.13, bf16[2,512,384]{2,1,0:T(8,128)(2,1)} %get-tuple-element.170.att_ref, bf16[2,512,1536]{2,1,0:T(8,128)(2,1)} %get-tuple-element.171.mix_ref, ...), custom_call_target="tpu_custom_call" | custom-call | flops 6039797760 | bytes 20971520 | tf_op jit(solution)/shard_map/output_step/pallas_call | solution.py:623
  164.5 2.8 collective-permute-start.51
  167.4 10.2 %mlp_backward.1 = (bf16[384,1920]{1,0:T(8,128)(2,1)}, bf16[384,1920]{1,0:T(8,128)(2,1)}, f32[512,768]{1,0:T(8,128)}, f32[512,768]{1,0:T(8,128)}) custom-call(s32[4]{0:T(128)} %copy-done.13, bf16[2,768,1024]{2,1,0:T(8,128)(2,1)} %copy-done.4, bf16[2,512,1536]{2,1,0:T(8,128)(2,1)} %get-tuple-element.185.d_ref, ...), custom_call_target="tpu_custom_call", output_to_operand_aliasing={{0}: (19, {}), {1}: (20, {})} | custom-call | flops 4831838208 | bytes 20971520 | tf_op jit(solution)/shard_map/mlp_backward/pallas_call | solution.py:676
  183.3 23.2 %attention_backward.1 = (bf16[384,1280]{1,0:T(8,128)(2,1)}, bf16[384,1280]{1,0:T(8,128)(2,1)}, f32[512,768]{1,0:T(8,128)}, f32[512,768]{1,0:T(8,128)}, f32[128,768]{1,0:T(8,128)}) custom-call(s32[4]{0:T(128)} %copy-done.13, bf16[2,768,1024]{2,1,0:T(8,128)(2,1)} %copy-done.4, bf16[2,512,384]{2,1,0:T(8,128)(2,1)} %get-tuple-element.196.q_ref, ...), custom_call_target="tpu_custom_call" | custom-call | flops 9059696640 | bytes 25165824 | tf_op jit(solution)/shard_map/attention_backward/pallas_call | solution.py:793
  209.8 2.5 add_convert_fusion
  215.6 2.5 collective-permute-start.58
  218.2 5.6 %collective-permute-done.57 = bf16[48,1920]{1,0:T(8,128)(2,1)S(1)} collective-permute-done((bf16[48,1920]{1,0:T(8,128)(2,1)S(1)}, bf16[48,1920]{1,0:T(8,128)(2,1)S(1)}, u32[]{:S(2)}, u32[]{:S(2)}) %collective-permute-start.57) | collective-permute-done | bytes 184352 | tf_op jit(solution)/shard_map/ppermute | solution.py:74
  223.8 7.0 %collective-permute-done.58 = bf16[48,1920]{1,0:T(8,128)(2,1)S(1)} collective-permute-done((bf16[48,1920]{1,0:T(8,128)(2,1)S(1)}, bf16[48,1920]{1,0:T(8,128)(2,1)S(1)}, u32[]{:S(2)}, u32[]{:S(2)}) %collective-permute-start.58) | collective-permute-done | bytes 184352 | tf_op jit(solution)/shard_map/ppermute | solution.py:74
  233.4 4.4 %collective-permute-start.62 = (bf16[48,1280]{1,0:T(8,128)(2,1)}, bf16[48,1280]{1,0:T(8,128)(2,1)S(1)}, u32[]{:S(2)}, u32[]{:S(2)}) collective-permute-start(bf16[48,1280]{1,0:T(8,128)(2,1)} %get-tuple-element.308), channel_id=1, source_target_pairs={{12,0},{13,1},{14,2},{15,3},{0,4},{1,5},{2,6},{3,7},{4,8},{5,9},{6... | collective-permute-start | bytes 368648 | tf_op jit(solution)/shard_map/ppermute | solution.py:74
  241.7 4.1 %all-to-all-start.1 = ((bf16[16,48,240]{2,1,0:T(8,128)(2,1)}), bf16[16,48,240]{2,1,0:T(8,128)(2,1)S(1)}, u32[]{:S(2)}, u32[]{:S(2)}) async-start(bf16[16,48,240]{2,1,0:T(8,128)(2,1)} %copy-done.7), calls=%async_computation.1 | async-start | bytes 786432 | tf_op jit(solution)/shard_map/all_to_all | solution.py:992
  248.4 2.5 token_gradient.1
  250.9 2.4 finish_mlp.1
  270.8 2.5 collective-permute-start.70
  279.0 3.2 %add_multiply_fusion.1 = (f32[240,768]{1,0:T(8,128)}, f32[240,768]{1,0:T(8,128)}, f32[240,768]{1,0:T(8,128)}) fusion(f32[240,768]{1,0:T(8,128)S(1)} %copy-done.19, f32[240,768]{1,0:T(8,128)} %get-tuple-element.278, f32[]{:T(128)S(6)} %min_shard_map.3, f32[240,768]{1,0:T(8,128)S(1)} %copy-done.30, f32[240,768]{1,0:T(8,128)} %param.22), kind=kLoop, calls=%fused_computation.10 | loop fusion | flops 2764800 | bytes 5160964 | tf_op jit(solution)/shard_map/mul | solution.py:859
  (308 shorter events, 95.5 us)
Async XLA Ops:
  4.0 75.1 %collective-permute-start.25 = (bf16[512,1536]{1,0:T(8,128)(2,1)S(1)}, bf16[512,1536]{1,0:T(8,128)(2,1)}, u32[]{:S(2)}, u32[]{:S(2)}) collective-permute-start(bf16[512,1536]{1,0:T(8,128)(2,1)S(1)} %normalize.1.own_ref.xo_ref.co_ref), channel_id=1, source_target_pairs={{0,16},{16,0},{1,17},{17,1},{2,18},{18,2},{3,19},{19,3},{4,20},{20... | collective-permute-start | bytes 4718600 | tf_op jit(solution)/shard_map/ppermute | solution.py:85
  15.4 46.8 %all-to-all-start = ((bf16[16,48,240]{2,1,0:T(8,128)(2,1)}), bf16[16,48,240]{2,1,0:T(8,128)(2,1)S(1)}, u32[]{:S(2)}, u32[]{:S(2)}) async-start(bf16[16,48,240]{2,1,0:T(8,128)(2,1)} %bitcast.20), calls=%async_computation | async-start | bytes 786432 | tf_op jit(solution)/shard_map/all_to_all | solution.py:908
  22.1 22.0 %collective-permute-start.1 = (bf16[48,1536]{1,0:T(8,128)(2,1)S(1)}, bf16[48,1536]{1,0:T(8,128)(2,1)}, u32[]{:S(2)}, u32[]{:S(2)}) collective-permute-start(bf16[48,1536]{1,0:T(8,128)(2,1)S(1)} %get-tuple-element.131.rest_0_), channel_id=1, source_target_pairs={{8,0},{9,1},{10,2},{11,3},{12,4},{13,5},{14,6},{15,7},{0,8},{1,9},... | collective-permute-start | bytes 442376 | tf_op jit(solution)/shard_map/ppermute | solution.py:74
  24.9 19.2 %collective-permute-start.2 = (bf16[48,1536]{1,0:T(8,128)(2,1)S(1)}, bf16[48,1536]{1,0:T(8,128)(2,1)}, u32[]{:S(2)}, u32[]{:S(2)}) collective-permute-start(bf16[48,1536]{1,0:T(8,128)(2,1)S(1)} %get-tuple-element.131.rest_0_), channel_id=1, source_target_pairs={{12,0},{13,1},{14,2},{15,3},{0,4},{1,5},{2,6},{3,7},{4,8},{5,9},{6... | collective-permute-start | bytes 442376 | tf_op jit(solution)/shard_map/ppermute | solution.py:74
  26.4 21.6 %collective-permute-start.11 = (bf16[48,1536]{1,0:T(8,128)(2,1)S(1)}, bf16[48,1536]{1,0:T(8,128)(2,1)S(1)}, u32[]{:S(2)}, u32[]{:S(2)}) collective-permute-start(bf16[48,1536]{1,0:T(8,128)(2,1)S(1)} %get-tuple-element.131.rest_0_), channel_id=1, source_target_pairs={{0,1},{1,0},{2,3},{3,2},{4,5},{5,4},{6,7},{7,6},{8,9},{9,8},{10,11... | collective-permute-start | bytes 442376 | tf_op jit(solution)/shard_map/ppermute | solution.py:82
  26.4 21.6 %collective-permute-start.4 = (bf16[48,1536]{1,0:T(8,128)(2,1)S(1)}, bf16[48,1536]{1,0:T(8,128)(2,1)S(1)}, u32[]{:S(2)}, u32[]{:S(2)}) collective-permute-start(bf16[48,1536]{1,0:T(8,128)(2,1)S(1)} %get-tuple-element.131.rest_0_), channel_id=1, source_target_pairs={{2,0},{3,1},{0,2},{1,3},{6,4},{7,5},{4,6},{5,7},{10,8},{11,9},{8,1... | collective-permute-start | bytes 442376 | tf_op jit(solution)/shard_map/ppermute | solution.py:78
  74.4 12.4 %collective-permute-start.26 = (bf16[48,1536]{1,0:T(8,128)(2,1)}, bf16[48,1536]{1,0:T(8,128)(2,1)S(1)}, u32[]{:S(2)}, u32[]{:S(2)}) collective-permute-start(bf16[48,1536]{1,0:T(8,128)(2,1)} %copy-done.60), channel_id=1, source_target_pairs={{0,1},{1,0},{2,3},{3,2},{4,5},{5,4},{6,7},{7,6},{8,9},{9,8},{10,11... | collective-permute-start | bytes 442376 | tf_op jit(solution)/shard_map/ppermute | solution.py:82
  83.9 15.7 %collective-permute-start.18 = (bf16[48,1920]{1,0:T(8,128)(2,1)S(1)}, bf16[48,1920]{1,0:T(8,128)(2,1)}, u32[]{:S(2)}, u32[]{:S(2)}) collective-permute-start(bf16[48,1920]{1,0:T(8,128)(2,1)S(1)} %pack_out.1.rest_0_), channel_id=1, source_target_pairs={{4,0},{5,1},{6,2},{7,3},{8,4},{9,5},{10,6},{11,7},{12,8},{13,9},{1... | collective-permute-start | bytes 552968 | tf_op jit(solution)/shard_map/ppermute | solution.py:74
  86.8 15.3 %collective-permute-start.19 = (bf16[48,1920]{1,0:T(8,128)(2,1)S(1)}, bf16[48,1920]{1,0:T(8,128)(2,1)}, u32[]{:S(2)}, u32[]{:S(2)}) collective-permute-start(bf16[48,1920]{1,0:T(8,128)(2,1)S(1)} %pack_out.1.rest_0_), channel_id=1, source_target_pairs={{8,0},{9,1},{10,2},{11,3},{12,4},{13,5},{14,6},{15,7},{0,8},{1,9},... | collective-permute-start | bytes 552968 | tf_op jit(solution)/shard_map/ppermute | solution.py:74
  86.8 15.3 %collective-permute-start.20 = (bf16[48,1920]{1,0:T(8,128)(2,1)S(1)}, bf16[48,1920]{1,0:T(8,128)(2,1)}, u32[]{:S(2)}, u32[]{:S(2)}) collective-permute-start(bf16[48,1920]{1,0:T(8,128)(2,1)S(1)} %pack_out.1.rest_0_), channel_id=1, source_target_pairs={{12,0},{13,1},{14,2},{15,3},{0,4},{1,5},{2,6},{3,7},{4,8},{5,9},{6... | collective-permute-start | bytes 552968 | tf_op jit(solution)/shard_map/ppermute | solution.py:74
  87.5 12.1 %collective-permute-start.23 = (bf16[48,1280]{1,0:T(8,128)(2,1)S(1)}, bf16[48,1280]{1,0:T(8,128)(2,1)S(1)}, u32[]{:S(2)}, u32[]{:S(2)}) collective-permute-start(bf16[48,1280]{1,0:T(8,128)(2,1)S(1)} %copy-done.34), channel_id=1, source_target_pairs={{0,1},{1,0},{2,3},{3,2},{4,5},{5,4},{6,7},{7,6},{8,9},{9,8},{10,11... | collective-permute-start | bytes 368648 | tf_op jit(solution)/shard_map/ppermute | solution.py:82
  87.6 12.0 %collective-permute-start.24 = (bf16[48,1280]{1,0:T(8,128)(2,1)S(1)}, bf16[48,1280]{1,0:T(8,128)(2,1)S(1)}, u32[]{:S(2)}, u32[]{:S(2)}) collective-permute-start(bf16[48,1280]{1,0:T(8,128)(2,1)S(1)} %collective-permute-done.10.rest_3_.rest_19_), channel_id=1, source_target_pairs={{0,1},{1,0},{2,3},{3,2},{4,5},{5,4},{6,7},{7,6},{8,9},{9,8},{10,11... | collective-permute-start | bytes 368648 | tf_op jit(solution)/shard_map/ppermute | solution.py:82
  102.1 39.6 %collective-permute-start.43 = (bf16[384,1536]{1,0:T(8,128)(2,1)}, bf16[384,1536]{1,0:T(8,128)(2,1)S(1)}, u32[]{:S(2)}, u32[]{:S(2)}) collective-permute-start(bf16[384,1536]{1,0:T(8,128)(2,1)} %get-tuple-element.168), channel_id=1, source_target_pairs={{0,1},{1,0},{2,3},{3,2},{4,5},{5,4},{6,7},{7,6},{8,9},{9,8},{10,11... | collective-permute-start | bytes 3538952 | tf_op jit(solution)/shard_map/ppermute | solution.py:82
  112.5 29.1 %collective-permute-start.35 = (bf16[48,1920]{1,0:T(8,128)(2,1)}, bf16[48,1920]{1,0:T(8,128)(2,1)}, u32[]{:S(2)}, u32[]{:S(2)}) collective-permute-start(bf16[48,1920]{1,0:T(8,128)(2,1)} %collective-permute-done.18.rest_1_), channel_id=1, source_target_pairs={{0,1},{1,0},{2,3},{3,2},{4,5},{5,4},{6,7},{7,6},{8,9},{9,8},{10,11... | collective-permute-start | bytes 552968 | tf_op jit(solution)/shard_map/ppermute | solution.py:82
  112.5 29.1 %collective-permute-start.36 = (bf16[48,1920]{1,0:T(8,128)(2,1)}, bf16[48,1920]{1,0:T(8,128)(2,1)}, u32[]{:S(2)}, u32[]{:S(2)}) collective-permute-start(bf16[48,1920]{1,0:T(8,128)(2,1)} %collective-permute-done.19.rest_2_), channel_id=1, source_target_pairs={{0,1},{1,0},{2,3},{3,2},{4,5},{5,4},{6,7},{7,6},{8,9},{9,8},{10,11... | collective-permute-start | bytes 552968 | tf_op jit(solution)/shard_map/ppermute | solution.py:82
  117.5 24.1 %collective-permute-start.33 = (bf16[48,1920]{1,0:T(8,128)(2,1)}, bf16[48,1920]{1,0:T(8,128)(2,1)}, u32[]{:S(2)}, u32[]{:S(2)}) collective-permute-start(bf16[48,1920]{1,0:T(8,128)(2,1)} %collective-permute-done.20.rest_3_), channel_id=1, source_target_pairs={{2,0},{3,1},{0,2},{1,3},{6,4},{7,5},{4,6},{5,7},{10,8},{11,9},{8,1... | collective-permute-start | bytes 552968 | tf_op jit(solution)/shard_map/ppermute | solution.py:78
  121.4 20.2 %collective-permute-start.37 = (bf16[48,1920]{1,0:T(8,128)(2,1)}, bf16[48,1920]{1,0:T(8,128)(2,1)}, u32[]{:S(2)}, u32[]{:S(2)}) collective-permute-start(bf16[48,1920]{1,0:T(8,128)(2,1)} %collective-permute-done.20.rest_3_), channel_id=1, source_target_pairs={{0,1},{1,0},{2,3},{3,2},{4,5},{5,4},{6,7},{7,6},{8,9},{9,8},{10,11... | collective-permute-start | bytes 552968 | tf_op jit(solution)/shard_map/ppermute | solution.py:82
  143.0 17.6 %collective-permute-start.44 = (bf16[192,1536]{1,0:T(8,128)(2,1)S(1)}, bf16[192,1536]{1,0:T(8,128)(2,1)S(1)}, u32[]{:S(2)}, u32[]{:S(2)}) collective-permute-start(bf16[192,1536]{1,0:T(8,128)(2,1)S(1)} %add_convert_fusion.2), channel_id=1, source_target_pairs={{2,0},{3,1},{0,2},{1,3},{6,4},{7,5},{4,6},{5,7},{10,8},{11,9},{8,1... | collective-permute-start | bytes 1769480 | tf_op jit(solution)/shard_map/ppermute | solution.py:78
  160.8 16.8 %collective-permute-start.49 = (bf16[48,1536]{1,0:T(8,128)(2,1)S(1)}, bf16[48,1536]{1,0:T(8,128)(2,1)S(1)}, u32[]{:S(2)}, u32[]{:S(2)}) collective-permute-start(bf16[48,1536]{1,0:T(8,128)(2,1)S(1)} %get-tuple-element.305), channel_id=1, source_target_pairs={{12,0},{13,1},{14,2},{15,3},{0,4},{1,5},{2,6},{3,7},{4,8},{5,9},{6... | collective-permute-start | bytes 442376 | tf_op jit(solution)/shard_map/ppermute | solution.py:74
  162.4 15.2 %collective-permute-start.50 = (bf16[48,1536]{1,0:T(8,128)(2,1)S(1)}, bf16[48,1536]{1,0:T(8,128)(2,1)S(1)}, u32[]{:S(2)}, u32[]{:S(2)}) collective-permute-start(bf16[48,1536]{1,0:T(8,128)(2,1)S(1)} %get-tuple-element.304), channel_id=1, source_target_pairs={{8,0},{9,1},{10,2},{11,3},{12,4},{13,5},{14,6},{15,7},{0,8},{1,9},... | collective-permute-start | bytes 442376 | tf_op jit(solution)/shard_map/ppermute | solution.py:74
  164.5 13.1 %collective-permute-start.51 = (bf16[48,1536]{1,0:T(8,128)(2,1)S(1)}, bf16[48,1536]{1,0:T(8,128)(2,1)S(1)}, u32[]{:S(2)}, u32[]{:S(2)}) collective-permute-start(bf16[48,1536]{1,0:T(8,128)(2,1)S(1)} %get-tuple-element.303), channel_id=1, source_target_pairs={{4,0},{5,1},{6,2},{7,3},{8,4},{9,5},{10,6},{11,7},{12,8},{13,9},{1... | collective-permute-start | bytes 442376 | tf_op jit(solution)/shard_map/ppermute | solution.py:74
  177.7 28.8 %collective-permute-start.55 = (bf16[512,768]{1,0:T(8,128)(2,1)}, bf16[512,768]{1,0:T(8,128)(2,1)}, u32[]{:S(2)}, u32[]{:S(2)}) collective-permute-start(bf16[512,768]{1,0:T(8,128)(2,1)} %get-tuple-element.216), channel_id=1, source_target_pairs={{0,16},{16,0},{1,17},{17,1},{2,18},{18,2},{3,19},{19,3},{4,20},{20... | collective-permute-start | bytes 2359304 | tf_op jit(solution)/shard_map/ppermute | solution.py:85
  179.3 27.2 %collective-permute-start.54 = (bf16[48,1536]{1,0:T(8,128)(2,1)S(1)}, bf16[48,1536]{1,0:T(8,128)(2,1)S(1)}, u32[]{:S(2)}, u32[]{:S(2)}) collective-permute-start(bf16[48,1536]{1,0:T(8,128)(2,1)S(1)} %add_convert_fusion.8.own_ref), channel_id=1, source_target_pairs={{0,16},{16,0},{1,17},{17,1},{2,18},{18,2},{3,19},{19,3},{4,20},{20... | collective-permute-start | bytes 442376 | tf_op jit(solution)/shard_map/ppermute | solution.py:85
  182.5 24.0 %collective-permute-start.53 = (bf16[192,1920]{1,0:T(8,128)(2,1)S(1)}, bf16[192,1920]{1,0:T(8,128)(2,1)S(1)}, u32[]{:S(2)}, u32[]{:S(2)}) collective-permute-start(bf16[192,1920]{1,0:T(8,128)(2,1)S(1)} %add_convert_fusion.1), channel_id=1, source_target_pairs={{2,0},{3,1},{0,2},{1,3},{6,4},{7,5},{4,6},{5,7},{10,8},{11,9},{8,1... | collective-permute-start | bytes 2211848 | tf_op jit(solution)/shard_map/ppermute | solution.py:78
  209.2 21.6 %collective-permute-start.61 = (bf16[512,768]{1,0:T(8,128)(2,1)S(1)}, bf16[512,768]{1,0:T(8,128)(2,1)S(1)}, u32[]{:S(2)}, u32[]{:S(2)}) collective-permute-start(bf16[512,768]{1,0:T(8,128)(2,1)S(1)} %convert_element_type.272), channel_id=1, source_target_pairs={{0,16},{16,0},{1,17},{17,1},{2,18},{18,2},{3,19},{19,3},{4,20},{20... | collective-permute-start | bytes 2359304 | tf_op jit(solution)/shard_map/ppermute | solution.py:85
  212.5 18.3 %collective-permute-start.60 = (bf16[192,1280]{1,0:T(8,128)(2,1)S(1)}, bf16[192,1280]{1,0:T(8,128)(2,1)S(1)}, u32[]{:S(2)}, u32[]{:S(2)}) collective-permute-start(bf16[192,1280]{1,0:T(8,128)(2,1)S(1)} %add_convert_fusion.3), channel_id=1, source_target_pairs={{2,0},{3,1},{0,2},{1,3},{6,4},{7,5},{4,6},{5,7},{10,8},{11,9},{8,1... | collective-permute-start | bytes 1474568 | tf_op jit(solution)/shard_map/ppermute | solution.py:78
  215.6 15.2 %collective-permute-start.58 = (bf16[48,1920]{1,0:T(8,128)(2,1)S(1)}, bf16[48,1920]{1,0:T(8,128)(2,1)S(1)}, u32[]{:S(2)}, u32[]{:S(2)}) collective-permute-start(bf16[48,1920]{1,0:T(8,128)(2,1)S(1)} %get-tuple-element.301), channel_id=1, source_target_pairs={{8,0},{9,1},{10,2},{11,3},{12,4},{13,5},{14,6},{15,7},{0,8},{1,9},... | collective-permute-start | bytes 552968 | tf_op jit(solution)/shard_map/ppermute | solution.py:74
  218.1 12.7 %collective-permute-start.59 = (bf16[48,1920]{1,0:T(8,128)(2,1)S(1)}, bf16[48,1920]{1,0:T(8,128)(2,1)S(1)}, u32[]{:S(2)}, u32[]{:S(2)}) collective-permute-start(bf16[48,1920]{1,0:T(8,128)(2,1)S(1)} %get-tuple-element.300), channel_id=1, source_target_pairs={{4,0},{5,1},{6,2},{7,3},{8,4},{9,5},{10,6},{11,7},{12,8},{13,9},{1... | collective-permute-start | bytes 552968 | tf_op jit(solution)/shard_map/ppermute | solution.py:74
  233.4 19.9 %collective-permute-start.62 = (bf16[48,1280]{1,0:T(8,128)(2,1)}, bf16[48,1280]{1,0:T(8,128)(2,1)S(1)}, u32[]{:S(2)}, u32[]{:S(2)}) collective-permute-start(bf16[48,1280]{1,0:T(8,128)(2,1)} %get-tuple-element.308), channel_id=1, source_target_pairs={{12,0},{13,1},{14,2},{15,3},{0,4},{1,5},{2,6},{3,7},{4,8},{5,9},{6... | collective-permute-start | bytes 368648 | tf_op jit(solution)/shard_map/ppermute | solution.py:74
  237.8 15.5 %collective-permute-start.63 = (bf16[48,1280]{1,0:T(8,128)(2,1)}, bf16[48,1280]{1,0:T(8,128)(2,1)}, u32[]{:S(2)}, u32[]{:S(2)}) collective-permute-start(bf16[48,1280]{1,0:T(8,128)(2,1)} %get-tuple-element.307), channel_id=1, source_target_pairs={{8,0},{9,1},{10,2},{11,3},{12,4},{13,5},{14,6},{15,7},{0,8},{1,9},... | collective-permute-start | bytes 368648 | tf_op jit(solution)/shard_map/ppermute | solution.py:74
  237.8 15.4 %collective-permute-start.64 = (bf16[48,1280]{1,0:T(8,128)(2,1)}, bf16[48,1280]{1,0:T(8,128)(2,1)}, u32[]{:S(2)}, u32[]{:S(2)}) collective-permute-start(bf16[48,1280]{1,0:T(8,128)(2,1)} %get-tuple-element.306), channel_id=1, source_target_pairs={{4,0},{5,1},{6,2},{7,3},{8,4},{9,5},{10,6},{11,7},{12,8},{13,9},{1... | collective-permute-start | bytes 368648 | tf_op jit(solution)/shard_map/ppermute | solution.py:74
  241.7 16.3 %all-to-all-start.1 = ((bf16[16,48,240]{2,1,0:T(8,128)(2,1)}), bf16[16,48,240]{2,1,0:T(8,128)(2,1)S(1)}, u32[]{:S(2)}, u32[]{:S(2)}) async-start(bf16[16,48,240]{2,1,0:T(8,128)(2,1)} %copy-done.7), calls=%async_computation.1 | async-start | bytes 786432 | tf_op jit(solution)/shard_map/all_to_all | solution.py:992
  (109 other events, 1178.0 us)

commit v3 on v2

--- a/solution.py
+++ b/solution.py
@@ -91,10 +91,14 @@
         return lax.psum(a.astype(F32), "dp", axis_index_groups=groups)
 
     def total(self, a):
-        m = 1
-        while m < self.n:
-            a = a + lax.ppermute(a, "fsdp", [(i, i ^ m) for i in range(self.n)])
-            m *= 2
+        a = a + self.swap_core(a)
+        for exchange, size in ((self.from_y, self.ys), (self.from_z, self.zs)):
+            if size == 2:
+                a = a + exchange(a, 1)
+            elif size == 4:
+                a = (a + exchange(a, 2)) + (exchange(a, 1) + exchange(a, 3))
+            elif size > 1:
+                a = sum([exchange(a, s) for s in range(1, size)], a)
         return a
 
     def row(self, pos_ref, piece, rows):
@@ -165,8 +169,10 @@
 
 
 def place(plan, pos_ref, refs, rows, out_ref):
-    for piece, ref in zip(plan.order, refs):
-        out_ref[pl.ds(plan.row(pos_ref, piece, rows), rows), :] = ref[...].astype(out_ref.dtype)
+    for i, piece in enumerate(plan.order):
+        ref, at = refs[i // plan.zs], i % plan.zs * rows
+        part = ref[at : at + rows, :].astype(out_ref.dtype)
+        out_ref[pl.ds(plan.row(pos_ref, piece, rows), rows), :] = part
 
 
 def turn(plan, pos_ref, from_ref, rows, put):
@@ -207,6 +213,27 @@
         cost_estimate=cost(2 * rows * 3 * D, 6 * rows * 7 * D),
         name="pack_in",
     )(plan.pos, in_weight, vec_t)
+
+
+def split_out(plan, out_weight, rows):
+    width = out_weight.shape[0]
+
+    def kernel(w_ref, out_ref):
+        full = w_ref[...].T.astype(BF16)
+        for i in range(plan.n):
+            out_ref[i] = full[i * rows : (i + 1) * rows]
+
+    shape = (plan.n, rows, width)
+    return pl.pallas_call(
+        kernel,
+        grid=(1,),
+        in_specs=[whole(out_weight.shape)],
+        out_specs=whole(shape),
+        out_shape=jax.ShapeDtypeStruct(shape, BF16),
+        compiler_params=params(16),
+        cost_estimate=cost(0, 6 * width * D),
+        name="split_out",
+    )(out_weight)
 
 
 def pack_out(plan, blocks):
@@ -234,32 +261,50 @@
     )(plan.pos, blocks)
 
 
-def unpack_out(plan, own, swap, own_heads, swap_heads):
+def unpack_out(plan, own, swap):
     rows = own.shape[0]
     width = (D + FF) // plan.n
 
-    def kernel(pos_ref, own_ref, swap_ref, own_h_ref, swap_h_ref, out_ref, full_ref):
+    def kernel(pos_ref, own_ref, swap_ref, out_ref, full_ref):
         first = pos_ref[3] == 0
-        pairs = ((own_h_ref, swap_h_ref, 0, DH), (own_ref, swap_ref, D, FH))
-        for a_ref, b_ref, at, size in pairs:
-            a, b = a_ref[...].astype(F32), b_ref[...].astype(F32)
-            full_ref[:, at : at + size] = jnp.where(first, a, b)
-            full_ref[:, at + size : at + 2 * size] = jnp.where(first, b, a)
+        a, b = own_ref[...].astype(F32), swap_ref[...].astype(F32)
+        for plane, part in enumerate((jnp.where(first, a, b), jnp.where(first, b, a))):
+            full_ref[:, D + plane * FH : D + (plane + 1) * FH] = part[:, :FH]
+            full_ref[:, plane * DH : (plane + 1) * DH] = part[:, FH:]
         for i in range(plan.n):
             out_ref[i] = full_ref[:, i * width : (i + 1) * width].astype(BF16)
 
     return pl.pallas_call(
         kernel,
         grid=(1,),
-        in_specs=[smem(), whole(own.shape), whole(own.shape)]
-        + [pl.BlockSpec((rows, DH), lambda j: (0, FH // DH))] * 2,
+        in_specs=[smem(), whole(own.shape), whole(own.shape)],
         out_specs=whole((plan.n, rows, width)),
         out_shape=jax.ShapeDtypeStruct((plan.n, rows, width), BF16),
         scratch_shapes=[pltpu.VMEM((rows, D + FF), F32)],
         compiler_params=params(16),
         cost_estimate=cost(rows * (D + FF), 6 * rows * D),
         name="unpack_out",
-    )(plan.pos, own, swap, own_heads, swap_heads)
+    )(plan.pos, own, swap)
+
+
+def stack(pieces):
+    rows, width = pieces[0].shape
+
+    def kernel(*refs):
+        for i, ref in enumerate(refs[:-1]):
+            refs[-1][i * rows : (i + 1) * rows, :] = ref[...]
+
+    shape = (len(pieces) * rows, width)
+    return pl.pallas_call(
+        kernel,
+        grid=(1,),
+        in_specs=[whole((rows, width))] * len(pieces),
+        out_specs=whole(shape),
+        out_shape=jax.ShapeDtypeStruct(shape, BF16),
+        compiler_params=params(8),
+        cost_estimate=cost(0, 4 * shape[0] * width),
+        name="stack",
+    )(*pieces)
 
 
 def fold(a):
@@ -331,8 +376,8 @@
     rows = in_weight.shape[0]
 
     def kernel(
-        pos_ref, own_ref, swap_ref, w_ref, vec_ref, _, sq_in_ref, dot_in_ref, sqo_ref,
-        grad_ref, vg_ref, total_ref, sq_ref, dot_ref,
+        pos_ref, own_ref, swap_ref, w_ref, vec_ref, _,
+        sq_in_ref, dot_in_ref, sqo_ref, grad_ref, vg_ref, total_ref, sq_ref, dot_ref,
     ):
         step = pl.program_id(0)
 
@@ -345,7 +390,7 @@
         parts = []
         for pair in range(PAIRS):
             at = pl.ds(pl.multiple_of(pair * QKV + step * PAIR, PAIR), PAIR)
-            parts.append((own_ref[:, at].astype(F32), swap_ref[:, at].astype(F32)))
+            parts.append([ref[:, at].astype(F32) for ref in (own_ref, swap_ref)])
         low = [jnp.where(first, a, b) for a, b in parts]
         high = [jnp.where(first, b, a) for a, b in parts]
         hat = jnp.concatenate(low + high, axis=1)
@@ -387,31 +432,36 @@
     )(plan.pos, own, swap, in_weight, vec_t, grad, sq, dot, sq_out)
 
 
-def normalize(tokens, cotangent):
+IDS = 16
+
+
+def normalize(tokens, cotangent, ids):
     tok = tokens.shape[0]
 
-    def kernel(t_ref, c_ref, out_ref):
+    def kernel(t_ref, c_ref, id_ref, out_ref):
         rows = t_ref[...].astype(F32)
         centre = rows - jnp.mean(rows, axis=-1, keepdims=True)
         r = lax.rsqrt(jnp.mean(centre * centre, axis=-1, keepdims=True) + norm_eps)
-        out_ref[:, :D] = (centre * r).astype(BF16)
-        out_ref[:, D:] = c_ref[...]
-
-    block = pl.BlockSpec((tok // 4, D), lambda j: (j, 0))
-    return pl.pallas_call(
-        kernel,
-        grid=(4,),
-        in_specs=[block, block],
-        out_specs=pl.BlockSpec((tok // 4, 2 * D), lambda j: (j, 0)),
-        out_shape=jax.ShapeDtypeStruct((tok, 2 * D), BF16),
+        out_ref[:tok, :D] = (centre * r).astype(BF16)
+        out_ref[:tok, D:] = c_ref[...]
+        out_ref[tok:, :] = jnp.zeros((IDS, 2 * D), BF16)
+        numbers = jnp.broadcast_to(id_ref[...].astype(F32), (IDS, tok))
+        out_ref[tok:, :tok] = numbers.astype(BF16)
+
+    return pl.pallas_call(
+        kernel,
+        grid=(1,),
+        in_specs=[whole((tok, D)), whole((tok, D)), whole((1, tok))],
+        out_specs=whole((tok + IDS, 2 * D)),
+        out_shape=jax.ShapeDtypeStruct((tok + IDS, 2 * D), BF16),
         compiler_params=params(16),
         cost_estimate=cost(10 * tok * D, 8 * tok * D),
         name="normalize",
-    )(tokens, cotangent)
+    )(tokens, cotangent, ids)
 
 
 def transposes(plan, xc_own, xc_other, rows):
-    tok = xc_own.shape[0]
+    tok = xc_own.shape[0] - IDS
     kind = row_type(rows)
 
     def kernel(pos_ref, own_ref, other_ref, out_ref, sum_ref, t_ref):
@@ -445,8 +495,8 @@
 
 
 def mlp_forward(plan, xc_own, xc_other, turned, pieces):
-    tok = xc_own.shape[0]
-    rows = pieces[0].shape[0]
+    tok = xc_own.shape[0] - IDS
+    rows = pieces[0].shape[0] // plan.zs
     tile = 512
     n = len(pieces)
 
@@ -477,10 +527,10 @@
         in_specs=[smem()]
         + [pl.BlockSpec((tok, D), lambda j: (0, 0))] * 2
         + [pl.BlockSpec((1, D, 2 * tok), lambda j: (1, 0, 0))]
-        + [pl.BlockSpec((rows, tile), lambda j: (0, j))] * n,
+        + [pl.BlockSpec((plan.zs * rows, tile), lambda j: (0, j))] * n,
         out_specs=[block, block, grad, grad],
         out_shape=[jax.ShapeDtypeStruct((2, tok, FH), BF16)] * 2
-        + [jax.ShapeDtypeStruct((half_d, FH), BF16)] * 2,
+        + [jax.ShapeDtypeStruct((half_d, FH + DH), BF16)] * 2,
         scratch_shapes=[pltpu.VMEM((D, tile), row_type(rows))],
         compiler_params=params(),
         cost_estimate=cost(8 * tok * D * FH, 12 * tok * FH, 2 * tok * FH),
@@ -494,14 +544,14 @@
     return mm(high, block_ref[...]) + mm(low, block_ref[...])
 
 
-def attention_forward(plan, xc_own, xc_other, pieces, id_row, id_col, block, turned):
-    tok = xc_own.shape[0]
-    rows = pieces[0].shape[0]
+def attention_forward(plan, xc_own, xc_other, pieces, block, turned, g_own, g_other):
+    tok = xc_own.shape[0] - IDS
+    rows = pieces[0].shape[0] // plan.zs
     n = len(pieces)
 
     half_d = D // 2
 
-    def kernel(pos_ref, xo_ref, xp_ref, idr_ref, idc_ref, block_ref, ct_ref, *rest):
+    def kernel(pos_ref, xo_ref, xp_ref, ido_ref, idp_ref, block_ref, ct_ref, _, __, *rest):
         refs, vec_refs = rest[:n], rest[n : 2 * n]
         (
             q_ref, k_ref, v_ref, nq_ref, nk_ref, rq_ref, rk_ref, att_ref, p_ref, gain_ref,
@@ -538,7 +588,8 @@
             k = normed(raw[:, PAIR : 2 * PAIR], k_gain, nk_ref, rk_ref, k_ref)
             v = raw[:, 2 * PAIR :].astype(BF16)
             v_ref[half] = v
-            same = idc_ref[half] == idr_ref[half]
+            numbers = (ido_ref, idp_ref)[half][:8].astype(F32)
+            same = numbers.T[:, :1] == numbers[:1]
             att = []
             zero = jnp.zeros_like(q)
             for head in range(2):
@@ -559,10 +610,12 @@
         grid=(PAIRS,),
         in_specs=[smem()]
         + [pl.BlockSpec((tok, D), lambda j: (0, 0))] * 2
-        + [whole((2, 1, tok)), whole((2, tok, 1)), whole((PAIR, PAIR))]
+        + [pl.BlockSpec((IDS, tok), lambda j: (tok // IDS, 0))] * 2
+        + [whole((PAIR, PAIR))]
         + [pl.BlockSpec((1, D, 2 * tok), lambda j: (1, 0, 0))]
-        + [pl.BlockSpec((rows, QKV), lambda j: (0, j))] * n
-        + [pl.BlockSpec((rows, VEC), lambda j: (0, QW // VEC))] * n,
+        + [pl.BlockSpec(memory_space=pl.ANY)] * 2
+        + [pl.BlockSpec((plan.zs * rows, QKV), lambda j: (0, j))] * n
+        + [pl.BlockSpec((plan.zs * rows, VEC), lambda j: (0, QW // VEC))] * n,
         out_specs=[pair] * 8
         + [pl.BlockSpec((2, 2, tok, tok), lambda j: (0, j, 0, 0)), whole((8, D))]
         + [pl.BlockSpec((half_d, PAIR), lambda j: (0, FH // PAIR + j))] * 2,
@@ -570,9 +623,10 @@
         + [
             jax.ShapeDtypeStruct((2, 2 * PAIRS, tok, tok), BF16),
             jax.ShapeDtypeStruct((8, D), F32),
-            jax.ShapeDtypeStruct((half_d, FH + DH), BF16),
-            jax.ShapeDtypeStruct((half_d, FH + DH), BF16),
-        ],
+            jax.ShapeDtypeStruct(g_own.shape, BF16),
+            jax.ShapeDtypeStruct(g_own.shape, BF16),
+        ],
+        input_output_aliases={7: 10, 8: 11},
         scratch_shapes=[
             pltpu.VMEM((D, QKV), row_type(rows)),
             pltpu.VMEM((D, VEC), row_type(rows)),
@@ -581,14 +635,20 @@
         cost_estimate=cost(4 * tok * D * QW, 20 * MIB, 12 * tok * tok),
         name="attention_forward",
     )(
-        plan.pos, xc_own, xc_other, id_row, id_col, block, turned,
+        plan.pos, xc_own, xc_other, xc_own, xc_other, block, turned, g_own, g_other,
         *pieces, *pieces,
     )
 
 
+def output_columns(plan, rows, tile, steps):
+    return pl.BlockSpec(
+        (plan.zs * rows, tile), lambda j: (0, jnp.where(j == 0, steps - 1, j - 1))
+    )
+
+
 def output_step(plan, att, mixed, slope, xc_own, xc_other, pieces):
-    tok = xc_own.shape[0]
-    rows = pieces[0].shape[0]
+    tok = xc_own.shape[0] - IDS
+    rows = pieces[0].shape[0] // plan.zs
     n = len(pieces)
     tile = DH
     steps = 1 + FH // tile
@@ -597,7 +657,6 @@
         refs = rest[:n]
         out_own_ref, out_other_ref, d_att_ref, d_in_ref, w_ref, acc_ref = rest[n:]
         step = pl.program_id(0)
-
         place(plan, pos_ref, refs, rows, w_ref)
         w = w_ref[...].astype(BF16)
 
@@ -625,7 +684,7 @@
         grid=(steps,),
         in_specs=[smem(), whole((2, tok, tile)), hidden, hidden]
         + [pl.BlockSpec((tok, D), lambda j: (0, 1))] * 2
-        + [pl.BlockSpec((rows, tile), lambda j: (0, jnp.where(j == 0, steps - 1, j - 1)))] * n,
+        + [output_columns(plan, rows, tile, steps)] * n,
         out_specs=[whole((tok, D)), whole((tok, D)), whole((2, tok, tile)), hidden],
         out_shape=[
             jax.ShapeDtypeStruct((tok, D), F32),
@@ -638,100 +697,126 @@
             pltpu.VMEM((2, tok, D), F32),
         ],
         compiler_params=params(),
-        cost_estimate=cost(4 * 2 * tok * steps * tile * D, 20 * MIB),
+        cost_estimate=cost(8 * tok * steps * tile * D, 20 * MIB),
         name="output_step",
     )(plan.pos, att, mixed, slope, xc_own, xc_other, *pieces)
 
 
-def mlp_backward(plan, turned, d_inner, pieces, g_own, g_other):
+def mlp_gradient(turned, d_inner):
     tok = d_inner.shape[1]
-    rows = pieces[0].shape[0]
-    n = len(pieces)
     half_d = D // 2
     tile = 512
-    steps = FH // tile
-
-    def kernel(pos_ref, xt_ref, d_ref, *rest):
-        refs = rest[:n]
-        g_own_ref, g_other_ref, e_own_ref, e_other_ref, w_ref, acc_ref = rest[n + 2 :]
-        step = pl.program_id(0)
-
-        @pl.when(step == 0)
-        def _():
-            acc_ref[...] = jnp.zeros_like(acc_ref)
-
-        place(plan, pos_ref, refs, rows, w_ref)
-        d = d_ref[...].reshape(2 * tok, tile)
-        g = mm(xt_ref[0], d).astype(BF16)
+
+    def kernel(xt_ref, d_ref, g_own_ref, g_other_ref):
+        g = mm(xt_ref[0], d_ref[...].reshape(2 * tok, tile)).astype(BF16)
         g_own_ref[...] = g[:half_d]
         g_other_ref[...] = g[half_d:]
-        acc_ref[...] += mm(d, w_ref[...].astype(BF16), NT)
+
+    grad = pl.BlockSpec((half_d, tile), lambda j: (0, j))
+    return pl.pallas_call(
+        kernel,
+        grid=(FH // tile,),
+        in_specs=[
+            pl.BlockSpec((1, D, 2 * tok), lambda j: (0, 0, 0)),
+            pl.BlockSpec((2, tok, tile), lambda j: (0, 0, j)),
+        ],
+        out_specs=[grad, grad],
+        out_shape=[jax.ShapeDtypeStruct((half_d, FH), BF16)] * 2,
+        compiler_params=params(),
+        cost_estimate=cost(4 * tok * D * FH, 8 * MIB),
+        name="mlp_gradient",
+    )(turned, d_inner)
+
+
+def scaled_gradient(plan, d_inner, d_qkv, mlp_pieces, qkv_pieces):
+    tok = d_inner.shape[1]
+    rows = mlp_pieces[0].shape[0] // plan.zs
+    n = len(mlp_pieces)
+    tile = QKV
+    count = FH // tile
+    steps = count + PAIRS
+
+    def kernel(pos_ref, dm_ref, dq_ref, *rest):
+        refs_m, refs_q = rest[:n], rest[n : 2 * n]
+        e_own_ref, e_other_ref, w_ref, acc_ref = rest[2 * n :]
+        step = pl.program_id(0)
+
+        @pl.when(step == 0)
+        def _():
+            acc_ref[...] = jnp.zeros_like(acc_ref)
+
+        def add(ref):
+            w = w_ref[...].astype(BF16)
+            for half in range(2):
+                acc_ref[half] += mm(ref[half], w, NT)
+
+        @pl.when(step < count)
+        def _():
+            place(plan, pos_ref, refs_m, rows, w_ref)
+            add(dm_ref)
+
+        @pl.when(step >= count)
+        def _():
+            place(plan, pos_ref, refs_q, rows, w_ref)
+            add(dq_ref)
 
         @pl.when(step == steps - 1)
         def _():
-            e_own_ref[...] = acc_ref[:tok]
-            e_other_ref[...] = acc_ref[tok:]
-
-    grad = pl.BlockSpec((half_d, tile), lambda j: (0, j))
+            e_own_ref[...] = acc_ref[0]
+            e_other_ref[...] = acc_ref[1].astype(BF16)
+
+    def mlp_at(j):
+        return jnp.minimum(j, count - 1)
+
+    def qkv_at(j):
+        return jnp.maximum(j - count, 0)
+
     return pl.pallas_call(
         kernel,
         grid=(steps,),
         in_specs=[
             smem(),
-            pl.BlockSpec((1, D, 2 * tok), lambda j: (0, 0, 0)),
-            pl.BlockSpec((2, tok, tile), lambda j: (0, 0, j)),
+            pl.BlockSpec((2, tok, tile), lambda j: (0, 0, mlp_at(j))),
+            pl.BlockSpec((2, tok, tile), lambda j: (0, 0, qkv_at(j))),
         ]
-        + [pl.BlockSpec((rows, tile), lambda j: (0, j))] * n
-        + [pl.BlockSpec(memory_space=pl.ANY)] * 2,
-        out_specs=[grad, grad] + [whole((tok, D))] * 2,
-        input_output_aliases={3 + n: 0, 4 + n: 1},
-        out_shape=[jax.ShapeDtypeStruct((half_d, FH + DH), BF16)] * 2
-        + [jax.ShapeDtypeStruct((tok, D), F32)] * 2,
+        + [pl.BlockSpec((plan.zs * rows, tile), lambda j: (0, mlp_at(j)))] * n
+        + [pl.BlockSpec((plan.zs * rows, tile), lambda j: (0, qkv_at(j)))] * n,
+        out_specs=[whole((tok, D)), whole((tok, D))],
+        out_shape=[
+            jax.ShapeDtypeStruct((tok, D), F32),
+            jax.ShapeDtypeStruct((tok, D), BF16),
+        ],
         scratch_shapes=[
             pltpu.VMEM((D, tile), row_type(rows)),
-            pltpu.VMEM((2 * tok, D), F32),
+            pltpu.VMEM((2, tok, D), F32),
         ],
         compiler_params=params(),
-        cost_estimate=cost(8 * tok * D * FH, 20 * MIB),
-        name="mlp_backward",
-    )(plan.pos, turned, d_inner, *pieces, g_own, g_other)
-
-
-def attention_backward(
-    plan, turned, saved, d_att, block, gains, cot_sum, pieces, e_own, e_other, before, begin, end
-):
+        cost_estimate=cost(4 * tok * steps * tile * D, 16 * MIB),
+        name="scaled_gradient",
+    )(plan.pos, d_inner, d_qkv, *mlp_pieces, *qkv_pieces)
+
+
+def attention_backward(plan, turned, saved, d_att, block, gains, cot_sum, before, begin, end, rows):
     q, k, v, nq, nk, rq, rk, probs = saved
     tok = d_att.shape[1]
-    rows = pieces[0].shape[0]
-    n = len(pieces)
     half_d = D // 2
     kind = row_type(rows)
-    n_before = len(before)
+    width = (end - begin) * QKV + (VEC if end == PAIRS else 0)
 
     def kernel(pos_ref, xt_ref, q_ref, k_ref, v_ref, nq_ref, nk_ref, rq_ref, rk_ref, p_ref,
-               da_ref, block_ref, gain_ref, cot_ref, ein_own_ref, ein_other_ref, *rest):
-        refs, rest = rest[:n], rest[n:]
-        befores, rest = rest[:n_before], rest[n_before:]
-        (
-            g_own_ref, g_other_ref, e_own_ref, e_other_ref, vec_ref, w_ref, d_ref, turn_ref,
-        ) = rest
+               da_ref, block_ref, gain_ref, cot_ref, *rest):
+        befores = rest[: len(before)]
+        g_own_ref, g_other_ref, d_ref, vec_ref, turn_ref = rest[len(before) :]
         step = pl.program_id(0) + begin
 
         @pl.when(step == begin)
         def _():
-            e_own_ref[...] = ein_own_ref[...]
-            e_other_ref[...] = ein_other_ref[...]
             if befores:
-                before_own_ref, before_other_ref, before_vec_ref = befores
-                vec_ref[...] = before_vec_ref[...]
-                g_own_ref[:, : begin * QKV] = before_own_ref[...]
-                g_other_ref[:, : begin * QKV] = before_other_ref[...]
+                vec_ref[...] = befores[0][...]
             else:
                 vec_ref[...] = jnp.zeros_like(vec_ref)
                 vec_ref[3:4, :] = cot_ref[0, :1]
 
-        place(plan, pos_ref, refs, rows, w_ref)
-        w = w_ref[...].astype(BF16)
         column = pl.ds(pl.multiple_of(pos_ref[3] * DH + step * PAIR, PAIR), PAIR)
         q_gain = gain_ref[1:2, column]
         k_gain = gain_ref[2:3, column]
@@ -764,17 +849,13 @@
                 along = head_means(e * normal, block_ref)
                 return (r_ref[half].astype(F32) * (e - mean - normal * along)).astype(BF16)
 
-            at = slice(half * tok, (half + 1) * tok)
-            d_ref[at, :PAIR] = back(d_query, q_gain, nq_ref, rq_ref, 1, HD ** (-0.5))
-            d_ref[at, PAIR : 2 * PAIR] = back(d_key, k_gain, nk_ref, rk_ref, 2, 1.0)
-            d_ref[at, 2 * PAIR :] = d_value.astype(BF16)
-        g = mm(xt_ref[0], d_ref[...]).astype(BF16)
-        at = pl.ds(pl.multiple_of(step * QKV, QKV), QKV)
+            d_ref[half, :, :PAIR] = back(d_query, q_gain, nq_ref, rq_ref, 1, HD ** (-0.5))
+            d_ref[half, :, PAIR : 2 * PAIR] = back(d_key, k_gain, nk_ref, rk_ref, 2, 1.0)
+            d_ref[half, :, 2 * PAIR :] = d_value.astype(BF16)
+        g = mm(xt_ref[0], d_ref[...].reshape(2 * tok, QKV)).astype(BF16)
+        at = pl.ds(pl.multiple_of((step - begin) * QKV, QKV), QKV)
         g_own_ref[:, at] = g[:half_d]
         g_other_ref[:, at] = g[half_d:]
-        e_own_ref[...] += mm(d_ref[:tok], w, NT)
-        e_other_ref[...] += mm(d_ref[tok:], w, NT)
-
         if end < PAIRS:
             return
 
@@ -784,11 +865,10 @@
 
             def put(at, a):
                 ref = g_own_ref if at < half_d else g_other_ref
-                ref[at % half_d : at % half_d + rows, QW:] = a.astype(BF16)
+                ref[at % half_d : at % half_d + rows, width - VEC :] = a.astype(BF16)
 
             turn(plan, pos_ref, turn_ref, rows, put)
 
-    width = QW + VEC if end == PAIRS else end * QKV
     pair = pl.BlockSpec((2, tok, PAIR), lambda j: (0, 0, begin + j))
     return pl.pallas_call(
         kernel,
@@ -801,26 +881,21 @@
             whole((PAIR, PAIR)),
             whole((8, D)),
             pl.BlockSpec((1, 8, D), lambda j: (1, 0, 0)),
-            whole((tok, D)),
-            whole((tok, D)),
         ]
-        + [pl.BlockSpec((rows, QKV), lambda j: (0, begin + j))] * n
         + [whole(a.shape) for a in before],
-        out_specs=[whole((half_d, width))] * 2 + [whole((tok, D))] * 2 + [whole((VEC, D))],
+        out_specs=[whole((half_d, width))] * 2
+        + [pl.BlockSpec((2, tok, QKV), lambda j: (0, 0, j)), whole((VEC, D))],
         out_shape=[jax.ShapeDtypeStruct((half_d, width), BF16)] * 2
-        + [jax.ShapeDtypeStruct((tok, D), F32)] * 2
-        + [jax.ShapeDtypeStruct((VEC, D), F32)],
-        scratch_shapes=[
-            pltpu.VMEM((D, QKV), kind),
-            pltpu.VMEM((2 * tok, QKV), BF16),
-            pltpu.VMEM((D, VEC), kind),
-        ],
+        + [
+            jax.ShapeDtypeStruct((2, tok, (end - begin) * QKV), BF16),
+            jax.ShapeDtypeStruct((VEC, D), F32),
+        ],
+        scratch_shapes=[pltpu.VMEM((D, VEC), kind)],
         compiler_params=params(),
-        cost_estimate=cost(20 * tok * D * QKV * (end - begin), 8 * MIB * (end - begin)),
+        cost_estimate=cost(16 * tok * D * QKV * (end - begin), 8 * MIB * (end - begin)),
         name="attention_backward",
     )(
-        plan.pos, turned, q, k, v, nq, nk, rq, rk, probs, d_att, block, gains, cot_sum,
-        e_own, e_other, *pieces, *before,
+        plan.pos, turned, q, k, v, nq, nk, rq, rk, probs, d_att, block, gains, cot_sum, *before,
     )
 
 
@@ -854,10 +929,60 @@
     clipped = grad * factor
     first_new = beta_one * first + (1.0 - beta_one) * clipped
     second_new = beta_two * second + (1.0 - beta_two) * clipped * clipped
-    first_hat = first_new / (1.0 - beta_one**ADAM_STEP)
-    second_hat = second_new / (1.0 - beta_two**ADAM_STEP)
+    first_hat = first_new * (1.0 / (1.0 - beta_one**ADAM_STEP))
+    second_hat = second_new * (1.0 / (1.0 - beta_two**ADAM_STEP))
     update = -learning * (first_hat / (jnp.sqrt(second_hat) + epsilon) + decay_rate * master)
     return (update, first_new, second_new)
+
+
+def optimize(total, vec_cols, ins, outs, vecs):
+    rows, out_rows = ins[0].shape[0], outs[0].shape[0]
+    steps = 3
+
+    def kernel(total_ref, cols_ref, *refs):
+        in_refs, out_refs, vec_refs, rest = refs[:4], refs[4:8], refs[8:11], refs[11:]
+        vec_grad_ref, norm_ref, pad_ref = rest[0], rest[1], rest[-1]
+        sums = jnp.sum(jnp.sum(total_ref[...], axis=1, keepdims=True), axis=0, keepdims=True)
+        norm = jnp.sqrt(sums)
+        factor = jnp.minimum(1.0, math.sqrt(PARAMS) / norm)
+        for group, results in ((in_refs, rest[2:5]), (out_refs, rest[5:8])):
+            for ref, value in zip(results, adamw(*[ref[...] for ref in group], factor)):
+                ref[...] = value
+
+        @pl.when(pl.program_id(0) == 0)
+        def _():
+            norm_ref[...] = jnp.broadcast_to(norm, (8, 128))
+            pad_ref[...] = jnp.zeros_like(pad_ref)
+            pad_ref[:rows] = cols_ref[...]
+            grad = pad_ref[...].T[:4, :rows]
+            vec_grad_ref[...] = grad
+            values = adamw(*[ref[...] for ref in vec_refs], grad, factor)
+            for ref, value in zip(rest[8:11], values):
+                ref[...] = value
+
+    in_block = pl.BlockSpec((rows, 7 * D // steps), lambda j: (0, j))
+    out_block = pl.BlockSpec((out_rows // steps, D), lambda j: (j, 0))
+    shapes = [jax.ShapeDtypeStruct(a.shape, F32) for a in (ins[0], outs[0], vecs[0])]
+    return pl.pallas_call(
+        kernel,
+        grid=(steps,),
+        in_specs=[whole((8, 128)), whole(vec_cols.shape)]
+        + [in_block] * 4
+        + [out_block] * 4
+        + [whole(vecs[0].shape)] * 3,
+        out_specs=[whole(vecs[0].shape), whole((8, 128))]
+        + [in_block] * 3
+        + [out_block] * 3
+        + [whole(vecs[0].shape)] * 3,
+        out_shape=[shapes[2], jax.ShapeDtypeStruct((8, 128), F32)]
+        + [shapes[0]] * 3
+        + [shapes[1]] * 3
+        + [shapes[2]] * 3,
+        scratch_shapes=[pltpu.VMEM((128, 128), F32)],
+        compiler_params=params(16),
+        cost_estimate=cost(20 * 7 * D * rows, 28 * 13 * D * rows),
+        name="optimize",
+    )(total, vec_cols, *ins, *outs, *vecs)
 
 
 def local(
@@ -876,144 +1001,127 @@
 ):
     plan = Plan(lax.axis_size("fsdp"), lax.axis_size("dp"))
     rows = in_weight.shape[0]
-    out_rows = out_weight.shape[0]
 
     low_vec = vectors.astype(BF16).astype(F32)
     vec_t = jnp.pad(low_vec.T, ((0, 0), (0, VEC - 4)))
+    blocks = lax.all_to_all(split_out(plan, out_weight, rows), "fsdp", 0, 0)
     mlp_piece, qkv_piece = pack_in(plan, in_weight, vec_t)
-    xc_own = normalize(tokens, cotangent)
+    xc_own = normalize(tokens, cotangent, image_ids[None, :])
 
     def z_all(piece):
         return [plan.from_z(piece, s) for s in range(1, plan.zs)]
 
-    def y_all(pieces):
-        return [[plan.from_y(a, t) for a in pieces] for t in range(1, plan.ys)]
-
-    def join(y_first, y_rest):
-        return [a for first, rest in zip(y_first, y_rest) for a in first + rest]
-
-    def core_all(pieces):
-        return [plan.swap_core(a) for a in pieces]
+    def y_all(column):
+        return [plan.from_y(column, t) for t in range(1, plan.ys)]
+
+    def core_all(arrays):
+        return [plan.swap_core(a) for a in arrays]
 
     def held(groups):
         flat = iter(fence(*[a for group in groups for a in group]))
         return [[next(flat) for _ in group] for group in groups]
 
     mlp_z = z_all(mlp_piece)
-    mlp_y0 = y_all([mlp_piece])
     xc_other = plan.swap_plane(xc_own)
-    ids_other = plan.swap_plane(image_ids)
-    out_now, mlp_z[0] = fence(out_weight, mlp_z[0])
-    blocks = out_now.astype(BF16).T.reshape(plan.n, rows, out_rows)
-    blocks = lax.all_to_all(blocks, "fsdp", 0, 0)
-    (qkv_piece,), mlp_z = held([[qkv_piece], mlp_z])
-    mlp_col = [mlp_piece] + mlp_z
-    mlp_y1 = y_all(mlp_z)
+    mlp_z, (qkv_piece,) = held([mlp_z, [qkv_piece]])
+    mlp_col = stack([mlp_piece] + mlp_z)
+    mlp_y = y_all(mlp_col)
+    mlp_core = core_all([mlp_col])
     qkv_z = z_all(qkv_piece)
-    qkv_y0 = y_all([qkv_piece])
-    mlp_core = core_all(mlp_col)
     out_piece = pack_out(plan, blocks)
-    mlp_y = join(mlp_y0, mlp_y1)
-    mlp_y, qkv_z, mlp_core, (out_piece,) = held([mlp_y, qkv_z, mlp_core, [out_piece]])
-    qkv_col = [qkv_piece] + qkv_z
-    mlp_core = mlp_core + core_all(mlp_y)
-    mlp_pieces = mlp_col + mlp_y + mlp_core
-    qkv_y1 = y_all(qkv_z)
+    mlp_y, mlp_core, qkv_z, (out_piece, xc_other) = held(
+        [mlp_y, mlp_core, qkv_z, [out_piece, xc_other]]
+    )
+    mlp_pieces = [mlp_col] + mlp_y + mlp_core + core_all(mlp_y)
+    qkv_col = stack([qkv_piece] + qkv_z)
+    qkv_y = y_all(qkv_col)
+    qkv_core = core_all([qkv_col])
     out_z = z_all(out_piece)
-    out_y0 = y_all([out_piece])
-    qkv_core = core_all(qkv_col)
     turned, cot_sum = transposes(plan, xc_own, xc_other, rows)
     mixed, slope, g_own, g_other = mlp_forward(plan, xc_own, xc_other, turned, mlp_pieces)
-    qkv_y = join(qkv_y0, qkv_y1)
     qkv_y, out_z, qkv_core, (mixed, slope, g_own, g_other) = held(
         [qkv_y, out_z, qkv_core, [mixed, slope, g_own, g_other]]
     )
+    qkv_pieces = [qkv_col] + qkv_y + qkv_core + core_all(qkv_y)
+    out_col = stack([out_piece] + out_z)
+    out_y = y_all(out_col)
+    out_core = core_all([out_col])
+    lane = jnp.arange(PAIR) // HD
+    block = jnp.where(lane[:, None] == lane[None, :], 1.0 / HD, 0.0).astype(BF16)
+    *saved, att, probs, gains, g_own, g_other = attention_forward(
+        plan, xc_own, xc_other, qkv_pieces, block, turned, g_own, g_other
+    )
+    saved = tuple(saved) + (probs,)
+    out_y, out_core, (att, g_own, g_other) = held([out_y, out_core, [att, g_own, g_other]])
     s_out = Scatter(plan, g_own, g_other)
     s_out.by_core()
-    out_col = [out_piece] + out_z
-    qkv_core = qkv_core + core_all(qkv_y)
-    qkv_pieces = qkv_col + qkv_y + qkv_core
-    out_y1 = y_all(out_z)
-    out_core = core_all(out_col)
-    ids = jnp.stack([image_ids, ids_other])
-    lane = jnp.arange(PAIR) // HD
-    block = jnp.where(lane[:, None] == lane[None, :], 1.0 / HD, 0.0).astype(BF16)
-    *saved, att, probs, gains, m_own, m_other = attention_forward(
-        plan, xc_own, xc_other, qkv_pieces, ids[:, None, :], ids[:, :, None], block, turned
-    )
-    saved = tuple(saved) + (probs,)
-    out_y = join(out_y0, out_y1)
-    out_y, out_core, (att, s_out.recv) = held([out_y, out_core, [att, s_out.recv]])
+    out_core = out_core + core_all(out_y)
+    s_out.recv, *out_core = fence(s_out.recv, *out_core)
     s_out.by_y()
-    out_core = out_core + core_all(out_y)
-    out_pieces = out_col + out_y + out_core
+    out_pieces = [out_col] + out_y + out_core
     out_mine, out_theirs, d_att, d_inner = output_step(
         plan, att, mixed, slope, xc_own, xc_other, out_pieces
     )
     s_out.y_got, (out_theirs, d_att, d_inner) = held([s_out.y_got, [out_theirs, d_att, d_inner]])
     s_out.by_z()
-    out_recv = plan.swap_plane(out_theirs)
-    g_own, g_other, e_own, e_other = mlp_backward(
-        plan, turned, d_inner, mlp_pieces, m_own, m_other
-    )
-    s_out.z_got, (g_own, g_other, e_own, e_other) = held(
-        [s_out.z_got, [g_own, g_other, e_own, e_other]]
-    )
+    g_own, g_other = mlp_gradient(turned, d_inner)
     s_mlp = Scatter(plan, g_own, g_other)
     s_mlp.by_core()
-    out_sum = s_out.total()
-    s_mlp.recv, e_own = fence(s_mlp.recv, e_own)
+    out_recv = plan.swap_plane(out_theirs)
+    s_mlp.recv, d_att = fence(s_mlp.recv, d_att)
     s_mlp.by_y()
-    out_swap = plan.swap_plane(out_sum)
-    g_own, g_other, e_own, e_other, _ = attention_backward(
-        plan, turned, saved, d_att, block, gains, cot_sum, qkv_pieces, e_own, e_other, (),
-        0, PAIRS,
-    )
-    s_mlp.y_got, (g_own, g_other, e_own, e_other, out_swap, out_recv) = held(
-        [s_mlp.y_got, [g_own, g_other, e_own, e_other, out_swap, out_recv]]
+    g_own, g_other, d_qkv, _ = attention_backward(
+        plan, turned, saved, d_att, block, gains, cot_sum, (), 0, PAIRS, rows
+    )
+    s_out.z_got, s_mlp.y_got, (g_own, g_other, d_qkv, out_recv) = held(
+        [s_out.z_got, s_mlp.y_got, [g_own, g_other, d_qkv, out_recv]]
     )
     s_qkv = Scatter(plan, g_own, g_other)
     s_qkv.by_core()
+    out_sum = s_out.total()
+    out_swap = plan.swap_plane(out_sum)
+    s_qkv.recv, out_sum = fence(s_qkv.recv, out_sum)
+    s_qkv.by_y()
     s_mlp.by_z()
-    e_recv = plan.swap_plane(e_other.astype(BF16))
+    blocks = unpack_out(plan, plan.over_pairs(out_sum), plan.over_pairs(out_swap))
     result = (
         tokens.astype(F32) + out_mine + out_recv.astype(F32) + gains[3][None, :]
     ).astype(BF16)
-    s_qkv.recv, result = fence(s_qkv.recv, result)
-    s_qkv.by_y()
-    s_mlp.z_got, s_qkv.y_got, (e_recv,) = held([s_mlp.z_got, s_qkv.y_got, [e_recv]])
+    s_qkv.y_got, (blocks, result, d_qkv) = held([s_qkv.y_got, [blocks, result, d_qkv]])
     s_qkv.by_z()
-    mlp_sum = s_mlp.total()
-    mlp_swap = plan.swap_plane(mlp_sum)
-    mlp_sum, mlp_swap = plan.over_pairs(mlp_sum), plan.over_pairs(mlp_swap)
-    blocks = unpack_out(
-        plan, plan.over_pairs(out_sum), plan.over_pairs(out_swap), mlp_sum, mlp_swap
-    )
     blocks = lax.all_to_all(blocks, "fsdp", 0, 0)
-    input_grad = token_gradient(tokens, cotangent, e_own, e_recv)
-    in_grad, sq, dot = finish_mlp(plan, mlp_sum, mlp_swap, in_weight, vec_t)
-    s_qkv.z_got, (input_grad, in_grad) = held([s_qkv.z_got, [input_grad, in_grad]])
-    qkv_sum = s_qkv.total()
-    qkv_swap = plan.swap_plane(qkv_sum)
+    e_own, e_other = scaled_gradient(plan, d_inner, d_qkv, mlp_pieces, qkv_pieces)
+    s_qkv.z_got, s_mlp.z_got, (e_other,) = held([s_qkv.z_got, s_mlp.z_got, [e_other]])
+    qkv_sum, mlp_sum = s_qkv.total(), s_mlp.total()
+    qkv_swap, mlp_swap = plan.swap_plane(qkv_sum), plan.swap_plane(mlp_sum)
     out_grad, sq_out = finish_out(blocks)
+    qkv_swap, mlp_swap, out_grad, e_other = fence(qkv_swap, mlp_swap, out_grad, e_other)
+    e_recv = plan.swap_plane(e_other)
+    in_grad, sq, dot = finish_mlp(
+        plan, plan.over_pairs(mlp_sum), plan.over_pairs(mlp_swap), in_weight, vec_t
+    )
     in_grad, vec_cols, square = finish_qkv(
         plan, plan.over_pairs(qkv_sum), plan.over_pairs(qkv_swap), in_weight, vec_t, in_grad,
         sq, dot, sq_out,
     )
-    vec_grad = vec_cols[:, :4].T
-    total = jnp.sum(plan.total(square))
-    grad_norm = jnp.sqrt(total)
-    factor = jnp.minimum(1.0, math.sqrt(PARAMS) / grad_norm)
-    in_update, in_mean, in_square = adamw(in_weight, in_moment, in_second, in_grad, factor)
-    out_update, out_mean, out_square = adamw(out_weight, out_moment, out_second, out_grad, factor)
-    vec_update, vec_mean, vec_square = adamw(vectors, vec_moment, vec_second, vec_grad, factor)
+    input_grad = token_gradient(tokens, cotangent, e_own, e_recv)
+    vec_grad, norm, *updates = optimize(
+        plan.total(square),
+        vec_cols,
+        (in_weight, in_moment, in_second, in_grad),
+        (out_weight, out_moment, out_second, out_grad),
+        (vectors, vec_moment, vec_second),
+    )
+    in_update, in_mean, in_square = updates[:3]
+    out_update, out_mean, out_square = updates[3:6]
+    vec_update, vec_mean, vec_square = updates[6:]
     return (
         result,
         input_grad,
         in_grad,
         out_grad,
         vec_grad,
-        grad_norm,
+        norm[0, 0],
         in_update,
         out_update,
         vec_update,

time: 286 us -> 233 us (0.81)
  waiting for transfers between devices: 76.4 us -> 42.1 us
  starting transfers between devices: 81.1 us -> 60 us
  Pallas kernels: 91.6 us -> 103 us
  local copies, waits for them, and re-layouts: 16.9 us -> 13.3 us
  other arithmetic: 16.1 us -> 13 us
    ppermute x18 -> x21, waiting for transfers between devices: 43.4 us -> 23.8 us  [from_z(): return lax.ppermute(a, 'fsdp', pairs)]
    pallas_call x2 -> x8, Pallas kernels: 11.2 us -> 26.2 us  [the longest x1 12 us: scaled_gradient(): pl.pallas_call(kernel, grid=(steps,), in_specs=[smem(), pl.BlockSpec((2,...]
    ppermute x15 -> x7, waiting for transfers between devices: 20 us -> 7.65 us  [from_y(): return lax.ppermute(a, 'fsdp', pairs)]
    ppermute x15 -> x7, starting transfers between devices: 18.6 us -> 7.32 us  [from_y(): return lax.ppermute(a, 'fsdp', pairs)]
    ppermute x27 -> x10, waiting for transfers between devices: 0.34 us -> 6.6 us  [swap_core(): return lax.ppermute(a, 'fsdp', pairs)]
    ppermute x4 -> x0, waiting for transfers between devices: 6.22 us -> none  [total(): a = a + lax.ppermute(a, 'fsdp', [(i, i ^ m) for i in range(self.n)])]
    ppermute x4 -> x0, starting transfers between devices: 5.81 us -> none  [total(): a = a + lax.ppermute(a, 'fsdp', [(i, i ^ m) for i in range(self.n)])]
    all_to_all x2 -> x1, starting transfers between devices: 10.8 us -> 5.16 us  [local(): blocks = lax.all_to_all(blocks, 'fsdp', 0, 0)]
  transfers between devices with their start and end apart: 73 -> 46, of which waited for: 24 -> 13; matrix products, arithmetic and copies ran while one was open for 5% -> 6% of each run, Pallas kernels for 31% -> 40%
where the time goes in v3:
time: 233 us; the launch traced here: 232 us
  Pallas kernels  103 us (44%)
  starting transfers between devices  60 us (26%)
  waiting for transfers between devices  42.1 us (18%)
  local copies, waits for them, and re-layouts  13.3 us (6%)
  other arithmetic  13 us (6%)
    ppermute x21, starting transfers between devices, from_z(): return lax.ppermute(a, 'fsdp', pairs)  32.5 us
    ppermute x21, waiting for transfers between devices, from_z(): return lax.ppermute(a, 'fsdp', pairs)  23.8 us
    pallas_call x1, Pallas kernels, attention_backward(): pl.pallas_call(kernel, grid=(end - begin,), in_specs=[smem(), pl.BlockSpe...  18.3 us
    pallas_call x1, Pallas kernels, attention_forward(): pl.pallas_call(kernel, grid=(PAIRS,), in_specs=[smem()] + [pl.BlockSpec((...  18.1 us
    pallas_call x1, Pallas kernels, output_step(): pl.pallas_call(kernel, grid=(steps,), in_specs=[smem(), whole((2, tok, ti...  14.4 us
    pallas_call x1, Pallas kernels, scaled_gradient(): pl.pallas_call(kernel, grid=(steps,), in_specs=[smem(), pl.BlockSpec((2,...  12 us
    unnamed x86, local copies, waits for them, and re-layouts  11.9 us
    pallas_call x1, Pallas kernels, mlp_forward(): pl.pallas_call(kernel, grid=(FH // tile,), in_specs=[smem()] + [pl.BlockS...  11.3 us
  transfers between devices with their start and end apart: 46, of which 13 were waited for; matrix products, arithmetic and copies ran while one was open for 6% of the time, Pallas kernels for 40%

profile of v3, /device:TPU:0, one launch (start us, length us, event | category | flops | bytes accessed | tf_op | source)
XLA Modules:
  0.0 232.2 jit_solution(2552756376637811878)
XLA Ops:
  4.1 3.0 %collective-permute-start.8 = (bf16[528,1536]{1,0:T(8,128)(2,1)S(1)}, bf16[528,1536]{1,0:T(8,128)(2,1)}, u32[]{:S(2)}, u32[]{:S(2)}) collective-permute-start(bf16[528,1536]{1,0:T(8,128)(2,1)S(1)} %normalize.1.own_ref.xo_ref.ido_ref.co_ref), channel_id=1, source_target_pairs={{0,16},{16,0},{1,17},{17,1},{2,18},{18,2},{3,19},{19,3},{4,20},{20... | collective-permute-start | bytes 4866056 | tf_op jit(solution)/shard_map/ppermute | solution.py:85
  8.7 3.6 %collective-permute-start = (bf16[48,1536]{1,0:T(8,128)(2,1)}, bf16[48,1536]{1,0:T(8,128)(2,1)}, u32[]{:S(2)}, u32[]{:S(2)}) collective-permute-start(bf16[48,1536]{1,0:T(8,128)(2,1)} %get-tuple-element.124.refs_0_), channel_id=1, source_target_pairs={{4,0},{5,1},{6,2},{7,3},{8,4},{9,5},{10,6},{11,7},{12,8},{13,9},{1... | collective-permute-start | bytes 442376 | tf_op jit(solution)/shard_map/ppermute | solution.py:74
  14.2 5.1 %all-to-all-start = ((bf16[16,48,240]{2,1,0:T(8,128)(2,1)}), bf16[16,48,240]{2,1,0:T(8,128)(2,1)S(1)}, u32[]{:S(2)}, u32[]{:S(2)}) async-start(bf16[16,48,240]{2,1,0:T(8,128)(2,1)} %copy-done.11), calls=%async_computation | async-start | bytes 786432 | tf_op jit(solution)/shard_map/all_to_all | solution.py:1007
  19.4 9.9 %collective-permute-done.1.refs_2_ = bf16[48,1536]{1,0:T(8,128)(2,1)} collective-permute-done((bf16[48,1536]{1,0:T(8,128)(2,1)}, bf16[48,1536]{1,0:T(8,128)(2,1)}, u32[]{:S(2)}, u32[]{:S(2)}) %collective-permute-start.1) | collective-permute-done | bytes 147488 | tf_op jit(solution)/shard_map/ppermute | solution.py:74
  32.3 3.8 %collective-permute-start.6 = (bf16[48,1280]{1,0:T(8,128)(2,1)S(1)}, bf16[48,1280]{1,0:T(8,128)(2,1)S(1)}, u32[]{:S(2)}, u32[]{:S(2)}) collective-permute-start(bf16[48,1280]{1,0:T(8,128)(2,1)S(1)} %get-tuple-element.129.refs_0_), channel_id=1, source_target_pairs={{8,0},{9,1},{10,2},{11,3},{12,4},{13,5},{14,6},{15,7},{0,8},{1,9},... | collective-permute-start | bytes 368648 | tf_op jit(solution)/shard_map/ppermute | solution.py:74
  36.2 2.1 collective-permute-done.5.refs_1_
  38.2 2.7 %collective-permute-start.7 = (bf16[48,1280]{1,0:T(8,128)(2,1)S(1)}, bf16[48,1280]{1,0:T(8,128)(2,1)}, u32[]{:S(2)}, u32[]{:S(2)}) collective-permute-start(bf16[48,1280]{1,0:T(8,128)(2,1)S(1)} %get-tuple-element.129.refs_0_), channel_id=1, source_target_pairs={{12,0},{13,1},{14,2},{15,3},{0,4},{1,5},{2,6},{3,7},{4,8},{5,9},{6... | collective-permute-start | bytes 368648 | tf_op jit(solution)/shard_map/ppermute | solution.py:74
  41.6 6.4 %collective-permute-done.6.refs_2_ = bf16[48,1280]{1,0:T(8,128)(2,1)S(1)} collective-permute-done((bf16[48,1280]{1,0:T(8,128)(2,1)S(1)}, bf16[48,1280]{1,0:T(8,128)(2,1)S(1)}, u32[]{:S(2)}, u32[]{:S(2)}) %collective-permute-start.6) | collective-permute-done | bytes 122912 | tf_op jit(solution)/shard_map/ppermute | solution.py:74
  51.2 2.6 %transposes.1 = (bf16[2,768,1024]{2,1,0:T(8,128)(2,1)S(1)}, f32[2,8,768]{2,1,0:T(8,128)S(1)}) custom-call(s32[4]{0:T(128)S(1)} %pad_add_fusion.pos_ref, bf16[528,1536]{1,0:T(8,128)(2,1)S(1)} %normalize.1.own_ref.xo_ref.ido_ref.co_ref, bf16[528,1536]{1,0:T(8,128)(2,1)} %collective-permute-done.8.other_ref.xp_ref.idp_ref.cp_ref), custom_call_target="tpu_custom_call" | custom-call | flops 3932160 | bytes 6291456 | tf_op jit(solution)/shard_map/transposes/pallas_call | solution.py:478
  57.9 11.3 %mlp_forward.1 = (bf16[2,512,1536]{2,1,0:T(8,128)(2,1)}, bf16[2,512,1536]{2,1,0:T(8,128)(2,1)}, bf16[384,1920]{1,0:T(8,128)(2,1)}, bf16[384,1920]{1,0:T(8,128)(2,1)}) custom-call(s32[4]{0:T(128)} %copy-done.19, bf16[528,1536]{1,0:T(8,128)(2,1)} %copy-done, bf16[528,1536]{1,0:T(8,128)(2,1)} %collective-permute-done.8.other_ref.xp_ref.idp_ref.cp_ref, ...), custom_call_target="tpu_custom_call" | custom-call | flops 4831838208 | bytes 9437184 | tf_op jit(solution)/shard_map/mlp_forward/pallas_call | solution.py:524
  74.2 18.1 %attention_forward.1 = (bf16[2,512,384]{2,1,0:T(8,128)(2,1)}, bf16[2,512,384]{2,1,0:T(8,128)(2,1)}, bf16[2,512,384]{2,1,0:T(8,128)(2,1)}, bf16[2,512,384]{2,1,0:...) custom-call(s32[4]{0:T(128)} %copy-done.19, ...), custom_call_target="tpu_custom_call", output_to_operand_aliasing={{10}: (7, {}), {11}: (8, {})} | custom-call | flops 1811939328 | bytes 20971520 | tf_op jit(solution)/shard_map/attention_forward/pallas_call | solution.py:608
  92.9 3.8 %collective-permute-done.19.rest_3_ = bf16[192,1920]{1,0:T(8,128)(2,1)S(1)} collective-permute-done((bf16[192,1920]{1,0:T(8,128)(2,1)S(1)}, bf16[192,1920]{1,0:T(8,128)(2,1)S(1)}, u32[]{:S(2)}, u32[]{:S(2)}) %collective-permute-start.19) | collective-permute-done | bytes 737312 | tf_op jit(solution)/shard_map/ppermute | solution.py:82
  99.2 14.4 %output_step.1 = (f32[512,768]{1,0:T(8,128)}, bf16[512,768]{1,0:T(8,128)(2,1)}, bf16[2,512,384]{2,1,0:T(8,128)(2,1)}, bf16[2,512,1536]{2,1,0:T(8,128)(2,1)}) custom-call(s32[4]{0:T(128)} %copy-done.19, bf16[2,512,384]{2,1,0:T(8,128)(2,1)} %get-tuple-element.157.att_ref, bf16[2,512,1536]{2,1,0:T(8,128)(2,1)} %get-tuple-element.158.mix_ref, ...), custom_call_target="tpu_custom_call" | custom-call | flops 6039797760 | bytes 20971520 | tf_op jit(solution)/shard_map/output_step/pallas_call | solution.py:682
  113.7 3.5 %collective-permute-done.20 = bf16[192,1920]{1,0:T(8,128)(2,1)} collective-permute-done((bf16[192,1920]{1,0:T(8,128)(2,1)S(1)}, bf16[192,1920]{1,0:T(8,128)(2,1)}, u32[]{:S(2)}, u32[]{:S(2)}) %collective-permute-start.20) | collective-permute-done | bytes 737312 | tf_op jit(solution)/shard_map/ppermute | solution.py:78
  117.2 6.0 %mlp_gradient.1 = (bf16[384,1536]{1,0:T(8,128)(2,1)}, bf16[384,1536]{1,0:T(8,128)(2,1)}) custom-call(bf16[2,768,1024]{2,1,0:T(8,128)(2,1)} %copy-done.6, bf16[2,512,1536]{2,1,0:T(8,128)(2,1)} %get-tuple-element.166.d_ref.dm_ref), custom_call_target="tpu_custom_call" | custom-call | flops 2415919104 | bytes 8388608 | tf_op jit(solution)/shard_map/mlp_gradient/pallas_call | solution.py:716
  126.1 2.3 %collective-permute-start.21 = (bf16[48,1920]{1,0:T(8,128)(2,1)}, bf16[48,1920]{1,0:T(8,128)(2,1)S(1)}, u32[]{:S(2)}, u32[]{:S(2)}) collective-permute-start(bf16[48,1920]{1,0:T(8,128)(2,1)} %get-tuple-element.235), channel_id=1, source_target_pairs={{12,0},{13,1},{14,2},{15,3},{0,4},{1,5},{2,6},{3,7},{4,8},{5,9},{6... | collective-permute-start | bytes 552968 | tf_op jit(solution)/shard_map/ppermute | solution.py:74
  129.3 2.5 %collective-permute-start.23 = (bf16[48,1920]{1,0:T(8,128)(2,1)}, bf16[48,1920]{1,0:T(8,128)(2,1)}, u32[]{:S(2)}, u32[]{:S(2)}) collective-permute-start(bf16[48,1920]{1,0:T(8,128)(2,1)} %get-tuple-element.233), channel_id=1, source_target_pairs={{4,0},{5,1},{6,2},{7,3},{8,4},{9,5},{10,6},{11,7},{12,8},{13,9},{1... | collective-permute-start | bytes 552968 | tf_op jit(solution)/shard_map/ppermute | solution.py:74
  133.6 18.3 %attention_backward.1 = (bf16[384,1280]{1,0:T(8,128)(2,1)}, bf16[384,1280]{1,0:T(8,128)(2,1)}, bf16[2,512,1152]{2,1,0:T(8,128)(2,1)}, f32[128,768]{1,0:T(8,128)}) custom-call(s32[4]{0:T(128)} %copy-done.19, bf16[2,768,1024]{2,1,0:T(8,128)(2,1)} %copy-done.6, bf16[2,512,384]{2,1,0:T(8,128)(2,1)} %get-tuple-element.171.q_ref, ...), custom_call_target="tpu_custom_call" | custom-call | flops 7247757312 | bytes 25165824 | tf_op jit(solution)/shard_map/attention_backward/pallas_call | solution.py:873
  157.2 2.1 add_convert_fusion.9
  160.9 2.2 collective-permute-start.35
  163.2 2.3 add_convert_fusion
  171.4 5.2 %all-to-all-start.1 = ((bf16[16,48,240]{2,1,0:T(8,128)(2,1)}), bf16[16,48,240]{2,1,0:T(8,128)(2,1)S(1)}, u32[]{:S(2)}, u32[]{:S(2)}) async-start(bf16[16,48,240]{2,1,0:T(8,128)(2,1)} %unpack_out.1), calls=%async_computation.1 | async-start | bytes 786432 | tf_op jit(solution)/shard_map/all_to_all | solution.py:1092
  176.5 3.8 %collective-permute-start.32 = (bf16[48,1280]{1,0:T(8,128)(2,1)S(1)}, bf16[48,1280]{1,0:T(8,128)(2,1)S(1)}, u32[]{:S(2)}, u32[]{:S(2)}) collective-permute-start(bf16[48,1280]{1,0:T(8,128)(2,1)S(1)} %get-tuple-element.239), channel_id=1, source_target_pairs={{4,0},{5,1},{6,2},{7,3},{8,4},{9,5},{10,6},{11,7},{12,8},{13,9},{1... | collective-permute-start | bytes 368648 | tf_op jit(solution)/shard_map/ppermute | solution.py:74
  180.3 12.0 %scaled_gradient.1 = (f32[512,768]{1,0:T(8,128)}, bf16[512,768]{1,0:T(8,128)(2,1)}) custom-call(s32[4]{0:T(128)} %copy-done.19, bf16[2,512,1536]{2,1,0:T(8,128)(2,1)} %get-tuple-element.166.d_ref.dm_ref, bf16[2,512,1152]{2,1,0:T(8,128)(2,1)} %get-tuple-element.197.dq_ref, bf16[192,1536]{1,0:T(8,128)(2,1)} %stack.23.rest_0_, ...), custom_call_target="tpu_custom_call" | custom-call | flops 4227858432 | bytes 16777216 | tf_op jit(solution)/shard_map/scaled_gradient/pallas_call | solution.py:774
  198.9 3.9 %collective-permute-done.36.swap_ref = bf16[48,1280]{1,0:T(8,128)(2,1)S(1)} collective-permute-done((bf16[48,1280]{1,0:T(8,128)(2,1)S(1)}, bf16[48,1280]{1,0:T(8,128)(2,1)S(1)}, u32[]{:S(2)}, u32[]{:S(2)}) %collective-permute-start.36) | collective-permute-done | bytes 122912 | tf_op jit(solution)/shard_map/ppermute | solution.py:85
  203.6 2.3 finish_mlp.1
  205.9 2.2 finish_qkv.1
  210.7 2.1 collective-permute-done.40
  213.4 3.4 %collective-permute-start.42 = (f32[8,128]{1,0:T(8,128)S(1)}, f32[8,128]{1,0:T(8,128)S(1)}, u32[]{:S(2)}, u32[]{:S(2)}) collective-permute-start(f32[8,128]{1,0:T(8,128)S(1)} %add.207), channel_id=1, source_target_pairs={{4,0},{5,1},{6,2},{7,3},{8,4},{9,5},{10,6},{11,7},{12,8},{13,9},{1... | collective-permute-start | bytes 12296 | tf_op jit(solution)/shard_map/ppermute | solution.py:74
  218.1 4.1 %collective-permute-done.43 = f32[8,128]{1,0:T(8,128)S(1)} collective-permute-done((f32[8,128]{1,0:T(8,128)S(1)}, f32[8,128]{1,0:T(8,128)S(1)}, u32[]{:S(2)}, u32[]{:S(2)}) %collective-permute-start.43) | collective-permute-done | bytes 4128 | tf_op jit(solution)/shard_map/ppermute | solution.py:74
  224.6 4.6 %optimize.1 = (f32[4,48]{1,0:T(4,128)}, f32[8,128]{1,0:T(8,128)S(1)}, f32[48,5376]{1,0:T(8,128)}, f32[48,5376]{1,0:T(8,128)}, f32[48,5376]{1,0:T(8,128)}, /*inde...) custom-call(f32[8,128]{1,0:T(8,128)S(1)} %add_add_fusion.total_ref, ...), custom_call_target="tpu_custom_call" | custom-call | flops 5160960 | bytes 13418496 | tf_op jit(solution)/shard_map/optimize/pallas_call | solution.py:966
  229.7 2.5 %token_gradient.1 = f32[512,768]{1,0:T(8,128)} custom-call(bf16[512,768]{1,0:T(8,128)(2,1)S(1)} %copy-done.3, bf16[512,768]{1,0:T(8,128)(2,1)S(1)} %copy-done.8, f32[512,768]{1,0:T(8,128)S(1)} %copy-done.12, bf16[512,768]{1,0:T(8,128)(2,1)S(1)} %collective-permute-done.38.recv_ref), custom_call_target="tpu_custom_call" | custom-call | flops 7864320 | bytes 5505024 | tf_op jit(solution)/shard_map/token_gradient/pallas_call | solution.py:916
  (187 shorter events, 58.7 us)
Async XLA Ops:
  4.1 43.9 %collective-permute-start.8 = (bf16[528,1536]{1,0:T(8,128)(2,1)S(1)}, bf16[528,1536]{1,0:T(8,128)(2,1)}, u32[]{:S(2)}, u32[]{:S(2)}) collective-permute-start(bf16[528,1536]{1,0:T(8,128)(2,1)S(1)} %normalize.1.own_ref.xo_ref.ido_ref.co_ref), channel_id=1, source_target_pairs={{0,16},{16,0},{1,17},{17,1},{2,18},{18,2},{3,19},{19,3},{4,20},{20... | collective-permute-start | bytes 4866056 | tf_op jit(solution)/shard_map/ppermute | solution.py:85
  8.7 10.7 %collective-permute-start = (bf16[48,1536]{1,0:T(8,128)(2,1)}, bf16[48,1536]{1,0:T(8,128)(2,1)}, u32[]{:S(2)}, u32[]{:S(2)}) collective-permute-start(bf16[48,1536]{1,0:T(8,128)(2,1)} %get-tuple-element.124.refs_0_), channel_id=1, source_target_pairs={{4,0},{5,1},{6,2},{7,3},{8,4},{9,5},{10,6},{11,7},{12,8},{13,9},{1... | collective-permute-start | bytes 442376 | tf_op jit(solution)/shard_map/ppermute | solution.py:74
  12.3 17.0 %collective-permute-start.1 = (bf16[48,1536]{1,0:T(8,128)(2,1)}, bf16[48,1536]{1,0:T(8,128)(2,1)}, u32[]{:S(2)}, u32[]{:S(2)}) collective-permute-start(bf16[48,1536]{1,0:T(8,128)(2,1)} %get-tuple-element.124.refs_0_), channel_id=1, source_target_pairs={{8,0},{9,1},{10,2},{11,3},{12,4},{13,5},{14,6},{15,7},{0,8},{1,9},... | collective-permute-start | bytes 442376 | tf_op jit(solution)/shard_map/ppermute | solution.py:74
  12.3 17.0 %collective-permute-start.2 = (bf16[48,1536]{1,0:T(8,128)(2,1)}, bf16[48,1536]{1,0:T(8,128)(2,1)}, u32[]{:S(2)}, u32[]{:S(2)}) collective-permute-start(bf16[48,1536]{1,0:T(8,128)(2,1)} %get-tuple-element.124.refs_0_), channel_id=1, source_target_pairs={{12,0},{13,1},{14,2},{15,3},{0,4},{1,5},{2,6},{3,7},{4,8},{5,9},{6... | collective-permute-start | bytes 442376 | tf_op jit(solution)/shard_map/ppermute | solution.py:74
  14.2 26.7 %all-to-all-start = ((bf16[16,48,240]{2,1,0:T(8,128)(2,1)}), bf16[16,48,240]{2,1,0:T(8,128)(2,1)S(1)}, u32[]{:S(2)}, u32[]{:S(2)}) async-start(bf16[16,48,240]{2,1,0:T(8,128)(2,1)} %copy-done.11), calls=%async_computation | async-start | bytes 786432 | tf_op jit(solution)/shard_map/all_to_all | solution.py:1007
  31.3 16.8 %collective-permute-start.3 = (bf16[192,1536]{1,0:T(8,128)(2,1)}, bf16[192,1536]{1,0:T(8,128)(2,1)}, u32[]{:S(2)}, u32[]{:S(2)}) collective-permute-start(bf16[192,1536]{1,0:T(8,128)(2,1)} %stack.23.rest_0_), channel_id=1, source_target_pairs={{2,0},{3,1},{0,2},{1,3},{6,4},{7,5},{4,6},{5,7},{10,8},{11,9},{8,1... | collective-permute-start | bytes 1769480 | tf_op jit(solution)/shard_map/ppermute | solution.py:78
  32.3 15.7 %collective-permute-start.4 = (bf16[192,1536]{1,0:T(8,128)(2,1)}, bf16[192,1536]{1,0:T(8,128)(2,1)}, u32[]{:S(2)}, u32[]{:S(2)}) collective-permute-start(bf16[192,1536]{1,0:T(8,128)(2,1)} %stack.23.rest_0_), channel_id=1, source_target_pairs={{0,1},{1,0},{2,3},{3,2},{4,5},{5,4},{6,7},{7,6},{8,9},{9,8},{10,11... | collective-permute-start | bytes 1769480 | tf_op jit(solution)/shard_map/ppermute | solution.py:82
  32.3 15.7 %collective-permute-start.6 = (bf16[48,1280]{1,0:T(8,128)(2,1)S(1)}, bf16[48,1280]{1,0:T(8,128)(2,1)S(1)}, u32[]{:S(2)}, u32[]{:S(2)}) collective-permute-start(bf16[48,1280]{1,0:T(8,128)(2,1)S(1)} %get-tuple-element.129.refs_0_), channel_id=1, source_target_pairs={{8,0},{9,1},{10,2},{11,3},{12,4},{13,5},{14,6},{15,7},{0,8},{1,9},... | collective-permute-start | bytes 368648 | tf_op jit(solution)/shard_map/ppermute | solution.py:74
  38.2 9.8 %collective-permute-start.7 = (bf16[48,1280]{1,0:T(8,128)(2,1)S(1)}, bf16[48,1280]{1,0:T(8,128)(2,1)}, u32[]{:S(2)}, u32[]{:S(2)}) collective-permute-start(bf16[48,1280]{1,0:T(8,128)(2,1)S(1)} %get-tuple-element.129.refs_0_), channel_id=1, source_target_pairs={{12,0},{13,1},{14,2},{15,3},{0,4},{1,5},{2,6},{3,7},{4,8},{5,9},{6... | collective-permute-start | bytes 368648 | tf_op jit(solution)/shard_map/ppermute | solution.py:74
  49.1 20.1 %collective-permute-start.13 = (bf16[192,1280]{1,0:T(8,128)(2,1)S(1)}, bf16[192,1280]{1,0:T(8,128)(2,1)}, u32[]{:S(2)}, u32[]{:S(2)}) collective-permute-start(bf16[192,1280]{1,0:T(8,128)(2,1)S(1)} %stack.24.rest_0_.rest_4_), channel_id=1, source_target_pairs={{0,1},{1,0},{2,3},{3,2},{4,5},{5,4},{6,7},{7,6},{8,9},{9,8},{10,11... | collective-permute-start | bytes 1474568 | tf_op jit(solution)/shard_map/ppermute | solution.py:82
  49.6 19.6 %collective-permute-start.9 = (bf16[192,1280]{1,0:T(8,128)(2,1)S(1)}, bf16[192,1280]{1,0:T(8,128)(2,1)}, u32[]{:S(2)}, u32[]{:S(2)}) collective-permute-start(bf16[192,1280]{1,0:T(8,128)(2,1)S(1)} %stack.24.rest_0_.rest_4_), channel_id=1, source_target_pairs={{2,0},{3,1},{0,2},{1,3},{6,4},{7,5},{4,6},{5,7},{10,8},{11,9},{8,1... | collective-permute-start | bytes 1474568 | tf_op jit(solution)/shard_map/ppermute | solution.py:78
  50.2 19.0 %collective-permute-start.10 = (bf16[48,1920]{1,0:T(8,128)(2,1)S(1)}, bf16[48,1920]{1,0:T(8,128)(2,1)S(1)}, u32[]{:S(2)}, u32[]{:S(2)}) collective-permute-start(bf16[48,1920]{1,0:T(8,128)(2,1)S(1)} %pack_out.1.refs_0_), channel_id=1, source_target_pairs={{4,0},{5,1},{6,2},{7,3},{8,4},{9,5},{10,6},{11,7},{12,8},{13,9},{1... | collective-permute-start | bytes 552968 | tf_op jit(solution)/shard_map/ppermute | solution.py:74
  51.2 18.0 %collective-permute-start.11 = (bf16[48,1920]{1,0:T(8,128)(2,1)S(1)}, bf16[48,1920]{1,0:T(8,128)(2,1)S(1)}, u32[]{:S(2)}, u32[]{:S(2)}) collective-permute-start(bf16[48,1920]{1,0:T(8,128)(2,1)S(1)} %pack_out.1.refs_0_), channel_id=1, source_target_pairs={{8,0},{9,1},{10,2},{11,3},{12,4},{13,5},{14,6},{15,7},{0,8},{1,9},... | collective-permute-start | bytes 552968 | tf_op jit(solution)/shard_map/ppermute | solution.py:74
  56.4 12.9 %collective-permute-start.12 = (bf16[48,1920]{1,0:T(8,128)(2,1)S(1)}, bf16[48,1920]{1,0:T(8,128)(2,1)S(1)}, u32[]{:S(2)}, u32[]{:S(2)}) collective-permute-start(bf16[48,1920]{1,0:T(8,128)(2,1)S(1)} %pack_out.1.refs_0_), channel_id=1, source_target_pairs={{12,0},{13,1},{14,2},{15,3},{0,4},{1,5},{2,6},{3,7},{4,8},{5,9},{6... | collective-permute-start | bytes 552968 | tf_op jit(solution)/shard_map/ppermute | solution.py:74
  69.3 23.0 %collective-permute-start.15 = (bf16[192,1920]{1,0:T(8,128)(2,1)S(1)}, bf16[192,1920]{1,0:T(8,128)(2,1)S(1)}, u32[]{:S(2)}, u32[]{:S(2)}) collective-permute-start(bf16[192,1920]{1,0:T(8,128)(2,1)S(1)} %stack.25.rest_0_), channel_id=1, source_target_pairs={{2,0},{3,1},{0,2},{1,3},{6,4},{7,5},{4,6},{5,7},{10,8},{11,9},{8,1... | collective-permute-start | bytes 2211848 | tf_op jit(solution)/shard_map/ppermute | solution.py:78
  70.6 21.8 %collective-permute-start.16 = (bf16[192,1920]{1,0:T(8,128)(2,1)S(1)}, bf16[192,1920]{1,0:T(8,128)(2,1)S(1)}, u32[]{:S(2)}, u32[]{:S(2)}) collective-permute-start(bf16[192,1920]{1,0:T(8,128)(2,1)S(1)} %stack.25.rest_0_), channel_id=1, source_target_pairs={{0,1},{1,0},{2,3},{3,2},{4,5},{5,4},{6,7},{7,6},{8,9},{9,8},{10,11... | collective-permute-start | bytes 2211848 | tf_op jit(solution)/shard_map/ppermute | solution.py:82
  98.3 18.9 %collective-permute-start.20 = (bf16[192,1920]{1,0:T(8,128)(2,1)S(1)}, bf16[192,1920]{1,0:T(8,128)(2,1)}, u32[]{:S(2)}, u32[]{:S(2)}) collective-permute-start(bf16[192,1920]{1,0:T(8,128)(2,1)S(1)} %add_convert_fusion.1), channel_id=1, source_target_pairs={{2,0},{3,1},{0,2},{1,3},{6,4},{7,5},{4,6},{5,7},{10,8},{11,9},{8,1... | collective-permute-start | bytes 2211848 | tf_op jit(solution)/shard_map/ppermute | solution.py:78
  123.2 28.7 %collective-permute-start.26 = (bf16[512,768]{1,0:T(8,128)(2,1)}, bf16[512,768]{1,0:T(8,128)(2,1)}, u32[]{:S(2)}, u32[]{:S(2)}) collective-permute-start(bf16[512,768]{1,0:T(8,128)(2,1)} %get-tuple-element.185), channel_id=1, source_target_pairs={{0,16},{16,0},{1,17},{17,1},{2,18},{18,2},{3,19},{19,3},{4,20},{20... | collective-permute-start | bytes 2359304 | tf_op jit(solution)/shard_map/ppermute | solution.py:85
  126.1 25.9 %collective-permute-start.21 = (bf16[48,1920]{1,0:T(8,128)(2,1)}, bf16[48,1920]{1,0:T(8,128)(2,1)S(1)}, u32[]{:S(2)}, u32[]{:S(2)}) collective-permute-start(bf16[48,1920]{1,0:T(8,128)(2,1)} %get-tuple-element.235), channel_id=1, source_target_pairs={{12,0},{13,1},{14,2},{15,3},{0,4},{1,5},{2,6},{3,7},{4,8},{5,9},{6... | collective-permute-start | bytes 552968 | tf_op jit(solution)/shard_map/ppermute | solution.py:74
  128.4 23.5 %collective-permute-start.22 = (bf16[48,1920]{1,0:T(8,128)(2,1)}, bf16[48,1920]{1,0:T(8,128)(2,1)}, u32[]{:S(2)}, u32[]{:S(2)}) collective-permute-start(bf16[48,1920]{1,0:T(8,128)(2,1)} %get-tuple-element.234), channel_id=1, source_target_pairs={{8,0},{9,1},{10,2},{11,3},{12,4},{13,5},{14,6},{15,7},{0,8},{1,9},... | collective-permute-start | bytes 552968 | tf_op jit(solution)/shard_map/ppermute | solution.py:74
  129.3 22.6 %collective-permute-start.23 = (bf16[48,1920]{1,0:T(8,128)(2,1)}, bf16[48,1920]{1,0:T(8,128)(2,1)}, u32[]{:S(2)}, u32[]{:S(2)}) collective-permute-start(bf16[48,1920]{1,0:T(8,128)(2,1)} %get-tuple-element.233), channel_id=1, source_target_pairs={{4,0},{5,1},{6,2},{7,3},{8,4},{9,5},{10,6},{11,7},{12,8},{13,9},{1... | collective-permute-start | bytes 552968 | tf_op jit(solution)/shard_map/ppermute | solution.py:74
  133.0 19.0 %collective-permute-start.25 = (bf16[192,1536]{1,0:T(8,128)(2,1)S(1)}, bf16[192,1536]{1,0:T(8,128)(2,1)}, u32[]{:S(2)}, u32[]{:S(2)}) collective-permute-start(bf16[192,1536]{1,0:T(8,128)(2,1)S(1)} %add_convert_fusion.2), channel_id=1, source_target_pairs={{2,0},{3,1},{0,2},{1,3},{6,4},{7,5},{4,6},{5,7},{10,8},{11,9},{8,1... | collective-permute-start | bytes 1769480 | tf_op jit(solution)/shard_map/ppermute | solution.py:78
  154.2 11.3 %collective-permute-start.29 = (bf16[48,1920]{1,0:T(8,128)(2,1)S(1)}, bf16[48,1920]{1,0:T(8,128)(2,1)S(1)}, u32[]{:S(2)}, u32[]{:S(2)}) collective-permute-start(bf16[48,1920]{1,0:T(8,128)(2,1)S(1)} %add_convert_fusion.4.own_ref), channel_id=1, source_target_pairs={{0,16},{16,0},{1,17},{17,1},{2,18},{18,2},{3,19},{19,3},{4,20},{20... | collective-permute-start | bytes 552968 | tf_op jit(solution)/shard_map/ppermute | solution.py:85
  155.7 13.3 %collective-permute-start.28 = (bf16[192,1280]{1,0:T(8,128)(2,1)S(1)}, bf16[192,1280]{1,0:T(8,128)(2,1)S(1)}, u32[]{:S(2)}, u32[]{:S(2)}) collective-permute-start(bf16[192,1280]{1,0:T(8,128)(2,1)S(1)} %add_convert_fusion.3), channel_id=1, source_target_pairs={{2,0},{3,1},{0,2},{1,3},{6,4},{7,5},{4,6},{5,7},{10,8},{11,9},{8,1... | collective-permute-start | bytes 1474568 | tf_op jit(solution)/shard_map/ppermute | solution.py:78
  159.4 17.2 %collective-permute-start.33 = (bf16[48,1536]{1,0:T(8,128)(2,1)}, bf16[48,1536]{1,0:T(8,128)(2,1)S(1)}, u32[]{:S(2)}, u32[]{:S(2)}) collective-permute-start(bf16[48,1536]{1,0:T(8,128)(2,1)} %get-tuple-element.238), channel_id=1, source_target_pairs={{12,0},{13,1},{14,2},{15,3},{0,4},{1,5},{2,6},{3,7},{4,8},{5,9},{6... | collective-permute-start | bytes 442376 | tf_op jit(solution)/shard_map/ppermute | solution.py:74
  159.4 33.0 %collective-permute-start.34 = (bf16[48,1536]{1,0:T(8,128)(2,1)}, bf16[48,1536]{1,0:T(8,128)(2,1)S(1)}, u32[]{:S(2)}, u32[]{:S(2)}) collective-permute-start(bf16[48,1536]{1,0:T(8,128)(2,1)} %get-tuple-element.237), channel_id=1, source_target_pairs={{8,0},{9,1},{10,2},{11,3},{12,4},{13,5},{14,6},{15,7},{0,8},{1,9},... | collective-permute-start | bytes 442376 | tf_op jit(solution)/shard_map/ppermute | solution.py:74
  160.9 31.4 %collective-permute-start.35 = (bf16[48,1536]{1,0:T(8,128)(2,1)S(1)}, bf16[48,1536]{1,0:T(8,128)(2,1)S(1)}, u32[]{:S(2)}, u32[]{:S(2)}) collective-permute-start(bf16[48,1536]{1,0:T(8,128)(2,1)S(1)} %get-tuple-element.236), channel_id=1, source_target_pairs={{4,0},{5,1},{6,2},{7,3},{8,4},{9,5},{10,6},{11,7},{12,8},{13,9},{1... | collective-permute-start | bytes 442376 | tf_op jit(solution)/shard_map/ppermute | solution.py:74
  169.8 22.6 %collective-permute-start.30 = (bf16[48,1280]{1,0:T(8,128)(2,1)S(1)}, bf16[48,1280]{1,0:T(8,128)(2,1)S(1)}, u32[]{:S(2)}, u32[]{:S(2)}) collective-permute-start(bf16[48,1280]{1,0:T(8,128)(2,1)S(1)} %get-tuple-element.241), channel_id=1, source_target_pairs={{12,0},{13,1},{14,2},{15,3},{0,4},{1,5},{2,6},{3,7},{4,8},{5,9},{6... | collective-permute-start | bytes 368648 | tf_op jit(solution)/shard_map/ppermute | solution.py:74
  169.8 22.6 %collective-permute-start.31 = (bf16[48,1280]{1,0:T(8,128)(2,1)S(1)}, bf16[48,1280]{1,0:T(8,128)(2,1)S(1)}, u32[]{:S(2)}, u32[]{:S(2)}) collective-permute-start(bf16[48,1280]{1,0:T(8,128)(2,1)S(1)} %get-tuple-element.240), channel_id=1, source_target_pairs={{8,0},{9,1},{10,2},{11,3},{12,4},{13,5},{14,6},{15,7},{0,8},{1,9},... | collective-permute-start | bytes 368648 | tf_op jit(solution)/shard_map/ppermute | solution.py:74
  171.4 26.5 %all-to-all-start.1 = ((bf16[16,48,240]{2,1,0:T(8,128)(2,1)}), bf16[16,48,240]{2,1,0:T(8,128)(2,1)S(1)}, u32[]{:S(2)}, u32[]{:S(2)}) async-start(bf16[16,48,240]{2,1,0:T(8,128)(2,1)} %unpack_out.1), calls=%async_computation.1 | async-start | bytes 786432 | tf_op jit(solution)/shard_map/all_to_all | solution.py:1092
  176.5 15.9 %collective-permute-start.32 = (bf16[48,1280]{1,0:T(8,128)(2,1)S(1)}, bf16[48,1280]{1,0:T(8,128)(2,1)S(1)}, u32[]{:S(2)}, u32[]{:S(2)}) collective-permute-start(bf16[48,1280]{1,0:T(8,128)(2,1)S(1)} %get-tuple-element.239), channel_id=1, source_target_pairs={{4,0},{5,1},{6,2},{7,3},{8,4},{9,5},{10,6},{11,7},{12,8},{13,9},{1... | collective-permute-start | bytes 368648 | tf_op jit(solution)/shard_map/ppermute | solution.py:74
  202.8 26.9 %collective-permute-start.38 = (bf16[512,768]{1,0:T(8,128)(2,1)}, bf16[512,768]{1,0:T(8,128)(2,1)S(1)}, u32[]{:S(2)}, u32[]{:S(2)}) collective-permute-start(bf16[512,768]{1,0:T(8,128)(2,1)} %get-tuple-element.211), channel_id=1, source_target_pairs={{0,16},{16,0},{1,17},{17,1},{2,18},{18,2},{3,19},{19,3},{4,20},{20... | collective-permute-start | bytes 2359304 | tf_op jit(solution)/shard_map/ppermute | solution.py:85
  (57 other events, 472.9 us)

commit v4 on v3

--- a/solution.py
+++ b/solution.py
@@ -92,13 +92,12 @@
 
     def total(self, a):
         a = a + self.swap_core(a)
-        for exchange, size in ((self.from_y, self.ys), (self.from_z, self.zs)):
-            if size == 2:
-                a = a + exchange(a, 1)
-            elif size == 4:
-                a = (a + exchange(a, 2)) + (exchange(a, 1) + exchange(a, 3))
-            elif size > 1:
-                a = sum([exchange(a, s) for s in range(1, size)], a)
+        for step, size in ((2, self.ys), (2 * self.ys, self.zs)):
+            m = 1
+            while m < size:
+                pairs = [(i, i ^ (m * step)) for i in range(self.n)]
+                a = a + lax.ppermute(a, "fsdp", pairs)
+                m *= 2
         return a
 
     def row(self, pos_ref, piece, rows):
@@ -124,12 +123,16 @@
             total = total + a.astype(F32)
         return total
 
-    def by_y(self):
+    def y_parts(self):
         size = self.plan.zs * self.rows
-        self.y_got = [
-            self.plan.from_y(self.sums(t * size, (t + 1) * size, ()).astype(BF16), -t)
+        return [
+            self.sums(t * size, (t + 1) * size, ()).astype(BF16)
             for t in range(1, self.plan.ys)
         ]
+
+    def by_y(self, parts=None):
+        parts = self.y_parts() if parts is None else parts
+        self.y_got = [self.plan.from_y(a, -t - 1) for t, a in enumerate(parts)]
 
     def part(self, s):
         at = slice(s * self.rows, (s + 1) * self.rows)
@@ -432,70 +435,53 @@
     )(plan.pos, own, swap, in_weight, vec_t, grad, sq, dot, sq_out)
 
 
-IDS = 16
-
-
-def normalize(tokens, cotangent, ids):
+def prepare(plan, tokens, other_tokens, cotangent, other_cotangent, rows):
     tok = tokens.shape[0]
-
-    def kernel(t_ref, c_ref, id_ref, out_ref):
-        rows = t_ref[...].astype(F32)
-        centre = rows - jnp.mean(rows, axis=-1, keepdims=True)
-        r = lax.rsqrt(jnp.mean(centre * centre, axis=-1, keepdims=True) + norm_eps)
-        out_ref[:tok, :D] = (centre * r).astype(BF16)
-        out_ref[:tok, D:] = c_ref[...]
-        out_ref[tok:, :] = jnp.zeros((IDS, 2 * D), BF16)
-        numbers = jnp.broadcast_to(id_ref[...].astype(F32), (IDS, tok))
-        out_ref[tok:, :tok] = numbers.astype(BF16)
-
+    kind = row_type(rows)
+
+    def kernel(pos_ref, to_ref, tp_ref, co_ref, cp_ref, xo_ref, xp_ref, turned_ref, sum_ref, t_ref):
+        for half, (from_ref, cot_ref, x_ref) in enumerate(
+            ((to_ref, co_ref, xo_ref), (tp_ref, cp_ref, xp_ref))
+        ):
+            values = from_ref[...].astype(F32)
+            centre = values - jnp.mean(values, axis=-1, keepdims=True)
+            r = lax.rsqrt(jnp.mean(centre * centre, axis=-1, keepdims=True) + norm_eps)
+            normal = centre * r
+            x_ref[...] = normal.astype(BF16)
+            cot = cot_ref[...].astype(F32)
+            if half == 0:
+                total = jnp.sum(cot, axis=0, keepdims=True)
+                sum_ref[...] = jnp.broadcast_to(total, (8, D))
+            for which, value in enumerate((normal, cot)):
+                t_ref[...] = value.T.astype(kind)
+
+                def put(at, a):
+                    columns = slice(half * tok, (half + 1) * tok)
+                    turned_ref[which, at : at + rows, columns] = a.astype(BF16)
+
+                turn(plan, pos_ref, t_ref, rows, put)
+
+    low = jax.ShapeDtypeStruct((tok, D), BF16)
     return pl.pallas_call(
         kernel,
         grid=(1,),
-        in_specs=[whole((tok, D)), whole((tok, D)), whole((1, tok))],
-        out_specs=whole((tok + IDS, 2 * D)),
-        out_shape=jax.ShapeDtypeStruct((tok + IDS, 2 * D), BF16),
-        compiler_params=params(16),
-        cost_estimate=cost(10 * tok * D, 8 * tok * D),
-        name="normalize",
-    )(tokens, cotangent, ids)
-
-
-def transposes(plan, xc_own, xc_other, rows):
-    tok = xc_own.shape[0] - IDS
-    kind = row_type(rows)
-
-    def kernel(pos_ref, own_ref, other_ref, out_ref, sum_ref, t_ref):
-        for half, ref in enumerate((own_ref, other_ref)):
-            t_ref[...] = ref[...].astype(F32).T.astype(kind)
-
-            def put(at, a):
-                out_ref[0, at : at + rows, half * tok : (half + 1) * tok] = a.astype(BF16)
-
-            turn(plan, pos_ref, t_ref, rows, put)
-        total = jnp.sum(own_ref[...].astype(F32), axis=0, keepdims=True)
-        sum_ref[0] = jnp.broadcast_to(total, (8, D))
-
-    return pl.pallas_call(
-        kernel,
-        grid=(2,),
-        in_specs=[smem()] + [pl.BlockSpec((tok, D), lambda j: (0, j))] * 2,
-        out_specs=[
-            pl.BlockSpec((1, D, 2 * tok), lambda j: (j, 0, 0)),
-            pl.BlockSpec((1, 8, D), lambda j: (j, 0, 0)),
-        ],
+        in_specs=[smem()] + [whole((tok, D))] * 4,
+        out_specs=[whole((tok, D))] * 2 + [whole((2, D, 2 * tok)), whole((8, D))],
         out_shape=[
+            low,
+            low,
             jax.ShapeDtypeStruct((2, D, 2 * tok), BF16),
-            jax.ShapeDtypeStruct((2, 8, D), F32),
+            jax.ShapeDtypeStruct((8, D), F32),
         ],
         scratch_shapes=[pltpu.VMEM((D, tok), kind)],
-        compiler_params=params(24),
-        cost_estimate=cost(10 * tok * D, 16 * tok * D),
-        name="transposes",
-    )(plan.pos, xc_own, xc_other)
-
-
-def mlp_forward(plan, xc_own, xc_other, turned, pieces):
-    tok = xc_own.shape[0] - IDS
+        compiler_params=params(),
+        cost_estimate=cost(40 * tok * D, 20 * tok * D),
+        name="prepare",
+    )(plan.pos, tokens, other_tokens, cotangent, other_cotangent)
+
+
+def mlp_forward(plan, x_own, x_other, turned, pieces):
+    tok = x_own.shape[0]
     rows = pieces[0].shape[0] // plan.zs
     tile = 512
     n = len(pieces)
@@ -525,7 +511,7 @@
         kernel,
         grid=(FH // tile,),
         in_specs=[smem()]
-        + [pl.BlockSpec((tok, D), lambda j: (0, 0))] * 2
+        + [whole((tok, D))] * 2
         + [pl.BlockSpec((1, D, 2 * tok), lambda j: (1, 0, 0))]
         + [pl.BlockSpec((plan.zs * rows, tile), lambda j: (0, j))] * n,
         out_specs=[block, block, grad, grad],
@@ -535,7 +521,7 @@
         compiler_params=params(),
         cost_estimate=cost(8 * tok * D * FH, 12 * tok * FH, 2 * tok * FH),
         name="mlp_forward",
-    )(plan.pos, xc_own, xc_other, turned, *pieces)
+    )(plan.pos, x_own, x_other, turned, *pieces)
 
 
 def head_means(a, block_ref):
@@ -544,18 +530,17 @@
     return mm(high, block_ref[...]) + mm(low, block_ref[...])
 
 
-def attention_forward(plan, xc_own, xc_other, pieces, block, turned, g_own, g_other):
-    tok = xc_own.shape[0] - IDS
+def attention_forward(plan, x_own, x_other, pieces, ids, block, turned, g_own, g_other):
+    tok = x_own.shape[0]
     rows = pieces[0].shape[0] // plan.zs
     n = len(pieces)
-
     half_d = D // 2
 
     def kernel(pos_ref, xo_ref, xp_ref, ido_ref, idp_ref, block_ref, ct_ref, _, __, *rest):
         refs, vec_refs = rest[:n], rest[n : 2 * n]
         (
-            q_ref, k_ref, v_ref, nq_ref, nk_ref, rq_ref, rk_ref, att_ref, p_ref, gain_ref,
-            g_own_ref, g_other_ref, w_ref, vs_ref,
+            qk_ref, v_ref, n_ref, r_ref, att_ref, p_ref, gain_ref, g_own_ref, g_other_ref,
+            w_ref, vs_ref, all_ref,
         ) = rest[2 * n :]
         step = pl.program_id(0)
 
@@ -567,29 +552,25 @@
         place(plan, pos_ref, refs, rows, w_ref)
         w = w_ref[...].astype(BF16)
         column = pl.ds(pl.multiple_of(pos_ref[3] * DH + step * PAIR, PAIR), PAIR)
-        q_gain = gain_ref[1:2, column] * (HD ** (-0.5))
-        k_gain = gain_ref[2:3, column]
-        lane = lax.broadcasted_iota(jnp.int32, (tok, PAIR), 1)
-        first = lane < HD
+        gain = jnp.concatenate(
+            [gain_ref[1:2, column] * (HD ** (-0.5)), gain_ref[2:3, column]], axis=1
+        )
+        first = lax.broadcasted_iota(jnp.int32, (tok, PAIR), 1) < HD
         for half, x_ref in enumerate((xo_ref, xp_ref)):
             raw = mm(x_ref[...], w)
-
-            def normed(a, gain, n_ref, r_ref, out_ref):
-                centre = a - head_means(a, block_ref)
-                r = lax.rsqrt(head_means(centre * centre, block_ref) + norm_eps)
-                normal = centre * r
-                n_ref[half] = normal.astype(BF16)
-                r_ref[half] = r.astype(BF16)
-                low = (normal * gain).astype(BF16)
-                out_ref[half] = low
-                return low
-
-            q = normed(raw[:, :PAIR], q_gain, nq_ref, rq_ref, q_ref)
-            k = normed(raw[:, PAIR : 2 * PAIR], k_gain, nk_ref, rk_ref, k_ref)
+            qk = raw[:, : 2 * PAIR]
+            centre = qk - head_means(qk, block_ref)
+            r = lax.rsqrt(mm((centre * centre).astype(BF16), block_ref[...]) + norm_eps)
+            normal = centre * r
+            n_ref[half] = normal.astype(BF16)
+            r_ref[half] = r.astype(BF16)
+            low = (normal * gain).astype(BF16)
+            qk_ref[half] = low
+            q, k = low[:, :PAIR], low[:, PAIR:]
             v = raw[:, 2 * PAIR :].astype(BF16)
             v_ref[half] = v
-            numbers = (ido_ref, idp_ref)[half][:8].astype(F32)
-            same = numbers.T[:, :1] == numbers[:1]
+            number = (ido_ref, idp_ref)[half][...].astype(F32)
+            same = jnp.broadcast_to(number, (8, tok)).T[:, :1] == number
             att = []
             zero = jnp.zeros_like(q)
             for head in range(2):
@@ -598,108 +579,136 @@
                 p = (e * (1.0 / jnp.sum(e, axis=1, keepdims=True))).astype(BF16)
                 p_ref[half, head] = p
                 att.append(mm(p, v))
-            att_ref[half] = jnp.where(first, att[0], att[1]).astype(BF16)
-        g = mm(ct_ref[0], att_ref[...].reshape(2 * tok, PAIR)).astype(BF16)
-        g_own_ref[...] = g[:half_d]
-        g_other_ref[...] = g[half_d:]
+            att_low = jnp.where(first, att[0], att[1]).astype(BF16)
+            att_ref[half] = att_low
+            at = pl.ds(pl.multiple_of(step * PAIR, PAIR), PAIR)
+            all_ref[half * tok : (half + 1) * tok, at] = att_low
+
+        @pl.when(step == PAIRS - 1)
+        def _():
+            g = mm(ct_ref[0], all_ref[...]).astype(BF16)
+            g_own_ref[...] = g[:half_d]
+            g_other_ref[...] = g[half_d:]
 
     pair = pl.BlockSpec((2, tok, PAIR), lambda j: (0, 0, j))
+    pair2 = pl.BlockSpec((2, tok, 2 * PAIR), lambda j: (0, 0, j))
     small = jax.ShapeDtypeStruct((2, tok, DH), BF16)
+    small2 = jax.ShapeDtypeStruct((2, tok, 2 * DH), BF16)
+    heads = pl.BlockSpec((half_d, DH), lambda j: (0, FH // DH))
     return pl.pallas_call(
         kernel,
         grid=(PAIRS,),
         in_specs=[smem()]
-        + [pl.BlockSpec((tok, D), lambda j: (0, 0))] * 2
-        + [pl.BlockSpec((IDS, tok), lambda j: (tok // IDS, 0))] * 2
-        + [whole((PAIR, PAIR))]
+        + [whole((tok, D))] * 2
+        + [whole((1, tok))] * 2
+        + [whole((2 * PAIR, 2 * PAIR))]
         + [pl.BlockSpec((1, D, 2 * tok), lambda j: (1, 0, 0))]
         + [pl.BlockSpec(memory_space=pl.ANY)] * 2
         + [pl.BlockSpec((plan.zs * rows, QKV), lambda j: (0, j))] * n
         + [pl.BlockSpec((plan.zs * rows, VEC), lambda j: (0, QW // VEC))] * n,
-        out_specs=[pair] * 8
+        out_specs=[pair2, pair, pair2, pair2, pair]
         + [pl.BlockSpec((2, 2, tok, tok), lambda j: (0, j, 0, 0)), whole((8, D))]
-        + [pl.BlockSpec((half_d, PAIR), lambda j: (0, FH // PAIR + j))] * 2,
-        out_shape=[small] * 8
+        + [heads, heads],
+        out_shape=[small2, small, small2, small2, small]
         + [
             jax.ShapeDtypeStruct((2, 2 * PAIRS, tok, tok), BF16),
             jax.ShapeDtypeStruct((8, D), F32),
             jax.ShapeDtypeStruct(g_own.shape, BF16),
             jax.ShapeDtypeStruct(g_own.shape, BF16),
         ],
-        input_output_aliases={7: 10, 8: 11},
+        input_output_aliases={7: 7, 8: 8},
         scratch_shapes=[
             pltpu.VMEM((D, QKV), row_type(rows)),
             pltpu.VMEM((D, VEC), row_type(rows)),
+            pltpu.VMEM((2 * tok, DH), BF16),
         ],
         compiler_params=params(),
         cost_estimate=cost(4 * tok * D * QW, 20 * MIB, 12 * tok * tok),
         name="attention_forward",
     )(
-        plan.pos, xc_own, xc_other, xc_own, xc_other, block, turned, g_own, g_other,
-        *pieces, *pieces,
-    )
-
-
-def output_columns(plan, rows, tile, steps):
-    return pl.BlockSpec(
-        (plan.zs * rows, tile), lambda j: (0, jnp.where(j == 0, steps - 1, j - 1))
-    )
-
-
-def output_step(plan, att, mixed, slope, xc_own, xc_other, pieces):
-    tok = xc_own.shape[0] - IDS
+        plan.pos, x_own, x_other, *ids, block, turned, g_own, g_other, *pieces, *pieces,
+    )
+
+
+TILE = 256
+
+
+def token_tiles(tok):
+    per = tok // TILE
+
+    def pair(j):
+        return (j // per, j % per, 0)
+
+    def own(j):
+        return jnp.minimum(j, per - 1)
+
+    def other(j):
+        return jnp.maximum(j - per, 0)
+
+    return per, pair, own, other
+
+
+def output_step(plan, att, mixed, slope, cot_own, cot_other, pieces):
+    tok = cot_own.shape[0]
     rows = pieces[0].shape[0] // plan.zs
     n = len(pieces)
-    tile = DH
-    steps = 1 + FH // tile
+    per, pair, own, other = token_tiles(tok)
 
     def kernel(pos_ref, att_ref, mix_ref, slope_ref, co_ref, cp_ref, *rest):
         refs = rest[:n]
-        out_own_ref, out_other_ref, d_att_ref, d_in_ref, w_ref, acc_ref = rest[n:]
+        out_own_ref, out_other_ref, d_att_ref, d_in_ref, w_ref = rest[n:]
         step = pl.program_id(0)
-        place(plan, pos_ref, refs, rows, w_ref)
+
+        @pl.when(step == 0)
+        def _():
+            place(plan, pos_ref, refs, rows, w_ref)
+
         w = w_ref[...].astype(BF16)
-
-        @pl.when(step == 0)
-        def _():
-            for half, ref in enumerate((co_ref, cp_ref)):
-                d_att_ref[half] = mm(ref[...], w).astype(BF16)
-                acc_ref[half] = mm(att_ref[half], w, NT)
-
-        @pl.when(step > 0)
-        def _():
-            for half, ref in enumerate((co_ref, cp_ref)):
-                d = mm(ref[...], w)
-                d_in_ref[half] = (d * slope_ref[half].astype(F32)).astype(BF16)
-                acc_ref[half] += mm(mix_ref[half], w, NT)
-
-        @pl.when(step == steps - 1)
-        def _():
-            out_own_ref[...] = acc_ref[0]
-            out_other_ref[...] = acc_ref[1].astype(BF16)
-
-    hidden = pl.BlockSpec((2, tok, tile), lambda j: (0, 0, jnp.maximum(j - 1, 0)))
-    return pl.pallas_call(
-        kernel,
-        grid=(steps,),
-        in_specs=[smem(), whole((2, tok, tile)), hidden, hidden]
-        + [pl.BlockSpec((tok, D), lambda j: (0, 1))] * 2
-        + [output_columns(plan, rows, tile, steps)] * n,
-        out_specs=[whole((tok, D)), whole((tok, D)), whole((2, tok, tile)), hidden],
+        cot = jnp.where(step < per, co_ref[...], cp_ref[...])
+        for at in range(0, FH, DH):
+            d = mm(cot, w[:, at : at + DH])
+            slopes = slope_ref[0, :, at : at + DH].astype(F32)
+            d_in_ref[0, :, at : at + DH] = (d * slopes).astype(BF16)
+        d_att_ref[0] = mm(cot, w[:, FH:]).astype(BF16)
+        out = mm(mix_ref[0], w[:, :FH], NT) + mm(att_ref[0], w[:, FH:], NT)
+
+        @pl.when(step < per)
+        def _():
+            out_own_ref[...] = out
+
+        @pl.when(step >= per)
+        def _():
+            out_other_ref[...] = out.astype(BF16)
+
+    return pl.pallas_call(
+        kernel,
+        grid=(2 * per,),
+        in_specs=[
+            smem(),
+            pl.BlockSpec((1, TILE, DH), pair),
+            pl.BlockSpec((1, TILE, FH), pair),
+            pl.BlockSpec((1, TILE, FH), pair),
+            pl.BlockSpec((TILE, D), lambda j: (own(j), 0)),
+            pl.BlockSpec((TILE, D), lambda j: (other(j), 0)),
+        ]
+        + [whole(pieces[0].shape)] * n,
+        out_specs=[
+            pl.BlockSpec((TILE, D), lambda j: (own(j), 0)),
+            pl.BlockSpec((TILE, D), lambda j: (other(j), 0)),
+            pl.BlockSpec((1, TILE, DH), pair),
+            pl.BlockSpec((1, TILE, FH), pair),
+        ],
         out_shape=[
             jax.ShapeDtypeStruct((tok, D), F32),
             jax.ShapeDtypeStruct((tok, D), BF16),
             jax.ShapeDtypeStruct((2, tok, DH), BF16),
             jax.ShapeDtypeStruct((2, tok, FH), BF16),
         ],
-        scratch_shapes=[
-            pltpu.VMEM((D, tile), row_type(rows)),
-            pltpu.VMEM((2, tok, D), F32),
-        ],
+        scratch_shapes=[pltpu.VMEM((D, FH + DH), row_type(rows))],
         compiler_params=params(),
-        cost_estimate=cost(8 * tok * steps * tile * D, 20 * MIB),
+        cost_estimate=cost(8 * tok * (FH + DH) * D, 20 * MIB),
         name="output_step",
-    )(plan.pos, att, mixed, slope, xc_own, xc_other, *pieces)
+    )(plan.pos, att, mixed, slope, cot_own, cot_other, *pieces)
 
 
 def mlp_gradient(turned, d_inner):
@@ -732,132 +741,107 @@
     tok = d_inner.shape[1]
     rows = mlp_pieces[0].shape[0] // plan.zs
     n = len(mlp_pieces)
-    tile = QKV
-    count = FH // tile
-    steps = count + PAIRS
+    per, pair, own, other = token_tiles(tok)
 
     def kernel(pos_ref, dm_ref, dq_ref, *rest):
         refs_m, refs_q = rest[:n], rest[n : 2 * n]
-        e_own_ref, e_other_ref, w_ref, acc_ref = rest[2 * n :]
+        e_own_ref, e_other_ref, wm_ref, wq_ref = rest[2 * n :]
         step = pl.program_id(0)
 
         @pl.when(step == 0)
         def _():
-            acc_ref[...] = jnp.zeros_like(acc_ref)
-
-        def add(ref):
-            w = w_ref[...].astype(BF16)
-            for half in range(2):
-                acc_ref[half] += mm(ref[half], w, NT)
-
-        @pl.when(step < count)
-        def _():
-            place(plan, pos_ref, refs_m, rows, w_ref)
-            add(dm_ref)
-
-        @pl.when(step >= count)
-        def _():
-            place(plan, pos_ref, refs_q, rows, w_ref)
-            add(dq_ref)
-
-        @pl.when(step == steps - 1)
-        def _():
-            e_own_ref[...] = acc_ref[0]
-            e_other_ref[...] = acc_ref[1].astype(BF16)
-
-    def mlp_at(j):
-        return jnp.minimum(j, count - 1)
-
-    def qkv_at(j):
-        return jnp.maximum(j - count, 0)
-
-    return pl.pallas_call(
-        kernel,
-        grid=(steps,),
+            place(plan, pos_ref, refs_m, rows, wm_ref)
+            place(plan, pos_ref, refs_q, rows, wq_ref)
+
+        e = mm(dm_ref[0], wm_ref[...].astype(BF16), NT)
+        e = e + mm(dq_ref[0], wq_ref[...].astype(BF16)[:, :QW], NT)
+
+        @pl.when(step < per)
+        def _():
+            e_own_ref[...] = e
+
+        @pl.when(step >= per)
+        def _():
+            e_other_ref[...] = e.astype(BF16)
+
+    return pl.pallas_call(
+        kernel,
+        grid=(2 * per,),
         in_specs=[
             smem(),
-            pl.BlockSpec((2, tok, tile), lambda j: (0, 0, mlp_at(j))),
-            pl.BlockSpec((2, tok, tile), lambda j: (0, 0, qkv_at(j))),
+            pl.BlockSpec((1, TILE, FH), pair),
+            pl.BlockSpec((1, TILE, QW), pair),
         ]
-        + [pl.BlockSpec((plan.zs * rows, tile), lambda j: (0, mlp_at(j)))] * n
-        + [pl.BlockSpec((plan.zs * rows, tile), lambda j: (0, qkv_at(j)))] * n,
-        out_specs=[whole((tok, D)), whole((tok, D))],
+        + [whole(mlp_pieces[0].shape)] * n
+        + [whole(qkv_pieces[0].shape)] * n,
+        out_specs=[
+            pl.BlockSpec((TILE, D), lambda j: (own(j), 0)),
+            pl.BlockSpec((TILE, D), lambda j: (other(j), 0)),
+        ],
         out_shape=[
             jax.ShapeDtypeStruct((tok, D), F32),
             jax.ShapeDtypeStruct((tok, D), BF16),
         ],
         scratch_shapes=[
-            pltpu.VMEM((D, tile), row_type(rows)),
-            pltpu.VMEM((2, tok, D), F32),
+            pltpu.VMEM((D, FH), row_type(rows)),
+            pltpu.VMEM((D, QW + VEC), row_type(rows)),
         ],
         compiler_params=params(),
-        cost_estimate=cost(4 * tok * steps * tile * D, 16 * MIB),
+        cost_estimate=cost(4 * tok * (FH + QW) * D, 16 * MIB),
         name="scaled_gradient",
     )(plan.pos, d_inner, d_qkv, *mlp_pieces, *qkv_pieces)
 
 
-def attention_backward(plan, turned, saved, d_att, block, gains, cot_sum, before, begin, end, rows):
-    q, k, v, nq, nk, rq, rk, probs = saved
+def attention_backward(plan, turned, saved, d_att, block, gains, cot_sum, rows):
+    qk, v, normals, factors, probs = saved
     tok = d_att.shape[1]
     half_d = D // 2
     kind = row_type(rows)
-    width = (end - begin) * QKV + (VEC if end == PAIRS else 0)
-
-    def kernel(pos_ref, xt_ref, q_ref, k_ref, v_ref, nq_ref, nk_ref, rq_ref, rk_ref, p_ref,
-               da_ref, block_ref, gain_ref, cot_ref, *rest):
-        befores = rest[: len(before)]
-        g_own_ref, g_other_ref, d_ref, vec_ref, turn_ref = rest[len(before) :]
-        step = pl.program_id(0) + begin
-
-        @pl.when(step == begin)
-        def _():
-            if befores:
-                vec_ref[...] = befores[0][...]
-            else:
-                vec_ref[...] = jnp.zeros_like(vec_ref)
-                vec_ref[3:4, :] = cot_ref[0, :1]
+
+    def kernel(pos_ref, xt_ref, qk_ref, v_ref, n_ref, r_ref, p_ref, da_ref, block_ref, gain_ref,
+               cot_ref, g_own_ref, g_other_ref, d_ref, vec_ref, turn_ref):
+        step = pl.program_id(0)
+
+        @pl.when(step == 0)
+        def _():
+            vec_ref[...] = jnp.zeros_like(vec_ref)
+            vec_ref[3:4, :] = cot_ref[:1]
 
         column = pl.ds(pl.multiple_of(pos_ref[3] * DH + step * PAIR, PAIR), PAIR)
-        q_gain = gain_ref[1:2, column]
-        k_gain = gain_ref[2:3, column]
+        gain = jnp.concatenate(
+            [gain_ref[1:2, column] * (HD ** (-0.5)), gain_ref[2:3, column]], axis=1
+        )
         first = lax.broadcasted_iota(jnp.int32, (tok, PAIR), 1) < HD
+
+        def heads(a):
+            zero = jnp.zeros_like(a)
+            return jnp.concatenate([jnp.where(first, a, zero), jnp.where(first, zero, a)], axis=0)
+
         for half in range(2):
-            qb, kb, vb, da = q_ref[half], k_ref[half], v_ref[half], da_ref[half]
-            q_t, da_t = qb.T, da.T
-            zero = jnp.zeros_like(da)
-            dq, dk_t, dv_t = [], [], []
-            for head in range(2):
-                at = slice(head * HD, (head + 1) * HD)
-                dah = jnp.where(first, da, zero) if head == 0 else jnp.where(first, zero, da)
-                p_low = p_ref[half, head]
-                p = p_low.astype(F32)
-                t = p * mm(dah, vb, NT)
-                ds = (t - p * jnp.sum(t, axis=1, keepdims=True)).astype(BF16)
-                dv_t.append(mm(da_t[at], p_low))
-                dk_t.append(mm(q_t[at], ds))
-                dq.append(mm(ds, kb))
-            d_query = jnp.where(first, dq[0], dq[1])
-            d_key = jnp.concatenate(dk_t, axis=0).T
-            d_value = jnp.concatenate(dv_t, axis=0).T
-
-            def back(d, gain, n_ref, r_ref, which, factor):
-                normal = n_ref[half].astype(F32)
-                d = d * factor
-                vec_ref[which : which + 1, column] += jnp.sum(d * normal, axis=0, keepdims=True)
-                e = d * gain
-                mean = head_means(e, block_ref)
-                along = head_means(e * normal, block_ref)
-                return (r_ref[half].astype(F32) * (e - mean - normal * along)).astype(BF16)
-
-            d_ref[half, :, :PAIR] = back(d_query, q_gain, nq_ref, rq_ref, 1, HD ** (-0.5))
-            d_ref[half, :, PAIR : 2 * PAIR] = back(d_key, k_gain, nk_ref, rk_ref, 2, 1.0)
+            qb, kb, vb = qk_ref[half, :, :PAIR], qk_ref[half, :, PAIR:], v_ref[half]
+            da = heads(da_ref[half])
+            p_low = p_ref[half].reshape(2 * tok, tok)
+            p = p_low.astype(F32)
+            t = p * mm(da, vb, NT)
+            ds = (t - p * jnp.sum(t, axis=1, keepdims=True)).astype(BF16)
+            d_value = mm(da.T, p_low).T
+            d_key = mm(heads(qb).T, ds).T
+            dq = mm(ds, kb)
+            d_query = jnp.where(first, dq[:tok], dq[tok:])
+            d = jnp.concatenate([d_query, d_key], axis=1)
+            normal = n_ref[half].astype(F32)
+            sums = jnp.sum(d * normal, axis=0, keepdims=True)
+            vec_ref[1:2, column] += sums[:, :PAIR] * (HD ** (-0.5))
+            vec_ref[2:3, column] += sums[:, PAIR:]
+            e = d * gain
+            along = mm((e * normal).astype(BF16), block_ref[...])
+            d_raw = r_ref[half].astype(F32) * (e - head_means(e, block_ref) - normal * along)
+            d_ref[half, :, : 2 * PAIR] = d_raw.astype(BF16)
             d_ref[half, :, 2 * PAIR :] = d_value.astype(BF16)
         g = mm(xt_ref[0], d_ref[...].reshape(2 * tok, QKV)).astype(BF16)
-        at = pl.ds(pl.multiple_of((step - begin) * QKV, QKV), QKV)
+        at = pl.ds(pl.multiple_of(step * QKV, QKV), QKV)
         g_own_ref[:, at] = g[:half_d]
         g_other_ref[:, at] = g[half_d:]
-        if end < PAIRS:
-            return
 
         @pl.when(step == PAIRS - 1)
         def _():
@@ -865,38 +849,33 @@
 
             def put(at, a):
                 ref = g_own_ref if at < half_d else g_other_ref
-                ref[at % half_d : at % half_d + rows, width - VEC :] = a.astype(BF16)
+                ref[at % half_d : at % half_d + rows, QW:] = a.astype(BF16)
 
             turn(plan, pos_ref, turn_ref, rows, put)
 
-    pair = pl.BlockSpec((2, tok, PAIR), lambda j: (0, 0, begin + j))
-    return pl.pallas_call(
-        kernel,
-        grid=(end - begin,),
+    pair = pl.BlockSpec((2, tok, PAIR), lambda j: (0, 0, j))
+    pair2 = pl.BlockSpec((2, tok, 2 * PAIR), lambda j: (0, 0, j))
+    return pl.pallas_call(
+        kernel,
+        grid=(PAIRS,),
         in_specs=[smem(), pl.BlockSpec((1, D, 2 * tok), lambda j: (0, 0, 0))]
-        + [pair] * 7
+        + [pair2, pair, pair2, pair2]
         + [
-            pl.BlockSpec((2, 2, tok, tok), lambda j: (0, begin + j, 0, 0)),
+            pl.BlockSpec((2, 2, tok, tok), lambda j: (0, j, 0, 0)),
             pair,
-            whole((PAIR, PAIR)),
+            whole((2 * PAIR, 2 * PAIR)),
             whole((8, D)),
-            pl.BlockSpec((1, 8, D), lambda j: (1, 0, 0)),
-        ]
-        + [whole(a.shape) for a in before],
-        out_specs=[whole((half_d, width))] * 2
-        + [pl.BlockSpec((2, tok, QKV), lambda j: (0, 0, j)), whole((VEC, D))],
-        out_shape=[jax.ShapeDtypeStruct((half_d, width), BF16)] * 2
-        + [
-            jax.ShapeDtypeStruct((2, tok, (end - begin) * QKV), BF16),
-            jax.ShapeDtypeStruct((VEC, D), F32),
-        ],
-        scratch_shapes=[pltpu.VMEM((D, VEC), kind)],
+            whole((8, D)),
+        ],
+        out_specs=[whole((half_d, QW + VEC))] * 2
+        + [pl.BlockSpec((2, tok, QKV), lambda j: (0, 0, j))],
+        out_shape=[jax.ShapeDtypeStruct((half_d, QW + VEC), BF16)] * 2
+        + [jax.ShapeDtypeStruct((2, tok, QW), BF16)],
+        scratch_shapes=[pltpu.VMEM((VEC, D), F32), pltpu.VMEM((D, VEC), kind)],
         compiler_params=params(),
-        cost_estimate=cost(16 * tok * D * QKV * (end - begin), 8 * MIB * (end - begin)),
+        cost_estimate=cost(16 * tok * D * QW, 24 * MIB),
         name="attention_backward",
-    )(
-        plan.pos, turned, q, k, v, nq, nk, rq, rk, probs, d_att, block, gains, cot_sum, *before,
-    )
+    )(plan.pos, turned, qk, v, normals, factors, probs, d_att, block, gains, cot_sum)
 
 
 def token_gradient(tokens, cotangent, e_own, e_recv):
@@ -951,7 +930,7 @@
 
         @pl.when(pl.program_id(0) == 0)
         def _():
-            norm_ref[...] = jnp.broadcast_to(norm, (8, 128))
+            norm_ref[...] = norm
             pad_ref[...] = jnp.zeros_like(pad_ref)
             pad_ref[:rows] = cols_ref[...]
             grad = pad_ref[...].T[:4, :rows]
@@ -970,11 +949,11 @@
         + [in_block] * 4
         + [out_block] * 4
         + [whole(vecs[0].shape)] * 3,
-        out_specs=[whole(vecs[0].shape), whole((8, 128))]
+        out_specs=[whole(vecs[0].shape), whole((1, 1))]
         + [in_block] * 3
         + [out_block] * 3
         + [whole(vecs[0].shape)] * 3,
-        out_shape=[shapes[2], jax.ShapeDtypeStruct((8, 128), F32)]
+        out_shape=[shapes[2], jax.ShapeDtypeStruct((1, 1), F32)]
         + [shapes[0]] * 3
         + [shapes[1]] * 3
         + [shapes[2]] * 3,
@@ -1004,9 +983,10 @@
 
     low_vec = vectors.astype(BF16).astype(F32)
     vec_t = jnp.pad(low_vec.T, ((0, 0), (0, VEC - 4)))
+    mlp_piece, qkv_piece = pack_in(plan, in_weight, vec_t)
+    other_tokens = plan.swap_plane(tokens)
+    other_cotangent = plan.swap_plane(cotangent)
     blocks = lax.all_to_all(split_out(plan, out_weight, rows), "fsdp", 0, 0)
-    mlp_piece, qkv_piece = pack_in(plan, in_weight, vec_t)
-    xc_own = normalize(tokens, cotangent, image_ids[None, :])
 
     def z_all(piece):
         return [plan.from_z(piece, s) for s in range(1, plan.zs)]
@@ -1022,34 +1002,35 @@
         return [[next(flat) for _ in group] for group in groups]
 
     mlp_z = z_all(mlp_piece)
-    xc_other = plan.swap_plane(xc_own)
     mlp_z, (qkv_piece,) = held([mlp_z, [qkv_piece]])
     mlp_col = stack([mlp_piece] + mlp_z)
     mlp_y = y_all(mlp_col)
-    mlp_core = core_all([mlp_col])
     qkv_z = z_all(qkv_piece)
     out_piece = pack_out(plan, blocks)
-    mlp_y, mlp_core, qkv_z, (out_piece, xc_other) = held(
-        [mlp_y, mlp_core, qkv_z, [out_piece, xc_other]]
-    )
-    mlp_pieces = [mlp_col] + mlp_y + mlp_core + core_all(mlp_y)
+    x_own, x_other, turned, cot_sum = prepare(
+        plan, tokens, other_tokens, cotangent, other_cotangent, rows
+    )
+    mlp_y, qkv_z, (mlp_col, out_piece, x_own) = held(
+        [mlp_y, qkv_z, [mlp_col, out_piece, x_own]]
+    )
+    mlp_pieces = [mlp_col] + mlp_y + core_all([mlp_col] + mlp_y)
     qkv_col = stack([qkv_piece] + qkv_z)
     qkv_y = y_all(qkv_col)
-    qkv_core = core_all([qkv_col])
     out_z = z_all(out_piece)
-    turned, cot_sum = transposes(plan, xc_own, xc_other, rows)
-    mixed, slope, g_own, g_other = mlp_forward(plan, xc_own, xc_other, turned, mlp_pieces)
-    qkv_y, out_z, qkv_core, (mixed, slope, g_own, g_other) = held(
-        [qkv_y, out_z, qkv_core, [mixed, slope, g_own, g_other]]
-    )
-    qkv_pieces = [qkv_col] + qkv_y + qkv_core + core_all(qkv_y)
+    mixed, slope, g_own, g_other = mlp_forward(plan, x_own, x_other, turned, mlp_pieces)
+    qkv_y, out_z, (qkv_col, mixed, slope, g_own, g_other, ids_now) = held(
+        [qkv_y, out_z, [qkv_col, mixed, slope, g_own, g_other, image_ids]]
+    )
+    other_ids = plan.swap_plane(ids_now)
+    qkv_pieces = [qkv_col] + qkv_y + core_all([qkv_col] + qkv_y)
     out_col = stack([out_piece] + out_z)
     out_y = y_all(out_col)
     out_core = core_all([out_col])
-    lane = jnp.arange(PAIR) // HD
+    lane = jnp.arange(2 * PAIR) // HD
     block = jnp.where(lane[:, None] == lane[None, :], 1.0 / HD, 0.0).astype(BF16)
     *saved, att, probs, gains, g_own, g_other = attention_forward(
-        plan, xc_own, xc_other, qkv_pieces, block, turned, g_own, g_other
+        plan, x_own, x_other, qkv_pieces, (image_ids[None, :], other_ids[None, :]), block,
+        turned, g_own, g_other,
     )
     saved = tuple(saved) + (probs,)
     out_y, out_core, (att, g_own, g_other) = held([out_y, out_core, [att, g_own, g_other]])
@@ -1060,18 +1041,18 @@
     s_out.by_y()
     out_pieces = [out_col] + out_y + out_core
     out_mine, out_theirs, d_att, d_inner = output_step(
-        plan, att, mixed, slope, xc_own, xc_other, out_pieces
-    )
-    s_out.y_got, (out_theirs, d_att, d_inner) = held([s_out.y_got, [out_theirs, d_att, d_inner]])
-    s_out.by_z()
+        plan, att, mixed, slope, cotangent, other_cotangent, out_pieces
+    )
     g_own, g_other = mlp_gradient(turned, d_inner)
     s_mlp = Scatter(plan, g_own, g_other)
     s_mlp.by_core()
+    s_out.y_got, (out_theirs, g_own) = held([s_out.y_got, [out_theirs, g_own]])
+    s_out.by_z()
     out_recv = plan.swap_plane(out_theirs)
     s_mlp.recv, d_att = fence(s_mlp.recv, d_att)
     s_mlp.by_y()
-    g_own, g_other, d_qkv, _ = attention_backward(
-        plan, turned, saved, d_att, block, gains, cot_sum, (), 0, PAIRS, rows
+    g_own, g_other, d_qkv = attention_backward(
+        plan, turned, saved, d_att, block, gains, cot_sum, rows
     )
     s_out.z_got, s_mlp.y_got, (g_own, g_other, d_qkv, out_recv) = held(
         [s_out.z_got, s_mlp.y_got, [g_own, g_other, d_qkv, out_recv]]
@@ -1080,26 +1061,29 @@
     s_qkv.by_core()
     out_sum = s_out.total()
     out_swap = plan.swap_plane(out_sum)
-    s_qkv.recv, out_sum = fence(s_qkv.recv, out_sum)
-    s_qkv.by_y()
+    parts, s_mlp.y_got, (out_sum, d_qkv) = held([s_qkv.y_parts(), s_mlp.y_got, [out_sum, d_qkv]])
+    s_qkv.by_y(parts)
     s_mlp.by_z()
+    e_own, e_other = scaled_gradient(plan, d_inner, d_qkv, mlp_pieces, qkv_pieces)
+    out_swap, e_other, e_own = fence(out_swap, e_other, e_own)
+    e_recv = plan.swap_plane(e_other)
     blocks = unpack_out(plan, plan.over_pairs(out_sum), plan.over_pairs(out_swap))
+    s_qkv.y_got, s_mlp.z_got, (blocks,) = held([s_qkv.y_got, s_mlp.z_got, [blocks]])
+    s_qkv.by_z()
+    blocks = lax.all_to_all(blocks, "fsdp", 0, 0)
     result = (
         tokens.astype(F32) + out_mine + out_recv.astype(F32) + gains[3][None, :]
     ).astype(BF16)
-    s_qkv.y_got, (blocks, result, d_qkv) = held([s_qkv.y_got, [blocks, result, d_qkv]])
-    s_qkv.by_z()
-    blocks = lax.all_to_all(blocks, "fsdp", 0, 0)
-    e_own, e_other = scaled_gradient(plan, d_inner, d_qkv, mlp_pieces, qkv_pieces)
-    s_qkv.z_got, s_mlp.z_got, (e_other,) = held([s_qkv.z_got, s_mlp.z_got, [e_other]])
-    qkv_sum, mlp_sum = s_qkv.total(), s_mlp.total()
-    qkv_swap, mlp_swap = plan.swap_plane(qkv_sum), plan.swap_plane(mlp_sum)
+    mlp_sum = s_mlp.total()
+    mlp_swap = plan.swap_plane(mlp_sum)
+    s_qkv.z_got, (result,) = held([s_qkv.z_got, [result]])
+    qkv_sum = s_qkv.total()
+    qkv_swap = plan.swap_plane(qkv_sum)
     out_grad, sq_out = finish_out(blocks)
-    qkv_swap, mlp_swap, out_grad, e_other = fence(qkv_swap, mlp_swap, out_grad, e_other)
-    e_recv = plan.swap_plane(e_other)
     in_grad, sq, dot = finish_mlp(
         plan, plan.over_pairs(mlp_sum), plan.over_pairs(mlp_swap), in_weight, vec_t
     )
+    qkv_swap, in_grad, out_grad = fence(qkv_swap, in_grad, out_grad)
     in_grad, vec_cols, square = finish_qkv(
         plan, plan.over_pairs(qkv_sum), plan.over_pairs(qkv_swap), in_weight, vec_t, in_grad,
         sq, dot, sq_out,
@@ -1121,7 +1105,7 @@
         in_grad,
         out_grad,
         vec_grad,
-        norm[0, 0],
+        norm.reshape(()),
         in_update,
         out_update,
         vec_update,

time: 233 us -> 216 us (0.927)
  waiting for transfers between devices: 42.1 us -> 29 us
  local copies, waits for them, and re-layouts: 13.3 us -> 5.14 us
  starting transfers between devices: 60 us -> 66 us
  Pallas kernels: 103 us -> 99.8 us
    ppermute x21 -> x18, waiting for transfers between devices: 23.8 us -> 10.8 us  [from_z(): return lax.ppermute(a, 'fsdp', pairs)]
    ppermute x7 -> x6, waiting for transfers between devices: 7.65 us -> 0.02 us  [from_y(): return lax.ppermute(a, 'fsdp', pairs)]
    unnamed x86 -> x84, local copies, waits for them, and re-layouts: 11.9 us -> 4.28 us
    ppermute x0 -> x3, waiting for transfers between devices: none -> 5.93 us  [total(): a = a + lax.ppermute(a, 'fsdp', pairs)]
    ppermute x21 -> x18, starting transfers between devices: 32.5 us -> 35.7 us  [from_z(): return lax.ppermute(a, 'fsdp', pairs)]
    ppermute x0 -> x3, starting transfers between devices: none -> 3.13 us  [total(): a = a + lax.ppermute(a, 'fsdp', pairs)]
    pallas_call x7 -> x6, Pallas kernels: 77.3 us -> 74.2 us  [the longest x1 18.1 us: attention_backward(): pl.pallas_call(kernel, grid=(PAIRS,), in_specs=[smem(), pl.BlockSpec((1,...]
    ppermute x6 -> x8, waiting for transfers between devices: 3.96 us -> 7.04 us  [swap_plane(): return lax.ppermute(a, 'dp', [(i, i ^ 1) for i in range(self.n_dp)])]
  transfers between devices with their start and end apart: 46 -> 47, of which waited for: 13 -> 10; matrix products, arithmetic and copies ran while one was open for 6% -> 6% of each run, Pallas kernels for 40% -> 44%
where the time goes in v4:
time: 216 us; the launch traced here: 215 us
  Pallas kernels  99.8 us (46%)
  starting transfers between devices  66 us (31%)
  waiting for transfers between devices  29 us (13%)
  other arithmetic  14.1 us (7%)
  local copies, waits for them, and re-layouts  5.14 us (2%)
    ppermute x18, starting transfers between devices, from_z(): return lax.ppermute(a, 'fsdp', pairs)  35.7 us
    pallas_call x1, Pallas kernels, attention_backward(): pl.pallas_call(kernel, grid=(PAIRS,), in_specs=[smem(), pl.BlockSpec((1,...  18.1 us
    pallas_call x1, Pallas kernels, attention_forward(): pl.pallas_call(kernel, grid=(PAIRS,), in_specs=[smem()] + [whole((tok, D)...  16.4 us
    pallas_call x1, Pallas kernels, output_step(): pl.pallas_call(kernel, grid=(2 * per,), in_specs=[smem(), pl.BlockSpec((1...  13.1 us
    pallas_call x1, Pallas kernels, mlp_forward(): pl.pallas_call(kernel, grid=(FH // tile,), in_specs=[smem()] + [whole((to...  11.5 us
    ppermute x18, waiting for transfers between devices, from_z(): return lax.ppermute(a, 'fsdp', pairs)  10.8 us
    ppermute x8, starting transfers between devices, swap_plane(): return lax.ppermute(a, 'dp', [(i, i ^ 1) for i in range(self.n_dp)])  9.62 us
    pallas_call x1, Pallas kernels, scaled_gradient(): pl.pallas_call(kernel, grid=(2 * per,), in_specs=[smem(), pl.BlockSpec((1...  9.6 us
  transfers between devices with their start and end apart: 47, of which 10 were waited for; matrix products, arithmetic and copies ran while one was open for 6% of the time, Pallas kernels for 44%

profile of v4, /device:TPU:0, one launch (start us, length us, event | category | flops | bytes accessed | tf_op | source)
XLA Modules:
  0.0 215.4 jit_solution(9109983263380519536)
XLA Ops:
  0.6 3.0 %collective-permute-start.8 = (bf16[512,768]{1,0:T(8,128)(2,1)}, bf16[512,768]{1,0:T(8,128)(2,1)S(1)}, u32[]{:S(2)}, u32[]{:S(2)}) collective-permute-start(bf16[512,768]{1,0:T(8,128)(2,1)} %c_ref.1), channel_id=1, source_target_pairs={{0,16},{16,0},{1,17},{17,1},{2,18},{18,2},{3,19},{19,3},{4,20},{20... | collective-permute-start | bytes 2359304 | tf_op jit(solution)/shard_map/ppermute | solution.py:85
  6.5 4.1 %collective-permute-start = (bf16[48,1536]{1,0:T(8,128)(2,1)S(1)}, bf16[48,1536]{1,0:T(8,128)(2,1)S(1)}, u32[]{:S(2)}, u32[]{:S(2)}) collective-permute-start(bf16[48,1536]{1,0:T(8,128)(2,1)S(1)} %get-tuple-element.124.refs_0_), channel_id=1, source_target_pairs={{4,0},{5,1},{6,2},{7,3},{8,4},{9,5},{10,6},{11,7},{12,8},{13,9},{1... | collective-permute-start | bytes 442376 | tf_op jit(solution)/shard_map/ppermute | solution.py:74
  12.5 5.1 %all-to-all-start = ((bf16[16,48,240]{2,1,0:T(8,128)(2,1)}), bf16[16,48,240]{2,1,0:T(8,128)(2,1)S(1)}, u32[]{:S(2)}, u32[]{:S(2)}) async-start(bf16[16,48,240]{2,1,0:T(8,128)(2,1)} %split_out.1), calls=%async_computation | async-start | bytes 786432 | tf_op jit(solution)/shard_map/all_to_all | solution.py:989
  17.7 7.7 %collective-permute-done.1.refs_2_ = bf16[48,1536]{1,0:T(8,128)(2,1)S(1)} collective-permute-done((bf16[48,1536]{1,0:T(8,128)(2,1)S(1)}, bf16[48,1536]{1,0:T(8,128)(2,1)S(1)}, u32[]{:S(2)}, u32[]{:S(2)}) %collective-permute-start.1) | collective-permute-done | bytes 147488 | tf_op jit(solution)/shard_map/ppermute | solution.py:74
  26.5 9.4 %collective-permute-start.5 = (bf16[48,1280]{1,0:T(8,128)(2,1)S(1)}, bf16[48,1280]{1,0:T(8,128)(2,1)S(1)}, u32[]{:S(2)}, u32[]{:S(2)}) collective-permute-start(bf16[48,1280]{1,0:T(8,128)(2,1)S(1)} %get-tuple-element.129.refs_0_), channel_id=1, source_target_pairs={{8,0},{9,1},{10,2},{11,3},{12,4},{13,5},{14,6},{15,7},{0,8},{1,9},... | collective-permute-start | bytes 368648 | tf_op jit(solution)/shard_map/ppermute | solution.py:74
  36.0 2.0 collective-permute-start.6
  38.8 5.5 %prepare.1 = (bf16[512,768]{1,0:T(8,128)(2,1)}, bf16[512,768]{1,0:T(8,128)(2,1)}, bf16[2,768,1024]{2,1,0:T(8,128)(2,1)}, f32[8,768]{1,0:T(8,128)}) custom-call(s32[4]{0:T(128)} %copy-done.15, bf16[512,768]{1,0:T(8,128)(2,1)} %t_ref.1, bf16[512,768]{1,0:T(8,128)(2,1)} %collective-permute-done.7.tp_ref, bf16[512,768]{1,0:T(8,128)(2,1)} %c_ref.1, ...), custom_call_target="tpu_custom_call" | custom-call | flops 15728640 | bytes 7864320 | tf_op jit(solution)/shard_map/prepare/pallas_call | solution.py:465
  46.4 3.6 %collective-permute-start.10 = (bf16[48,1920]{1,0:T(8,128)(2,1)S(1)}, bf16[48,1920]{1,0:T(8,128)(2,1)S(1)}, u32[]{:S(2)}, u32[]{:S(2)}) collective-permute-start(bf16[48,1920]{1,0:T(8,128)(2,1)S(1)} %pack_out.1.refs_0_), channel_id=1, source_target_pairs={{4,0},{5,1},{6,2},{7,3},{8,4},{9,5},{10,6},{11,7},{12,8},{13,9},{1... | collective-permute-start | bytes 552968 | tf_op jit(solution)/shard_map/ppermute | solution.py:74
  51.8 11.5 %mlp_forward.1 = (bf16[2,512,1536]{2,1,0:T(8,128)(2,1)}, bf16[2,512,1536]{2,1,0:T(8,128)(2,1)}, bf16[384,1920]{1,0:T(8,128)(2,1)}, bf16[384,1920]{1,0:T(8,128)(2,1)}) custom-call(s32[4]{0:T(128)} %copy-done.15, bf16[512,768]{1,0:T(8,128)(2,1)} %get-tuple-element.135.xo_ref, bf16[512,768]{1,0:T(8,128)(2,1)} %get-tuple-element.136.xp_ref, ...), custom_call_target="tpu_custom_call" | custom-call | flops 4831838208 | bytes 9437184 | tf_op jit(solution)/shard_map/mlp_forward/pallas_call | solution.py:510
  63.3 2.2 %collective-permute-done.11.refs_2_ = bf16[48,1920]{1,0:T(8,128)(2,1)S(1)} collective-permute-done((bf16[48,1920]{1,0:T(8,128)(2,1)S(1)}, bf16[48,1920]{1,0:T(8,128)(2,1)S(1)}, u32[]{:S(2)}, u32[]{:S(2)}) %collective-permute-start.11) | collective-permute-done | bytes 184352 | tf_op jit(solution)/shard_map/ppermute | solution.py:74
  71.4 16.4 %attention_forward.1 = (bf16[2,512,768]{2,1,0:T(8,128)(2,1)}, bf16[2,512,384]{2,1,0:T(8,128)(2,1)}, bf16[2,512,768]{2,1,0:T(8,128)(2,1)}, bf16[2,512,768]{2,1,0:...) custom-call(s32[4]{0:T(128)} %copy-done.15, ...), custom_call_target="tpu_custom_call", output_to_operand_aliasing={{7}: (7, {}), {8}: (8, {})} | custom-call | flops 1811939328 | bytes 20971520 | tf_op jit(solution)/shard_map/attention_forward/pallas_call | solution.py:598
  88.4 3.5 %collective-permute-done.21.rest_3_ = bf16[192,1920]{1,0:T(8,128)(2,1)S(1)} collective-permute-done((bf16[192,1920]{1,0:T(8,128)(2,1)S(1)}, bf16[192,1920]{1,0:T(8,128)(2,1)S(1)}, u32[]{:S(2)}, u32[]{:S(2)}) %collective-permute-start.21) | collective-permute-done | bytes 737312 | tf_op jit(solution)/shard_map/ppermute | solution.py:82
  92.5 1.9 add_convert_fusion.1
  95.9 13.1 %output_step.1 = (f32[512,768]{1,0:T(8,128)}, bf16[512,768]{1,0:T(8,128)(2,1)}, bf16[2,512,384]{2,1,0:T(8,128)(2,1)}, bf16[2,512,1536]{2,1,0:T(8,128)(2,1)}) custom-call(s32[4]{0:T(128)} %copy-done.15, bf16[2,512,384]{2,1,0:T(8,128)(2,1)} %get-tuple-element.160.att_ref, bf16[2,512,1536]{2,1,0:T(8,128)(2,1)} %get-tuple-element.161.mix_ref, ...), custom_call_target="tpu_custom_call" | custom-call | flops 6039797760 | bytes 20971520 | tf_op jit(solution)/shard_map/output_step/pallas_call | solution.py:683
  109.0 6.1 %mlp_gradient.1 = (bf16[384,1536]{1,0:T(8,128)(2,1)}, bf16[384,1536]{1,0:T(8,128)(2,1)}) custom-call(bf16[2,768,1024]{2,1,0:T(8,128)(2,1)} %get-tuple-element.137.ct_ref.xt_ref, bf16[2,512,1536]{2,1,0:T(8,128)(2,1)} %get-tuple-element.166.d_ref.dm_ref), custom_call_target="tpu_custom_call" | custom-call | flops 2415919104 | bytes 8388608 | tf_op jit(solution)/shard_map/mlp_gradient/pallas_call | solution.py:725
  118.5 1.9 collective-permute-start.24
  120.4 2.9 %collective-permute-start.25 = (bf16[48,1920]{1,0:T(8,128)(2,1)}, bf16[48,1920]{1,0:T(8,128)(2,1)}, u32[]{:S(2)}, u32[]{:S(2)}) collective-permute-start(bf16[48,1920]{1,0:T(8,128)(2,1)} %get-tuple-element.233), channel_id=1, source_target_pairs={{4,0},{5,1},{6,2},{7,3},{8,4},{9,5},{10,6},{11,7},{12,8},{13,9},{1... | collective-permute-start | bytes 552968 | tf_op jit(solution)/shard_map/ppermute | solution.py:74
  124.4 18.1 %attention_backward.1 = (bf16[384,1280]{1,0:T(8,128)(2,1)}, bf16[384,1280]{1,0:T(8,128)(2,1)}, bf16[2,512,1152]{2,1,0:T(8,128)(2,1)}) custom-call(s32[4]{0:T(128)} %copy-done.15, bf16[2,768,1024]{2,1,0:T(8,128)(2,1)} %get-tuple-element.137.ct_ref.xt_ref, bf16[2,512,768]{2,1,0:T(8,128)(2,1)} %get-tuple-element.172.qk_ref, ...), custom_call_target="tpu_custom_call" | custom-call | flops 7247757312 | bytes 25165824 | tf_op jit(solution)/shard_map/attention_backward/pallas_call | solution.py:858
  146.1 2.5 %add_convert_fusion = bf16[512,768]{1,0:T(8,128)(2,1)} fusion(bf16[512,768]{1,0:T(8,128)(2,1)} %collective-permute-done.28, f32[512,768]{1,0:T(8,128)S(1)} %copy-done.24, bf16[512,768]{1,0:T(8,128)(2,1)S(1)} %copy-done.2, f32[768]{0:T(1024)S(1)} %slice_reduce_fusion), kind=kLoop, calls=%fused_computation | loop fusion | flops 2359296 | bytes 3935232 | tf_op jit(solution)/shard_map/convert_element_type | solution.py:1076
  152.7 3.2 %collective-permute-start.33 = (bf16[48,1536]{1,0:T(8,128)(2,1)S(1)}, bf16[48,1536]{1,0:T(8,128)(2,1)}, u32[]{:S(2)}, u32[]{:S(2)}) collective-permute-start(bf16[48,1536]{1,0:T(8,128)(2,1)S(1)} %get-tuple-element.236), channel_id=1, source_target_pairs={{4,0},{5,1},{6,2},{7,3},{8,4},{9,5},{10,6},{11,7},{12,8},{13,9},{1... | collective-permute-start | bytes 442376 | tf_op jit(solution)/shard_map/ppermute | solution.py:74
  156.0 9.6 %scaled_gradient.1 = (f32[512,768]{1,0:T(8,128)}, bf16[512,768]{1,0:T(8,128)(2,1)}) custom-call(s32[4]{0:T(128)} %copy-done.15, bf16[2,512,1536]{2,1,0:T(8,128)(2,1)} %get-tuple-element.166.d_ref.dm_ref, bf16[2,512,1152]{2,1,0:T(8,128)(2,1)} %get-tuple-element.194.dq_ref, bf16[192,1536]{1,0:T(8,128)(2,1)} %copy-done.14, ...), custom_call_target="tpu_custom_call" | custom-call | flops 4227858432 | bytes 16777216 | tf_op jit(solution)/shard_map/scaled_gradient/pallas_call | solution.py:767
  171.7 2.9 %collective-permute-start.37 = (bf16[48,1280]{1,0:T(8,128)(2,1)}, bf16[48,1280]{1,0:T(8,128)(2,1)}, u32[]{:S(2)}, u32[]{:S(2)}) collective-permute-start(bf16[48,1280]{1,0:T(8,128)(2,1)} %get-tuple-element.239), channel_id=1, source_target_pairs={{4,0},{5,1},{6,2},{7,3},{8,4},{9,5},{10,6},{11,7},{12,8},{13,9},{1... | collective-permute-start | bytes 368648 | tf_op jit(solution)/shard_map/ppermute | solution.py:74
  174.6 4.2 %all-to-all-start.1 = ((bf16[16,48,240]{2,1,0:T(8,128)(2,1)}), bf16[16,48,240]{2,1,0:T(8,128)(2,1)}, u32[]{:S(2)}, u32[]{:S(2)}) async-start(bf16[16,48,240]{2,1,0:T(8,128)(2,1)} %unpack_out.1), calls=%async_computation.1 | async-start | bytes 786432 | tf_op jit(solution)/shard_map/all_to_all | solution.py:1073
  183.5 5.7 %collective-permute-done.40.swap_ref = bf16[48,1536]{1,0:T(8,128)(2,1)S(1)} collective-permute-done((bf16[48,1536]{1,0:T(8,128)(2,1)S(1)}, bf16[48,1536]{1,0:T(8,128)(2,1)S(1)}, u32[]{:S(2)}, u32[]{:S(2)}) %collective-permute-start.40) | collective-permute-done | bytes 147488 | tf_op jit(solution)/shard_map/ppermute | solution.py:85
  189.2 2.2 %finish_mlp.1 = (f32[48,5376]{1,0:T(8,128)}, f32[48,128]{1,0:T(8,128)S(1)}, f32[48,128]{1,0:T(8,128)S(1)}) custom-call(s32[4]{0:T(128)S(1)} %copy-done.16, bf16[48,1536]{1,0:T(8,128)(2,1)S(1)} %add_convert_fusion.8.own_ref, bf16[48,1536]{1,0:T(8,128)(2,1)S(1)} %collective-permute-done.40.swap_ref, f32[48,5376]{1,0:T(8,128)S(1)} %copy-done.1, ...), custom_call_target="tpu_custom_call" | custom-call | flops 1179648 | bytes 1769472 | tf_op jit(solution)/shard_map/finish_mlp/pallas_call | solution.py:366
  191.4 2.2 %finish_out.1 = (f32[240,768]{1,0:T(8,128)}, f32[8,128]{1,0:T(8,128)S(1)}) custom-call(bf16[16,48,240]{2,1,0:T(8,128)(2,1)} %all-to-all-done.1.in_ref), custom_call_target="tpu_custom_call" | custom-call | flops 737280 | bytes 1105920 | tf_op jit(solution)/shard_map/finish_out/pallas_call | solution.py:330
  193.6 2.5 %finish_qkv.1 = (f32[48,5376]{1,0:T(8,128)}, f32[48,128]{1,0:T(8,128)S(1)}, f32[8,128]{1,0:T(8,128)S(1)}) custom-call(s32[4]{0:T(128)S(1)} %copy-done.16, bf16[48,1280]{1,0:T(8,128)(2,1)S(1)} %add_convert_fusion.12.own_ref, bf16[48,1280]{1,0:T(8,128)(2,1)} %collective-permute-done.39.swap_ref, ...), custom_call_target="tpu_custom_call", output_to_operand_aliasing={{0}: (5, {})} | custom-call | flops 884736 | bytes 1327104 | tf_op jit(solution)/shard_map/finish_qkv/pallas_call | solution.py:417
  198.1 2.8 %collective-permute-done.42 = f32[8,128]{1,0:T(8,128)S(1)} collective-permute-done((f32[8,128]{1,0:T(8,128)S(1)}, f32[8,128]{1,0:T(8,128)S(1)}, u32[]{:S(2)}, u32[]{:S(2)}) %collective-permute-start.42) | collective-permute-done | bytes 4128 | tf_op jit(solution)/shard_map/ppermute | solution.py:99
  201.4 3.1 %collective-permute-done.43 = f32[8,128]{1,0:T(8,128)S(1)} collective-permute-done((f32[8,128]{1,0:T(8,128)S(1)}, f32[8,128]{1,0:T(8,128)S(1)}, u32[]{:S(2)}, u32[]{:S(2)}) %collective-permute-start.43) | collective-permute-done | bytes 4128 | tf_op jit(solution)/shard_map/ppermute | solution.py:99
  204.6 1.8 collective-permute-start.44
  206.5 4.1 %token_gradient.1 = f32[512,768]{1,0:T(8,128)} custom-call(bf16[512,768]{1,0:T(8,128)(2,1)S(1)} %copy-done.2, bf16[512,768]{1,0:T(8,128)(2,1)S(1)} %copy-done.5, f32[512,768]{1,0:T(8,128)S(1)} %copy-done.7, bf16[512,768]{1,0:T(8,128)(2,1)} %collective-permute-done.38.recv_ref), custom_call_target="tpu_custom_call" | custom-call | flops 7864320 | bytes 5505024 | tf_op jit(solution)/shard_map/token_gradient/pallas_call | solution.py:895
  210.6 4.6 %optimize.1 = (f32[4,48]{1,0:T(4,128)}, f32[1,1]{1,0:T(1,128)}, f32[48,5376]{1,0:T(8,128)}, f32[48,5376]{1,0:T(8,128)}, f32[48,5376]{1,0:T(8,128)}, /*index=5*/f...) custom-call(f32[8,128]{1,0:T(8,128)S(1)} %add.206.total_ref, ...), custom_call_target="tpu_custom_call" | custom-call | flops 5160960 | bytes 13418496 | tf_op jit(solution)/shard_map/optimize/pallas_call | solution.py:945
  (186 shorter events, 44.5 us)
Async XLA Ops:
  0.6 35.3 %collective-permute-start.8 = (bf16[512,768]{1,0:T(8,128)(2,1)}, bf16[512,768]{1,0:T(8,128)(2,1)S(1)}, u32[]{:S(2)}, u32[]{:S(2)}) collective-permute-start(bf16[512,768]{1,0:T(8,128)(2,1)} %c_ref.1), channel_id=1, source_target_pairs={{0,16},{16,0},{1,17},{17,1},{2,18},{18,2},{3,19},{19,3},{4,20},{20... | collective-permute-start | bytes 2359304 | tf_op jit(solution)/shard_map/ppermute | solution.py:85
  3.6 35.1 %collective-permute-start.7 = (bf16[512,768]{1,0:T(8,128)(2,1)}, bf16[512,768]{1,0:T(8,128)(2,1)}, u32[]{:S(2)}, u32[]{:S(2)}) collective-permute-start(bf16[512,768]{1,0:T(8,128)(2,1)} %t_ref.1), channel_id=1, source_target_pairs={{0,16},{16,0},{1,17},{17,1},{2,18},{18,2},{3,19},{19,3},{4,20},{20... | collective-permute-start | bytes 2359304 | tf_op jit(solution)/shard_map/ppermute | solution.py:85
  6.5 11.2 %collective-permute-start = (bf16[48,1536]{1,0:T(8,128)(2,1)S(1)}, bf16[48,1536]{1,0:T(8,128)(2,1)S(1)}, u32[]{:S(2)}, u32[]{:S(2)}) collective-permute-start(bf16[48,1536]{1,0:T(8,128)(2,1)S(1)} %get-tuple-element.124.refs_0_), channel_id=1, source_target_pairs={{4,0},{5,1},{6,2},{7,3},{8,4},{9,5},{10,6},{11,7},{12,8},{13,9},{1... | collective-permute-start | bytes 442376 | tf_op jit(solution)/shard_map/ppermute | solution.py:74
  10.6 14.8 %collective-permute-start.1 = (bf16[48,1536]{1,0:T(8,128)(2,1)S(1)}, bf16[48,1536]{1,0:T(8,128)(2,1)S(1)}, u32[]{:S(2)}, u32[]{:S(2)}) collective-permute-start(bf16[48,1536]{1,0:T(8,128)(2,1)S(1)} %get-tuple-element.124.refs_0_), channel_id=1, source_target_pairs={{8,0},{9,1},{10,2},{11,3},{12,4},{13,5},{14,6},{15,7},{0,8},{1,9},... | collective-permute-start | bytes 442376 | tf_op jit(solution)/shard_map/ppermute | solution.py:74
  10.6 14.8 %collective-permute-start.2 = (bf16[48,1536]{1,0:T(8,128)(2,1)S(1)}, bf16[48,1536]{1,0:T(8,128)(2,1)S(1)}, u32[]{:S(2)}, u32[]{:S(2)}) collective-permute-start(bf16[48,1536]{1,0:T(8,128)(2,1)S(1)} %get-tuple-element.124.refs_0_), channel_id=1, source_target_pairs={{12,0},{13,1},{14,2},{15,3},{0,4},{1,5},{2,6},{3,7},{4,8},{5,9},{6... | collective-permute-start | bytes 442376 | tf_op jit(solution)/shard_map/ppermute | solution.py:74
  12.5 25.5 %all-to-all-start = ((bf16[16,48,240]{2,1,0:T(8,128)(2,1)}), bf16[16,48,240]{2,1,0:T(8,128)(2,1)S(1)}, u32[]{:S(2)}, u32[]{:S(2)}) async-start(bf16[16,48,240]{2,1,0:T(8,128)(2,1)} %split_out.1), calls=%async_computation | async-start | bytes 786432 | tf_op jit(solution)/shard_map/all_to_all | solution.py:989
  25.4 18.9 %collective-permute-start.3 = (bf16[192,1536]{1,0:T(8,128)(2,1)S(1)}, bf16[192,1536]{1,0:T(8,128)(2,1)}, u32[]{:S(2)}, u32[]{:S(2)}) collective-permute-start(bf16[192,1536]{1,0:T(8,128)(2,1)S(1)} %stack.23.rest_0_), channel_id=1, source_target_pairs={{2,0},{3,1},{0,2},{1,3},{6,4},{7,5},{4,6},{5,7},{10,8},{11,9},{8,1... | collective-permute-start | bytes 1769480 | tf_op jit(solution)/shard_map/ppermute | solution.py:78
  26.5 17.7 %collective-permute-start.4 = (bf16[48,1280]{1,0:T(8,128)(2,1)S(1)}, bf16[48,1280]{1,0:T(8,128)(2,1)S(1)}, u32[]{:S(2)}, u32[]{:S(2)}) collective-permute-start(bf16[48,1280]{1,0:T(8,128)(2,1)S(1)} %get-tuple-element.129.refs_0_), channel_id=1, source_target_pairs={{4,0},{5,1},{6,2},{7,3},{8,4},{9,5},{10,6},{11,7},{12,8},{13,9},{1... | collective-permute-start | bytes 368648 | tf_op jit(solution)/shard_map/ppermute | solution.py:74
  26.5 17.7 %collective-permute-start.5 = (bf16[48,1280]{1,0:T(8,128)(2,1)S(1)}, bf16[48,1280]{1,0:T(8,128)(2,1)S(1)}, u32[]{:S(2)}, u32[]{:S(2)}) collective-permute-start(bf16[48,1280]{1,0:T(8,128)(2,1)S(1)} %get-tuple-element.129.refs_0_), channel_id=1, source_target_pairs={{8,0},{9,1},{10,2},{11,3},{12,4},{13,5},{14,6},{15,7},{0,8},{1,9},... | collective-permute-start | bytes 368648 | tf_op jit(solution)/shard_map/ppermute | solution.py:74
  44.9 20.6 %collective-permute-start.9 = (bf16[192,1280]{1,0:T(8,128)(2,1)S(1)}, bf16[192,1280]{1,0:T(8,128)(2,1)S(1)}, u32[]{:S(2)}, u32[]{:S(2)}) collective-permute-start(bf16[192,1280]{1,0:T(8,128)(2,1)S(1)} %stack.24.rest_0_.rest_4_), channel_id=1, source_target_pairs={{2,0},{3,1},{0,2},{1,3},{6,4},{7,5},{4,6},{5,7},{10,8},{11,9},{8,1... | collective-permute-start | bytes 1474568 | tf_op jit(solution)/shard_map/ppermute | solution.py:78
  46.4 17.0 %collective-permute-start.10 = (bf16[48,1920]{1,0:T(8,128)(2,1)S(1)}, bf16[48,1920]{1,0:T(8,128)(2,1)S(1)}, u32[]{:S(2)}, u32[]{:S(2)}) collective-permute-start(bf16[48,1920]{1,0:T(8,128)(2,1)S(1)} %pack_out.1.refs_0_), channel_id=1, source_target_pairs={{4,0},{5,1},{6,2},{7,3},{8,4},{9,5},{10,6},{11,7},{12,8},{13,9},{1... | collective-permute-start | bytes 552968 | tf_op jit(solution)/shard_map/ppermute | solution.py:74
  50.0 15.6 %collective-permute-start.11 = (bf16[48,1920]{1,0:T(8,128)(2,1)S(1)}, bf16[48,1920]{1,0:T(8,128)(2,1)S(1)}, u32[]{:S(2)}, u32[]{:S(2)}) collective-permute-start(bf16[48,1920]{1,0:T(8,128)(2,1)S(1)} %pack_out.1.refs_0_), channel_id=1, source_target_pairs={{8,0},{9,1},{10,2},{11,3},{12,4},{13,5},{14,6},{15,7},{0,8},{1,9},... | collective-permute-start | bytes 552968 | tf_op jit(solution)/shard_map/ppermute | solution.py:74
  50.0 15.6 %collective-permute-start.12 = (bf16[48,1920]{1,0:T(8,128)(2,1)S(1)}, bf16[48,1920]{1,0:T(8,128)(2,1)S(1)}, u32[]{:S(2)}, u32[]{:S(2)}) collective-permute-start(bf16[48,1920]{1,0:T(8,128)(2,1)S(1)} %pack_out.1.refs_0_), channel_id=1, source_target_pairs={{12,0},{13,1},{14,2},{15,3},{0,4},{1,5},{2,6},{3,7},{4,8},{5,9},{6... | collective-permute-start | bytes 552968 | tf_op jit(solution)/shard_map/ppermute | solution.py:74
  65.7 22.1 %collective-permute-start.15 = (bf16[192,1920]{1,0:T(8,128)(2,1)S(1)}, bf16[192,1920]{1,0:T(8,128)(2,1)S(1)}, u32[]{:S(2)}, u32[]{:S(2)}) collective-permute-start(bf16[192,1920]{1,0:T(8,128)(2,1)S(1)} %stack.25.rest_0_), channel_id=1, source_target_pairs={{2,0},{3,1},{0,2},{1,3},{6,4},{7,5},{4,6},{5,7},{10,8},{11,9},{8,1... | collective-permute-start | bytes 2211848 | tf_op jit(solution)/shard_map/ppermute | solution.py:78
  66.2 21.6 %collective-permute-start.16 = (bf16[192,1920]{1,0:T(8,128)(2,1)S(1)}, bf16[192,1920]{1,0:T(8,128)(2,1)S(1)}, u32[]{:S(2)}, u32[]{:S(2)}) collective-permute-start(bf16[192,1920]{1,0:T(8,128)(2,1)S(1)} %stack.25.rest_0_), channel_id=1, source_target_pairs={{0,1},{1,0},{2,3},{3,2},{4,5},{5,4},{6,7},{7,6},{8,9},{9,8},{10,11... | collective-permute-start | bytes 2211848 | tf_op jit(solution)/shard_map/ppermute | solution.py:82
  94.3 20.7 %collective-permute-start.22 = (bf16[192,1920]{1,0:T(8,128)(2,1)S(1)}, bf16[192,1920]{1,0:T(8,128)(2,1)S(1)}, u32[]{:S(2)}, u32[]{:S(2)}) collective-permute-start(bf16[192,1920]{1,0:T(8,128)(2,1)S(1)} %add_convert_fusion.1), channel_id=1, source_target_pairs={{2,0},{3,1},{0,2},{1,3},{6,4},{7,5},{4,6},{5,7},{10,8},{11,9},{8,1... | collective-permute-start | bytes 2211848 | tf_op jit(solution)/shard_map/ppermute | solution.py:78
  115.1 27.4 %collective-permute-start.28 = (bf16[512,768]{1,0:T(8,128)(2,1)}, bf16[512,768]{1,0:T(8,128)(2,1)}, u32[]{:S(2)}, u32[]{:S(2)}) collective-permute-start(bf16[512,768]{1,0:T(8,128)(2,1)} %get-tuple-element.183), channel_id=1, source_target_pairs={{0,16},{16,0},{1,17},{17,1},{2,18},{18,2},{3,19},{19,3},{4,20},{20... | collective-permute-start | bytes 2359304 | tf_op jit(solution)/shard_map/ppermute | solution.py:85
  117.6 24.9 %collective-permute-start.23 = (bf16[48,1920]{1,0:T(8,128)(2,1)}, bf16[48,1920]{1,0:T(8,128)(2,1)}, u32[]{:S(2)}, u32[]{:S(2)}) collective-permute-start(bf16[48,1920]{1,0:T(8,128)(2,1)} %get-tuple-element.235), channel_id=1, source_target_pairs={{12,0},{13,1},{14,2},{15,3},{0,4},{1,5},{2,6},{3,7},{4,8},{5,9},{6... | collective-permute-start | bytes 552968 | tf_op jit(solution)/shard_map/ppermute | solution.py:74
  118.5 24.0 %collective-permute-start.24 = (bf16[48,1920]{1,0:T(8,128)(2,1)}, bf16[48,1920]{1,0:T(8,128)(2,1)}, u32[]{:S(2)}, u32[]{:S(2)}) collective-permute-start(bf16[48,1920]{1,0:T(8,128)(2,1)} %get-tuple-element.234), channel_id=1, source_target_pairs={{8,0},{9,1},{10,2},{11,3},{12,4},{13,5},{14,6},{15,7},{0,8},{1,9},... | collective-permute-start | bytes 552968 | tf_op jit(solution)/shard_map/ppermute | solution.py:74
  120.4 22.1 %collective-permute-start.25 = (bf16[48,1920]{1,0:T(8,128)(2,1)}, bf16[48,1920]{1,0:T(8,128)(2,1)}, u32[]{:S(2)}, u32[]{:S(2)}) collective-permute-start(bf16[48,1920]{1,0:T(8,128)(2,1)} %get-tuple-element.233), channel_id=1, source_target_pairs={{4,0},{5,1},{6,2},{7,3},{8,4},{9,5},{10,6},{11,7},{12,8},{13,9},{1... | collective-permute-start | bytes 552968 | tf_op jit(solution)/shard_map/ppermute | solution.py:74
  123.5 19.0 %collective-permute-start.27 = (bf16[192,1536]{1,0:T(8,128)(2,1)S(1)}, bf16[192,1536]{1,0:T(8,128)(2,1)S(1)}, u32[]{:S(2)}, u32[]{:S(2)}) collective-permute-start(bf16[192,1536]{1,0:T(8,128)(2,1)S(1)} %add_convert_fusion.2), channel_id=1, source_target_pairs={{2,0},{3,1},{0,2},{1,3},{6,4},{7,5},{4,6},{5,7},{10,8},{11,9},{8,1... | collective-permute-start | bytes 1769480 | tf_op jit(solution)/shard_map/ppermute | solution.py:78
  145.5 20.1 %collective-permute-start.34 = (bf16[48,1920]{1,0:T(8,128)(2,1)S(1)}, bf16[48,1920]{1,0:T(8,128)(2,1)S(1)}, u32[]{:S(2)}, u32[]{:S(2)}) collective-permute-start(bf16[48,1920]{1,0:T(8,128)(2,1)S(1)} %add_convert_fusion.4.own_ref), channel_id=1, source_target_pairs={{0,16},{16,0},{1,17},{17,1},{2,18},{18,2},{3,19},{19,3},{4,20},{20... | collective-permute-start | bytes 552968 | tf_op jit(solution)/shard_map/ppermute | solution.py:85
  149.5 19.2 %collective-permute-start.30 = (bf16[192,1280]{1,0:T(8,128)(2,1)}, bf16[192,1280]{1,0:T(8,128)(2,1)S(1)}, u32[]{:S(2)}, u32[]{:S(2)}) collective-permute-start(bf16[192,1280]{1,0:T(8,128)(2,1)} %add_convert_fusion.3), channel_id=1, source_target_pairs={{2,0},{3,1},{0,2},{1,3},{6,4},{7,5},{4,6},{5,7},{10,8},{11,9},{8,1... | collective-permute-start | bytes 1474568 | tf_op jit(solution)/shard_map/ppermute | solution.py:78
  152.1 16.6 %collective-permute-start.31 = (bf16[48,1536]{1,0:T(8,128)(2,1)S(1)}, bf16[48,1536]{1,0:T(8,128)(2,1)S(1)}, u32[]{:S(2)}, u32[]{:S(2)}) collective-permute-start(bf16[48,1536]{1,0:T(8,128)(2,1)S(1)} %get-tuple-element.238), channel_id=1, source_target_pairs={{12,0},{13,1},{14,2},{15,3},{0,4},{1,5},{2,6},{3,7},{4,8},{5,9},{6... | collective-permute-start | bytes 442376 | tf_op jit(solution)/shard_map/ppermute | solution.py:74
  152.2 16.5 %collective-permute-start.32 = (bf16[48,1536]{1,0:T(8,128)(2,1)S(1)}, bf16[48,1536]{1,0:T(8,128)(2,1)}, u32[]{:S(2)}, u32[]{:S(2)}) collective-permute-start(bf16[48,1536]{1,0:T(8,128)(2,1)S(1)} %get-tuple-element.237), channel_id=1, source_target_pairs={{8,0},{9,1},{10,2},{11,3},{12,4},{13,5},{14,6},{15,7},{0,8},{1,9},... | collective-permute-start | bytes 442376 | tf_op jit(solution)/shard_map/ppermute | solution.py:74
  152.7 16.0 %collective-permute-start.33 = (bf16[48,1536]{1,0:T(8,128)(2,1)S(1)}, bf16[48,1536]{1,0:T(8,128)(2,1)}, u32[]{:S(2)}, u32[]{:S(2)}) collective-permute-start(bf16[48,1536]{1,0:T(8,128)(2,1)S(1)} %get-tuple-element.236), channel_id=1, source_target_pairs={{4,0},{5,1},{6,2},{7,3},{8,4},{9,5},{10,6},{11,7},{12,8},{13,9},{1... | collective-permute-start | bytes 442376 | tf_op jit(solution)/shard_map/ppermute | solution.py:74
  165.6 40.9 %collective-permute-start.38 = (bf16[512,768]{1,0:T(8,128)(2,1)}, bf16[512,768]{1,0:T(8,128)(2,1)}, u32[]{:S(2)}, u32[]{:S(2)}) collective-permute-start(bf16[512,768]{1,0:T(8,128)(2,1)} %get-tuple-element.203), channel_id=1, source_target_pairs={{0,16},{16,0},{1,17},{17,1},{2,18},{18,2},{3,19},{19,3},{4,20},{20... | collective-permute-start | bytes 2359304 | tf_op jit(solution)/shard_map/ppermute | solution.py:85
  169.6 11.0 %collective-permute-start.35 = (bf16[48,1280]{1,0:T(8,128)(2,1)}, bf16[48,1280]{1,0:T(8,128)(2,1)}, u32[]{:S(2)}, u32[]{:S(2)}) collective-permute-start(bf16[48,1280]{1,0:T(8,128)(2,1)} %get-tuple-element.241), channel_id=1, source_target_pairs={{12,0},{13,1},{14,2},{15,3},{0,4},{1,5},{2,6},{3,7},{4,8},{5,9},{6... | collective-permute-start | bytes 368648 | tf_op jit(solution)/shard_map/ppermute | solution.py:74
  170.2 11.3 %collective-permute-start.36 = (bf16[48,1280]{1,0:T(8,128)(2,1)}, bf16[48,1280]{1,0:T(8,128)(2,1)}, u32[]{:S(2)}, u32[]{:S(2)}) collective-permute-start(bf16[48,1280]{1,0:T(8,128)(2,1)} %get-tuple-element.240), channel_id=1, source_target_pairs={{8,0},{9,1},{10,2},{11,3},{12,4},{13,5},{14,6},{15,7},{0,8},{1,9},... | collective-permute-start | bytes 368648 | tf_op jit(solution)/shard_map/ppermute | solution.py:74
  171.7 9.8 %collective-permute-start.37 = (bf16[48,1280]{1,0:T(8,128)(2,1)}, bf16[48,1280]{1,0:T(8,128)(2,1)}, u32[]{:S(2)}, u32[]{:S(2)}) collective-permute-start(bf16[48,1280]{1,0:T(8,128)(2,1)} %get-tuple-element.239), channel_id=1, source_target_pairs={{4,0},{5,1},{6,2},{7,3},{8,4},{9,5},{10,6},{11,7},{12,8},{13,9},{1... | collective-permute-start | bytes 368648 | tf_op jit(solution)/shard_map/ppermute | solution.py:74
  174.6 16.9 %all-to-all-start.1 = ((bf16[16,48,240]{2,1,0:T(8,128)(2,1)}), bf16[16,48,240]{2,1,0:T(8,128)(2,1)}, u32[]{:S(2)}, u32[]{:S(2)}) async-start(bf16[16,48,240]{2,1,0:T(8,128)(2,1)} %unpack_out.1), calls=%async_computation.1 | async-start | bytes 786432 | tf_op jit(solution)/shard_map/all_to_all | solution.py:1073
  182.8 10.8 %collective-permute-start.39 = (bf16[48,1280]{1,0:T(8,128)(2,1)S(1)}, bf16[48,1280]{1,0:T(8,128)(2,1)}, u32[]{:S(2)}, u32[]{:S(2)}) collective-permute-start(bf16[48,1280]{1,0:T(8,128)(2,1)S(1)} %add_convert_fusion.12.own_ref), channel_id=1, source_target_pairs={{0,16},{16,0},{1,17},{17,1},{2,18},{18,2},{3,19},{19,3},{4,20},{20... | collective-permute-start | bytes 368648 | tf_op jit(solution)/shard_map/ppermute | solution.py:85
  (57 other events, 430.2 us)

commit v5 on v4

--- a/solution.py
+++ b/solution.py
@@ -90,15 +90,20 @@
         groups = [list(range(p, self.n_dp, 2)) for p in range(2)]
         return lax.psum(a.astype(F32), "dp", axis_index_groups=groups)
 
-    def total(self, a):
+    def total(self, a, *beside):
         a = a + self.swap_core(a)
+        beside = list(beside)
+        count = 0
         for step, size in ((2, self.ys), (2 * self.ys, self.zs)):
             m = 1
             while m < size:
                 pairs = [(i, i ^ (m * step)) for i in range(self.n)]
-                a = a + lax.ppermute(a, "fsdp", pairs)
-                m *= 2
-        return a
+                got = lax.ppermute(a, "fsdp", pairs)
+                if count < len(beside):
+                    got, beside[count] = fence(got, beside[count])
+                a = a + got
+                m, count = 2 * m, count + 1
+        return [a] + beside
 
     def row(self, pos_ref, piece, rows):
         c, t, s = piece
@@ -317,78 +322,119 @@
     return total
 
 
+def partial_sums(plan, mlp, qkv, out, in_weight, vec_t):
+    rows = in_weight.shape[0]
+
+    def kernel(pos_ref, mlp_ref, qkv_ref, out_ref, w_ref, vec_ref, block_ref):
+        plane = pos_ref[3]
+        gain = vec_ref[:, :1]
+        square = jnp.zeros((rows, PAIR), F32)
+        dot = jnp.zeros((rows, PAIR), F32)
+
+        def add(square, dot, hat, source, width):
+            at = pl.ds(pl.multiple_of(source, PAIR), width)
+            low = w_ref[:, at].astype(BF16).astype(F32)
+            grad = hat * gain
+            return square + fold(grad * grad), dot + fold(low * hat)
+
+        hat = mlp_ref[:, :FH].astype(F32)
+        square, dot = add(square, dot, hat, 3 * D + plane * FH, FH)
+        for pair in range(PAIRS):
+            for which in range(3):
+                at = pair * QKV + which * PAIR
+                hat = qkv_ref[:, at : at + PAIR].astype(F32)
+                source = which * D + plane * DH + pair * PAIR
+                square, dot = add(square, dot, hat, source, PAIR)
+        value = out_ref[...].astype(F32)
+        square = square + fold(value * value)
+        lane = lax.broadcasted_iota(jnp.int32, (rows, VEC), 1)
+        total = jnp.sum(dot, axis=1, keepdims=True)
+        block_ref[:rows, :] = jnp.where(lane == 0, total, qkv_ref[:, QW:].astype(F32))
+        square = jnp.sum(square, axis=0, keepdims=True) * 0.125
+        block_ref[rows:, :] = jnp.broadcast_to(square, (8, PAIR))
+
+    shape = (rows + 8, VEC)
+    arrays = (mlp, qkv, out, in_weight, vec_t)
+    return pl.pallas_call(
+        kernel,
+        grid=(1,),
+        in_specs=[smem()] + [whole(a.shape) for a in arrays],
+        out_specs=whole(shape),
+        out_shape=jax.ShapeDtypeStruct(shape, F32),
+        compiler_params=params(16),
+        cost_estimate=cost(8 * rows * 6 * D, 14 * rows * 6 * D),
+        name="partial_sums",
+    )(plan.pos, *arrays)
+
+
+def join_sums(own, swap):
+    rows = own.shape[0] - 8
+
+    def kernel(own_ref, swap_ref, vec_ref, total_ref):
+        vec = own_ref[:rows, :] + swap_ref[:rows, :]
+        vec_ref[...] = vec
+        square = jnp.sum(vec * vec, axis=0, keepdims=True) * 0.125
+        total_ref[...] = own_ref[rows:, :] + swap_ref[rows:, :] + jnp.broadcast_to(square, (8, VEC))
+
+    return pl.pallas_call(
+        kernel,
+        grid=(1,),
+        in_specs=[whole(own.shape)] * 2,
+        out_specs=[whole((rows, VEC)), whole((8, VEC))],
+        out_shape=[
+            jax.ShapeDtypeStruct((rows, VEC), F32),
+            jax.ShapeDtypeStruct((8, VEC), F32),
+        ],
+        compiler_params=params(16),
+        cost_estimate=cost(4 * own.size, 12 * own.size),
+        name="join_sums",
+    )(own, swap)
+
+
 def finish_out(blocks):
     n, rows, width = blocks.shape
 
-    def kernel(in_ref, out_ref, sq_ref):
-        grad = in_ref[...].reshape(n * rows, width).astype(F32).T
-        out_ref[...] = grad
-        sq_ref[...] = jnp.broadcast_to(
-            jnp.sum(fold(grad * grad), axis=0, keepdims=True) * 0.125, (8, PAIR)
-        )
+    def kernel(in_ref, out_ref):
+        out_ref[...] = in_ref[...].reshape(n * rows, width).astype(F32).T
 
     return pl.pallas_call(
         kernel,
         grid=(1,),
         in_specs=[whole(blocks.shape)],
-        out_specs=[whole((width, D)), whole((8, PAIR))],
-        out_shape=[
-            jax.ShapeDtypeStruct((width, D), F32),
-            jax.ShapeDtypeStruct((8, PAIR), F32),
-        ],
+        out_specs=whole((width, D)),
+        out_shape=jax.ShapeDtypeStruct((width, D), F32),
         compiler_params=params(16),
-        cost_estimate=cost(4 * width * D, 6 * width * D),
+        cost_estimate=cost(0, 6 * width * D),
         name="finish_out",
     )(blocks)
 
 
-def finish_mlp(plan, own, swap, in_weight, vec_t):
-    rows = in_weight.shape[0]
-
-    def kernel(pos_ref, own_ref, swap_ref, w_ref, vec_ref, grad_ref, sq_ref, dot_ref):
+def finish_mlp(plan, own, swap, like, vec_t):
+    rows = like.shape[0]
+
+    def kernel(pos_ref, own_ref, swap_ref, vec_ref, grad_ref):
+        mine = pl.program_id(0) // 2 == pos_ref[3]
+        hat = jnp.where(mine, own_ref[...].astype(F32), swap_ref[...].astype(F32))
+        grad_ref[...] = hat * vec_ref[:, :1]
+
+    part = pl.BlockSpec((rows, D), lambda j: (0, j % 2))
+    return pl.pallas_call(
+        kernel,
+        grid=(FF // D,),
+        in_specs=[smem(), part, part, whole((rows, VEC))],
+        out_specs=pl.BlockSpec((rows, D), lambda j: (0, 3 + j)),
+        out_shape=jax.ShapeDtypeStruct(like.shape, F32),
+        compiler_params=params(16),
+        cost_estimate=cost(2 * rows * FF, 8 * rows * FF),
+        name="finish_mlp",
+    )(plan.pos, own, swap, vec_t)
+
+
+def finish_qkv(plan, own, swap, vec_t, grad):
+    rows = grad.shape[0]
+
+    def kernel(pos_ref, own_ref, swap_ref, vec_ref, _, grad_ref):
         step = pl.program_id(0)
-
-        @pl.when(step == 0)
-        def _():
-            sq_ref[...] = jnp.zeros_like(sq_ref)
-            dot_ref[...] = jnp.zeros_like(dot_ref)
-
-        mine = step // 2 == pos_ref[3]
-        hat = jnp.where(mine, own_ref[...].astype(F32), swap_ref[...].astype(F32))
-        grad = hat * vec_ref[:, :1]
-        grad_ref[...] = grad
-        sq_ref[...] += fold(grad * grad)
-        dot_ref[...] += fold(w_ref[...].astype(BF16).astype(F32) * hat)
-
-    part = pl.BlockSpec((rows, D), lambda j: (0, j % 2))
-    columns = pl.BlockSpec((rows, D), lambda j: (0, 3 + j))
-    small = jax.ShapeDtypeStruct((rows, VEC), F32)
-    return pl.pallas_call(
-        kernel,
-        grid=(FF // D,),
-        in_specs=[smem(), part, part, columns, whole((rows, VEC))],
-        out_specs=[columns, whole((rows, VEC)), whole((rows, VEC))],
-        out_shape=[jax.ShapeDtypeStruct(in_weight.shape, F32), small, small],
-        compiler_params=params(16),
-        cost_estimate=cost(8 * rows * FF, 12 * rows * FF),
-        name="finish_mlp",
-    )(plan.pos, own, swap, in_weight, vec_t)
-
-
-def finish_qkv(plan, own, swap, in_weight, vec_t, grad, sq, dot, sq_out):
-    rows = in_weight.shape[0]
-
-    def kernel(
-        pos_ref, own_ref, swap_ref, w_ref, vec_ref, _,
-        sq_in_ref, dot_in_ref, sqo_ref, grad_ref, vg_ref, total_ref, sq_ref, dot_ref,
-    ):
-        step = pl.program_id(0)
-
-        @pl.when(step == 0)
-        def _():
-            sq_ref[...] = sq_in_ref[...]
-            dot_ref[...] = dot_in_ref[...]
-
         first = pos_ref[3] == 0
         parts = []
         for pair in range(PAIRS):
@@ -396,43 +442,25 @@
             parts.append([ref[:, at].astype(F32) for ref in (own_ref, swap_ref)])
         low = [jnp.where(first, a, b) for a, b in parts]
         high = [jnp.where(first, b, a) for a, b in parts]
-        hat = jnp.concatenate(low + high, axis=1)
-        grad = hat * vec_ref[:, :1]
-        grad_ref[...] = grad
-        sq_ref[...] += fold(grad * grad)
-        dot_ref[...] += fold(w_ref[...].astype(BF16).astype(F32) * hat)
-
-        @pl.when(step == 2)
-        def _():
-            tail = own_ref[:, QW:].astype(F32) + swap_ref[:, QW:].astype(F32)
-            gain = jnp.sum(dot_ref[...], axis=1, keepdims=True)
-            lane = lax.broadcasted_iota(jnp.int32, tail.shape, 1)
-            vec = jnp.where(lane == 0, gain, tail)
-            vg_ref[...] = vec
-            total = jnp.sum(sq_ref[...] + vec * vec, axis=0, keepdims=True)
-            total_ref[...] = jnp.broadcast_to(total * 0.125, (8, PAIR)) + sqo_ref[...]
-
-    columns = pl.BlockSpec((rows, D), lambda j: (0, j))
-    small = whole((rows, VEC))
+        grad_ref[...] = jnp.concatenate(low + high, axis=1) * vec_ref[:, :1]
+
     return pl.pallas_call(
         kernel,
         grid=(3,),
         in_specs=[
-            smem(), whole(own.shape), whole(own.shape), columns, small,
-            pl.BlockSpec(memory_space=pl.ANY), small, small, whole((8, PAIR)),
-        ],
-        out_specs=[columns, small, whole((8, PAIR))],
-        out_shape=[
-            jax.ShapeDtypeStruct(in_weight.shape, F32),
-            jax.ShapeDtypeStruct((rows, VEC), F32),
-            jax.ShapeDtypeStruct((8, PAIR), F32),
-        ],
-        scratch_shapes=[pltpu.VMEM((rows, VEC), F32)] * 2,
-        input_output_aliases={5: 0},
+            smem(),
+            whole(own.shape),
+            whole(own.shape),
+            whole((rows, VEC)),
+            pl.BlockSpec(memory_space=pl.ANY),
+        ],
+        out_specs=pl.BlockSpec((rows, D), lambda j: (0, j)),
+        out_shape=jax.ShapeDtypeStruct(grad.shape, F32),
+        input_output_aliases={4: 0},
         compiler_params=params(16),
-        cost_estimate=cost(24 * rows * D, 36 * rows * D),
+        cost_estimate=cost(6 * rows * D, 24 * rows * D),
         name="finish_qkv",
-    )(plan.pos, own, swap, in_weight, vec_t, grad, sq, dot, sq_out)
+    )(plan.pos, own, swap, vec_t, grad)
 
 
 def prepare(plan, tokens, other_tokens, cotangent, other_cotangent, rows):
@@ -705,7 +733,7 @@
             jax.ShapeDtypeStruct((2, tok, FH), BF16),
         ],
         scratch_shapes=[pltpu.VMEM((D, FH + DH), row_type(rows))],
-        compiler_params=params(),
+        compiler_params=params(40),
         cost_estimate=cost(8 * tok * (FH + DH) * D, 20 * MIB),
         name="output_step",
     )(plan.pos, att, mixed, slope, cot_own, cot_other, *pieces)
@@ -731,7 +759,7 @@
         ],
         out_specs=[grad, grad],
         out_shape=[jax.ShapeDtypeStruct((half_d, FH), BF16)] * 2,
-        compiler_params=params(),
+        compiler_params=params(40),
         cost_estimate=cost(4 * tok * D * FH, 8 * MIB),
         name="mlp_gradient",
     )(turned, d_inner)
@@ -786,7 +814,7 @@
             pltpu.VMEM((D, FH), row_type(rows)),
             pltpu.VMEM((D, QW + VEC), row_type(rows)),
         ],
-        compiler_params=params(),
+        compiler_params=params(48),
         cost_estimate=cost(4 * tok * (FH + QW) * D, 16 * MIB),
         name="scaled_gradient",
     )(plan.pos, d_inner, d_qkv, *mlp_pieces, *qkv_pieces)
@@ -872,7 +900,7 @@
         out_shape=[jax.ShapeDtypeStruct((half_d, QW + VEC), BF16)] * 2
         + [jax.ShapeDtypeStruct((2, tok, QW), BF16)],
         scratch_shapes=[pltpu.VMEM((VEC, D), F32), pltpu.VMEM((D, VEC), kind)],
-        compiler_params=params(),
+        compiler_params=params(48),
         cost_estimate=cost(16 * tok * D * QW, 24 * MIB),
         name="attention_backward",
     )(plan.pos, turned, qk, v, normals, factors, probs, d_att, block, gains, cot_sum)
@@ -1077,20 +1105,20 @@
     mlp_sum = s_mlp.total()
     mlp_swap = plan.swap_plane(mlp_sum)
     s_qkv.z_got, (result,) = held([s_qkv.z_got, [result]])
-    qkv_sum = s_qkv.total()
+    qkv_sum = plan.over_pairs(s_qkv.total())
+    mlp_sum, out_sum = plan.over_pairs(mlp_sum), plan.over_pairs(out_sum)
+    own = partial_sums(plan, mlp_sum, qkv_sum, out_sum, in_weight, vec_t)
+    swap = plan.swap_plane(own)
+    swap, qkv_sum, mlp_swap = fence(swap, qkv_sum, mlp_swap)
+    vec_cols, square = join_sums(own, swap)
     qkv_swap = plan.swap_plane(qkv_sum)
-    out_grad, sq_out = finish_out(blocks)
-    in_grad, sq, dot = finish_mlp(
-        plan, plan.over_pairs(mlp_sum), plan.over_pairs(mlp_swap), in_weight, vec_t
-    )
-    qkv_swap, in_grad, out_grad = fence(qkv_swap, in_grad, out_grad)
-    in_grad, vec_cols, square = finish_qkv(
-        plan, plan.over_pairs(qkv_sum), plan.over_pairs(qkv_swap), in_weight, vec_t, in_grad,
-        sq, dot, sq_out,
-    )
+    in_grad = finish_mlp(plan, mlp_sum, plan.over_pairs(mlp_swap), in_weight, vec_t)
+    in_grad = finish_qkv(plan, qkv_sum, qkv_swap, vec_t, in_grad)
+    out_grad = finish_out(blocks)
     input_grad = token_gradient(tokens, cotangent, e_own, e_recv)
+    total, out_grad, in_grad = plan.total(square, out_grad, in_grad)
     vec_grad, norm, *updates = optimize(
-        plan.total(square),
+        total,
         vec_cols,
         (in_weight, in_moment, in_second, in_grad),
         (out_weight, out_moment, out_second, out_grad),

time: 216 us -> 208 us (0.963)
  waiting for transfers between devices: 29 us -> 19.6 us
  Pallas kernels: 99.8 us -> 92.4 us
  starting transfers between devices: 66 us -> 73.2 us
  local copies, waits for them, and re-layouts: 5.14 us -> 8.81 us
  other arithmetic: 14.1 us -> 11.3 us
    ppermute x3, waiting for transfers between devices: 5.93 us -> 0.02 us  [total(): got = lax.ppermute(a, 'fsdp', pairs)]
    unnamed x84 -> x124, local copies, waits for them, and re-layouts: 4.28 us -> 8.68 us
    ppermute x3, starting transfers between devices: 3.13 us -> 7.28 us  [total(): got = lax.ppermute(a, 'fsdp', pairs)]
    ppermute x8 -> x9, waiting for transfers between devices: 7.04 us -> 3.26 us  [swap_plane(): return lax.ppermute(a, 'dp', [(i, i ^ 1) for i in range(self.n_dp)])]
    pallas_call x1, Pallas kernels: 13.1 us -> 10.2 us  [output_step(): pl.pallas_call(kernel, grid=(2 * per,), in_specs=[smem(), pl.BlockSpec((1...]
    pallas_call x1, Pallas kernels: 6.06 us -> 3.32 us  [mlp_gradient(): pl.pallas_call(kernel, grid=(FH // tile,), in_specs=[pl.BlockSpec((1, D,...]
    ppermute x8 -> x9, starting transfers between devices: 9.62 us -> 12 us  [swap_plane(): return lax.ppermute(a, 'dp', [(i, i ^ 1) for i in range(self.n_dp)])]
  transfers between devices with their start and end apart: 47 -> 48, of which waited for: 10 -> 8; matrix products, arithmetic and copies ran while one was open for 6% -> 5% of each run, Pallas kernels for 44% -> 42%
where the time goes in v5:
time: 208 us; the launch traced here: 207 us
  Pallas kernels  92.4 us (44%)
  starting transfers between devices  73.2 us (35%)
  waiting for transfers between devices  19.6 us (9%)
  other arithmetic  11.3 us (5%)
  local copies, waits for them, and re-layouts  8.81 us (4%)
    ppermute x18, starting transfers between devices, from_z(): return lax.ppermute(a, 'fsdp', pairs)  35.8 us
    pallas_call x1, Pallas kernels, attention_backward(): pl.pallas_call(kernel, grid=(PAIRS,), in_specs=[smem(), pl.BlockSpec((1,...  17.2 us
    pallas_call x1, Pallas kernels, attention_forward(): pl.pallas_call(kernel, grid=(PAIRS,), in_specs=[smem()] + [whole((tok, D)...  16.5 us
    ppermute x9, starting transfers between devices, swap_plane(): return lax.ppermute(a, 'dp', [(i, i ^ 1) for i in range(self.n_dp)])  12 us
    pallas_call x1, Pallas kernels, mlp_forward(): pl.pallas_call(kernel, grid=(FH // tile,), in_specs=[smem()] + [whole((to...  11.4 us
    pallas_call x1, Pallas kernels, output_step(): pl.pallas_call(kernel, grid=(2 * per,), in_specs=[smem(), pl.BlockSpec((1...  10.2 us
    ppermute x18, waiting for transfers between devices, from_z(): return lax.ppermute(a, 'fsdp', pairs)  10 us
    unnamed x124, local copies, waits for them, and re-layouts  8.68 us
  transfers between devices with their start and end apart: 48, of which 8 were waited for; matrix products, arithmetic and copies ran while one was open for 5% of the time, Pallas kernels for 42%

profile of v5, /device:TPU:0, one launch (start us, length us, event | category | flops | bytes accessed | tf_op | source)
XLA Modules:
  0.0 206.9 jit_solution(9618149410833331820)
XLA Ops:
  0.6 3.0 %collective-permute-start.8 = (bf16[512,768]{1,0:T(8,128)(2,1)}, bf16[512,768]{1,0:T(8,128)(2,1)S(1)}, u32[]{:S(2)}, u32[]{:S(2)}) collective-permute-start(bf16[512,768]{1,0:T(8,128)(2,1)} %c_ref.1), channel_id=1, source_target_pairs={{0,16},{16,0},{1,17},{17,1},{2,18},{18,2},{3,19},{19,3},{4,20},{20... | collective-permute-start | bytes 2359304 | tf_op jit(solution)/shard_map/ppermute | solution.py:85
  6.5 4.1 %collective-permute-start = (bf16[48,1536]{1,0:T(8,128)(2,1)S(1)}, bf16[48,1536]{1,0:T(8,128)(2,1)S(1)}, u32[]{:S(2)}, u32[]{:S(2)}) collective-permute-start(bf16[48,1536]{1,0:T(8,128)(2,1)S(1)} %get-tuple-element.122.refs_0_), channel_id=1, source_target_pairs={{4,0},{5,1},{6,2},{7,3},{8,4},{9,5},{10,6},{11,7},{12,8},{13,9},{1... | collective-permute-start | bytes 442376 | tf_op jit(solution)/shard_map/ppermute | solution.py:74
  12.5 5.1 %all-to-all-start = ((bf16[16,48,240]{2,1,0:T(8,128)(2,1)}), bf16[16,48,240]{2,1,0:T(8,128)(2,1)S(1)}, u32[]{:S(2)}, u32[]{:S(2)}) async-start(bf16[16,48,240]{2,1,0:T(8,128)(2,1)} %split_out.1), calls=%async_computation | async-start | bytes 786432 | tf_op jit(solution)/shard_map/all_to_all | solution.py:1017
  17.7 7.7 %collective-permute-done.1.refs_2_ = bf16[48,1536]{1,0:T(8,128)(2,1)S(1)} collective-permute-done((bf16[48,1536]{1,0:T(8,128)(2,1)S(1)}, bf16[48,1536]{1,0:T(8,128)(2,1)S(1)}, u32[]{:S(2)}, u32[]{:S(2)}) %collective-permute-start.1) | collective-permute-done | bytes 147488 | tf_op jit(solution)/shard_map/ppermute | solution.py:74
  26.5 9.4 %collective-permute-start.5 = (bf16[48,1280]{1,0:T(8,128)(2,1)S(1)}, bf16[48,1280]{1,0:T(8,128)(2,1)S(1)}, u32[]{:S(2)}, u32[]{:S(2)}) collective-permute-start(bf16[48,1280]{1,0:T(8,128)(2,1)S(1)} %get-tuple-element.127.refs_0_), channel_id=1, source_target_pairs={{8,0},{9,1},{10,2},{11,3},{12,4},{13,5},{14,6},{15,7},{0,8},{1,9},... | collective-permute-start | bytes 368648 | tf_op jit(solution)/shard_map/ppermute | solution.py:74
  36.0 2.0 collective-permute-start.6
  38.8 5.5 %prepare.1 = (bf16[512,768]{1,0:T(8,128)(2,1)}, bf16[512,768]{1,0:T(8,128)(2,1)}, bf16[2,768,1024]{2,1,0:T(8,128)(2,1)}, f32[8,768]{1,0:T(8,128)}) custom-call(s32[4]{0:T(128)} %copy-done.33, bf16[512,768]{1,0:T(8,128)(2,1)} %t_ref.1, bf16[512,768]{1,0:T(8,128)(2,1)} %collective-permute-done.7.tp_ref, bf16[512,768]{1,0:T(8,128)(2,1)} %c_ref.1, ...), custom_call_target="tpu_custom_call" | custom-call | flops 15728640 | bytes 7864320 | tf_op jit(solution)/shard_map/prepare/pallas_call | solution.py:493
  46.4 3.6 %collective-permute-start.10 = (bf16[48,1920]{1,0:T(8,128)(2,1)S(1)}, bf16[48,1920]{1,0:T(8,128)(2,1)S(1)}, u32[]{:S(2)}, u32[]{:S(2)}) collective-permute-start(bf16[48,1920]{1,0:T(8,128)(2,1)S(1)} %pack_out.1.refs_0_), channel_id=1, source_target_pairs={{4,0},{5,1},{6,2},{7,3},{8,4},{9,5},{10,6},{11,7},{12,8},{13,9},{1... | collective-permute-start | bytes 552968 | tf_op jit(solution)/shard_map/ppermute | solution.py:74
  51.8 11.4 %mlp_forward.1 = (bf16[2,512,1536]{2,1,0:T(8,128)(2,1)}, bf16[2,512,1536]{2,1,0:T(8,128)(2,1)}, bf16[384,1920]{1,0:T(8,128)(2,1)}, bf16[384,1920]{1,0:T(8,128)(2,1)}) custom-call(s32[4]{0:T(128)} %copy-done.33, bf16[512,768]{1,0:T(8,128)(2,1)} %get-tuple-element.133.xo_ref, bf16[512,768]{1,0:T(8,128)(2,1)} %get-tuple-element.134.xp_ref, ...), custom_call_target="tpu_custom_call" | custom-call | flops 4831838208 | bytes 9437184 | tf_op jit(solution)/shard_map/mlp_forward/pallas_call | solution.py:538
  63.3 2.3 %collective-permute-done.11.refs_2_ = bf16[48,1920]{1,0:T(8,128)(2,1)S(1)} collective-permute-done((bf16[48,1920]{1,0:T(8,128)(2,1)S(1)}, bf16[48,1920]{1,0:T(8,128)(2,1)S(1)}, u32[]{:S(2)}, u32[]{:S(2)}) %collective-permute-start.11) | collective-permute-done | bytes 184352 | tf_op jit(solution)/shard_map/ppermute | solution.py:74
  71.4 16.5 %attention_forward.1 = (bf16[2,512,768]{2,1,0:T(8,128)(2,1)}, bf16[2,512,384]{2,1,0:T(8,128)(2,1)}, bf16[2,512,768]{2,1,0:T(8,128)(2,1)}, bf16[2,512,768]{2,1,0:...) custom-call(s32[4]{0:T(128)} %copy-done.33, ...), custom_call_target="tpu_custom_call", output_to_operand_aliasing={{7}: (7, {}), {8}: (8, {})} | custom-call | flops 1811939328 | bytes 20971520 | tf_op jit(solution)/shard_map/attention_forward/pallas_call | solution.py:626
  88.5 3.5 %collective-permute-done.21.rest_3_ = bf16[192,1920]{1,0:T(8,128)(2,1)S(1)} collective-permute-done((bf16[192,1920]{1,0:T(8,128)(2,1)S(1)}, bf16[192,1920]{1,0:T(8,128)(2,1)S(1)}, u32[]{:S(2)}, u32[]{:S(2)}) %collective-permute-start.21) | collective-permute-done | bytes 737312 | tf_op jit(solution)/shard_map/ppermute | solution.py:82
  92.5 1.9 add_convert_fusion.1
  98.2 10.2 %output_step.1 = (f32[512,768]{1,0:T(8,128)S(1)}, bf16[512,768]{1,0:T(8,128)(2,1)S(1)}, bf16[2,512,384]{2,1,0:T(8,128)(2,1)S(1)}, bf16[2,512,1536]{2,1,0:T(8,128)(2,1)S(1)}) custom-call(s32[4]{0:T(128)S(1)} %copy-done.34, bf16[2,512,384]{2,1,0:T(8,128)(2,1)S(1)} %copy-done.41, bf16[2,512,1536]{2,1,0:T(8,128)(2,1)} %get-tuple-element.159.mix_ref, ...), custom_call_target="tpu_custom_call" | custom-call | flops 6039797760 | bytes 20971520 | tf_op jit(solution)/shard_map/output_step/pallas_call | solution.py:711
  108.5 3.3 %mlp_gradient.1 = (bf16[384,1536]{1,0:T(8,128)(2,1)S(1)}, bf16[384,1536]{1,0:T(8,128)(2,1)S(1)}) custom-call(bf16[2,768,1024]{2,1,0:T(8,128)(2,1)S(1)} %copy-done.6, bf16[2,512,1536]{2,1,0:T(8,128)(2,1)S(1)} %get-tuple-element.164.d_ref.dm_ref), custom_call_target="tpu_custom_call" | custom-call | flops 2415919104 | bytes 8388608 | tf_op jit(solution)/shard_map/mlp_gradient/pallas_call | solution.py:753
  115.7 2.0 collective-permute-start.24
  117.7 2.8 %collective-permute-start.25 = (bf16[48,1920]{1,0:T(8,128)(2,1)S(1)}, bf16[48,1920]{1,0:T(8,128)(2,1)S(1)}, u32[]{:S(2)}, u32[]{:S(2)}) collective-permute-start(bf16[48,1920]{1,0:T(8,128)(2,1)S(1)} %get-tuple-element.229), channel_id=1, source_target_pairs={{4,0},{5,1},{6,2},{7,3},{8,4},{9,5},{10,6},{11,7},{12,8},{13,9},{1... | collective-permute-start | bytes 552968 | tf_op jit(solution)/shard_map/ppermute | solution.py:74
  122.4 17.2 %attention_backward.1 = (bf16[384,1280]{1,0:T(8,128)(2,1)S(1)}, bf16[384,1280]{1,0:T(8,128)(2,1)S(1)}, bf16[2,512,1152]{2,1,0:T(8,128)(2,1)}) custom-call(s32[4]{0:T(128)S(1)} %copy-done.34, bf16[2,768,1024]{2,1,0:T(8,128)(2,1)} %get-tuple-element.135.ct_ref.xt_ref, bf16[2,512,768]{2,1,0:T(8,128)(2,1)S(1)} %copy-done.39, ...), custom_call_target="tpu_custom_call" | custom-call | flops 7247757312 | bytes 25165824 | tf_op jit(solution)/shard_map/attention_backward/pallas_call | solution.py:886
  139.7 1.8 add_convert_fusion.4.own_ref.out_ref
  144.9 3.3 %collective-permute-start.33 = (bf16[48,1536]{1,0:T(8,128)(2,1)S(1)}, bf16[48,1536]{1,0:T(8,128)(2,1)S(1)}, u32[]{:S(2)}, u32[]{:S(2)}) collective-permute-start(bf16[48,1536]{1,0:T(8,128)(2,1)S(1)} %get-tuple-element.232), channel_id=1, source_target_pairs={{4,0},{5,1},{6,2},{7,3},{8,4},{9,5},{10,6},{11,7},{12,8},{13,9},{1... | collective-permute-start | bytes 442376 | tf_op jit(solution)/shard_map/ppermute | solution.py:74
  148.2 8.5 %scaled_gradient.1 = (f32[512,768]{1,0:T(8,128)}, bf16[512,768]{1,0:T(8,128)(2,1)}) custom-call(s32[4]{0:T(128)S(1)} %copy-done.34, bf16[2,512,1536]{2,1,0:T(8,128)(2,1)} %copy-done.49, bf16[2,512,1152]{2,1,0:T(8,128)(2,1)} %get-tuple-element.192.dq_ref, bf16[192,1536]{1,0:T(8,128)(2,1)S(1)} %copy-done.29, bf16[192,1536]{1,0:T(8,128)(2,1)} %collective-permute-done.3.rest_1_, ...), custom_call_target="tpu_custom_call" | custom-call | flops 4227858432 | bytes 16777216 | tf_op jit(solution)/shard_map/scaled_gradient/pallas_call | solution.py:795
  163.0 2.8 %collective-permute-start.37 = (bf16[48,1280]{1,0:T(8,128)(2,1)}, bf16[48,1280]{1,0:T(8,128)(2,1)}, u32[]{:S(2)}, u32[]{:S(2)}) collective-permute-start(bf16[48,1280]{1,0:T(8,128)(2,1)} %get-tuple-element.235), channel_id=1, source_target_pairs={{4,0},{5,1},{6,2},{7,3},{8,4},{9,5},{10,6},{11,7},{12,8},{13,9},{1... | collective-permute-start | bytes 368648 | tf_op jit(solution)/shard_map/ppermute | solution.py:74
  165.9 4.2 %all-to-all-start.1 = ((bf16[16,48,240]{2,1,0:T(8,128)(2,1)}), bf16[16,48,240]{2,1,0:T(8,128)(2,1)}, u32[]{:S(2)}, u32[]{:S(2)}) async-start(bf16[16,48,240]{2,1,0:T(8,128)(2,1)} %copy-done.16), calls=%async_computation.1 | async-start | bytes 786432 | tf_op jit(solution)/shard_map/all_to_all | solution.py:1101
  172.1 2.0 add_convert_fusion.12.qkv_ref.own_ref
  176.7 1.9 collective-permute-done.40.swap_ref
  183.6 2.0 finish_out.1.refs_7_
  185.7 2.2 %collective-permute-start.43 = (f32[8,128]{1,0:T(8,128)S(1)}, f32[8,128]{1,0:T(8,128)S(1)}, u32[]{:S(2)}, u32[]{:S(2)}) collective-permute-start(f32[8,128]{1,0:T(8,128)S(1)} %add.204), channel_id=1, source_target_pairs={{0,4},{1,5},{2,6},{3,7},{4,0},{5,1},{6,2},{7,3},{8,12},{9,13},{10,... | collective-permute-start | bytes 12296 | tf_op jit(solution)/shard_map/ppermute | solution.py:101
  189.6 2.2 %finish_mlp.1._ = f32[48,5376]{1,0:T(8,128)} custom-call(s32[4]{0:T(128)S(1)} %copy-done.34, bf16[48,1536]{1,0:T(8,128)(2,1)S(1)} %copy-done.19, bf16[48,1536]{1,0:T(8,128)(2,1)S(1)} %copy-done.32, f32[48,128]{1,0:T(8,128)S(1)} %pad_convert_fusion.vec_ref), custom_call_target="tpu_custom_call" | custom-call | flops 294912 | bytes 1179648 | tf_op jit(solution)/shard_map/finish_mlp/pallas_call | solution.py:421
  191.8 2.5 %finish_qkv.1.refs_3_ = f32[48,5376]{1,0:T(8,128)} custom-call(s32[4]{0:T(128)S(1)} %copy-done.34, bf16[48,1280]{1,0:T(8,128)(2,1)} %add_convert_fusion.12.qkv_ref.own_ref, bf16[48,1280]{1,0:T(8,128)(2,1)S(1)} %collective-permute-done.44.swap_ref, f32[48,128]{1,0:T(8,128)S(1)} %pad_convert_fusion.vec_ref, ...), custom_call_target="tpu_custom_call", output_to_operand_aliasing={{}: (4, {})} | custom-call | flops 221184 | bytes 884736 | tf_op jit(solution)/shard_map/finish_qkv/pallas_call | solution.py:447
  194.5 3.6 %collective-permute-start.45 = (f32[8,128]{1,0:T(8,128)S(1)}, f32[8,128]{1,0:T(8,128)S(1)}, u32[]{:S(2)}, u32[]{:S(2)}) collective-permute-start(f32[8,128]{1,0:T(8,128)S(1)} %add.205), channel_id=1, source_target_pairs={{0,8},{1,9},{2,10},{3,11},{4,12},{5,13},{6,14},{7,15},{8,0},{9,1},... | collective-permute-start | bytes 12296 | tf_op jit(solution)/shard_map/ppermute | solution.py:101
  198.0 4.0 %token_gradient.1 = f32[512,768]{1,0:T(8,128)} custom-call(bf16[512,768]{1,0:T(8,128)(2,1)S(1)} %copy-done.3, bf16[512,768]{1,0:T(8,128)(2,1)S(1)} %copy-done.7, f32[512,768]{1,0:T(8,128)S(1)} %copy-done.17, bf16[512,768]{1,0:T(8,128)(2,1)} %collective-permute-done.38.recv_ref), custom_call_target="tpu_custom_call" | custom-call | flops 7864320 | bytes 5505024 | tf_op jit(solution)/shard_map/token_gradient/pallas_call | solution.py:923
  202.2 4.6 %optimize.1 = (f32[4,48]{1,0:T(4,128)}, f32[1,1]{1,0:T(1,128)}, f32[48,5376]{1,0:T(8,128)}, f32[48,5376]{1,0:T(8,128)}, f32[48,5376]{1,0:T(8,128)}, /*index=5*/f...) custom-call(f32[8,128]{1,0:T(8,128)S(1)} %add.206.total_ref, ...), custom_call_target="tpu_custom_call" | custom-call | flops 5160960 | bytes 13418496 | tf_op jit(solution)/shard_map/optimize/pallas_call | solution.py:973
  (230 shorter events, 48.0 us)
Async XLA Ops:
  0.6 35.3 %collective-permute-start.8 = (bf16[512,768]{1,0:T(8,128)(2,1)}, bf16[512,768]{1,0:T(8,128)(2,1)S(1)}, u32[]{:S(2)}, u32[]{:S(2)}) collective-permute-start(bf16[512,768]{1,0:T(8,128)(2,1)} %c_ref.1), channel_id=1, source_target_pairs={{0,16},{16,0},{1,17},{17,1},{2,18},{18,2},{3,19},{19,3},{4,20},{20... | collective-permute-start | bytes 2359304 | tf_op jit(solution)/shard_map/ppermute | solution.py:85
  3.6 35.1 %collective-permute-start.7 = (bf16[512,768]{1,0:T(8,128)(2,1)}, bf16[512,768]{1,0:T(8,128)(2,1)}, u32[]{:S(2)}, u32[]{:S(2)}) collective-permute-start(bf16[512,768]{1,0:T(8,128)(2,1)} %t_ref.1), channel_id=1, source_target_pairs={{0,16},{16,0},{1,17},{17,1},{2,18},{18,2},{3,19},{19,3},{4,20},{20... | collective-permute-start | bytes 2359304 | tf_op jit(solution)/shard_map/ppermute | solution.py:85
  6.5 11.2 %collective-permute-start = (bf16[48,1536]{1,0:T(8,128)(2,1)S(1)}, bf16[48,1536]{1,0:T(8,128)(2,1)S(1)}, u32[]{:S(2)}, u32[]{:S(2)}) collective-permute-start(bf16[48,1536]{1,0:T(8,128)(2,1)S(1)} %get-tuple-element.122.refs_0_), channel_id=1, source_target_pairs={{4,0},{5,1},{6,2},{7,3},{8,4},{9,5},{10,6},{11,7},{12,8},{13,9},{1... | collective-permute-start | bytes 442376 | tf_op jit(solution)/shard_map/ppermute | solution.py:74
  10.6 14.8 %collective-permute-start.1 = (bf16[48,1536]{1,0:T(8,128)(2,1)S(1)}, bf16[48,1536]{1,0:T(8,128)(2,1)S(1)}, u32[]{:S(2)}, u32[]{:S(2)}) collective-permute-start(bf16[48,1536]{1,0:T(8,128)(2,1)S(1)} %get-tuple-element.122.refs_0_), channel_id=1, source_target_pairs={{8,0},{9,1},{10,2},{11,3},{12,4},{13,5},{14,6},{15,7},{0,8},{1,9},... | collective-permute-start | bytes 442376 | tf_op jit(solution)/shard_map/ppermute | solution.py:74
  10.6 14.8 %collective-permute-start.2 = (bf16[48,1536]{1,0:T(8,128)(2,1)S(1)}, bf16[48,1536]{1,0:T(8,128)(2,1)S(1)}, u32[]{:S(2)}, u32[]{:S(2)}) collective-permute-start(bf16[48,1536]{1,0:T(8,128)(2,1)S(1)} %get-tuple-element.122.refs_0_), channel_id=1, source_target_pairs={{12,0},{13,1},{14,2},{15,3},{0,4},{1,5},{2,6},{3,7},{4,8},{5,9},{6... | collective-permute-start | bytes 442376 | tf_op jit(solution)/shard_map/ppermute | solution.py:74
  12.5 25.5 %all-to-all-start = ((bf16[16,48,240]{2,1,0:T(8,128)(2,1)}), bf16[16,48,240]{2,1,0:T(8,128)(2,1)S(1)}, u32[]{:S(2)}, u32[]{:S(2)}) async-start(bf16[16,48,240]{2,1,0:T(8,128)(2,1)} %split_out.1), calls=%async_computation | async-start | bytes 786432 | tf_op jit(solution)/shard_map/all_to_all | solution.py:1017
  25.4 18.9 %collective-permute-start.3 = (bf16[192,1536]{1,0:T(8,128)(2,1)S(1)}, bf16[192,1536]{1,0:T(8,128)(2,1)}, u32[]{:S(2)}, u32[]{:S(2)}) collective-permute-start(bf16[192,1536]{1,0:T(8,128)(2,1)S(1)} %stack.23.rest_0_), channel_id=1, source_target_pairs={{2,0},{3,1},{0,2},{1,3},{6,4},{7,5},{4,6},{5,7},{10,8},{11,9},{8,1... | collective-permute-start | bytes 1769480 | tf_op jit(solution)/shard_map/ppermute | solution.py:78
  26.5 17.7 %collective-permute-start.4 = (bf16[48,1280]{1,0:T(8,128)(2,1)S(1)}, bf16[48,1280]{1,0:T(8,128)(2,1)S(1)}, u32[]{:S(2)}, u32[]{:S(2)}) collective-permute-start(bf16[48,1280]{1,0:T(8,128)(2,1)S(1)} %get-tuple-element.127.refs_0_), channel_id=1, source_target_pairs={{4,0},{5,1},{6,2},{7,3},{8,4},{9,5},{10,6},{11,7},{12,8},{13,9},{1... | collective-permute-start | bytes 368648 | tf_op jit(solution)/shard_map/ppermute | solution.py:74
  26.5 17.7 %collective-permute-start.5 = (bf16[48,1280]{1,0:T(8,128)(2,1)S(1)}, bf16[48,1280]{1,0:T(8,128)(2,1)S(1)}, u32[]{:S(2)}, u32[]{:S(2)}) collective-permute-start(bf16[48,1280]{1,0:T(8,128)(2,1)S(1)} %get-tuple-element.127.refs_0_), channel_id=1, source_target_pairs={{8,0},{9,1},{10,2},{11,3},{12,4},{13,5},{14,6},{15,7},{0,8},{1,9},... | collective-permute-start | bytes 368648 | tf_op jit(solution)/shard_map/ppermute | solution.py:74
  44.9 20.6 %collective-permute-start.9 = (bf16[192,1280]{1,0:T(8,128)(2,1)S(1)}, bf16[192,1280]{1,0:T(8,128)(2,1)S(1)}, u32[]{:S(2)}, u32[]{:S(2)}) collective-permute-start(bf16[192,1280]{1,0:T(8,128)(2,1)S(1)} %stack.24.rest_0_.rest_4_), channel_id=1, source_target_pairs={{2,0},{3,1},{0,2},{1,3},{6,4},{7,5},{4,6},{5,7},{10,8},{11,9},{8,1... | collective-permute-start | bytes 1474568 | tf_op jit(solution)/shard_map/ppermute | solution.py:78
  46.4 16.9 %collective-permute-start.10 = (bf16[48,1920]{1,0:T(8,128)(2,1)S(1)}, bf16[48,1920]{1,0:T(8,128)(2,1)S(1)}, u32[]{:S(2)}, u32[]{:S(2)}) collective-permute-start(bf16[48,1920]{1,0:T(8,128)(2,1)S(1)} %pack_out.1.refs_0_), channel_id=1, source_target_pairs={{4,0},{5,1},{6,2},{7,3},{8,4},{9,5},{10,6},{11,7},{12,8},{13,9},{1... | collective-permute-start | bytes 552968 | tf_op jit(solution)/shard_map/ppermute | solution.py:74
  50.0 15.6 %collective-permute-start.11 = (bf16[48,1920]{1,0:T(8,128)(2,1)S(1)}, bf16[48,1920]{1,0:T(8,128)(2,1)S(1)}, u32[]{:S(2)}, u32[]{:S(2)}) collective-permute-start(bf16[48,1920]{1,0:T(8,128)(2,1)S(1)} %pack_out.1.refs_0_), channel_id=1, source_target_pairs={{8,0},{9,1},{10,2},{11,3},{12,4},{13,5},{14,6},{15,7},{0,8},{1,9},... | collective-permute-start | bytes 552968 | tf_op jit(solution)/shard_map/ppermute | solution.py:74
  50.0 15.6 %collective-permute-start.12 = (bf16[48,1920]{1,0:T(8,128)(2,1)S(1)}, bf16[48,1920]{1,0:T(8,128)(2,1)S(1)}, u32[]{:S(2)}, u32[]{:S(2)}) collective-permute-start(bf16[48,1920]{1,0:T(8,128)(2,1)S(1)} %pack_out.1.refs_0_), channel_id=1, source_target_pairs={{12,0},{13,1},{14,2},{15,3},{0,4},{1,5},{2,6},{3,7},{4,8},{5,9},{6... | collective-permute-start | bytes 552968 | tf_op jit(solution)/shard_map/ppermute | solution.py:74
  65.6 22.2 %collective-permute-start.15 = (bf16[192,1920]{1,0:T(8,128)(2,1)S(1)}, bf16[192,1920]{1,0:T(8,128)(2,1)S(1)}, u32[]{:S(2)}, u32[]{:S(2)}) collective-permute-start(bf16[192,1920]{1,0:T(8,128)(2,1)S(1)} %stack.25.rest_0_), channel_id=1, source_target_pairs={{2,0},{3,1},{0,2},{1,3},{6,4},{7,5},{4,6},{5,7},{10,8},{11,9},{8,1... | collective-permute-start | bytes 2211848 | tf_op jit(solution)/shard_map/ppermute | solution.py:78
  66.2 21.7 %collective-permute-start.16 = (bf16[192,1920]{1,0:T(8,128)(2,1)S(1)}, bf16[192,1920]{1,0:T(8,128)(2,1)}, u32[]{:S(2)}, u32[]{:S(2)}) collective-permute-start(bf16[192,1920]{1,0:T(8,128)(2,1)S(1)} %stack.25.rest_0_), channel_id=1, source_target_pairs={{0,1},{1,0},{2,3},{3,2},{4,5},{5,4},{6,7},{7,6},{8,9},{9,8},{10,11... | collective-permute-start | bytes 2211848 | tf_op jit(solution)/shard_map/ppermute | solution.py:82
  94.4 18.6 %collective-permute-start.22 = (bf16[192,1920]{1,0:T(8,128)(2,1)S(1)}, bf16[192,1920]{1,0:T(8,128)(2,1)S(1)}, u32[]{:S(2)}, u32[]{:S(2)}) collective-permute-start(bf16[192,1920]{1,0:T(8,128)(2,1)S(1)} %add_convert_fusion.1), channel_id=1, source_target_pairs={{2,0},{3,1},{0,2},{1,3},{6,4},{7,5},{4,6},{5,7},{10,8},{11,9},{8,1... | collective-permute-start | bytes 2211848 | tf_op jit(solution)/shard_map/ppermute | solution.py:78
  113.0 26.5 %collective-permute-start.28 = (bf16[512,768]{1,0:T(8,128)(2,1)S(1)}, bf16[512,768]{1,0:T(8,128)(2,1)S(1)}, u32[]{:S(2)}, u32[]{:S(2)}) collective-permute-start(bf16[512,768]{1,0:T(8,128)(2,1)S(1)} %get-tuple-element.181), channel_id=1, source_target_pairs={{0,16},{16,0},{1,17},{17,1},{2,18},{18,2},{3,19},{19,3},{4,20},{20... | collective-permute-start | bytes 2359304 | tf_op jit(solution)/shard_map/ppermute | solution.py:85
  114.8 24.8 %collective-permute-start.23 = (bf16[48,1920]{1,0:T(8,128)(2,1)S(1)}, bf16[48,1920]{1,0:T(8,128)(2,1)S(1)}, u32[]{:S(2)}, u32[]{:S(2)}) collective-permute-start(bf16[48,1920]{1,0:T(8,128)(2,1)S(1)} %get-tuple-element.231), channel_id=1, source_target_pairs={{12,0},{13,1},{14,2},{15,3},{0,4},{1,5},{2,6},{3,7},{4,8},{5,9},{6... | collective-permute-start | bytes 552968 | tf_op jit(solution)/shard_map/ppermute | solution.py:74
  115.7 23.8 %collective-permute-start.24 = (bf16[48,1920]{1,0:T(8,128)(2,1)S(1)}, bf16[48,1920]{1,0:T(8,128)(2,1)S(1)}, u32[]{:S(2)}, u32[]{:S(2)}) collective-permute-start(bf16[48,1920]{1,0:T(8,128)(2,1)S(1)} %get-tuple-element.230), channel_id=1, source_target_pairs={{8,0},{9,1},{10,2},{11,3},{12,4},{13,5},{14,6},{15,7},{0,8},{1,9},... | collective-permute-start | bytes 552968 | tf_op jit(solution)/shard_map/ppermute | solution.py:74
  117.7 21.8 %collective-permute-start.25 = (bf16[48,1920]{1,0:T(8,128)(2,1)S(1)}, bf16[48,1920]{1,0:T(8,128)(2,1)S(1)}, u32[]{:S(2)}, u32[]{:S(2)}) collective-permute-start(bf16[48,1920]{1,0:T(8,128)(2,1)S(1)} %get-tuple-element.229), channel_id=1, source_target_pairs={{4,0},{5,1},{6,2},{7,3},{8,4},{9,5},{10,6},{11,7},{12,8},{13,9},{1... | collective-permute-start | bytes 552968 | tf_op jit(solution)/shard_map/ppermute | solution.py:74
  120.7 18.9 %collective-permute-start.27 = (bf16[192,1536]{1,0:T(8,128)(2,1)S(1)}, bf16[192,1536]{1,0:T(8,128)(2,1)S(1)}, u32[]{:S(2)}, u32[]{:S(2)}) collective-permute-start(bf16[192,1536]{1,0:T(8,128)(2,1)S(1)} %add_convert_fusion.2), channel_id=1, source_target_pairs={{2,0},{3,1},{0,2},{1,3},{6,4},{7,5},{4,6},{5,7},{10,8},{11,9},{8,1... | collective-permute-start | bytes 1769480 | tf_op jit(solution)/shard_map/ppermute | solution.py:78
  141.5 15.2 %collective-permute-start.34 = (bf16[48,1920]{1,0:T(8,128)(2,1)S(1)}, bf16[48,1920]{1,0:T(8,128)(2,1)S(1)}, u32[]{:S(2)}, u32[]{:S(2)}) collective-permute-start(bf16[48,1920]{1,0:T(8,128)(2,1)S(1)} %add_convert_fusion.4.own_ref.out_ref), channel_id=1, source_target_pairs={{0,16},{16,0},{1,17},{17,1},{2,18},{18,2},{3,19},{19,3},{4,20},{20... | collective-permute-start | bytes 552968 | tf_op jit(solution)/shard_map/ppermute | solution.py:85
  143.5 16.3 %collective-permute-start.30 = (bf16[192,1280]{1,0:T(8,128)(2,1)S(1)}, bf16[192,1280]{1,0:T(8,128)(2,1)S(1)}, u32[]{:S(2)}, u32[]{:S(2)}) collective-permute-start(bf16[192,1280]{1,0:T(8,128)(2,1)S(1)} %add_convert_fusion.3), channel_id=1, source_target_pairs={{2,0},{3,1},{0,2},{1,3},{6,4},{7,5},{4,6},{5,7},{10,8},{11,9},{8,1... | collective-permute-start | bytes 1474568 | tf_op jit(solution)/shard_map/ppermute | solution.py:78
  144.3 15.6 %collective-permute-start.31 = (bf16[48,1536]{1,0:T(8,128)(2,1)S(1)}, bf16[48,1536]{1,0:T(8,128)(2,1)S(1)}, u32[]{:S(2)}, u32[]{:S(2)}) collective-permute-start(bf16[48,1536]{1,0:T(8,128)(2,1)S(1)} %get-tuple-element.234), channel_id=1, source_target_pairs={{12,0},{13,1},{14,2},{15,3},{0,4},{1,5},{2,6},{3,7},{4,8},{5,9},{6... | collective-permute-start | bytes 442376 | tf_op jit(solution)/shard_map/ppermute | solution.py:74
  144.3 15.5 %collective-permute-start.32 = (bf16[48,1536]{1,0:T(8,128)(2,1)S(1)}, bf16[48,1536]{1,0:T(8,128)(2,1)S(1)}, u32[]{:S(2)}, u32[]{:S(2)}) collective-permute-start(bf16[48,1536]{1,0:T(8,128)(2,1)S(1)} %get-tuple-element.233), channel_id=1, source_target_pairs={{8,0},{9,1},{10,2},{11,3},{12,4},{13,5},{14,6},{15,7},{0,8},{1,9},... | collective-permute-start | bytes 442376 | tf_op jit(solution)/shard_map/ppermute | solution.py:74
  144.9 15.0 %collective-permute-start.33 = (bf16[48,1536]{1,0:T(8,128)(2,1)S(1)}, bf16[48,1536]{1,0:T(8,128)(2,1)S(1)}, u32[]{:S(2)}, u32[]{:S(2)}) collective-permute-start(bf16[48,1536]{1,0:T(8,128)(2,1)S(1)} %get-tuple-element.232), channel_id=1, source_target_pairs={{4,0},{5,1},{6,2},{7,3},{8,4},{9,5},{10,6},{11,7},{12,8},{13,9},{1... | collective-permute-start | bytes 442376 | tf_op jit(solution)/shard_map/ppermute | solution.py:74
  156.7 41.3 %collective-permute-start.38 = (bf16[512,768]{1,0:T(8,128)(2,1)}, bf16[512,768]{1,0:T(8,128)(2,1)}, u32[]{:S(2)}, u32[]{:S(2)}) collective-permute-start(bf16[512,768]{1,0:T(8,128)(2,1)} %get-tuple-element.201), channel_id=1, source_target_pairs={{0,16},{16,0},{1,17},{17,1},{2,18},{18,2},{3,19},{19,3},{4,20},{20... | collective-permute-start | bytes 2359304 | tf_op jit(solution)/shard_map/ppermute | solution.py:85
  160.9 11.2 %collective-permute-start.35 = (bf16[48,1280]{1,0:T(8,128)(2,1)}, bf16[48,1280]{1,0:T(8,128)(2,1)}, u32[]{:S(2)}, u32[]{:S(2)}) collective-permute-start(bf16[48,1280]{1,0:T(8,128)(2,1)} %get-tuple-element.237), channel_id=1, source_target_pairs={{12,0},{13,1},{14,2},{15,3},{0,4},{1,5},{2,6},{3,7},{4,8},{5,9},{6... | collective-permute-start | bytes 368648 | tf_op jit(solution)/shard_map/ppermute | solution.py:74
  161.5 10.6 %collective-permute-start.36 = (bf16[48,1280]{1,0:T(8,128)(2,1)}, bf16[48,1280]{1,0:T(8,128)(2,1)}, u32[]{:S(2)}, u32[]{:S(2)}) collective-permute-start(bf16[48,1280]{1,0:T(8,128)(2,1)} %get-tuple-element.236), channel_id=1, source_target_pairs={{8,0},{9,1},{10,2},{11,3},{12,4},{13,5},{14,6},{15,7},{0,8},{1,9},... | collective-permute-start | bytes 368648 | tf_op jit(solution)/shard_map/ppermute | solution.py:74
  163.0 9.1 %collective-permute-start.37 = (bf16[48,1280]{1,0:T(8,128)(2,1)}, bf16[48,1280]{1,0:T(8,128)(2,1)}, u32[]{:S(2)}, u32[]{:S(2)}) collective-permute-start(bf16[48,1280]{1,0:T(8,128)(2,1)} %get-tuple-element.235), channel_id=1, source_target_pairs={{4,0},{5,1},{6,2},{7,3},{8,4},{9,5},{10,6},{11,7},{12,8},{13,9},{1... | collective-permute-start | bytes 368648 | tf_op jit(solution)/shard_map/ppermute | solution.py:74
  165.9 17.7 %all-to-all-start.1 = ((bf16[16,48,240]{2,1,0:T(8,128)(2,1)}), bf16[16,48,240]{2,1,0:T(8,128)(2,1)}, u32[]{:S(2)}, u32[]{:S(2)}) async-start(bf16[16,48,240]{2,1,0:T(8,128)(2,1)} %copy-done.16), calls=%async_computation.1 | async-start | bytes 786432 | tf_op jit(solution)/shard_map/all_to_all | solution.py:1101
  179.3 12.5 %collective-permute-start.44 = (bf16[48,1280]{1,0:T(8,128)(2,1)}, bf16[48,1280]{1,0:T(8,128)(2,1)S(1)}, u32[]{:S(2)}, u32[]{:S(2)}) collective-permute-start(bf16[48,1280]{1,0:T(8,128)(2,1)} %add_convert_fusion.12.qkv_ref.own_ref), channel_id=1, source_target_pairs={{0,16},{16,0},{1,17},{17,1},{2,18},{18,2},{3,19},{19,3},{4,20},{20... | collective-permute-start | bytes 368648 | tf_op jit(solution)/shard_map/ppermute | solution.py:85
  (78 other events, 555.9 us)

commit v6 on v5

--- a/solution.py
+++ b/solution.py
@@ -100,9 +100,13 @@
                 pairs = [(i, i ^ (m * step)) for i in range(self.n)]
                 got = lax.ppermute(a, "fsdp", pairs)
                 if count < len(beside):
+                    if callable(beside[count]):
+                        beside[count] = beside[count](beside[count - 1])
                     got, beside[count] = fence(got, beside[count])
                 a = a + got
                 m, count = 2 * m, count + 1
+        for i in range(count, len(beside)):
+            beside[i] = beside[i](beside[i - 1])
         return [a] + beside
 
     def row(self, pos_ref, piece, rows):
@@ -1109,14 +1113,15 @@
     mlp_sum, out_sum = plan.over_pairs(mlp_sum), plan.over_pairs(out_sum)
     own = partial_sums(plan, mlp_sum, qkv_sum, out_sum, in_weight, vec_t)
     swap = plan.swap_plane(own)
-    swap, qkv_sum, mlp_swap = fence(swap, qkv_sum, mlp_swap)
+    input_grad = token_gradient(tokens, cotangent, e_own, e_recv)
+    swap, qkv_sum, mlp_swap, input_grad = fence(swap, qkv_sum, mlp_swap, input_grad)
     vec_cols, square = join_sums(own, swap)
     qkv_swap = plan.swap_plane(qkv_sum)
     in_grad = finish_mlp(plan, mlp_sum, plan.over_pairs(mlp_swap), in_weight, vec_t)
-    in_grad = finish_qkv(plan, qkv_sum, qkv_swap, vec_t, in_grad)
     out_grad = finish_out(blocks)
-    input_grad = token_gradient(tokens, cotangent, e_own, e_recv)
-    total, out_grad, in_grad = plan.total(square, out_grad, in_grad)
+    total, out_grad, _, in_grad = plan.total(
+        square, out_grad, in_grad, lambda a: finish_qkv(plan, qkv_sum, qkv_swap, vec_t, a)
+    )
     vec_grad, norm, *updates = optimize(
         total,
         vec_cols,

time: 208 us -> 206 us (level)
  transfers between devices with their start and end apart: 48 -> 48, of which waited for: 8 -> 8; matrix products, arithmetic and copies ran while one was open for 5% -> 5% of each run, Pallas kernels for 42% -> 43%
where the time goes in v6:
time: 206 us; the launch traced here: 205 us
  Pallas kernels  92.4 us (45%)
  starting transfers between devices  71.7 us (35%)
  waiting for transfers between devices  17.7 us (9%)
  other arithmetic  11.5 us (6%)
  local copies, waits for them, and re-layouts  10 us (5%)
    ppermute x18, starting transfers between devices, from_z(): return lax.ppermute(a, 'fsdp', pairs)  35.8 us
    pallas_call x1, Pallas kernels, attention_backward(): pl.pallas_call(kernel, grid=(PAIRS,), in_specs=[smem(), pl.BlockSpec((1,...  17.2 us
    pallas_call x1, Pallas kernels, attention_forward(): pl.pallas_call(kernel, grid=(PAIRS,), in_specs=[smem()] + [whole((tok, D)...  16.5 us
    ppermute x9, starting transfers between devices, swap_plane(): return lax.ppermute(a, 'dp', [(i, i ^ 1) for i in range(self.n_dp)])  12 us
    pallas_call x1, Pallas kernels, mlp_forward(): pl.pallas_call(kernel, grid=(FH // tile,), in_specs=[smem()] + [whole((to...  11.4 us
    pallas_call x1, Pallas kernels, output_step(): pl.pallas_call(kernel, grid=(2 * per,), in_specs=[smem(), pl.BlockSpec((1...  10.2 us
    ppermute x18, waiting for transfers between devices, from_z(): return lax.ppermute(a, 'fsdp', pairs)  10 us
    unnamed x124, local copies, waits for them, and re-layouts  9.88 us
  transfers between devices with their start and end apart: 48, of which 8 were waited for; matrix products, arithmetic and copies ran while one was open for 5% of the time, Pallas kernels for 43%

profile of v6, /device:TPU:0, one launch (start us, length us, event | category | flops | bytes accessed | tf_op | source)
XLA Modules:
  0.0 204.9 jit_solution(4580920532075639175)
XLA Ops:
  0.6 3.0 %collective-permute-start.8 = (bf16[512,768]{1,0:T(8,128)(2,1)}, bf16[512,768]{1,0:T(8,128)(2,1)S(1)}, u32[]{:S(2)}, u32[]{:S(2)}) collective-permute-start(bf16[512,768]{1,0:T(8,128)(2,1)} %c_ref.1), channel_id=1, source_target_pairs={{0,16},{16,0},{1,17},{17,1},{2,18},{18,2},{3,19},{19,3},{4,20},{20... | collective-permute-start | bytes 2359304 | tf_op jit(solution)/shard_map/ppermute | solution.py:85
  6.5 4.1 %collective-permute-start = (bf16[48,1536]{1,0:T(8,128)(2,1)S(1)}, bf16[48,1536]{1,0:T(8,128)(2,1)S(1)}, u32[]{:S(2)}, u32[]{:S(2)}) collective-permute-start(bf16[48,1536]{1,0:T(8,128)(2,1)S(1)} %get-tuple-element.125.refs_0_), channel_id=1, source_target_pairs={{4,0},{5,1},{6,2},{7,3},{8,4},{9,5},{10,6},{11,7},{12,8},{13,9},{1... | collective-permute-start | bytes 442376 | tf_op jit(solution)/shard_map/ppermute | solution.py:74
  12.5 5.1 %all-to-all-start = ((bf16[16,48,240]{2,1,0:T(8,128)(2,1)}), bf16[16,48,240]{2,1,0:T(8,128)(2,1)S(1)}, u32[]{:S(2)}, u32[]{:S(2)}) async-start(bf16[16,48,240]{2,1,0:T(8,128)(2,1)} %split_out.1), calls=%async_computation | async-start | bytes 786432 | tf_op jit(solution)/shard_map/all_to_all | solution.py:1021
  17.7 7.7 %collective-permute-done.1.refs_2_ = bf16[48,1536]{1,0:T(8,128)(2,1)S(1)} collective-permute-done((bf16[48,1536]{1,0:T(8,128)(2,1)S(1)}, bf16[48,1536]{1,0:T(8,128)(2,1)S(1)}, u32[]{:S(2)}, u32[]{:S(2)}) %collective-permute-start.1) | collective-permute-done | bytes 147488 | tf_op jit(solution)/shard_map/ppermute | solution.py:74
  26.5 9.4 %collective-permute-start.5 = (bf16[48,1280]{1,0:T(8,128)(2,1)S(1)}, bf16[48,1280]{1,0:T(8,128)(2,1)S(1)}, u32[]{:S(2)}, u32[]{:S(2)}) collective-permute-start(bf16[48,1280]{1,0:T(8,128)(2,1)S(1)} %get-tuple-element.130.refs_0_), channel_id=1, source_target_pairs={{8,0},{9,1},{10,2},{11,3},{12,4},{13,5},{14,6},{15,7},{0,8},{1,9},... | collective-permute-start | bytes 368648 | tf_op jit(solution)/shard_map/ppermute | solution.py:74
  36.0 2.0 collective-permute-start.6
  38.8 5.5 %prepare.1 = (bf16[512,768]{1,0:T(8,128)(2,1)}, bf16[512,768]{1,0:T(8,128)(2,1)}, bf16[2,768,1024]{2,1,0:T(8,128)(2,1)}, f32[8,768]{1,0:T(8,128)}) custom-call(s32[4]{0:T(128)} %copy-done.33, bf16[512,768]{1,0:T(8,128)(2,1)} %t_ref.1, bf16[512,768]{1,0:T(8,128)(2,1)} %collective-permute-done.7.tp_ref, bf16[512,768]{1,0:T(8,128)(2,1)} %c_ref.1, ...), custom_call_target="tpu_custom_call" | custom-call | flops 15728640 | bytes 7864320 | tf_op jit(solution)/shard_map/prepare/pallas_call | solution.py:497
  46.4 3.6 %collective-permute-start.10 = (bf16[48,1920]{1,0:T(8,128)(2,1)S(1)}, bf16[48,1920]{1,0:T(8,128)(2,1)S(1)}, u32[]{:S(2)}, u32[]{:S(2)}) collective-permute-start(bf16[48,1920]{1,0:T(8,128)(2,1)S(1)} %pack_out.1.refs_0_), channel_id=1, source_target_pairs={{4,0},{5,1},{6,2},{7,3},{8,4},{9,5},{10,6},{11,7},{12,8},{13,9},{1... | collective-permute-start | bytes 552968 | tf_op jit(solution)/shard_map/ppermute | solution.py:74
  51.8 11.4 %mlp_forward.1 = (bf16[2,512,1536]{2,1,0:T(8,128)(2,1)}, bf16[2,512,1536]{2,1,0:T(8,128)(2,1)}, bf16[384,1920]{1,0:T(8,128)(2,1)}, bf16[384,1920]{1,0:T(8,128)(2,1)}) custom-call(s32[4]{0:T(128)} %copy-done.33, bf16[512,768]{1,0:T(8,128)(2,1)} %get-tuple-element.136.xo_ref, bf16[512,768]{1,0:T(8,128)(2,1)} %get-tuple-element.137.xp_ref, ...), custom_call_target="tpu_custom_call" | custom-call | flops 4831838208 | bytes 9437184 | tf_op jit(solution)/shard_map/mlp_forward/pallas_call | solution.py:542
  63.3 2.3 %collective-permute-done.11.refs_2_ = bf16[48,1920]{1,0:T(8,128)(2,1)S(1)} collective-permute-done((bf16[48,1920]{1,0:T(8,128)(2,1)S(1)}, bf16[48,1920]{1,0:T(8,128)(2,1)S(1)}, u32[]{:S(2)}, u32[]{:S(2)}) %collective-permute-start.11) | collective-permute-done | bytes 184352 | tf_op jit(solution)/shard_map/ppermute | solution.py:74
  71.4 16.5 %attention_forward.1 = (bf16[2,512,768]{2,1,0:T(8,128)(2,1)}, bf16[2,512,384]{2,1,0:T(8,128)(2,1)}, bf16[2,512,768]{2,1,0:T(8,128)(2,1)}, bf16[2,512,768]{2,1,0:...) custom-call(s32[4]{0:T(128)} %copy-done.33, ...), custom_call_target="tpu_custom_call", output_to_operand_aliasing={{7}: (7, {}), {8}: (8, {})} | custom-call | flops 1811939328 | bytes 20971520 | tf_op jit(solution)/shard_map/attention_forward/pallas_call | solution.py:630
  88.5 3.5 %collective-permute-done.21.rest_3_ = bf16[192,1920]{1,0:T(8,128)(2,1)S(1)} collective-permute-done((bf16[192,1920]{1,0:T(8,128)(2,1)S(1)}, bf16[192,1920]{1,0:T(8,128)(2,1)S(1)}, u32[]{:S(2)}, u32[]{:S(2)}) %collective-permute-start.21) | collective-permute-done | bytes 737312 | tf_op jit(solution)/shard_map/ppermute | solution.py:82
  92.5 1.9 add_convert_fusion.1
  98.2 10.2 %output_step.1 = (f32[512,768]{1,0:T(8,128)S(1)}, bf16[512,768]{1,0:T(8,128)(2,1)S(1)}, bf16[2,512,384]{2,1,0:T(8,128)(2,1)S(1)}, bf16[2,512,1536]{2,1,0:T(8,128)(2,1)S(1)}) custom-call(s32[4]{0:T(128)S(1)} %copy-done.34, bf16[2,512,384]{2,1,0:T(8,128)(2,1)S(1)} %copy-done.41, bf16[2,512,1536]{2,1,0:T(8,128)(2,1)} %get-tuple-element.162.mix_ref, ...), custom_call_target="tpu_custom_call" | custom-call | flops 6039797760 | bytes 20971520 | tf_op jit(solution)/shard_map/output_step/pallas_call | solution.py:715
  108.5 3.3 %mlp_gradient.1 = (bf16[384,1536]{1,0:T(8,128)(2,1)S(1)}, bf16[384,1536]{1,0:T(8,128)(2,1)S(1)}) custom-call(bf16[2,768,1024]{2,1,0:T(8,128)(2,1)S(1)} %copy-done.6, bf16[2,512,1536]{2,1,0:T(8,128)(2,1)S(1)} %get-tuple-element.167.d_ref.dm_ref), custom_call_target="tpu_custom_call" | custom-call | flops 2415919104 | bytes 8388608 | tf_op jit(solution)/shard_map/mlp_gradient/pallas_call | solution.py:757
  115.7 2.0 collective-permute-start.24
  117.7 2.8 %collective-permute-start.25 = (bf16[48,1920]{1,0:T(8,128)(2,1)S(1)}, bf16[48,1920]{1,0:T(8,128)(2,1)S(1)}, u32[]{:S(2)}, u32[]{:S(2)}) collective-permute-start(bf16[48,1920]{1,0:T(8,128)(2,1)S(1)} %get-tuple-element.235), channel_id=1, source_target_pairs={{4,0},{5,1},{6,2},{7,3},{8,4},{9,5},{10,6},{11,7},{12,8},{13,9},{1... | collective-permute-start | bytes 552968 | tf_op jit(solution)/shard_map/ppermute | solution.py:74
  120.7 1.6 collective-permute-start.27
  122.4 17.2 %attention_backward.1 = (bf16[384,1280]{1,0:T(8,128)(2,1)S(1)}, bf16[384,1280]{1,0:T(8,128)(2,1)S(1)}, bf16[2,512,1152]{2,1,0:T(8,128)(2,1)}) custom-call(s32[4]{0:T(128)S(1)} %copy-done.34, bf16[2,768,1024]{2,1,0:T(8,128)(2,1)} %get-tuple-element.138.ct_ref.xt_ref, bf16[2,512,768]{2,1,0:T(8,128)(2,1)S(1)} %copy-done.39, ...), custom_call_target="tpu_custom_call" | custom-call | flops 7247757312 | bytes 25165824 | tf_op jit(solution)/shard_map/attention_backward/pallas_call | solution.py:890
  139.7 1.8 add_convert_fusion.4.own_ref.out_ref
  144.9 3.3 %collective-permute-start.33 = (bf16[48,1536]{1,0:T(8,128)(2,1)S(1)}, bf16[48,1536]{1,0:T(8,128)(2,1)S(1)}, u32[]{:S(2)}, u32[]{:S(2)}) collective-permute-start(bf16[48,1536]{1,0:T(8,128)(2,1)S(1)} %get-tuple-element.238), channel_id=1, source_target_pairs={{4,0},{5,1},{6,2},{7,3},{8,4},{9,5},{10,6},{11,7},{12,8},{13,9},{1... | collective-permute-start | bytes 442376 | tf_op jit(solution)/shard_map/ppermute | solution.py:74
  148.2 8.5 %scaled_gradient.1 = (f32[512,768]{1,0:T(8,128)}, bf16[512,768]{1,0:T(8,128)(2,1)}) custom-call(s32[4]{0:T(128)S(1)} %copy-done.34, bf16[2,512,1536]{2,1,0:T(8,128)(2,1)} %copy-done.49, bf16[2,512,1152]{2,1,0:T(8,128)(2,1)} %get-tuple-element.195.dq_ref, bf16[192,1536]{1,0:T(8,128)(2,1)S(1)} %copy-done.29, bf16[192,1536]{1,0:T(8,128)(2,1)} %collective-permute-done.3.rest_1_, ...), custom_call_target="tpu_custom_call" | custom-call | flops 4227858432 | bytes 16777216 | tf_op jit(solution)/shard_map/scaled_gradient/pallas_call | solution.py:799
  163.0 2.8 %collective-permute-start.37 = (bf16[48,1280]{1,0:T(8,128)(2,1)}, bf16[48,1280]{1,0:T(8,128)(2,1)}, u32[]{:S(2)}, u32[]{:S(2)}) collective-permute-start(bf16[48,1280]{1,0:T(8,128)(2,1)} %get-tuple-element.241), channel_id=1, source_target_pairs={{4,0},{5,1},{6,2},{7,3},{8,4},{9,5},{10,6},{11,7},{12,8},{13,9},{1... | collective-permute-start | bytes 368648 | tf_op jit(solution)/shard_map/ppermute | solution.py:74
  165.9 4.2 %all-to-all-start.1 = ((bf16[16,48,240]{2,1,0:T(8,128)(2,1)}), bf16[16,48,240]{2,1,0:T(8,128)(2,1)}, u32[]{:S(2)}, u32[]{:S(2)}) async-start(bf16[16,48,240]{2,1,0:T(8,128)(2,1)} %copy-done.16), calls=%async_computation.1 | async-start | bytes 786432 | tf_op jit(solution)/shard_map/all_to_all | solution.py:1105
  172.2 2.0 add_convert_fusion.12.qkv_ref.own_ref
  176.8 4.1 %token_gradient.1 = f32[512,768]{1,0:T(8,128)} custom-call(bf16[512,768]{1,0:T(8,128)(2,1)S(1)} %copy-done.3, bf16[512,768]{1,0:T(8,128)(2,1)S(1)} %copy-done.7, f32[512,768]{1,0:T(8,128)S(1)} %copy-done.17, bf16[512,768]{1,0:T(8,128)(2,1)} %collective-permute-done.40.recv_ref), custom_call_target="tpu_custom_call" | custom-call | flops 7864320 | bytes 5505024 | tf_op jit(solution)/shard_map/token_gradient/pallas_call | solution.py:927
  185.7 2.1 %finish_out.1.refs_7_ = f32[240,768]{1,0:T(8,128)} custom-call(bf16[16,48,240]{2,1,0:T(8,128)(2,1)} %all-to-all-done.1.in_ref), custom_call_target="tpu_custom_call" | custom-call | bytes 1105920 | tf_op jit(solution)/shard_map/finish_out/pallas_call | solution.py:404
  187.9 2.2 %collective-permute-start.43 = (f32[8,128]{1,0:T(8,128)S(1)}, f32[8,128]{1,0:T(8,128)S(1)}, u32[]{:S(2)}, u32[]{:S(2)}) collective-permute-start(f32[8,128]{1,0:T(8,128)S(1)} %add.204), channel_id=1, source_target_pairs={{0,4},{1,5},{2,6},{3,7},{4,0},{5,1},{6,2},{7,3},{8,12},{9,13},{10,... | collective-permute-start | bytes 12296 | tf_op jit(solution)/shard_map/ppermute | solution.py:101
  191.9 2.2 %finish_mlp.1._ = f32[48,5376]{1,0:T(8,128)} custom-call(s32[4]{0:T(128)S(1)} %copy-done.34, bf16[48,1536]{1,0:T(8,128)(2,1)S(1)} %copy-done.19, bf16[48,1536]{1,0:T(8,128)(2,1)S(1)} %copy-done.32, f32[48,128]{1,0:T(8,128)S(1)} %pad_convert_fusion.vec_ref), custom_call_target="tpu_custom_call" | custom-call | flops 294912 | bytes 1179648 | tf_op jit(solution)/shard_map/finish_mlp/pallas_call | solution.py:425
  194.2 2.2 %collective-permute-start.44 = (f32[8,128]{1,0:T(8,128)S(1)}, f32[8,128]{1,0:T(8,128)S(1)}, u32[]{:S(2)}, u32[]{:S(2)}) collective-permute-start(f32[8,128]{1,0:T(8,128)S(1)} %add.205), channel_id=1, source_target_pairs={{0,8},{1,9},{2,10},{3,11},{4,12},{5,13},{6,14},{7,15},{8,0},{9,1},... | collective-permute-start | bytes 12296 | tf_op jit(solution)/shard_map/ppermute | solution.py:101
  196.4 2.4 %finish_qkv.1.refs_3_ = f32[48,5376]{1,0:T(8,128)} custom-call(s32[4]{0:T(128)S(1)} %copy-done.34, bf16[48,1280]{1,0:T(8,128)(2,1)} %add_convert_fusion.12.qkv_ref.own_ref, bf16[48,1280]{1,0:T(8,128)(2,1)S(1)} %collective-permute-done.45.swap_ref, f32[48,128]{1,0:T(8,128)S(1)} %pad_convert_fusion.vec_ref, ...), custom_call_target="tpu_custom_call", output_to_operand_aliasing={{}: (4, {})} | custom-call | flops 221184 | bytes 884736 | tf_op jit(solution)/shard_map/finish_qkv/pallas_call | solution.py:451
  200.1 4.6 %optimize.1 = (f32[4,48]{1,0:T(4,128)}, f32[1,1]{1,0:T(1,128)}, f32[48,5376]{1,0:T(8,128)}, f32[48,5376]{1,0:T(8,128)}, f32[48,5376]{1,0:T(8,128)}, /*index=5*/f...) custom-call(f32[8,128]{1,0:T(8,128)S(1)} %add.206.total_ref, ...), custom_call_target="tpu_custom_call" | custom-call | flops 5160960 | bytes 13418496 | tf_op jit(solution)/shard_map/optimize/pallas_call | solution.py:977
  (230 shorter events, 47.6 us)
Async XLA Ops:
  0.6 35.3 %collective-permute-start.8 = (bf16[512,768]{1,0:T(8,128)(2,1)}, bf16[512,768]{1,0:T(8,128)(2,1)S(1)}, u32[]{:S(2)}, u32[]{:S(2)}) collective-permute-start(bf16[512,768]{1,0:T(8,128)(2,1)} %c_ref.1), channel_id=1, source_target_pairs={{0,16},{16,0},{1,17},{17,1},{2,18},{18,2},{3,19},{19,3},{4,20},{20... | collective-permute-start | bytes 2359304 | tf_op jit(solution)/shard_map/ppermute | solution.py:85
  3.6 35.1 %collective-permute-start.7 = (bf16[512,768]{1,0:T(8,128)(2,1)}, bf16[512,768]{1,0:T(8,128)(2,1)}, u32[]{:S(2)}, u32[]{:S(2)}) collective-permute-start(bf16[512,768]{1,0:T(8,128)(2,1)} %t_ref.1), channel_id=1, source_target_pairs={{0,16},{16,0},{1,17},{17,1},{2,18},{18,2},{3,19},{19,3},{4,20},{20... | collective-permute-start | bytes 2359304 | tf_op jit(solution)/shard_map/ppermute | solution.py:85
  6.5 11.2 %collective-permute-start = (bf16[48,1536]{1,0:T(8,128)(2,1)S(1)}, bf16[48,1536]{1,0:T(8,128)(2,1)S(1)}, u32[]{:S(2)}, u32[]{:S(2)}) collective-permute-start(bf16[48,1536]{1,0:T(8,128)(2,1)S(1)} %get-tuple-element.125.refs_0_), channel_id=1, source_target_pairs={{4,0},{5,1},{6,2},{7,3},{8,4},{9,5},{10,6},{11,7},{12,8},{13,9},{1... | collective-permute-start | bytes 442376 | tf_op jit(solution)/shard_map/ppermute | solution.py:74
  10.6 14.8 %collective-permute-start.1 = (bf16[48,1536]{1,0:T(8,128)(2,1)S(1)}, bf16[48,1536]{1,0:T(8,128)(2,1)S(1)}, u32[]{:S(2)}, u32[]{:S(2)}) collective-permute-start(bf16[48,1536]{1,0:T(8,128)(2,1)S(1)} %get-tuple-element.125.refs_0_), channel_id=1, source_target_pairs={{8,0},{9,1},{10,2},{11,3},{12,4},{13,5},{14,6},{15,7},{0,8},{1,9},... | collective-permute-start | bytes 442376 | tf_op jit(solution)/shard_map/ppermute | solution.py:74
  10.6 14.8 %collective-permute-start.2 = (bf16[48,1536]{1,0:T(8,128)(2,1)S(1)}, bf16[48,1536]{1,0:T(8,128)(2,1)S(1)}, u32[]{:S(2)}, u32[]{:S(2)}) collective-permute-start(bf16[48,1536]{1,0:T(8,128)(2,1)S(1)} %get-tuple-element.125.refs_0_), channel_id=1, source_target_pairs={{12,0},{13,1},{14,2},{15,3},{0,4},{1,5},{2,6},{3,7},{4,8},{5,9},{6... | collective-permute-start | bytes 442376 | tf_op jit(solution)/shard_map/ppermute | solution.py:74
  12.5 25.5 %all-to-all-start = ((bf16[16,48,240]{2,1,0:T(8,128)(2,1)}), bf16[16,48,240]{2,1,0:T(8,128)(2,1)S(1)}, u32[]{:S(2)}, u32[]{:S(2)}) async-start(bf16[16,48,240]{2,1,0:T(8,128)(2,1)} %split_out.1), calls=%async_computation | async-start | bytes 786432 | tf_op jit(solution)/shard_map/all_to_all | solution.py:1021
  25.4 18.9 %collective-permute-start.3 = (bf16[192,1536]{1,0:T(8,128)(2,1)S(1)}, bf16[192,1536]{1,0:T(8,128)(2,1)}, u32[]{:S(2)}, u32[]{:S(2)}) collective-permute-start(bf16[192,1536]{1,0:T(8,128)(2,1)S(1)} %stack.23.rest_0_), channel_id=1, source_target_pairs={{2,0},{3,1},{0,2},{1,3},{6,4},{7,5},{4,6},{5,7},{10,8},{11,9},{8,1... | collective-permute-start | bytes 1769480 | tf_op jit(solution)/shard_map/ppermute | solution.py:78
  26.5 17.7 %collective-permute-start.4 = (bf16[48,1280]{1,0:T(8,128)(2,1)S(1)}, bf16[48,1280]{1,0:T(8,128)(2,1)S(1)}, u32[]{:S(2)}, u32[]{:S(2)}) collective-permute-start(bf16[48,1280]{1,0:T(8,128)(2,1)S(1)} %get-tuple-element.130.refs_0_), channel_id=1, source_target_pairs={{4,0},{5,1},{6,2},{7,3},{8,4},{9,5},{10,6},{11,7},{12,8},{13,9},{1... | collective-permute-start | bytes 368648 | tf_op jit(solution)/shard_map/ppermute | solution.py:74
  26.5 17.7 %collective-permute-start.5 = (bf16[48,1280]{1,0:T(8,128)(2,1)S(1)}, bf16[48,1280]{1,0:T(8,128)(2,1)S(1)}, u32[]{:S(2)}, u32[]{:S(2)}) collective-permute-start(bf16[48,1280]{1,0:T(8,128)(2,1)S(1)} %get-tuple-element.130.refs_0_), channel_id=1, source_target_pairs={{8,0},{9,1},{10,2},{11,3},{12,4},{13,5},{14,6},{15,7},{0,8},{1,9},... | collective-permute-start | bytes 368648 | tf_op jit(solution)/shard_map/ppermute | solution.py:74
  44.9 20.6 %collective-permute-start.9 = (bf16[192,1280]{1,0:T(8,128)(2,1)S(1)}, bf16[192,1280]{1,0:T(8,128)(2,1)S(1)}, u32[]{:S(2)}, u32[]{:S(2)}) collective-permute-start(bf16[192,1280]{1,0:T(8,128)(2,1)S(1)} %stack.24.rest_0_.rest_4_), channel_id=1, source_target_pairs={{2,0},{3,1},{0,2},{1,3},{6,4},{7,5},{4,6},{5,7},{10,8},{11,9},{8,1... | collective-permute-start | bytes 1474568 | tf_op jit(solution)/shard_map/ppermute | solution.py:78
  46.4 16.9 %collective-permute-start.10 = (bf16[48,1920]{1,0:T(8,128)(2,1)S(1)}, bf16[48,1920]{1,0:T(8,128)(2,1)S(1)}, u32[]{:S(2)}, u32[]{:S(2)}) collective-permute-start(bf16[48,1920]{1,0:T(8,128)(2,1)S(1)} %pack_out.1.refs_0_), channel_id=1, source_target_pairs={{4,0},{5,1},{6,2},{7,3},{8,4},{9,5},{10,6},{11,7},{12,8},{13,9},{1... | collective-permute-start | bytes 552968 | tf_op jit(solution)/shard_map/ppermute | solution.py:74
  50.0 15.6 %collective-permute-start.11 = (bf16[48,1920]{1,0:T(8,128)(2,1)S(1)}, bf16[48,1920]{1,0:T(8,128)(2,1)S(1)}, u32[]{:S(2)}, u32[]{:S(2)}) collective-permute-start(bf16[48,1920]{1,0:T(8,128)(2,1)S(1)} %pack_out.1.refs_0_), channel_id=1, source_target_pairs={{8,0},{9,1},{10,2},{11,3},{12,4},{13,5},{14,6},{15,7},{0,8},{1,9},... | collective-permute-start | bytes 552968 | tf_op jit(solution)/shard_map/ppermute | solution.py:74
  50.0 15.6 %collective-permute-start.12 = (bf16[48,1920]{1,0:T(8,128)(2,1)S(1)}, bf16[48,1920]{1,0:T(8,128)(2,1)S(1)}, u32[]{:S(2)}, u32[]{:S(2)}) collective-permute-start(bf16[48,1920]{1,0:T(8,128)(2,1)S(1)} %pack_out.1.refs_0_), channel_id=1, source_target_pairs={{12,0},{13,1},{14,2},{15,3},{0,4},{1,5},{2,6},{3,7},{4,8},{5,9},{6... | collective-permute-start | bytes 552968 | tf_op jit(solution)/shard_map/ppermute | solution.py:74
  65.6 22.2 %collective-permute-start.15 = (bf16[192,1920]{1,0:T(8,128)(2,1)S(1)}, bf16[192,1920]{1,0:T(8,128)(2,1)S(1)}, u32[]{:S(2)}, u32[]{:S(2)}) collective-permute-start(bf16[192,1920]{1,0:T(8,128)(2,1)S(1)} %stack.25.rest_0_), channel_id=1, source_target_pairs={{2,0},{3,1},{0,2},{1,3},{6,4},{7,5},{4,6},{5,7},{10,8},{11,9},{8,1... | collective-permute-start | bytes 2211848 | tf_op jit(solution)/shard_map/ppermute | solution.py:78
  66.2 21.7 %collective-permute-start.16 = (bf16[192,1920]{1,0:T(8,128)(2,1)S(1)}, bf16[192,1920]{1,0:T(8,128)(2,1)}, u32[]{:S(2)}, u32[]{:S(2)}) collective-permute-start(bf16[192,1920]{1,0:T(8,128)(2,1)S(1)} %stack.25.rest_0_), channel_id=1, source_target_pairs={{0,1},{1,0},{2,3},{3,2},{4,5},{5,4},{6,7},{7,6},{8,9},{9,8},{10,11... | collective-permute-start | bytes 2211848 | tf_op jit(solution)/shard_map/ppermute | solution.py:82
  94.4 18.6 %collective-permute-start.22 = (bf16[192,1920]{1,0:T(8,128)(2,1)S(1)}, bf16[192,1920]{1,0:T(8,128)(2,1)S(1)}, u32[]{:S(2)}, u32[]{:S(2)}) collective-permute-start(bf16[192,1920]{1,0:T(8,128)(2,1)S(1)} %add_convert_fusion.1), channel_id=1, source_target_pairs={{2,0},{3,1},{0,2},{1,3},{6,4},{7,5},{4,6},{5,7},{10,8},{11,9},{8,1... | collective-permute-start | bytes 2211848 | tf_op jit(solution)/shard_map/ppermute | solution.py:78
  113.0 26.5 %collective-permute-start.28 = (bf16[512,768]{1,0:T(8,128)(2,1)S(1)}, bf16[512,768]{1,0:T(8,128)(2,1)S(1)}, u32[]{:S(2)}, u32[]{:S(2)}) collective-permute-start(bf16[512,768]{1,0:T(8,128)(2,1)S(1)} %get-tuple-element.184), channel_id=1, source_target_pairs={{0,16},{16,0},{1,17},{17,1},{2,18},{18,2},{3,19},{19,3},{4,20},{20... | collective-permute-start | bytes 2359304 | tf_op jit(solution)/shard_map/ppermute | solution.py:85
  114.8 24.8 %collective-permute-start.23 = (bf16[48,1920]{1,0:T(8,128)(2,1)S(1)}, bf16[48,1920]{1,0:T(8,128)(2,1)S(1)}, u32[]{:S(2)}, u32[]{:S(2)}) collective-permute-start(bf16[48,1920]{1,0:T(8,128)(2,1)S(1)} %get-tuple-element.237), channel_id=1, source_target_pairs={{12,0},{13,1},{14,2},{15,3},{0,4},{1,5},{2,6},{3,7},{4,8},{5,9},{6... | collective-permute-start | bytes 552968 | tf_op jit(solution)/shard_map/ppermute | solution.py:74
  115.7 23.8 %collective-permute-start.24 = (bf16[48,1920]{1,0:T(8,128)(2,1)S(1)}, bf16[48,1920]{1,0:T(8,128)(2,1)S(1)}, u32[]{:S(2)}, u32[]{:S(2)}) collective-permute-start(bf16[48,1920]{1,0:T(8,128)(2,1)S(1)} %get-tuple-element.236), channel_id=1, source_target_pairs={{8,0},{9,1},{10,2},{11,3},{12,4},{13,5},{14,6},{15,7},{0,8},{1,9},... | collective-permute-start | bytes 552968 | tf_op jit(solution)/shard_map/ppermute | solution.py:74
  117.7 21.8 %collective-permute-start.25 = (bf16[48,1920]{1,0:T(8,128)(2,1)S(1)}, bf16[48,1920]{1,0:T(8,128)(2,1)S(1)}, u32[]{:S(2)}, u32[]{:S(2)}) collective-permute-start(bf16[48,1920]{1,0:T(8,128)(2,1)S(1)} %get-tuple-element.235), channel_id=1, source_target_pairs={{4,0},{5,1},{6,2},{7,3},{8,4},{9,5},{10,6},{11,7},{12,8},{13,9},{1... | collective-permute-start | bytes 552968 | tf_op jit(solution)/shard_map/ppermute | solution.py:74
  120.7 18.9 %collective-permute-start.27 = (bf16[192,1536]{1,0:T(8,128)(2,1)S(1)}, bf16[192,1536]{1,0:T(8,128)(2,1)S(1)}, u32[]{:S(2)}, u32[]{:S(2)}) collective-permute-start(bf16[192,1536]{1,0:T(8,128)(2,1)S(1)} %add_convert_fusion.2), channel_id=1, source_target_pairs={{2,0},{3,1},{0,2},{1,3},{6,4},{7,5},{4,6},{5,7},{10,8},{11,9},{8,1... | collective-permute-start | bytes 1769480 | tf_op jit(solution)/shard_map/ppermute | solution.py:78
  141.5 15.2 %collective-permute-start.34 = (bf16[48,1920]{1,0:T(8,128)(2,1)S(1)}, bf16[48,1920]{1,0:T(8,128)(2,1)S(1)}, u32[]{:S(2)}, u32[]{:S(2)}) collective-permute-start(bf16[48,1920]{1,0:T(8,128)(2,1)S(1)} %add_convert_fusion.4.own_ref.out_ref), channel_id=1, source_target_pairs={{0,16},{16,0},{1,17},{17,1},{2,18},{18,2},{3,19},{19,3},{4,20},{20... | collective-permute-start | bytes 552968 | tf_op jit(solution)/shard_map/ppermute | solution.py:85
  143.5 16.3 %collective-permute-start.30 = (bf16[192,1280]{1,0:T(8,128)(2,1)S(1)}, bf16[192,1280]{1,0:T(8,128)(2,1)S(1)}, u32[]{:S(2)}, u32[]{:S(2)}) collective-permute-start(bf16[192,1280]{1,0:T(8,128)(2,1)S(1)} %add_convert_fusion.3), channel_id=1, source_target_pairs={{2,0},{3,1},{0,2},{1,3},{6,4},{7,5},{4,6},{5,7},{10,8},{11,9},{8,1... | collective-permute-start | bytes 1474568 | tf_op jit(solution)/shard_map/ppermute | solution.py:78
  144.3 15.6 %collective-permute-start.31 = (bf16[48,1536]{1,0:T(8,128)(2,1)S(1)}, bf16[48,1536]{1,0:T(8,128)(2,1)S(1)}, u32[]{:S(2)}, u32[]{:S(2)}) collective-permute-start(bf16[48,1536]{1,0:T(8,128)(2,1)S(1)} %get-tuple-element.240), channel_id=1, source_target_pairs={{12,0},{13,1},{14,2},{15,3},{0,4},{1,5},{2,6},{3,7},{4,8},{5,9},{6... | collective-permute-start | bytes 442376 | tf_op jit(solution)/shard_map/ppermute | solution.py:74
  144.3 15.5 %collective-permute-start.32 = (bf16[48,1536]{1,0:T(8,128)(2,1)S(1)}, bf16[48,1536]{1,0:T(8,128)(2,1)S(1)}, u32[]{:S(2)}, u32[]{:S(2)}) collective-permute-start(bf16[48,1536]{1,0:T(8,128)(2,1)S(1)} %get-tuple-element.239), channel_id=1, source_target_pairs={{8,0},{9,1},{10,2},{11,3},{12,4},{13,5},{14,6},{15,7},{0,8},{1,9},... | collective-permute-start | bytes 442376 | tf_op jit(solution)/shard_map/ppermute | solution.py:74
  144.9 15.0 %collective-permute-start.33 = (bf16[48,1536]{1,0:T(8,128)(2,1)S(1)}, bf16[48,1536]{1,0:T(8,128)(2,1)S(1)}, u32[]{:S(2)}, u32[]{:S(2)}) collective-permute-start(bf16[48,1536]{1,0:T(8,128)(2,1)S(1)} %get-tuple-element.238), channel_id=1, source_target_pairs={{4,0},{5,1},{6,2},{7,3},{8,4},{9,5},{10,6},{11,7},{12,8},{13,9},{1... | collective-permute-start | bytes 442376 | tf_op jit(solution)/shard_map/ppermute | solution.py:74
  156.7 20.1 %collective-permute-start.40 = (bf16[512,768]{1,0:T(8,128)(2,1)}, bf16[512,768]{1,0:T(8,128)(2,1)}, u32[]{:S(2)}, u32[]{:S(2)}) collective-permute-start(bf16[512,768]{1,0:T(8,128)(2,1)} %get-tuple-element.210), channel_id=1, source_target_pairs={{0,16},{16,0},{1,17},{17,1},{2,18},{18,2},{3,19},{19,3},{4,20},{20... | collective-permute-start | bytes 2359304 | tf_op jit(solution)/shard_map/ppermute | solution.py:85
  160.9 11.3 %collective-permute-start.35 = (bf16[48,1280]{1,0:T(8,128)(2,1)}, bf16[48,1280]{1,0:T(8,128)(2,1)}, u32[]{:S(2)}, u32[]{:S(2)}) collective-permute-start(bf16[48,1280]{1,0:T(8,128)(2,1)} %get-tuple-element.243), channel_id=1, source_target_pairs={{12,0},{13,1},{14,2},{15,3},{0,4},{1,5},{2,6},{3,7},{4,8},{5,9},{6... | collective-permute-start | bytes 368648 | tf_op jit(solution)/shard_map/ppermute | solution.py:74
  161.5 10.7 %collective-permute-start.36 = (bf16[48,1280]{1,0:T(8,128)(2,1)}, bf16[48,1280]{1,0:T(8,128)(2,1)}, u32[]{:S(2)}, u32[]{:S(2)}) collective-permute-start(bf16[48,1280]{1,0:T(8,128)(2,1)} %get-tuple-element.242), channel_id=1, source_target_pairs={{8,0},{9,1},{10,2},{11,3},{12,4},{13,5},{14,6},{15,7},{0,8},{1,9},... | collective-permute-start | bytes 368648 | tf_op jit(solution)/shard_map/ppermute | solution.py:74
  165.9 19.9 %all-to-all-start.1 = ((bf16[16,48,240]{2,1,0:T(8,128)(2,1)}), bf16[16,48,240]{2,1,0:T(8,128)(2,1)}, u32[]{:S(2)}, u32[]{:S(2)}) async-start(bf16[16,48,240]{2,1,0:T(8,128)(2,1)} %copy-done.16), calls=%async_computation.1 | async-start | bytes 786432 | tf_op jit(solution)/shard_map/all_to_all | solution.py:1105
  171.6 9.3 %collective-permute-start.39 = (bf16[48,1536]{1,0:T(8,128)(2,1)S(1)}, bf16[48,1536]{1,0:T(8,128)(2,1)S(1)}, u32[]{:S(2)}, u32[]{:S(2)}) collective-permute-start(bf16[48,1536]{1,0:T(8,128)(2,1)S(1)} %add_convert_fusion.8.mlp_ref.own_ref), channel_id=1, source_target_pairs={{0,16},{16,0},{1,17},{17,1},{2,18},{18,2},{3,19},{19,3},{4,20},{20... | collective-permute-start | bytes 442376 | tf_op jit(solution)/shard_map/ppermute | solution.py:85
  181.6 14.8 %collective-permute-start.45 = (bf16[48,1280]{1,0:T(8,128)(2,1)}, bf16[48,1280]{1,0:T(8,128)(2,1)S(1)}, u32[]{:S(2)}, u32[]{:S(2)}) collective-permute-start(bf16[48,1280]{1,0:T(8,128)(2,1)} %add_convert_fusion.12.qkv_ref.own_ref), channel_id=1, source_target_pairs={{0,16},{16,0},{1,17},{17,1},{2,18},{18,2},{3,19},{19,3},{4,20},{20... | collective-permute-start | bytes 368648 | tf_op jit(solution)/shard_map/ppermute | solution.py:85
  (78 other events, 543.0 us)

commit v7 on v6

--- a/solution.py
+++ b/solution.py
@@ -2,6 +2,7 @@
 
 import jax
 import jax.numpy as jnp
+import numpy as np
 from jax import lax
 from jax.experimental import pallas as pl
 from jax.experimental.pallas import tpu as pltpu
@@ -1058,8 +1059,8 @@
     out_col = stack([out_piece] + out_z)
     out_y = y_all(out_col)
     out_core = core_all([out_col])
-    lane = jnp.arange(2 * PAIR) // HD
-    block = jnp.where(lane[:, None] == lane[None, :], 1.0 / HD, 0.0).astype(BF16)
+    lane = np.arange(2 * PAIR) // HD
+    block = jnp.asarray(np.where(lane[:, None] == lane[None, :], 1.0 / HD, 0.0), BF16)
     *saved, att, probs, gains, g_own, g_other = attention_forward(
         plan, x_own, x_other, qkv_pieces, (image_ids[None, :], other_ids[None, :]), block,
         turned, g_own, g_other,

time: 206 us -> 206 us (level)
  transfers between devices with their start and end apart: 48 -> 48, of which waited for: 8 -> 8; matrix products, arithmetic and copies ran while one was open for 5% -> 4% of each run, Pallas kernels for 43% -> 43%
where the time goes in v7:
time: 206 us; the launch traced here: 205 us
  Pallas kernels  92.4 us (45%)
  starting transfers between devices  71.7 us (35%)
  waiting for transfers between devices  18.5 us (9%)
  other arithmetic  10.7 us (5%)
  local copies, waits for them, and re-layouts  10 us (5%)
    ppermute x18, starting transfers between devices, from_z(): return lax.ppermute(a, 'fsdp', pairs)  35.8 us
    pallas_call x1, Pallas kernels, attention_backward(): pl.pallas_call(kernel, grid=(PAIRS,), in_specs=[smem(), pl.BlockSpec((1,...  17.2 us
    pallas_call x1, Pallas kernels, attention_forward(): pl.pallas_call(kernel, grid=(PAIRS,), in_specs=[smem()] + [whole((tok, D)...  16.4 us
    ppermute x9, starting transfers between devices, swap_plane(): return lax.ppermute(a, 'dp', [(i, i ^ 1) for i in range(self.n_dp)])  11.9 us
    pallas_call x1, Pallas kernels, mlp_forward(): pl.pallas_call(kernel, grid=(FH // tile,), in_specs=[smem()] + [whole((to...  11.4 us
    pallas_call x1, Pallas kernels, output_step(): pl.pallas_call(kernel, grid=(2 * per,), in_specs=[smem(), pl.BlockSpec((1...  10.2 us
    ppermute x18, waiting for transfers between devices, from_z(): return lax.ppermute(a, 'fsdp', pairs)  10 us
    unnamed x124, local copies, waits for them, and re-layouts  9.88 us
  transfers between devices with their start and end apart: 48, of which 8 were waited for; matrix products, arithmetic and copies ran while one was open for 4% of the time, Pallas kernels for 43%

profile of v7, /device:TPU:0, one launch (start us, length us, event | category | flops | bytes accessed | tf_op | source)
XLA Modules:
  0.0 204.8 jit_solution(13916293318686389671)
XLA Ops:
  0.6 3.0 %collective-permute-start.8 = (bf16[512,768]{1,0:T(8,128)(2,1)}, bf16[512,768]{1,0:T(8,128)(2,1)S(1)}, u32[]{:S(2)}, u32[]{:S(2)}) collective-permute-start(bf16[512,768]{1,0:T(8,128)(2,1)} %c_ref.1), channel_id=1, source_target_pairs={{0,16},{16,0},{1,17},{17,1},{2,18},{18,2},{3,19},{19,3},{4,20},{20... | collective-permute-start | bytes 2359304 | tf_op jit(solution)/shard_map/ppermute | solution.py:86
  6.5 4.1 %collective-permute-start = (bf16[48,1536]{1,0:T(8,128)(2,1)S(1)}, bf16[48,1536]{1,0:T(8,128)(2,1)S(1)}, u32[]{:S(2)}, u32[]{:S(2)}) collective-permute-start(bf16[48,1536]{1,0:T(8,128)(2,1)S(1)} %get-tuple-element.125.refs_0_), channel_id=1, source_target_pairs={{4,0},{5,1},{6,2},{7,3},{8,4},{9,5},{10,6},{11,7},{12,8},{13,9},{1... | collective-permute-start | bytes 442376 | tf_op jit(solution)/shard_map/ppermute | solution.py:75
  12.5 5.1 %all-to-all-start = ((bf16[16,48,240]{2,1,0:T(8,128)(2,1)}), bf16[16,48,240]{2,1,0:T(8,128)(2,1)S(1)}, u32[]{:S(2)}, u32[]{:S(2)}) async-start(bf16[16,48,240]{2,1,0:T(8,128)(2,1)} %split_out.1), calls=%async_computation | async-start | bytes 786432 | tf_op jit(solution)/shard_map/all_to_all | solution.py:1022
  17.7 7.7 %collective-permute-done.1.refs_2_ = bf16[48,1536]{1,0:T(8,128)(2,1)S(1)} collective-permute-done((bf16[48,1536]{1,0:T(8,128)(2,1)S(1)}, bf16[48,1536]{1,0:T(8,128)(2,1)S(1)}, u32[]{:S(2)}, u32[]{:S(2)}) %collective-permute-start.1) | collective-permute-done | bytes 147488 | tf_op jit(solution)/shard_map/ppermute | solution.py:75
  26.5 9.4 %collective-permute-start.5 = (bf16[48,1280]{1,0:T(8,128)(2,1)S(1)}, bf16[48,1280]{1,0:T(8,128)(2,1)S(1)}, u32[]{:S(2)}, u32[]{:S(2)}) collective-permute-start(bf16[48,1280]{1,0:T(8,128)(2,1)S(1)} %get-tuple-element.130.refs_0_), channel_id=1, source_target_pairs={{8,0},{9,1},{10,2},{11,3},{12,4},{13,5},{14,6},{15,7},{0,8},{1,9},... | collective-permute-start | bytes 368648 | tf_op jit(solution)/shard_map/ppermute | solution.py:75
  36.0 2.0 collective-permute-start.6
  38.8 5.5 %prepare.1 = (bf16[512,768]{1,0:T(8,128)(2,1)}, bf16[512,768]{1,0:T(8,128)(2,1)}, bf16[2,768,1024]{2,1,0:T(8,128)(2,1)}, f32[8,768]{1,0:T(8,128)}) custom-call(s32[4]{0:T(128)} %copy-done.33, bf16[512,768]{1,0:T(8,128)(2,1)} %t_ref.1, bf16[512,768]{1,0:T(8,128)(2,1)} %collective-permute-done.7.tp_ref, bf16[512,768]{1,0:T(8,128)(2,1)} %c_ref.1, ...), custom_call_target="tpu_custom_call" | custom-call | flops 15728640 | bytes 7864320 | tf_op jit(solution)/shard_map/prepare/pallas_call | solution.py:498
  46.4 3.6 %collective-permute-start.10 = (bf16[48,1920]{1,0:T(8,128)(2,1)S(1)}, bf16[48,1920]{1,0:T(8,128)(2,1)S(1)}, u32[]{:S(2)}, u32[]{:S(2)}) collective-permute-start(bf16[48,1920]{1,0:T(8,128)(2,1)S(1)} %pack_out.1.refs_0_), channel_id=1, source_target_pairs={{4,0},{5,1},{6,2},{7,3},{8,4},{9,5},{10,6},{11,7},{12,8},{13,9},{1... | collective-permute-start | bytes 552968 | tf_op jit(solution)/shard_map/ppermute | solution.py:75
  51.8 11.4 %mlp_forward.1 = (bf16[2,512,1536]{2,1,0:T(8,128)(2,1)}, bf16[2,512,1536]{2,1,0:T(8,128)(2,1)}, bf16[384,1920]{1,0:T(8,128)(2,1)}, bf16[384,1920]{1,0:T(8,128)(2,1)}) custom-call(s32[4]{0:T(128)} %copy-done.33, bf16[512,768]{1,0:T(8,128)(2,1)} %get-tuple-element.136.xo_ref, bf16[512,768]{1,0:T(8,128)(2,1)} %get-tuple-element.137.xp_ref, ...), custom_call_target="tpu_custom_call" | custom-call | flops 4831838208 | bytes 9437184 | tf_op jit(solution)/shard_map/mlp_forward/pallas_call | solution.py:543
  63.3 2.3 %collective-permute-done.11.refs_2_ = bf16[48,1920]{1,0:T(8,128)(2,1)S(1)} collective-permute-done((bf16[48,1920]{1,0:T(8,128)(2,1)S(1)}, bf16[48,1920]{1,0:T(8,128)(2,1)S(1)}, u32[]{:S(2)}, u32[]{:S(2)}) %collective-permute-start.11) | collective-permute-done | bytes 184352 | tf_op jit(solution)/shard_map/ppermute | solution.py:75
  68.2 2.1 %collective-permute-done.17 = s32[512]{0:T(512)S(1)} collective-permute-done((s32[512]{0:T(512)S(1)}, s32[512]{0:T(512)S(1)}, u32[]{:S(2)}, u32[]{:S(2)}) %collective-permute-start.17) | collective-permute-done | bytes 2080 | tf_op jit(solution)/shard_map/ppermute | solution.py:86
  71.3 16.4 %attention_forward.1 = (bf16[2,512,768]{2,1,0:T(8,128)(2,1)}, bf16[2,512,384]{2,1,0:T(8,128)(2,1)}, bf16[2,512,768]{2,1,0:T(8,128)(2,1)}, bf16[2,512,768]{2,1,0:...) custom-call(s32[4]{0:T(128)} %copy-done.33, ...), custom_call_target="tpu_custom_call", output_to_operand_aliasing={{7}: (7, {}), {8}: (8, {})} | custom-call | flops 1811939328 | bytes 20971520 | tf_op jit(solution)/shard_map/attention_forward/pallas_call | solution.py:631
  88.4 3.5 %collective-permute-done.21.rest_3_ = bf16[192,1920]{1,0:T(8,128)(2,1)S(1)} collective-permute-done((bf16[192,1920]{1,0:T(8,128)(2,1)S(1)}, bf16[192,1920]{1,0:T(8,128)(2,1)S(1)}, u32[]{:S(2)}, u32[]{:S(2)}) %collective-permute-start.21) | collective-permute-done | bytes 737312 | tf_op jit(solution)/shard_map/ppermute | solution.py:83
  92.4 1.9 add_convert_fusion.1
  98.2 10.2 %output_step.1 = (f32[512,768]{1,0:T(8,128)S(1)}, bf16[512,768]{1,0:T(8,128)(2,1)S(1)}, bf16[2,512,384]{2,1,0:T(8,128)(2,1)S(1)}, bf16[2,512,1536]{2,1,0:T(8,128)(2,1)S(1)}) custom-call(s32[4]{0:T(128)S(1)} %copy-done.34, bf16[2,512,384]{2,1,0:T(8,128)(2,1)S(1)} %copy-done.41, bf16[2,512,1536]{2,1,0:T(8,128)(2,1)} %get-tuple-element.162.mix_ref, ...), custom_call_target="tpu_custom_call" | custom-call | flops 6039797760 | bytes 20971520 | tf_op jit(solution)/shard_map/output_step/pallas_call | solution.py:716
  108.4 3.3 %mlp_gradient.1 = (bf16[384,1536]{1,0:T(8,128)(2,1)S(1)}, bf16[384,1536]{1,0:T(8,128)(2,1)S(1)}) custom-call(bf16[2,768,1024]{2,1,0:T(8,128)(2,1)S(1)} %copy-done.6, bf16[2,512,1536]{2,1,0:T(8,128)(2,1)S(1)} %get-tuple-element.167.d_ref.dm_ref), custom_call_target="tpu_custom_call" | custom-call | flops 2415919104 | bytes 8388608 | tf_op jit(solution)/shard_map/mlp_gradient/pallas_call | solution.py:758
  115.7 2.0 collective-permute-start.24
  117.7 2.8 %collective-permute-start.25 = (bf16[48,1920]{1,0:T(8,128)(2,1)S(1)}, bf16[48,1920]{1,0:T(8,128)(2,1)S(1)}, u32[]{:S(2)}, u32[]{:S(2)}) collective-permute-start(bf16[48,1920]{1,0:T(8,128)(2,1)S(1)} %get-tuple-element.235), channel_id=1, source_target_pairs={{4,0},{5,1},{6,2},{7,3},{8,4},{9,5},{10,6},{11,7},{12,8},{13,9},{1... | collective-permute-start | bytes 552968 | tf_op jit(solution)/shard_map/ppermute | solution.py:75
  122.3 17.2 %attention_backward.1 = (bf16[384,1280]{1,0:T(8,128)(2,1)S(1)}, bf16[384,1280]{1,0:T(8,128)(2,1)S(1)}, bf16[2,512,1152]{2,1,0:T(8,128)(2,1)}) custom-call(s32[4]{0:T(128)S(1)} %copy-done.34, bf16[2,768,1024]{2,1,0:T(8,128)(2,1)} %get-tuple-element.138.ct_ref.xt_ref, bf16[2,512,768]{2,1,0:T(8,128)(2,1)S(1)} %copy-done.39, ...), custom_call_target="tpu_custom_call" | custom-call | flops 7247757312 | bytes 25165824 | tf_op jit(solution)/shard_map/attention_backward/pallas_call | solution.py:891
  139.6 1.8 add_convert_fusion.4.own_ref.out_ref
  144.8 3.3 %collective-permute-start.33 = (bf16[48,1536]{1,0:T(8,128)(2,1)S(1)}, bf16[48,1536]{1,0:T(8,128)(2,1)S(1)}, u32[]{:S(2)}, u32[]{:S(2)}) collective-permute-start(bf16[48,1536]{1,0:T(8,128)(2,1)S(1)} %get-tuple-element.238), channel_id=1, source_target_pairs={{4,0},{5,1},{6,2},{7,3},{8,4},{9,5},{10,6},{11,7},{12,8},{13,9},{1... | collective-permute-start | bytes 442376 | tf_op jit(solution)/shard_map/ppermute | solution.py:75
  148.1 8.5 %scaled_gradient.1 = (f32[512,768]{1,0:T(8,128)}, bf16[512,768]{1,0:T(8,128)(2,1)}) custom-call(s32[4]{0:T(128)S(1)} %copy-done.34, bf16[2,512,1536]{2,1,0:T(8,128)(2,1)} %copy-done.49, bf16[2,512,1152]{2,1,0:T(8,128)(2,1)} %get-tuple-element.195.dq_ref, bf16[192,1536]{1,0:T(8,128)(2,1)S(1)} %copy-done.29, bf16[192,1536]{1,0:T(8,128)(2,1)} %collective-permute-done.3.rest_1_, ...), custom_call_target="tpu_custom_call" | custom-call | flops 4227858432 | bytes 16777216 | tf_op jit(solution)/shard_map/scaled_gradient/pallas_call | solution.py:800
  163.0 2.8 %collective-permute-start.37 = (bf16[48,1280]{1,0:T(8,128)(2,1)}, bf16[48,1280]{1,0:T(8,128)(2,1)}, u32[]{:S(2)}, u32[]{:S(2)}) collective-permute-start(bf16[48,1280]{1,0:T(8,128)(2,1)} %get-tuple-element.241), channel_id=1, source_target_pairs={{4,0},{5,1},{6,2},{7,3},{8,4},{9,5},{10,6},{11,7},{12,8},{13,9},{1... | collective-permute-start | bytes 368648 | tf_op jit(solution)/shard_map/ppermute | solution.py:75
  165.8 4.2 %all-to-all-start.1 = ((bf16[16,48,240]{2,1,0:T(8,128)(2,1)}), bf16[16,48,240]{2,1,0:T(8,128)(2,1)}, u32[]{:S(2)}, u32[]{:S(2)}) async-start(bf16[16,48,240]{2,1,0:T(8,128)(2,1)} %copy-done.16), calls=%async_computation.1 | async-start | bytes 786432 | tf_op jit(solution)/shard_map/all_to_all | solution.py:1106
  172.1 2.0 add_convert_fusion.12.qkv_ref.own_ref
  176.8 4.1 %token_gradient.1 = f32[512,768]{1,0:T(8,128)} custom-call(bf16[512,768]{1,0:T(8,128)(2,1)S(1)} %copy-done.3, bf16[512,768]{1,0:T(8,128)(2,1)S(1)} %copy-done.7, f32[512,768]{1,0:T(8,128)S(1)} %copy-done.17, bf16[512,768]{1,0:T(8,128)(2,1)} %collective-permute-done.40.recv_ref), custom_call_target="tpu_custom_call" | custom-call | flops 7864320 | bytes 5505024 | tf_op jit(solution)/shard_map/token_gradient/pallas_call | solution.py:928
  185.7 2.1 %finish_out.1.refs_7_ = f32[240,768]{1,0:T(8,128)} custom-call(bf16[16,48,240]{2,1,0:T(8,128)(2,1)} %all-to-all-done.1.in_ref), custom_call_target="tpu_custom_call" | custom-call | bytes 1105920 | tf_op jit(solution)/shard_map/finish_out/pallas_call | solution.py:405
  187.9 2.2 %collective-permute-start.43 = (f32[8,128]{1,0:T(8,128)S(1)}, f32[8,128]{1,0:T(8,128)S(1)}, u32[]{:S(2)}, u32[]{:S(2)}) collective-permute-start(f32[8,128]{1,0:T(8,128)S(1)} %add.195), channel_id=1, source_target_pairs={{0,4},{1,5},{2,6},{3,7},{4,0},{5,1},{6,2},{7,3},{8,12},{9,13},{10,... | collective-permute-start | bytes 12296 | tf_op jit(solution)/shard_map/ppermute | solution.py:102
  191.9 2.2 %finish_mlp.1._ = f32[48,5376]{1,0:T(8,128)} custom-call(s32[4]{0:T(128)S(1)} %copy-done.34, bf16[48,1536]{1,0:T(8,128)(2,1)S(1)} %copy-done.19, bf16[48,1536]{1,0:T(8,128)(2,1)S(1)} %copy-done.31, f32[48,128]{1,0:T(8,128)S(1)} %pad_convert_fusion.vec_ref), custom_call_target="tpu_custom_call" | custom-call | flops 294912 | bytes 1179648 | tf_op jit(solution)/shard_map/finish_mlp/pallas_call | solution.py:426
  194.1 2.2 %collective-permute-start.44 = (f32[8,128]{1,0:T(8,128)S(1)}, f32[8,128]{1,0:T(8,128)S(1)}, u32[]{:S(2)}, u32[]{:S(2)}) collective-permute-start(f32[8,128]{1,0:T(8,128)S(1)} %add.196), channel_id=1, source_target_pairs={{0,8},{1,9},{2,10},{3,11},{4,12},{5,13},{6,14},{7,15},{8,0},{9,1},... | collective-permute-start | bytes 12296 | tf_op jit(solution)/shard_map/ppermute | solution.py:102
  196.3 2.4 %finish_qkv.1.refs_3_ = f32[48,5376]{1,0:T(8,128)} custom-call(s32[4]{0:T(128)S(1)} %copy-done.34, bf16[48,1280]{1,0:T(8,128)(2,1)} %add_convert_fusion.12.qkv_ref.own_ref, bf16[48,1280]{1,0:T(8,128)(2,1)S(1)} %collective-permute-done.45.swap_ref, f32[48,128]{1,0:T(8,128)S(1)} %pad_convert_fusion.vec_ref, ...), custom_call_target="tpu_custom_call", output_to_operand_aliasing={{}: (4, {})} | custom-call | flops 221184 | bytes 884736 | tf_op jit(solution)/shard_map/finish_qkv/pallas_call | solution.py:452
  200.0 4.6 %optimize.1 = (f32[4,48]{1,0:T(4,128)}, f32[1,1]{1,0:T(1,128)}, f32[48,5376]{1,0:T(8,128)}, f32[48,5376]{1,0:T(8,128)}, f32[48,5376]{1,0:T(8,128)}, /*index=5*/f...) custom-call(f32[8,128]{1,0:T(8,128)S(1)} %add.197.total_ref, ...), custom_call_target="tpu_custom_call" | custom-call | flops 5160960 | bytes 13418496 | tf_op jit(solution)/shard_map/optimize/pallas_call | solution.py:978
  (228 shorter events, 47.1 us)
Async XLA Ops:
  0.6 35.3 %collective-permute-start.8 = (bf16[512,768]{1,0:T(8,128)(2,1)}, bf16[512,768]{1,0:T(8,128)(2,1)S(1)}, u32[]{:S(2)}, u32[]{:S(2)}) collective-permute-start(bf16[512,768]{1,0:T(8,128)(2,1)} %c_ref.1), channel_id=1, source_target_pairs={{0,16},{16,0},{1,17},{17,1},{2,18},{18,2},{3,19},{19,3},{4,20},{20... | collective-permute-start | bytes 2359304 | tf_op jit(solution)/shard_map/ppermute | solution.py:86
  3.6 35.1 %collective-permute-start.7 = (bf16[512,768]{1,0:T(8,128)(2,1)}, bf16[512,768]{1,0:T(8,128)(2,1)}, u32[]{:S(2)}, u32[]{:S(2)}) collective-permute-start(bf16[512,768]{1,0:T(8,128)(2,1)} %t_ref.1), channel_id=1, source_target_pairs={{0,16},{16,0},{1,17},{17,1},{2,18},{18,2},{3,19},{19,3},{4,20},{20... | collective-permute-start | bytes 2359304 | tf_op jit(solution)/shard_map/ppermute | solution.py:86
  6.5 11.2 %collective-permute-start = (bf16[48,1536]{1,0:T(8,128)(2,1)S(1)}, bf16[48,1536]{1,0:T(8,128)(2,1)S(1)}, u32[]{:S(2)}, u32[]{:S(2)}) collective-permute-start(bf16[48,1536]{1,0:T(8,128)(2,1)S(1)} %get-tuple-element.125.refs_0_), channel_id=1, source_target_pairs={{4,0},{5,1},{6,2},{7,3},{8,4},{9,5},{10,6},{11,7},{12,8},{13,9},{1... | collective-permute-start | bytes 442376 | tf_op jit(solution)/shard_map/ppermute | solution.py:75
  10.6 14.8 %collective-permute-start.1 = (bf16[48,1536]{1,0:T(8,128)(2,1)S(1)}, bf16[48,1536]{1,0:T(8,128)(2,1)S(1)}, u32[]{:S(2)}, u32[]{:S(2)}) collective-permute-start(bf16[48,1536]{1,0:T(8,128)(2,1)S(1)} %get-tuple-element.125.refs_0_), channel_id=1, source_target_pairs={{8,0},{9,1},{10,2},{11,3},{12,4},{13,5},{14,6},{15,7},{0,8},{1,9},... | collective-permute-start | bytes 442376 | tf_op jit(solution)/shard_map/ppermute | solution.py:75
  10.6 14.8 %collective-permute-start.2 = (bf16[48,1536]{1,0:T(8,128)(2,1)S(1)}, bf16[48,1536]{1,0:T(8,128)(2,1)S(1)}, u32[]{:S(2)}, u32[]{:S(2)}) collective-permute-start(bf16[48,1536]{1,0:T(8,128)(2,1)S(1)} %get-tuple-element.125.refs_0_), channel_id=1, source_target_pairs={{12,0},{13,1},{14,2},{15,3},{0,4},{1,5},{2,6},{3,7},{4,8},{5,9},{6... | collective-permute-start | bytes 442376 | tf_op jit(solution)/shard_map/ppermute | solution.py:75
  12.5 25.5 %all-to-all-start = ((bf16[16,48,240]{2,1,0:T(8,128)(2,1)}), bf16[16,48,240]{2,1,0:T(8,128)(2,1)S(1)}, u32[]{:S(2)}, u32[]{:S(2)}) async-start(bf16[16,48,240]{2,1,0:T(8,128)(2,1)} %split_out.1), calls=%async_computation | async-start | bytes 786432 | tf_op jit(solution)/shard_map/all_to_all | solution.py:1022
  25.4 18.9 %collective-permute-start.3 = (bf16[192,1536]{1,0:T(8,128)(2,1)S(1)}, bf16[192,1536]{1,0:T(8,128)(2,1)}, u32[]{:S(2)}, u32[]{:S(2)}) collective-permute-start(bf16[192,1536]{1,0:T(8,128)(2,1)S(1)} %stack.23.rest_0_), channel_id=1, source_target_pairs={{2,0},{3,1},{0,2},{1,3},{6,4},{7,5},{4,6},{5,7},{10,8},{11,9},{8,1... | collective-permute-start | bytes 1769480 | tf_op jit(solution)/shard_map/ppermute | solution.py:79
  26.5 17.7 %collective-permute-start.4 = (bf16[48,1280]{1,0:T(8,128)(2,1)S(1)}, bf16[48,1280]{1,0:T(8,128)(2,1)S(1)}, u32[]{:S(2)}, u32[]{:S(2)}) collective-permute-start(bf16[48,1280]{1,0:T(8,128)(2,1)S(1)} %get-tuple-element.130.refs_0_), channel_id=1, source_target_pairs={{4,0},{5,1},{6,2},{7,3},{8,4},{9,5},{10,6},{11,7},{12,8},{13,9},{1... | collective-permute-start | bytes 368648 | tf_op jit(solution)/shard_map/ppermute | solution.py:75
  26.5 17.7 %collective-permute-start.5 = (bf16[48,1280]{1,0:T(8,128)(2,1)S(1)}, bf16[48,1280]{1,0:T(8,128)(2,1)S(1)}, u32[]{:S(2)}, u32[]{:S(2)}) collective-permute-start(bf16[48,1280]{1,0:T(8,128)(2,1)S(1)} %get-tuple-element.130.refs_0_), channel_id=1, source_target_pairs={{8,0},{9,1},{10,2},{11,3},{12,4},{13,5},{14,6},{15,7},{0,8},{1,9},... | collective-permute-start | bytes 368648 | tf_op jit(solution)/shard_map/ppermute | solution.py:75
  44.9 20.6 %collective-permute-start.9 = (bf16[192,1280]{1,0:T(8,128)(2,1)S(1)}, bf16[192,1280]{1,0:T(8,128)(2,1)S(1)}, u32[]{:S(2)}, u32[]{:S(2)}) collective-permute-start(bf16[192,1280]{1,0:T(8,128)(2,1)S(1)} %stack.24.rest_0_.rest_4_), channel_id=1, source_target_pairs={{2,0},{3,1},{0,2},{1,3},{6,4},{7,5},{4,6},{5,7},{10,8},{11,9},{8,1... | collective-permute-start | bytes 1474568 | tf_op jit(solution)/shard_map/ppermute | solution.py:79
  46.4 16.9 %collective-permute-start.10 = (bf16[48,1920]{1,0:T(8,128)(2,1)S(1)}, bf16[48,1920]{1,0:T(8,128)(2,1)S(1)}, u32[]{:S(2)}, u32[]{:S(2)}) collective-permute-start(bf16[48,1920]{1,0:T(8,128)(2,1)S(1)} %pack_out.1.refs_0_), channel_id=1, source_target_pairs={{4,0},{5,1},{6,2},{7,3},{8,4},{9,5},{10,6},{11,7},{12,8},{13,9},{1... | collective-permute-start | bytes 552968 | tf_op jit(solution)/shard_map/ppermute | solution.py:75
  50.0 15.6 %collective-permute-start.11 = (bf16[48,1920]{1,0:T(8,128)(2,1)S(1)}, bf16[48,1920]{1,0:T(8,128)(2,1)S(1)}, u32[]{:S(2)}, u32[]{:S(2)}) collective-permute-start(bf16[48,1920]{1,0:T(8,128)(2,1)S(1)} %pack_out.1.refs_0_), channel_id=1, source_target_pairs={{8,0},{9,1},{10,2},{11,3},{12,4},{13,5},{14,6},{15,7},{0,8},{1,9},... | collective-permute-start | bytes 552968 | tf_op jit(solution)/shard_map/ppermute | solution.py:75
  50.0 15.6 %collective-permute-start.12 = (bf16[48,1920]{1,0:T(8,128)(2,1)S(1)}, bf16[48,1920]{1,0:T(8,128)(2,1)S(1)}, u32[]{:S(2)}, u32[]{:S(2)}) collective-permute-start(bf16[48,1920]{1,0:T(8,128)(2,1)S(1)} %pack_out.1.refs_0_), channel_id=1, source_target_pairs={{12,0},{13,1},{14,2},{15,3},{0,4},{1,5},{2,6},{3,7},{4,8},{5,9},{6... | collective-permute-start | bytes 552968 | tf_op jit(solution)/shard_map/ppermute | solution.py:75
  65.6 22.1 %collective-permute-start.15 = (bf16[192,1920]{1,0:T(8,128)(2,1)S(1)}, bf16[192,1920]{1,0:T(8,128)(2,1)S(1)}, u32[]{:S(2)}, u32[]{:S(2)}) collective-permute-start(bf16[192,1920]{1,0:T(8,128)(2,1)S(1)} %stack.25.rest_0_), channel_id=1, source_target_pairs={{2,0},{3,1},{0,2},{1,3},{6,4},{7,5},{4,6},{5,7},{10,8},{11,9},{8,1... | collective-permute-start | bytes 2211848 | tf_op jit(solution)/shard_map/ppermute | solution.py:79
  66.2 21.6 %collective-permute-start.16 = (bf16[192,1920]{1,0:T(8,128)(2,1)S(1)}, bf16[192,1920]{1,0:T(8,128)(2,1)}, u32[]{:S(2)}, u32[]{:S(2)}) collective-permute-start(bf16[192,1920]{1,0:T(8,128)(2,1)S(1)} %stack.25.rest_0_), channel_id=1, source_target_pairs={{0,1},{1,0},{2,3},{3,2},{4,5},{5,4},{6,7},{7,6},{8,9},{9,8},{10,11... | collective-permute-start | bytes 2211848 | tf_op jit(solution)/shard_map/ppermute | solution.py:83
  94.3 18.6 %collective-permute-start.22 = (bf16[192,1920]{1,0:T(8,128)(2,1)S(1)}, bf16[192,1920]{1,0:T(8,128)(2,1)S(1)}, u32[]{:S(2)}, u32[]{:S(2)}) collective-permute-start(bf16[192,1920]{1,0:T(8,128)(2,1)S(1)} %add_convert_fusion.1), channel_id=1, source_target_pairs={{2,0},{3,1},{0,2},{1,3},{6,4},{7,5},{4,6},{5,7},{10,8},{11,9},{8,1... | collective-permute-start | bytes 2211848 | tf_op jit(solution)/shard_map/ppermute | solution.py:79
  113.0 26.6 %collective-permute-start.28 = (bf16[512,768]{1,0:T(8,128)(2,1)S(1)}, bf16[512,768]{1,0:T(8,128)(2,1)S(1)}, u32[]{:S(2)}, u32[]{:S(2)}) collective-permute-start(bf16[512,768]{1,0:T(8,128)(2,1)S(1)} %get-tuple-element.184), channel_id=1, source_target_pairs={{0,16},{16,0},{1,17},{17,1},{2,18},{18,2},{3,19},{19,3},{4,20},{20... | collective-permute-start | bytes 2359304 | tf_op jit(solution)/shard_map/ppermute | solution.py:86
  114.7 24.8 %collective-permute-start.23 = (bf16[48,1920]{1,0:T(8,128)(2,1)S(1)}, bf16[48,1920]{1,0:T(8,128)(2,1)S(1)}, u32[]{:S(2)}, u32[]{:S(2)}) collective-permute-start(bf16[48,1920]{1,0:T(8,128)(2,1)S(1)} %get-tuple-element.237), channel_id=1, source_target_pairs={{12,0},{13,1},{14,2},{15,3},{0,4},{1,5},{2,6},{3,7},{4,8},{5,9},{6... | collective-permute-start | bytes 552968 | tf_op jit(solution)/shard_map/ppermute | solution.py:75
  115.7 23.8 %collective-permute-start.24 = (bf16[48,1920]{1,0:T(8,128)(2,1)S(1)}, bf16[48,1920]{1,0:T(8,128)(2,1)S(1)}, u32[]{:S(2)}, u32[]{:S(2)}) collective-permute-start(bf16[48,1920]{1,0:T(8,128)(2,1)S(1)} %get-tuple-element.236), channel_id=1, source_target_pairs={{8,0},{9,1},{10,2},{11,3},{12,4},{13,5},{14,6},{15,7},{0,8},{1,9},... | collective-permute-start | bytes 552968 | tf_op jit(solution)/shard_map/ppermute | solution.py:75
  117.7 21.8 %collective-permute-start.25 = (bf16[48,1920]{1,0:T(8,128)(2,1)S(1)}, bf16[48,1920]{1,0:T(8,128)(2,1)S(1)}, u32[]{:S(2)}, u32[]{:S(2)}) collective-permute-start(bf16[48,1920]{1,0:T(8,128)(2,1)S(1)} %get-tuple-element.235), channel_id=1, source_target_pairs={{4,0},{5,1},{6,2},{7,3},{8,4},{9,5},{10,6},{11,7},{12,8},{13,9},{1... | collective-permute-start | bytes 552968 | tf_op jit(solution)/shard_map/ppermute | solution.py:75
  120.7 18.9 %collective-permute-start.27 = (bf16[192,1536]{1,0:T(8,128)(2,1)S(1)}, bf16[192,1536]{1,0:T(8,128)(2,1)S(1)}, u32[]{:S(2)}, u32[]{:S(2)}) collective-permute-start(bf16[192,1536]{1,0:T(8,128)(2,1)S(1)} %add_convert_fusion.2), channel_id=1, source_target_pairs={{2,0},{3,1},{0,2},{1,3},{6,4},{7,5},{4,6},{5,7},{10,8},{11,9},{8,1... | collective-permute-start | bytes 1769480 | tf_op jit(solution)/shard_map/ppermute | solution.py:79
  141.5 15.2 %collective-permute-start.34 = (bf16[48,1920]{1,0:T(8,128)(2,1)S(1)}, bf16[48,1920]{1,0:T(8,128)(2,1)S(1)}, u32[]{:S(2)}, u32[]{:S(2)}) collective-permute-start(bf16[48,1920]{1,0:T(8,128)(2,1)S(1)} %add_convert_fusion.4.own_ref.out_ref), channel_id=1, source_target_pairs={{0,16},{16,0},{1,17},{17,1},{2,18},{18,2},{3,19},{19,3},{4,20},{20... | collective-permute-start | bytes 552968 | tf_op jit(solution)/shard_map/ppermute | solution.py:86
  143.4 16.3 %collective-permute-start.30 = (bf16[192,1280]{1,0:T(8,128)(2,1)S(1)}, bf16[192,1280]{1,0:T(8,128)(2,1)S(1)}, u32[]{:S(2)}, u32[]{:S(2)}) collective-permute-start(bf16[192,1280]{1,0:T(8,128)(2,1)S(1)} %add_convert_fusion.3), channel_id=1, source_target_pairs={{2,0},{3,1},{0,2},{1,3},{6,4},{7,5},{4,6},{5,7},{10,8},{11,9},{8,1... | collective-permute-start | bytes 1474568 | tf_op jit(solution)/shard_map/ppermute | solution.py:79
  144.2 15.6 %collective-permute-start.31 = (bf16[48,1536]{1,0:T(8,128)(2,1)S(1)}, bf16[48,1536]{1,0:T(8,128)(2,1)S(1)}, u32[]{:S(2)}, u32[]{:S(2)}) collective-permute-start(bf16[48,1536]{1,0:T(8,128)(2,1)S(1)} %get-tuple-element.240), channel_id=1, source_target_pairs={{12,0},{13,1},{14,2},{15,3},{0,4},{1,5},{2,6},{3,7},{4,8},{5,9},{6... | collective-permute-start | bytes 442376 | tf_op jit(solution)/shard_map/ppermute | solution.py:75
  144.2 15.5 %collective-permute-start.32 = (bf16[48,1536]{1,0:T(8,128)(2,1)S(1)}, bf16[48,1536]{1,0:T(8,128)(2,1)S(1)}, u32[]{:S(2)}, u32[]{:S(2)}) collective-permute-start(bf16[48,1536]{1,0:T(8,128)(2,1)S(1)} %get-tuple-element.239), channel_id=1, source_target_pairs={{8,0},{9,1},{10,2},{11,3},{12,4},{13,5},{14,6},{15,7},{0,8},{1,9},... | collective-permute-start | bytes 442376 | tf_op jit(solution)/shard_map/ppermute | solution.py:75
  144.8 15.0 %collective-permute-start.33 = (bf16[48,1536]{1,0:T(8,128)(2,1)S(1)}, bf16[48,1536]{1,0:T(8,128)(2,1)S(1)}, u32[]{:S(2)}, u32[]{:S(2)}) collective-permute-start(bf16[48,1536]{1,0:T(8,128)(2,1)S(1)} %get-tuple-element.238), channel_id=1, source_target_pairs={{4,0},{5,1},{6,2},{7,3},{8,4},{9,5},{10,6},{11,7},{12,8},{13,9},{1... | collective-permute-start | bytes 442376 | tf_op jit(solution)/shard_map/ppermute | solution.py:75
  156.6 20.1 %collective-permute-start.40 = (bf16[512,768]{1,0:T(8,128)(2,1)}, bf16[512,768]{1,0:T(8,128)(2,1)}, u32[]{:S(2)}, u32[]{:S(2)}) collective-permute-start(bf16[512,768]{1,0:T(8,128)(2,1)} %get-tuple-element.210), channel_id=1, source_target_pairs={{0,16},{16,0},{1,17},{17,1},{2,18},{18,2},{3,19},{19,3},{4,20},{20... | collective-permute-start | bytes 2359304 | tf_op jit(solution)/shard_map/ppermute | solution.py:86
  160.8 11.3 %collective-permute-start.35 = (bf16[48,1280]{1,0:T(8,128)(2,1)}, bf16[48,1280]{1,0:T(8,128)(2,1)}, u32[]{:S(2)}, u32[]{:S(2)}) collective-permute-start(bf16[48,1280]{1,0:T(8,128)(2,1)} %get-tuple-element.243), channel_id=1, source_target_pairs={{12,0},{13,1},{14,2},{15,3},{0,4},{1,5},{2,6},{3,7},{4,8},{5,9},{6... | collective-permute-start | bytes 368648 | tf_op jit(solution)/shard_map/ppermute | solution.py:75
  161.4 10.7 %collective-permute-start.36 = (bf16[48,1280]{1,0:T(8,128)(2,1)}, bf16[48,1280]{1,0:T(8,128)(2,1)}, u32[]{:S(2)}, u32[]{:S(2)}) collective-permute-start(bf16[48,1280]{1,0:T(8,128)(2,1)} %get-tuple-element.242), channel_id=1, source_target_pairs={{8,0},{9,1},{10,2},{11,3},{12,4},{13,5},{14,6},{15,7},{0,8},{1,9},... | collective-permute-start | bytes 368648 | tf_op jit(solution)/shard_map/ppermute | solution.py:75
  165.8 19.9 %all-to-all-start.1 = ((bf16[16,48,240]{2,1,0:T(8,128)(2,1)}), bf16[16,48,240]{2,1,0:T(8,128)(2,1)}, u32[]{:S(2)}, u32[]{:S(2)}) async-start(bf16[16,48,240]{2,1,0:T(8,128)(2,1)} %copy-done.16), calls=%async_computation.1 | async-start | bytes 786432 | tf_op jit(solution)/shard_map/all_to_all | solution.py:1106
  171.5 9.3 %collective-permute-start.39 = (bf16[48,1536]{1,0:T(8,128)(2,1)S(1)}, bf16[48,1536]{1,0:T(8,128)(2,1)S(1)}, u32[]{:S(2)}, u32[]{:S(2)}) collective-permute-start(bf16[48,1536]{1,0:T(8,128)(2,1)S(1)} %add_convert_fusion.8.mlp_ref.own_ref), channel_id=1, source_target_pairs={{0,16},{16,0},{1,17},{17,1},{2,18},{18,2},{3,19},{19,3},{4,20},{20... | collective-permute-start | bytes 442376 | tf_op jit(solution)/shard_map/ppermute | solution.py:86
  181.5 14.8 %collective-permute-start.45 = (bf16[48,1280]{1,0:T(8,128)(2,1)}, bf16[48,1280]{1,0:T(8,128)(2,1)S(1)}, u32[]{:S(2)}, u32[]{:S(2)}) collective-permute-start(bf16[48,1280]{1,0:T(8,128)(2,1)} %add_convert_fusion.12.qkv_ref.own_ref), channel_id=1, source_target_pairs={{0,16},{16,0},{1,17},{17,1},{2,18},{18,2},{3,19},{19,3},{4,20},{20... | collective-permute-start | bytes 368648 | tf_op jit(solution)/shard_map/ppermute | solution.py:86
  (78 other events, 542.8 us)
